TPU v7x, 32 devices: a whole 2x2x4 slice. The times are simulated.
32 devices in a mesh: dp: 16 (over z, x, core), mp: 2 (over y).
Axes of the slice: x: 2, y: 2, z: 4, core: 2. Of those that a mesh axis runs over, the one named last changes fastest.
Arguments:
- tokens: bfloat16 [2, 16384, 768], P(None, ('dp', 'mp')), may hold values from -6 to 6
- lengths: int32 [16, 4], P('dp'), may hold values from 1 to 682, 1024 in all within a row
- block_size: int32 [1], replicated, may hold values from 4 to 16
- cotangent: bfloat16 [2, 16384, 768], P(None, ('dp', 'mp')), may hold values from -6 to 6
- ln1_gain: float32 [768], replicated, may hold values from 0.5 to 1.5
- ln1_bias: float32 [768], replicated, may hold values from -1.5 to 1.5
- w_qkv: bfloat16 [768, 3, 768], P(None, None, 'mp'), may hold values from -0.21875 to 0.21875
- w_out: bfloat16 [768, 768], P('mp'), may hold values from -0.875 to 0.875
- ln2_gain: float32 [768], replicated, may hold values from 0.5 to 1.5
- ln2_bias: float32 [768], replicated, may hold values from -1.5 to 1.5
- w_up: bfloat16 [768, 3072], P(None, 'mp'), may hold values from -0.21875 to 0.21875
- b_up: bfloat16 [3072], P('mp'), may hold values from -1.5 to 1.5
- w_down: bfloat16 [3072, 768], P('mp'), may hold values from -0.109375 to 0.109375
- b_down: float32 [768], replicated, may hold values from -1.5 to 1.5
Outputs:
- out: bfloat16 [2, 16384, 768], P(None, ('dp', 'mp'))
- grad_tokens: float32 [2, 16384, 768], P(None, ('dp', 'mp'))
- grad_ln1_gain: float32 [768], replicated
- grad_ln1_bias: float32 [768], replicated
- grad_w_qkv: float32 [768, 3, 768], P(None, None, 'mp')
- grad_w_out: float32 [768, 768], P('mp')
- grad_ln2_gain: float32 [768], replicated
- grad_ln2_bias: float32 [768], replicated
- grad_w_up: float32 [768, 3072], P(None, 'mp')
- grad_b_up: float32 [3072], P('mp')
- grad_w_down: float32 [3072, 768], P('mp')
- grad_b_down: float32 [768], replicated
Inputs may be any that keep to these rules, and one draw needn't show every extreme that they name: Each row lists the lengths of the 4 sequences packed in order into one pack of 1024 tokens; they sum to 1024 and the longest of each row is exactly 682.
All inputs are finite; a program needn't handle non-finite values.
Results may differ from a plain program's by a relative error of at most 0.011.
Values may be sent and summed in bfloat16 or wider, within the bound.
A program may use at most 256 MiB of HBM per device.

v0:
```python
import functools
import math

import jax
import jax.numpy as jnp
from jax import lax
from jax.experimental import pallas as pl
from jax.experimental.pallas import tpu as pltpu
from jax.sharding import PartitionSpec as P

HD = 64
TOK_DEV = 1024
HALF = TOK_DEV // 2
EDGE = 16
CLEAN_OWN = HALF
NOISY_BASE = 2 * HALF + EDGE
NOISY_OWN = NOISY_BASE + EDGE
KEY_ROWS = NOISY_OWN + HALF + EDGE
TILE = 128
TILES = HALF // TILE
WINDOW = TILE + 2 * EDGE
KEY_TILE = 192
LANES = 128
HIDDEN_TILE = 256
ROW_TILE = 256

epsilon = 1e-05
neg_large = -1e30
to_base2 = 0.125 * math.log2(math.e)
f32 = jnp.float32
bf16 = jnp.bfloat16

NN = (((1,), (0,)), ((), ()))
NT = (((1,), (1,)), ((), ()))


def dot(left, right, dims=NN):
    return lax.dot_general(left, right, dims, preferred_element_type=f32)


def low_lanes(shape):
    return lax.broadcasted_iota(jnp.int32, shape, 1) < HD


def turn(values, cosine, sine):
    lane = lax.broadcasted_iota(jnp.int32, values.shape, 1)
    first_half = (lane & (HD - 1)) < HD // 2
    swapped = jnp.where(
        first_half,
        pltpu.roll(values, LANES - HD // 2, 1),
        pltpu.roll(values, HD // 2, 1),
    )
    return values * cosine + swapped * sine


def project_rows(rows, w_ref, cosine, sine, q_ref, k_ref, v_ref, at):
    for part, out_ref in ((0, q_ref), (1, k_ref)):
        field = dot(rows, w_ref[part])
        for pair in range(field.shape[1] // LANES):
            cols = slice(pair * LANES, (pair + 1) * LANES)
            out_ref[at, cols] = turn(field[:, cols], cosine, sine).astype(bf16)
    v_ref[at, :] = dot(rows, w_ref[2]).astype(bf16)


def project_kernel(rows_ref, w_ref, cos_ref, sin_ref, q_ref, k_ref, v_ref):
    at = slice(0, rows_ref.shape[0])
    project_rows(rows_ref[...], w_ref, cos_ref[...], sin_ref[...], q_ref, k_ref, v_ref, at)


def project(rows, weights, cosine, sine):
    count, width = rows.shape
    cols = weights.shape[2]
    step = count // 3
    row_spec = pl.BlockSpec((step, width), lambda i: (i, 0))
    table_spec = pl.BlockSpec((step, LANES), lambda i: (i, 0))
    out_spec = pl.BlockSpec((step, cols), lambda i: (i, 0))
    shape = jax.ShapeDtypeStruct((count, cols), bf16)
    return pl.pallas_call(
        project_kernel,
        grid=(3,),
        in_specs=[
            row_spec,
            pl.BlockSpec(weights.shape, lambda i: (0, 0, 0)),
            table_spec,
            table_spec,
        ],
        out_specs=[out_spec] * 3,
        out_shape=[shape] * 3,
        name="project",
        cost_estimate=pl.CostEstimate(
            flops=2 * count * width * 3 * cols,
            bytes_accessed=2 * (count * (width + 3 * cols) + 3 * width * cols),
            transcendentals=0,
        ),
    )(rows, weights, cosine, sine)


def normal(values):
    average = jnp.mean(values, axis=-1, keepdims=True)
    centred = values - average
    variance = jnp.mean(centred * centred, axis=-1, keepdims=True)
    scale = lax.rsqrt(variance + epsilon)
    return centred * scale, scale


def enter_kernel(
    tokens_ref,
    context_ref,
    vectors_ref,
    w_ref,
    cos_ref,
    sin_ref,
    rows_ref,
    rows_t_ref,
    q_ref,
    k_ref,
    v_ref,
):
    def norm(values):
        unit = normal(values.astype(f32))[0]
        return (unit * vectors_ref[0:1, :] + vectors_ref[1:2, :]).astype(bf16)

    def blocks(i, _):
        source = pl.ds(pl.multiple_of(i * TILE, TILE), TILE)
        rows_ref[source, :] = norm(context_ref[source, :])
        at = pl.ds(pl.multiple_of(CLEAN_OWN + i * TILE, TILE), TILE)
        rows_ref[at, :] = norm(tokens_ref[1, source, :])
        at = pl.ds(pl.multiple_of(NOISY_OWN + i * TILE, EDGE), TILE)
        rows_ref[at, :] = norm(tokens_ref[0, source, :])
        return 0

    lax.fori_loop(0, TILES, blocks, 0)
    rows_ref[2 * HALF : NOISY_BASE, :] = rows_ref[:EDGE, :]
    edge = norm(context_ref[HALF:, :])
    rows_ref[NOISY_BASE:NOISY_OWN, :] = edge
    rows_ref[NOISY_OWN + HALF :, :] = edge
    step = KEY_ROWS // 3

    def fields(i, _):
        at = pl.ds(pl.multiple_of(i * step, EDGE), step)
        project_rows(
            rows_ref[at, :], w_ref, cos_ref[at, :], sin_ref[at, :], q_ref, k_ref, v_ref, at
        )
        return 0

    lax.fori_loop(0, 3, fields, 0)
    for c in range(rows_t_ref.shape[0] // LANES):
        cols = slice(c * LANES, (c + 1) * LANES)
        rows_t_ref[cols, :] = rows_ref[:, cols].T


def enter(tokens, context, vectors, weights, cosine, sine):
    width, cols = weights.shape[1:]
    vmem = pl.BlockSpec(memory_space=pltpu.VMEM)
    shape = jax.ShapeDtypeStruct
    field = shape((KEY_ROWS, cols), bf16)
    return pl.pallas_call(
        enter_kernel,
        in_specs=[vmem] * 6,
        out_specs=[vmem] * 5,
        out_shape=[shape((KEY_ROWS, width), bf16), shape((width, KEY_ROWS), bf16)] + [field] * 3,
        name="enter",
        cost_estimate=pl.CostEstimate(
            flops=10**10, bytes_accessed=16 * 10**6, transcendentals=0
        ),
    )(tokens, context, vectors, weights, cosine, sine)


def split_heads(rows):
    low = low_lanes(rows.shape)
    zero = jnp.zeros_like(rows)
    return jnp.where(low, rows, zero), jnp.where(low, zero, rows)


def between(shape, offset, low, high):
    index = lax.broadcasted_iota(jnp.int32, shape, 0) + offset
    return jnp.logical_and(index >= low, index < high)


def fold(values, combine):
    rows, cols = values.shape
    groups = values.reshape(rows // 8, 8, cols)
    return combine(groups, axis=0)


def forward_kernel(
    span_ref, clean_ref, noisy_ref, q_ref, k_ref, v_ref, out_ref, lse_ref, bias_ref, window_ref
):
    pairs = q_ref.shape[1] // LANES
    lanes = [slice(p * LANES, (p + 1) * LANES) for p in range(pairs)]

    def one_tile(t, _):
        clean_at = pl.multiple_of(CLEAN_OWN + t * TILE, TILE)
        noisy_at = pl.multiple_of(NOISY_OWN + t * TILE, EDGE)
        window_at = pl.multiple_of(NOISY_BASE + t * TILE, EDGE)
        key_low, key_high = clean_ref[t, 0:1, :], clean_ref[t, 1:2, :]
        own_low, own_high = noisy_ref[t, 0:1, :], noisy_ref[t, 1:2, :]
        allowed = between((WINDOW, TILE), 0, own_low, own_high)
        window_ref[...] = jnp.where(allowed, 0.0, neg_large)
        first_key, trips = span_ref[t, 0], span_ref[t, 1]
        queries, tops = [], []
        for cols in lanes:
            query = jnp.concatenate(
                [q_ref[pl.ds(noisy_at, TILE), cols], q_ref[pl.ds(clean_at, TILE), cols]], axis=0
            )
            heads = split_heads(query)
            queries += heads
            keys = k_ref[pl.ds(window_at, WINDOW), cols]
            for head in range(2):
                scores = dot(keys, heads[head][:TILE], NT) + window_ref[...]
                top = fold(scores, jnp.max)
                tops.append(
                    jnp.concatenate([top, jnp.full((8, TILE), neg_large, f32)], axis=1)
                )

        def first_pass(j, tops):
            at = pl.multiple_of(first_key + j * KEY_TILE, EDGE)
            allowed = between((KEY_TILE, 2 * TILE), at, key_low, key_high)
            bias_ref[j] = jnp.where(allowed, 0.0, neg_large)
            after = []
            for p, cols in enumerate(lanes):
                keys = k_ref[pl.ds(at, KEY_TILE), cols]
                for head in range(2):
                    scores = dot(keys, queries[2 * p + head], NT) + bias_ref[j]
                    after.append(jnp.maximum(tops[2 * p + head], fold(scores, jnp.max)))
            return tuple(after)

        tops = lax.fori_loop(0, trips, first_pass, tuple(tops))
        tops = [jnp.max(top, axis=0, keepdims=True) * to_base2 for top in tops]
        state = []
        keys = [k_ref[pl.ds(window_at, WINDOW), cols] for cols in lanes]
        values_t = [v_ref[pl.ds(window_at, WINDOW), cols].T for cols in lanes]
        scores = dot(keys[0], queries[0][:TILE], NT)
        late = None
        for h in range(2 * pairs):
            if h + 1 < 2 * pairs:
                ahead = dot(keys[(h + 1) // 2], queries[h + 1][:TILE], NT)
            expo = jnp.exp2(scores * to_base2 - tops[h][:, :TILE] + window_ref[...])
            if late is not None:
                state.append(jnp.concatenate([late, jnp.zeros((HD, TILE), f32)], axis=1))
            total = fold(expo, jnp.sum)
            state.append(jnp.concatenate([total, jnp.zeros((8, TILE), f32)], axis=1))
            side = slice(h % 2 * HD, (h % 2 + 1) * HD)
            late = dot(values_t[h // 2][side], expo.astype(bf16))
            scores = ahead
        state.append(jnp.concatenate([late, jnp.zeros((HD, TILE), f32)], axis=1))

        def second_pass(j, state):
            at = pl.multiple_of(first_key + j * KEY_TILE, EDGE)
            keys = [k_ref[pl.ds(at, KEY_TILE), cols] for cols in lanes]
            values_t = [v_ref[pl.ds(at, KEY_TILE), cols].T for cols in lanes]
            after = list(state)
            scores = dot(keys[0], queries[0], NT)
            late = None
            for h in range(2 * pairs):
                ahead = dot(keys[(h + 1) // 2], queries[h + 1], NT) if h + 1 < 2 * pairs else None
                expo = jnp.exp2(scores * to_base2 - tops[h] + bias_ref[j])
                after[2 * h] = state[2 * h] + fold(expo, jnp.sum)
                if late is not None:
                    after[2 * h - 1] = state[2 * h - 1] + late
                side = slice(h % 2 * HD, (h % 2 + 1) * HD)
                late = dot(values_t[h // 2][side], expo.astype(bf16))
                scores = ahead
            after[-1] = state[-1] + late
            return tuple(after)

        state = lax.fori_loop(0, trips, second_pass, tuple(state))
        low_at = pl.ds(pl.multiple_of(t * TILE, TILE), TILE)
        high_at = pl.ds(pl.multiple_of(HALF + t * TILE, TILE), TILE)
        for p, cols in enumerate(lanes):
            halves = []
            for head in range(2):
                h = 2 * p + head
                total = jnp.sum(state[2 * h], axis=0, keepdims=True)
                halves.append(state[2 * h + 1] / total)
                lse_ref[p, t, head : head + 1, :] = tops[h] + jnp.log2(total)
            pair = jnp.concatenate(halves, axis=0).T.astype(bf16)
            out_ref[low_at, cols] = pair[:TILE]
            out_ref[high_at, cols] = pair[TILE:]
        return 0

    lax.fori_loop(0, TILES, one_tile, 0)


def attend_forward(spans, clean_bounds, noisy_bounds, query, keys, values):
    count, cols = query.shape
    pairs = cols // LANES
    vmem = pl.BlockSpec(memory_space=pltpu.VMEM)
    work = pairs * 2 * 2 * HALF * TOK_DEV
    return pl.pallas_call(
        forward_kernel,
        in_specs=[pl.BlockSpec(memory_space=pltpu.SMEM)] + [vmem] * 5,
        out_specs=[vmem] * 2,
        out_shape=[
            jax.ShapeDtypeStruct((TOK_DEV, cols), bf16),
            jax.ShapeDtypeStruct((pairs, TILES, 2, 2 * TILE), f32),
        ],
        scratch_shapes=[
            pltpu.VMEM((NOISY_BASE // KEY_TILE + 1, KEY_TILE, 2 * TILE), f32),
            pltpu.VMEM((WINDOW, TILE), f32),
        ],
        name="attend_forward",
        cost_estimate=pl.CostEstimate(
            flops=4 * work * HD, bytes_accessed=8 * count * cols, transcendentals=work
        ),
    )(spans, clean_bounds, noisy_bounds, query, keys, values)


def backward_kernel(
    span_ref,
    clean_ref,
    noisy_ref,
    q_ref,
    k_ref,
    v_ref,
    o_ref,
    d_ref,
    lse_ref,
    cos_ref,
    sin_ref,
    rows_ref,
    out_ref,
    grad_ref,
    dk_ref,
    dv_ref,
    bias_ref,
):
    pairs = q_ref.shape[1] // LANES
    lanes = [slice(p * LANES, (p + 1) * LANES) for p in range(pairs)]
    dk_ref[...] = jnp.zeros_like(dk_ref)
    dv_ref[...] = jnp.zeros_like(dv_ref)
    out_ref[0] = jnp.zeros_like(out_ref[0])

    def one_tile(t, _):
        clean_at = pl.multiple_of(CLEAN_OWN + t * TILE, TILE)
        noisy_at = pl.multiple_of(NOISY_OWN + t * TILE, EDGE)
        window_at = pl.multiple_of(NOISY_BASE + t * TILE, EDGE)
        low_at = pl.multiple_of(t * TILE, TILE)
        high_at = pl.multiple_of(HALF + t * TILE, TILE)
        key_low, key_high = clean_ref[t, 0:1, :], clean_ref[t, 1:2, :]
        own_low, own_high = noisy_ref[t, 0:1, :], noisy_ref[t, 1:2, :]
        queries, d_outs, inners, lses = [], [], [], []
        for p, cols in enumerate(lanes):

            def both(ref, low, high):
                return jnp.concatenate(
                    [ref[pl.ds(low, TILE), cols], ref[pl.ds(high, TILE), cols]], axis=0
                )

            queries.append(split_heads(both(q_ref, noisy_at, clean_at)))
            d_rows = both(d_ref, low_at, high_at)
            o_rows = both(o_ref, low_at, high_at)
            product = (d_rows.astype(f32) * o_rows.astype(f32)).T
            d_outs.append(split_heads(d_rows))
            inners.append(
                [
                    jnp.sum(product[head * HD : (head + 1) * HD], axis=0, keepdims=True) * 0.125
                    for head in range(2)
                ]
            )
            lses.append([lse_ref[p, t, head : head + 1, :] for head in range(2)])

        def accumulate(at, rows, cols, allowed, d_query):
            bias_ref[:rows, :cols] = jnp.where(allowed, 0.0, neg_large)
            after = list(d_query)
            keys = [k_ref[pl.ds(at, rows), span] for span in lanes]
            eighth = [v_ref[pl.ds(at, rows), span] * jnp.asarray(0.125, bf16) for span in lanes]
            keys_t = [part.T for part in keys]
            stack = lambda parts: jnp.concatenate([part[:cols] for part in parts], axis=0)

            def begin(h):
                p, head = h // 2, h % 2
                return (
                    dot(keys[p], queries[p][head][:cols], NT),
                    dot(eighth[p], d_outs[p][head][:cols], NT),
                )

            def finish_pair(p, weights, d_scores):
                span = lanes[p]
                for head in range(2):
                    side = slice(head * HD, (head + 1) * HD)
                    h = 2 * p + head
                    after[h] = d_query[h] + dot(keys_t[p][side], d_scores[head])
                dv_ref[pl.ds(at, rows), span] += dot(
                    jnp.concatenate(weights, axis=1), stack(d_outs[p])
                )
                dk_ref[pl.ds(at, rows), span] += dot(
                    jnp.concatenate(d_scores, axis=1), stack(queries[p])
                )

            ready = begin(0)
            held = None
            weights, d_scores = [], []
            for h in range(2 * pairs):
                ahead = begin(h + 1) if h + 1 < 2 * pairs else None
                p, head = h // 2, h % 2
                scores = ready[0] * to_base2 - lses[p][head][:, :cols] + bias_ref[:rows, :cols]
                probs = jnp.exp2(scores)
                d_score = (probs * (ready[1] - inners[p][head][:, :cols])).astype(bf16)
                weights.append(probs.astype(bf16))
                d_scores.append(d_score)
                if held is not None:
                    finish_pair(*held)
                    held = None
                if head == 1:
                    held = (p, weights, d_scores)
                    weights, d_scores = [], []
                ready = ahead
            finish_pair(*held)
            return tuple(after)

        allowed = between((WINDOW, TILE), 0, own_low, own_high)
        zero = jnp.zeros((HD, TILE), f32)
        start = accumulate(window_at, WINDOW, TILE, allowed, (zero,) * (2 * pairs))
        start = tuple(jnp.concatenate([part, zero], axis=1) for part in start)
        first_key, trips = span_ref[t, 0], span_ref[t, 1]

        def one_step(j, d_query):
            at = pl.multiple_of(first_key + j * KEY_TILE, EDGE)
            allowed = between((KEY_TILE, 2 * TILE), at, key_low, key_high)
            return accumulate(at, KEY_TILE, 2 * TILE, allowed, d_query)

        d_query = lax.fori_loop(0, trips, one_step, start)
        for p, span in enumerate(lanes):
            pair = jnp.concatenate(d_query[2 * p : 2 * p + 2], axis=0).T
            for at, part in ((noisy_at, pair[:TILE]), (clean_at, pair[TILE:])):
                turned = turn(part, cos_ref[pl.ds(at, TILE), :], -sin_ref[pl.ds(at, TILE), :])
                out_ref[0, pl.ds(at, TILE), span] = turned.astype(bf16)
        return 0

    lax.fori_loop(0, TILES, one_tile, 0)
    step = KEY_ROWS // 9

    def finish(i, _):
        rows = pl.ds(pl.multiple_of(i * step, EDGE), step)
        for span in lanes:
            out_ref[1, rows, span] = turn(
                dk_ref[rows, span], cos_ref[rows, :], -sin_ref[rows, :]
            ).astype(bf16)
        out_ref[2, rows, :] = dv_ref[rows, :].astype(bf16)
        return 0

    lax.fori_loop(0, 9, finish, 0)

    def weight_rows(i, _):
        rows = pl.ds(pl.multiple_of(i * ROW_TILE, LANES), ROW_TILE)
        for c in range(3):
            grad_ref[c, rows, :] = dot(rows_ref[rows, :], out_ref[c]).astype(bf16)
        return 0

    lax.fori_loop(0, rows_ref.shape[0] // ROW_TILE, weight_rows, 0)


def attend_backward(
    spans,
    clean_bounds,
    noisy_bounds,
    query,
    keys,
    values,
    attended,
    d_attended,
    lse,
    cosine,
    sine,
    rows_t,
):
    count, cols = query.shape
    width = rows_t.shape[0]
    vmem = pl.BlockSpec(memory_space=pltpu.VMEM)
    return pl.pallas_call(
        backward_kernel,
        in_specs=[pl.BlockSpec(memory_space=pltpu.SMEM)] + [vmem] * 11,
        out_specs=[vmem] * 2,
        scratch_shapes=[
            pltpu.VMEM((count, cols), f32),
            pltpu.VMEM((count, cols), f32),
            pltpu.VMEM((max(KEY_TILE, WINDOW), 2 * TILE), f32),
        ],
        out_shape=[
            jax.ShapeDtypeStruct((3, count, cols), bf16),
            jax.ShapeDtypeStruct((3, width, cols), bf16),
        ],
        name="attend_backward",
        cost_estimate=pl.CostEstimate(
            flops=36 * 10**9, bytes_accessed=36 * 10**6, transcendentals=6 * 10**6
        ),
    )(
        spans,
        clean_bounds,
        noisy_bounds,
        query,
        keys,
        values,
        attended,
        d_attended,
        lse,
        cosine,
        sine,
        rows_t,
    )


PIECES = 16
MESH = pl.DeviceIdType.MESH


def flip(value, mask):
    result = value
    for b in range(mask.bit_length()):
        if mask >> b & 1:
            result = result + (1 << b) * (1 - 2 * ((value // (1 << b)) % 2))
    return result


class Exchange:
    def __init__(self, bits, count, rows, width, back=True):
        self.bits, self.count, self.rows, self.width = bits, count, rows, width
        self.back = back
        self.half, self.quarter, self.piece = rows // 2, rows // 4, rows // PIECES
        self.extra = list(range(4, bits))

    def slots(self):
        return 8 + 2 * (6 if self.back else 4) + (3 if self.extra else 0)

    def scratch(self):
        k, w = self.count, self.width
        cross = k if not self.back else 1
        shapes = [
            pltpu.VMEM((k, 2 - self.back, self.half, w), bf16),
            pltpu.VMEM((cross, self.half, w), bf16),
            pltpu.VMEM((cross, self.half, w), bf16),
            pltpu.VMEM((k, self.quarter, w), bf16),
            pltpu.VMEM((k, self.quarter, w), bf16),
            pltpu.VMEM((k, self.quarter, w), f32),
            pltpu.VMEM((k, 3, self.piece, w), bf16),
            pltpu.VMEM((k, 3, self.piece, w), bf16),
        ]
        lanes_of = (1, 0, 1, 3, 3, 1, 1) if self.back else (2, 1, 1, 3, 0, 0, 0)
        for lanes in [lanes for lanes in lanes_of if lanes]:
            shapes += [pltpu.SemaphoreType.DMA((k, lanes))] * 2
        if self.extra:
            n = len(self.extra)
            shapes += [pltpu.VMEM((k, 2 * n, self.piece, w), bf16)]
            shapes += [pltpu.SemaphoreType.DMA((k, n))] * 2
        return shapes

    def bind(self, place, part, refs):
        (self.a_in, self.b_out, self.b_in, self.c_out, self.c_in, self.keep) = refs[:6]
        self.d_out, self.d_in = refs[6:8]
        names = "acdefg" if self.back else "abcd"
        self.sems = {name: (refs[8 + 2 * i], refs[9 + 2 * i]) for i, name in enumerate(names)}
        if self.extra:
            at = 8 + 2 * len(names)
            self.x_buf, self.x_send, self.x_recv = refs[at : at + 3]
        self.place, self.part = place, part
        self.core, self.x, self.z = place % 2, (place // 2) % 2, (place // 4) % 4
        self.sibling = {"dp": flip(place, 1)}
        self.beside = {"dp": flip(place, 2)}
        self.across = {"mp": 1 - part}
        self.peers = [{"dp": flip(place, j << 2)} for j in range(1, 4)]
        self.partners = [self.sibling, self.beside, self.across] + self.peers
        self.partners += [{"dp": flip(place, 1 << b)} for b in self.extra]
        return self

    def greet(self):
        barrier = pltpu.get_barrier_semaphore()
        for partner in self.partners:
            pl.semaphore_signal(barrier, inc=1, device_id=partner, device_id_type=MESH)
        pl.semaphore_wait(barrier, len(self.partners))

    def copy(self, name, k, lane, source, target, device):
        out, into = self.sems[name]
        return pltpu.make_async_remote_copy(
            src_ref=source,
            dst_ref=target,
            send_sem=out.at[k, lane],
            recv_sem=into.at[k, lane],
            device_id=device,
            device_id_type=MESH,
        )

    def rows_at(self, start, size):
        return pl.ds(pl.multiple_of(start, PIECES), size)

    def copy_a(self, k, lane, grads):
        source = grads.at[k, self.rows_at((1 - self.core) * self.half, self.half)]
        return self.copy("a", k, lane, source, self.a_in.at[k, lane], self.sibling)

    def copy_b(self, k):
        return self.copy("b", k, 0, self.b_out.at[k], self.b_in.at[k], self.across)

    def copy_c(self, k):
        return self.copy("c", k, 0, self.c_out.at[k], self.c_in.at[k], self.beside)

    def copy_d(self, k, j):
        return self.copy("d", k, j, self.d_out.at[k, j], self.d_in.at[k, j], self.peers[j])

    def spot(self, change=0):
        start = self.core * self.half + self.x * self.quarter
        return self.rows_at(start + flip(self.z, change) * self.piece, self.piece)

    def copy_e(self, k, j, full):
        rows = full.at[k, self.spot()]
        return self.copy("e", k, j, rows, rows, self.peers[j])

    def copy_f(self, k, full):
        start = self.core * self.half + self.x * self.quarter
        rows = full.at[k, self.rows_at(start, self.quarter)]
        return self.copy("f", k, 0, rows, rows, self.beside)

    def copy_g(self, k, full):
        rows = full.at[k, self.rows_at(self.core * self.half, self.half)]
        return self.copy("g", k, 0, rows, rows, self.sibling)

    def start_a(self, k, lane, grads):
        self.copy_a(k, lane, grads).start()

    def stage_b(self, k, others):
        self.copy_a(k, 0, others).wait()
        mine = others[k, self.rows_at(self.core * self.half, self.half), :].astype(f32)
        self.b_out[k] = (mine + self.a_in[k, 0].astype(f32)).astype(bf16)
        self.copy_b(k).start()

    def stage_c(self, k, grads, crossed=None):
        lane = 0 if self.back else 1
        self.copy_a(k, lane, grads).wait()
        if not self.back:
            self.copy_b(k).wait()

        def total(which):
            inner = which * self.quarter
            rows = self.rows_at(inner, self.quarter)
            mine = grads[k, self.rows_at(self.core * self.half + inner, self.quarter), :]
            got = self.a_in[k, lane, rows, :].astype(f32)
            if not self.back:
                got = got + self.b_in[k, rows, :].astype(f32)
            elif crossed is not None:
                got = got + crossed(rows)
            return mine.astype(f32) + got

        self.c_out[k] = total(1 - self.x).astype(bf16)
        self.copy_c(k).start()
        self.keep[k] = total(self.x)

    def stage_d(self, k):
        self.copy_c(k).wait()
        for j in range(4):
            rows = self.rows_at(flip(self.z, j) * self.piece, self.piece)
            total = self.keep[k, rows, :] + self.c_in[k, rows, :].astype(f32)
            if j:
                self.d_out[k, j - 1] = total.astype(bf16)
                self.copy_d(k, j - 1).start()
            else:
                self.keep[k, rows, :] = total

    def gather_d(self, k):
        rows = self.rows_at(self.z * self.piece, self.piece)
        total = self.keep[k, rows, :]
        for j in range(3):
            self.copy_d(k, j).wait()
            total = total + self.d_in[k, j].astype(f32)
        for i, b in enumerate(self.extra):
            mine = self.x_buf.at[k, 2 * i]
            mine[...] = total.astype(bf16)
            swap = pltpu.make_async_remote_copy(
                src_ref=mine,
                dst_ref=self.x_buf.at[k, 2 * i + 1],
                send_sem=self.x_send.at[k, i],
                recv_sem=self.x_recv.at[k, i],
                device_id={"dp": flip(self.place, 1 << b)},
                device_id_type=MESH,
            )
            swap.start()
            swap.wait()
            total = total.astype(bf16).astype(f32) + self.x_buf[k, 2 * i + 1].astype(f32)
        return total.astype(bf16)

    def stage_e(self, k, full):
        full[k, self.spot(), :] = self.gather_d(k)
        for j in range(3):
            self.copy_e(k, j, full).start()

    def stage_f(self, k, full):
        for j in range(3):
            self.copy_e(k, j, full).wait()
        self.copy_f(k, full).start()

    def stage_g(self, k, full):
        self.copy_f(k, full).wait()
        self.copy_g(k, full).start()

    def stage_h(self, k, full):
        self.copy_g(k, full).wait()


def at_step(step, count, action):
    @pl.when(jnp.logical_and(step >= 0, step < count))
    def _():
        action(step)


def middle_kernel(exchanges, tiles, *refs):
    (
        x_ref,
        att_ref,
        att2_ref,
        wout_ref,
        wout2_ref,
        dy_ref,
        vectors_ref,
        bup_ref,
        up_mine,
        up_here,
        up_beside,
        down_mine,
        down_here,
        down_beside,
        out_ref,
        mid_ref,
        datt_ref,
        datt2_ref,
        gout_ref,
        gout2_ref,
        gbup_ref,
        small_ref,
        pieces_ref,
        up_there,
        down_there,
        pass_up,
        pass_down,
        up_buf,
        down_buf,
        load_sem,
        n2_ref,
        total_ref,
        dn2_ref,
        act_ref,
        dpre_ref,
        n2_t,
        down_grad,
        up_grad,
        *rest,
    ) = refs
    place, part = lax.axis_index("dp"), lax.axis_index("mp")
    ex = exchanges[0].bind(place, part, rest)
    ex_up = exchanges[1].bind(place, part, rest[exchanges[0].slots() :])
    sides = ((ex, down_grad), (ex_up, up_grad))
    core = ex.core
    count = tiles // 2
    rows_all = x_ref.shape[0]
    blocks = rows_all // ROW_TILE
    width = x_ref.shape[1]
    lanes = width // 2

    def which(i):
        other = jnp.logical_or(i == 0, jnp.logical_and(i % 2 == 1, i < tiles - 1))
        mine = jnp.where(i == tiles - 1, count - 1, i // 2 - 1)
        return other, jnp.where(other, (i + 1) // 2, mine)

    quarter = width // 4
    strip = HIDDEN_TILE // 2
    held = 2 * core + ex.x
    kept = 2 * core + 1 - ex.x

    def load_up(i, source, h):
        target = up_buf.at[i % 2, h * quarter : (h + 1) * quarter]
        return pltpu.make_async_copy(source, target, load_sem.at[i % 2, h])

    def load_down(i, source, h):
        target = down_buf.at[i % 2, h * strip : (h + 1) * strip]
        return pltpu.make_async_copy(source, target, load_sem.at[i % 2, 4 + h])

    def hand_up(k, part_of):
        cols = pl.ds(pl.multiple_of(k * HIDDEN_TILE, HIDDEN_TILE), HIDDEN_TILE)
        side = ex.x if part_of == 0 else 1 - ex.x
        rows = pl.ds(pl.multiple_of(side * quarter, EDGE), quarter)
        return pltpu.make_async_remote_copy(
            src_ref=(up_here, up_beside)[part_of].at[:, cols],
            dst_ref=up_there.at[k, rows],
            send_sem=pass_up.at[k, 2 * part_of],
            recv_sem=pass_up.at[k, 2 * part_of + 1],
            device_id=ex.sibling,
            device_id_type=MESH,
        )

    def hand_down(b, part_of):
        side = ex.x if part_of == 0 else 1 - ex.x
        return pltpu.make_async_remote_copy(
            src_ref=(down_here, down_beside)[part_of].at[strip_rows(b)],
            dst_ref=down_there.at[side * (count // 2) + b],
            send_sem=pass_down.at[side * (count // 2) + b, 0],
            recv_sem=pass_down.at[side * (count // 2) + b, 1],
            device_id=ex.sibling,
            device_id_type=MESH,
        )

    def strip_rows(b):
        return pl.ds(pl.multiple_of(b * strip, strip), strip)

    def got_down(slot):
        return pltpu.make_async_remote_copy(
            src_ref=down_there.at[slot],
            dst_ref=down_there.at[slot],
            send_sem=pass_down.at[slot, 0],
            recv_sem=pass_down.at[slot, 1],
            device_id=ex.sibling,
            device_id_type=MESH,
        )

    def start_loads(i):
        other, k = which(i)
        mine = jnp.logical_not(other)
        cols = pl.ds(pl.multiple_of(k * HIDDEN_TILE, HIDDEN_TILE), HIDDEN_TILE)
        span = count // 2

        @pl.when(other)
        def _():
            hand_up(k, 0).wait()
            hand_up(k, 1).wait()

        for h in range(4):

            @pl.when(mine)
            def _():
                load_up(i, up_mine.at[h * quarter : (h + 1) * quarter, cols], h).start()

            @pl.when(jnp.logical_and(other, held == h))
            def _():
                load_up(i, up_here.at[:, cols], h).start()

            @pl.when(jnp.logical_and(other, kept == h))
            def _():
                load_up(i, up_beside.at[:, cols], h).start()

            @pl.when(jnp.logical_and(other, core != h // 2))
            def _():
                rows = slice(h % 2 * quarter, (h % 2 + 1) * quarter)
                load_up(i, up_there.at[k, rows], h).start()

        for h in range(2):
            b = 2 * k + h
            piece, inner = b // span, b % span

            @pl.when(mine)
            def _():
                load_down(i, down_mine.at[strip_rows(b), :], h).start()

            @pl.when(jnp.logical_and(other, held == piece))
            def _():
                load_down(i, down_here.at[strip_rows(inner), :], h).start()

            @pl.when(jnp.logical_and(other, kept == piece))
            def _():
                load_down(i, down_beside.at[strip_rows(inner), :], h).start()

            @pl.when(jnp.logical_and(other, core != piece // 2))
            def _():
                slot = piece % 2 * span + inner
                got_down(slot).wait_recv()
                load_down(i, down_there.at[slot], h).start()

    def wait_loads(i):
        for h in range(4):
            load_up(i, up_mine.at[:quarter, :HIDDEN_TILE], h).wait()
        for h in range(2):
            load_down(i, down_mine.at[:strip, :], h).wait()

    ex.greet()

    def hand(k, _):
        hand_up(k, 0).start()
        hand_up(k, 1).start()

        @pl.when(k < count // 2)
        def _():
            hand_down(k, 0).start()
            hand_down(k, 1).start()

        return 0

    lax.fori_loop(0, count, hand, 0)

    def prologue(r, _):
        rows = pl.ds(pl.multiple_of(r * ROW_TILE, ROW_TILE), ROW_TILE)
        branch = dot(att_ref[rows, :], wout_ref[...]) + dot(att2_ref[rows, :], wout2_ref[...])
        mid = x_ref[rows, :].astype(f32) + branch
        mid_ref[rows, :] = mid
        unit = normal(mid)[0]
        n2_ref[rows, :] = (unit * vectors_ref[2:3, :] + vectors_ref[3:4, :]).astype(bf16)
        total_ref[rows, :] = mid + vectors_ref[4:5, :]
        dn2_ref[rows, :] = jnp.zeros((ROW_TILE, width), f32)
        return 0

    lax.fori_loop(0, blocks, prologue, 0)
    start_loads(0)
    for c in range(width // LANES):
        cols = slice(c * LANES, (c + 1) * LANES)
        n2_t[cols, :] = n2_ref[:, cols].T

    def tile(i):
        other, k = which(i)
        slot = i % 2
        wait_loads(i)

        @pl.when(i + 1 < tiles)
        def _():
            start_loads(i + 1)

        up, down = up_buf.at[slot], down_buf.at[slot]
        bias_at = jnp.where(other, k, count + k)
        bias_grad = jnp.zeros((1, HIDDEN_TILE), f32)
        block = lambda r: slice(r * ROW_TILE, (r + 1) * ROW_TILE)

        def begin(r):
            return dot(n2_ref[block(r), :], up[...]), dot(dy_ref[block(r), :], down[...], NT)

        ready = begin(0)
        for r in range(blocks):
            rows = block(r)
            ahead = begin(r + 1) if r + 1 < blocks else None
            pre = ready[0] + bup_ref[bias_at]
            square = pre * pre
            bend = jnp.tanh(0.7978845608028654 * (pre + 0.044715 * square * pre))
            part_one = 0.5 * (1.0 + bend)
            act = (pre * part_one).astype(bf16)
            slope = part_one + (0.5 * pre) * (1.0 - bend * bend) * (
                0.7978845608028654 * (1.0 + 3.0 * 0.044715 * square)
            )
            d_pre = (ready[1] * slope).astype(bf16)
            act_ref[rows, :] = act
            dpre_ref[rows, :] = d_pre
            bias_grad = bias_grad + jnp.sum(d_pre.astype(f32), axis=0, keepdims=True)
            total_ref[rows, :] += dot(act, down[...])
            dn2_ref[rows, :] += dot(d_pre, up[...], NT)
            ready = ahead
        gbup_ref[bias_at] = bias_grad
        down_grad[k] = dot(act_ref[...].T, dy_ref[...]).astype(bf16)

        def start(lane):
            for side, grad in sides:
                side.start_a(k, lane, grad)

        up_grad[k] = dot(n2_t[...], dpre_ref[...]).astype(bf16)
        pl.when(other)(functools.partial(start, 0))
        pl.when(jnp.logical_not(other))(functools.partial(start, 1))

    def each(k, when, action):
        @pl.when(jnp.logical_and(when, jnp.logical_and(k >= 0, k < count)))
        def _():
            for n, (side, grad) in enumerate(sides):
                action(n, side, grad, k)

    def stage_b(n, side, grad, k):
        side.stage_b(k, grad)

    def stage_c(n, side, grad, k):
        side.stage_c(k, grad)

    def stage_d(n, side, grad, k):
        side.stage_d(k)

    def arrive(n, side, grad, k):
        piece = side.gather_d(k)
        if n == 0:
            pieces_ref[k] = piece
        else:
            for c in range(width // HIDDEN_TILE):
                cols = slice(c * HIDDEN_TILE, (c + 1) * HIDDEN_TILE)
                pieces_ref[count + k, :, cols] = piece[c * PIECES : (c + 1) * PIECES]

    def steps(i):
        even = i % 2 == 0
        odd = jnp.logical_not(even)
        each((i - 6) // 2, even, arrive)
        each((i - 5) // 2, odd, stage_d)
        each((i - 4) // 2, even, stage_c)
        crossing = jnp.logical_or(i == 1, jnp.logical_and(even, i >= 2))
        each(i // 2, crossing, stage_b)

    def epilogue(r, _):
        rows = pl.ds(pl.multiple_of(r * ROW_TILE, ROW_TILE), ROW_TILE)
        out_ref[rows, :] = total_ref[rows, :].astype(bf16)
        unit, scale = normal(mid_ref[rows, :])
        d_rows = dn2_ref[rows, :]
        dy = dy_ref[rows, :].astype(f32)
        lean = d_rows * vectors_ref[2:3, :]
        d_mid = dy + scale * (
            lean
            - jnp.mean(lean, axis=-1, keepdims=True)
            - unit * jnp.mean(lean * unit, axis=-1, keepdims=True)
        )
        mid_ref[rows, :] = d_mid
        d_branch = d_mid.astype(bf16)
        n2_ref[rows, :] = d_branch
        datt_ref[rows, :] = dot(d_branch, wout_ref[...], NT).astype(bf16)
        datt2_ref[rows, :] = dot(d_branch, wout2_ref[...], NT).astype(bf16)
        add = lambda values: jnp.sum(values, axis=0, keepdims=True)
        small_ref[0:1, :] += add(d_rows * unit)
        small_ref[1:2, :] += add(d_rows)
        small_ref[2:3, :] += add(dy)
        return 0

    def out_grads():
        depth = wout_ref.shape[0]
        for source, target in ((att_ref, gout_ref), (att2_ref, gout2_ref)):
            grad = dot(source[...].T, n2_ref[...]).astype(bf16)
            target[:depth, :] = grad[:, :lanes]
            target[depth:, :] = grad[:, lanes:]

    def main(i, _):
        pl.when(i < tiles)(functools.partial(tile, i))

        @pl.when(jnp.logical_and(i >= tiles, i < tiles + 2))
        def _():
            first = (i - tiles) * (blocks // 2)
            lax.fori_loop(first, first + blocks // 2, epilogue, 0)

        pl.when(i == tiles + 2)(out_grads)
        steps(i)
        return 0

    small_ref[...] = jnp.zeros_like(small_ref)
    lax.fori_loop(0, tiles + 5, main, 0)

    def handed(slot, _):
        got_down(slot).wait_send()
        return 0

    lax.fori_loop(0, count, handed, 0)


def middle(bits, x, att, att2, wout, wout2, dy, vectors, bup, ups, downs):
    rows, width = x.shape
    hidden = ups[0].shape[1]
    count = hidden // HIDDEN_TILE
    tiles = 2 * count
    exchanges = (
        Exchange(bits, count, HIDDEN_TILE, width, False),
        Exchange(bits, count, width, HIDDEN_TILE, False),
    )
    vmem = pl.BlockSpec(memory_space=pltpu.VMEM)
    hbm = pl.BlockSpec(memory_space=pl.ANY)
    shape = jax.ShapeDtypeStruct
    depth = wout.shape[0]
    return pl.pallas_call(
        functools.partial(middle_kernel, exchanges, tiles),
        in_specs=[vmem] * 8 + [hbm] * 6,
        out_specs=[vmem] * 9,
        out_shape=[
            shape((rows, width), bf16),
            shape((rows, width), f32),
            shape(att.shape, bf16),
            shape(att2.shape, bf16),
            shape((2 * depth, width // 2), bf16),
            shape((2 * depth, width // 2), bf16),
            shape((tiles, 1, HIDDEN_TILE), f32),
            shape((8, width), f32),
            shape((2 * count, PIECES, width), bf16),
        ],
        scratch_shapes=[
            pltpu.VMEM((count, width // 2, HIDDEN_TILE), bf16),
            pltpu.VMEM((count, HIDDEN_TILE // 2, width), bf16),
            pltpu.SemaphoreType.DMA((count, 4)),
            pltpu.SemaphoreType.DMA((count, 2)),
            pltpu.VMEM((2, width, HIDDEN_TILE), bf16),
            pltpu.VMEM((2, HIDDEN_TILE, width), bf16),
            pltpu.SemaphoreType.DMA((2, 6)),
            pltpu.VMEM((rows, width), bf16),
            pltpu.VMEM((rows, width), f32),
            pltpu.VMEM((rows, width), f32),
            pltpu.VMEM((rows, HIDDEN_TILE), bf16),
            pltpu.VMEM((rows, HIDDEN_TILE), bf16),
            pltpu.VMEM((width, rows), bf16),
            pltpu.VMEM((count, HIDDEN_TILE, width), bf16),
            pltpu.VMEM((count, width, HIDDEN_TILE), bf16),
        ]
        + exchanges[0].scratch()
        + exchanges[1].scratch(),
        compiler_params=pltpu.CompilerParams(
            collective_id=0, has_side_effects=True, vmem_limit_bytes=67043328
        ),
        name="middle",
        cost_estimate=pl.CostEstimate(
            flops=60 * 10**9, bytes_accessed=40 * 10**6, transcendentals=4 * 10**6
        ),
    )(x, att, att2, wout, wout2, dy, vectors, bup, *ups, *downs)


def leave_kernel(exchange, *refs):
    (
        mine_ref,
        mine_out_ref,
        crossed_ref,
        crossed_out_ref,
        d_hbm,
        d2_hbm,
        w_hbm,
        w2_hbm,
        tokens_ref,
        context_ref,
        vectors_ref,
        dmid_hbm,
        small_ref,
        small2_ref,
        full_ref,
        back_ref,
        sums_ref,
        out_buf,
        d_ref,
        d2_ref,
        w_ref,
        w2_ref,
        dmid_ref,
        load_sem,
        rows_ref,
        give_ref,
        take_ref,
        swap_sem,
        norm_ref,
        near_ref,
        far_ref,
        near_sem,
        far_sem,
        *rest,
    ) = refs
    place, part = lax.axis_index("dp"), lax.axis_index("mp")
    ex = exchange.bind(place, part, rest)
    count, bits = ex.count, ex.bits
    first = mine_ref.shape[0]
    loads = [
        pltpu.make_async_copy(source, target, load_sem.at[n])
        for n, (source, target) in enumerate(
            ((w_hbm, w_ref), (d_hbm, d_ref), (w2_hbm, w2_ref), (d2_hbm, d2_ref), (dmid_hbm, dmid_ref))
        )
    ]
    for load in loads:
        load.start()
    near_id = part * 4 + place % 4
    near = [
        {"dp": flip(place, j % 4), "mp": part if j < 4 else 1 - part} for j in range(1, 8)
    ]
    ex.partners += [near[j - 1] for j in (3, 5, 6, 7)]
    ex.greet()

    def begin(k, _):
        ex.start_a(k, 0, mine_ref)
        return 0

    lax.fori_loop(0, first, begin, 0)

    def begin_out(k, _):
        total = mine_out_ref[k].astype(f32) + crossed_out_ref[k].astype(f32)
        out_buf[first + k] = total.astype(bf16)
        ex.start_a(first + k, 0, out_buf)
        return 0

    lax.fori_loop(0, count - first, begin_out, 0)

    def back_of(rows):
        total = 0.0
        for grads, weights in ((d_ref, w_ref), (d2_ref, w2_ref)):
            for c in range(3):
                total = total + dot(grads[c, rows, :], weights[c], NT)
        return total

    def stage_c(k):
        @pl.when(k < first)
        def _():
            ex.stage_c(k, mine_ref, lambda rows: crossed_ref[k, rows, :].astype(f32))

        @pl.when(k >= first)
        def _():
            ex.stage_c(k, out_buf)

    def steps(i):
        at_step(i - 10, count, lambda k: ex.stage_h(k, full_ref))
        at_step(i - 8, count, lambda k: ex.stage_g(k, full_ref))
        at_step(i - 6, count, lambda k: ex.stage_f(k, full_ref))
        at_step(i - 4, count, lambda k: ex.stage_e(k, full_ref))
        at_step(i - 2, count, lambda k: ex.stage_d(k))
        at_step(i, count, stage_c)

    width = tokens_ref.shape[1]

    def swap(rows, lane):
        return pltpu.make_async_remote_copy(
            src_ref=give_ref.at[rows],
            dst_ref=take_ref.at[rows],
            send_sem=swap_sem.at[lane, 0],
            recv_sem=swap_sem.at[lane, 1],
            device_id=ex.across,
            device_id_type=MESH,
        )

    def sums_of(d_rows, units):
        add = lambda values: jnp.sum(values, axis=0, keepdims=True)
        norm_ref[0:1, :] += add(d_rows * units)
        norm_ref[1:2, :] += add(d_rows)

    main = slice(0, HALF)
    edges = slice(HALF, HALF + 2 * EDGE)
    parts = tokens_ref.shape[0] // TILE
    own = NOISY_OWN - 2 * HALF
    lead = small_ref.shape[0] - 2
    bias = lead - 3
    norm_ref[...] = jnp.zeros_like(norm_ref)

    def give_main():
        for load in loads[:4]:
            load.wait()
        given = back_of(main)
        give_ref[main, :] = given.astype(bf16)
        rows_ref[:HALF, :] = given
        swap(main, 0).start()

    def give_edges():
        def context_sums(b, _):
            rows = pl.ds(pl.multiple_of(b * TILE, TILE), TILE)
            sums_of(rows_ref[rows, :], normal(context_ref[rows, :].astype(f32))[0])
            return 0

        lax.fori_loop(0, HALF // TILE, context_sums, 0)
        tail = back_of(slice(2 * HALF, KEY_ROWS))
        rows_ref[:HALF, :] = tail[own : own + HALF]
        side = tail[EDGE:own] + tail[own + HALF :]
        give_ref[HALF : HALF + EDGE, :] = tail[:EDGE].astype(bf16)
        give_ref[HALF + EDGE :, :] = side.astype(bf16)
        swap(edges, 1).start()
        sums_of(tail[:EDGE], normal(context_ref[:EDGE, :].astype(f32))[0])
        sums_of(side, normal(context_ref[HALF:, :].astype(f32))[0])

    def own_clean():
        rows_ref[HALF:, :] = back_of(slice(CLEAN_OWN, CLEAN_OWN + HALF))

    def tell_near():
        def own_sums(b, _):
            rows = pl.ds(pl.multiple_of(b * TILE, TILE), TILE)
            sums_of(rows_ref[rows, :], normal(tokens_ref[rows, :].astype(f32))[0])
            return 0

        lax.fori_loop(0, parts, own_sums, 0)
        mine = near_ref.at[near_id]
        mine[:lead, :] = small_ref[:lead, :]
        mine[lead : lead + 2, :] = norm_ref[:2, :]
        mine[lead + 2 : lead + 2 + bias, :] = small2_ref[:bias, :]
        rest_rows = 16 - lead - 2 - bias
        mine[16 - rest_rows :, :] = jnp.zeros((rest_rows, width), f32)
        for j in range(1, 8):
            near_copy(j).start()

    def near_copy(j):
        return pltpu.make_async_remote_copy(
            src_ref=near_ref.at[near_id],
            dst_ref=near_ref.at[near_id],
            send_sem=near_sem.at[j, 0],
            recv_sem=near_sem.at[j, 1],
            device_id=near[j - 1],
            device_id_type=MESH,
        )

    def near_got(j):
        came = (part + j // 4) % 2 * 4 + flip(place % 4, j % 4)
        return pltpu.make_async_remote_copy(
            src_ref=near_ref.at[came],
            dst_ref=near_ref.at[came],
            send_sem=near_sem.at[j, 0],
            recv_sem=near_sem.at[j, 1],
            device_id=near[j - 1],
            device_id_type=MESH,
        )

    def far_copy(j, at):
        return pltpu.make_async_remote_copy(
            src_ref=far_ref.at[at],
            dst_ref=far_ref.at[at],
            send_sem=far_sem.at[j, 0],
            recv_sem=far_sem.at[j, 1],
            device_id=ex.peers[j - 1],
            device_id_type=MESH,
        )

    def tell_far():
        for j in range(1, 8):
            near_copy(j).wait_send()
            near_got(j).wait_recv()
        total = near_ref[0]
        for j in range(1, 8):
            total = total + near_ref[j]
        plane = near_ref[part * 4]
        other = near_ref[(1 - part) * 4]
        for j in range(1, 4):
            plane = plane + near_ref[part * 4 + j]
            other = other + near_ref[(1 - part) * 4 + j]
        spot = far_ref.at[ex.z]
        spot[...] = total
        spot[:bias, :] = plane[:bias] + other[lead + 2 : lead + 2 + bias]
        for j in range(1, 4):
            far_copy(j, ex.z).start()

    def take_back():
        loads[4].wait()
        swap(main, 0).wait()
        swap(edges, 1).wait()
        rows_ref[HALF:, :] += take_ref[main, :].astype(f32)
        rows_ref[HALF : HALF + EDGE, :] += take_ref[HALF : HALF + EDGE, :].astype(f32)
        edge = pl.ds(pl.multiple_of((1 - part) * (HALF - EDGE), EDGE), EDGE)
        rows_ref[edge, :] += take_ref[HALF + EDGE :, :].astype(f32)

    def norm_back(b):
        rows = pl.ds(pl.multiple_of(b * TILE, TILE), TILE)
        unit, scale = normal(tokens_ref[rows, :].astype(f32))
        lean = rows_ref[rows, :] * vectors_ref[0:1, :]
        back_ref[rows, :] = dmid_ref[rows, :] + scale * (
            lean
            - jnp.mean(lean, axis=-1, keepdims=True)
            - unit * jnp.mean(lean * unit, axis=-1, keepdims=True)
        )

    def end_far():
        for j in range(1, 4):
            far_copy(j, ex.z).wait_send()
            far_copy(j, flip(ex.z, j)).wait_recv()
        total = far_ref[0]
        for j in range(1, 4):
            total = total + far_ref[j]
        for i, b in enumerate(ex.extra):
            far_ref[4 + 2 * i] = total
            trade = pltpu.make_async_remote_copy(
                src_ref=far_ref.at[4 + 2 * i],
                dst_ref=far_ref.at[5 + 2 * i],
                send_sem=far_sem.at[4 + i, 0],
                recv_sem=far_sem.at[4 + i, 1],
                device_id={"dp": flip(place, 1 << b)},
                device_id_type=MESH,
            )
            trade.start()
            trade.wait()
            total = total + far_ref[5 + 2 * i]
        sums_ref[...] = total

    actions = [give_main, give_edges, own_clean, tell_near, tell_far, take_back]
    ticks = [0, 2, 5, 8, 12, 13]

    def phase(p, _):
        for n, action in enumerate(actions):
            pl.when(p == n)(action)
        block = p - len(actions)

        @pl.when(jnp.logical_and(block >= 0, block < parts))
        def _():
            norm_back(block)

        pl.when(block == parts)(end_far)
        low = jnp.maximum(block, 0) + ticks[-1]
        high = low + 1
        for n in reversed(range(len(actions))):
            low = jnp.where(p == n, ticks[n], low)
            high = jnp.where(p == n, ticks[n + 1] if n + 1 < len(ticks) else ticks[n], high)
        lax.fori_loop(low, high, lambda i, _: (steps(i), 0)[1], 0)
        return 0

    lax.fori_loop(0, len(actions) + count + 10 - ticks[-1], phase, 0)


def leave(bits, mine, crossed, d_fields, weights, tokens, context, vectors, d_mid, small, small2):
    total = mine[0].shape[0] + mine[1].shape[0]
    rows, cols = mine[0].shape[1:]
    exchange = Exchange(bits, total, rows, cols)
    count, width = tokens.shape
    vmem = pl.BlockSpec(memory_space=pltpu.VMEM)
    hbm = pl.BlockSpec(memory_space=pl.ANY)
    shape = jax.ShapeDtypeStruct
    return pl.pallas_call(
        functools.partial(leave_kernel, exchange),
        in_specs=[vmem] * 4 + [hbm] * 4 + [vmem] * 3 + [hbm] + [vmem] * 2,
        out_specs=[vmem] * 3,
        out_shape=[
            shape((total, rows, cols), bf16),
            shape((count, width), f32),
            shape((16, width), f32),
        ],
        scratch_shapes=[
            pltpu.VMEM((total, rows, cols), bf16),
            pltpu.VMEM(d_fields[0].shape, bf16),
            pltpu.VMEM(d_fields[1].shape, bf16),
            pltpu.VMEM(weights[0].shape, bf16),
            pltpu.VMEM(weights[1].shape, bf16),
            pltpu.VMEM(d_mid.shape, f32),
            pltpu.SemaphoreType.DMA((5,)),
            pltpu.VMEM((count, width), f32),
            pltpu.VMEM((HALF + 2 * EDGE, width), bf16),
            pltpu.VMEM((HALF + 2 * EDGE, width), bf16),
            pltpu.SemaphoreType.DMA((2, 2)),
            pltpu.VMEM((8, width), f32),
            pltpu.VMEM((8, 16, width), f32),
            pltpu.VMEM((4 + 2 * len(exchange.extra), 16, width), f32),
            pltpu.SemaphoreType.DMA((8, 2)),
            pltpu.SemaphoreType.DMA((4 + len(exchange.extra), 2)),
        ]
        + exchange.scratch(),
        compiler_params=pltpu.CompilerParams(
            collective_id=1, has_side_effects=True, vmem_limit_bytes=67043328
        ),
        name="leave",
        cost_estimate=pl.CostEstimate(
            flops=40 * 10**9, bytes_accessed=40 * 10**6, transcendentals=0
        ),
    )(
        *mine, *crossed, *d_fields, *weights, tokens, context, vectors, d_mid, small, small2
    )


def key_layout(seq_lengths, block_len, part):
    index = jnp.arange(KEY_ROWS, dtype=jnp.int32)
    own = part * HALF
    token = jnp.where(
        index < NOISY_BASE, index + (own - HALF), index - NOISY_BASE + (own - EDGE)
    )
    ends = jnp.cumsum(seq_lengths)
    passed = token[:, None] >= ends[None, :]
    starts = jnp.sum(jnp.where(passed, seq_lengths[None, :], 0), axis=1)
    lengths_here = jnp.where(passed, 0, ends[None, :])
    stops = jnp.min(jnp.where(passed, TOK_DEV, lengths_here), axis=1)
    positions = token - starts
    block_start = starts + positions // block_len * block_len
    block_stop = jnp.minimum(block_start + block_len, stops)
    mine = slice(CLEAN_OWN, CLEAN_OWN + HALF)
    low, start, stop = starts[mine], block_start[mine], block_stop[mine]
    to_clean = own - HALF
    tiles = lambda column: column.reshape(TILES, 1, TILE)
    clean_bounds = jnp.concatenate(
        [
            jnp.concatenate([tiles(low - to_clean), tiles(low - to_clean)], axis=2),
            jnp.concatenate([tiles(start - to_clean), tiles(stop - to_clean)], axis=2),
        ],
        axis=1,
    )
    to_window = own - EDGE + TILE * jnp.arange(TILES, dtype=jnp.int32)[:, None, None]
    noisy_bounds = jnp.concatenate(
        [tiles(start) - to_window, tiles(stop) - to_window], axis=1
    )
    first = jnp.min(clean_bounds[:, 0], axis=1) // EDGE * EDGE
    last = jnp.max(clean_bounds[:, 1], axis=1)
    trips = (last - first + KEY_TILE - 1) // KEY_TILE
    spans = jnp.stack([first, trips], axis=1)
    lane = jnp.arange(LANES, dtype=jnp.int32)
    frequency = jnp.exp(
        (lane % (HD // 2)).astype(f32) * (-math.log(10000.0) / (HD // 2))
    )
    angles = positions.astype(f32)[:, None] * frequency[None, :]
    sign = jnp.where(lane % HD < HD // 2, -1.0, 1.0)
    return spans, clean_bounds, noisy_bounds, jnp.cos(angles), jnp.sin(angles) * sign


def in_order(bit, mine, theirs, axis=0):
    order = bit == 0
    return jnp.concatenate(
        [jnp.where(order, mine, theirs), jnp.where(order, theirs, mine)], axis=axis
    )


def tie(first, second):
    return lax.optimization_barrier((first, second))


def local(
    dp_size,
    tokens,
    lengths,
    block_size,
    cotangent,
    ln1_gain,
    ln1_bias,
    w_qkv,
    w_out,
    ln2_gain,
    ln2_bias,
    w_up,
    b_up,
    w_down,
    b_down,
):
    width = tokens.shape[2]
    part = lax.axis_index("mp")
    place = lax.axis_index("dp")
    bits = dp_size.bit_length() - 1
    core = place & 1

    def across(array):
        return lax.ppermute(array, "mp", [(0, 1), (1, 0)])

    def sibling(array):
        return lax.ppermute(array, "dp", [(i, i ^ 1) for i in range(dp_size)])

    def beside(array):
        return lax.ppermute(array, "dp", [(i, i ^ 2) for i in range(dp_size)])

    edge = jnp.where(part == 0, tokens[0, HALF - EDGE :], tokens[0, :EDGE])
    context = across(jnp.concatenate([tokens[1], edge], axis=0))
    qkv_mine = w_qkv.transpose(1, 0, 2)
    side = (place >> 1) & 1

    def quarter_of(array, axis=0):
        size = array.shape[axis] // 4
        return lax.dynamic_slice_in_dim(array, (2 * core + side) * size, size, axis)

    quarters = [
        quarter_of(qkv_mine, 1),
        quarter_of(w_up),
        quarter_of(w_down),
        quarter_of(w_out),
    ]
    layout = key_layout(lengths[0], block_size[0], part)
    vectors = jnp.stack([ln1_gain, ln1_bias, ln2_gain, ln2_bias, b_down])
    context, (quarters, layout, vectors) = tie(context, (quarters, layout, vectors))
    qkv_here, up_here, down_here, out_here = [across(piece) for piece in quarters]
    bias_other = across(b_up)

    spans, clean_bounds, noisy_bounds, cosine, sine = layout
    normed1, normed1_t, *fields = enter(tokens, context, vectors, qkv_mine, cosine, sine)
    qkv_here, fields = tie(qkv_here, fields)
    qkv_beside = beside(qkv_here)
    mine = [*fields, *attend_forward(spans, clean_bounds, noisy_bounds, *fields)]
    (qkv_here, qkv_beside, up_here), _ = tie((qkv_here, qkv_beside, up_here), mine[3])
    qkv_half = in_order(side, qkv_here, qkv_beside, axis=1)
    qkv_other = in_order(core, qkv_half, sibling(qkv_half), axis=1)
    up_beside = beside(up_here)
    fields = project(normed1, qkv_other, cosine, sine)
    (down_here, out_here), fields = tie((down_here, out_here), fields)
    out_beside = beside(out_here)
    down_beside = beside(down_here)
    other = [*fields, *attend_forward(spans, clean_bounds, noisy_bounds, *fields)]
    (out_here, out_beside, up_here, up_beside, down_here, down_beside, bias_other), _ = tie(
        (out_here, out_beside, up_here, up_beside, down_here, down_beside, bias_other), other[3]
    )
    out_half = in_order(side, out_here, out_beside)
    out_other = in_order(core, out_half, sibling(out_half))
    bias_all = jnp.concatenate([bias_other, b_up]).astype(f32).reshape(-1, 1, HIDDEN_TILE)

    x_rows = tokens.reshape(TOK_DEV, width)
    out, d_mid, d_att, d_att2, grad_out, grad_out2, grad_bias, norms, pieces = middle(
        bits,
        x_rows,
        mine[3],
        other[3],
        w_out,
        out_other,
        cotangent.reshape(TOK_DEV, width),
        vectors,
        bias_all,
        (w_up, up_here, up_beside),
        (w_down, down_here, down_beside),
    )
    hidden = b_up.shape[0]

    crossed_out = across(grad_out2)
    spread = [(b, min(2, min(bits, 4) - b)) for b in range(2, min(bits, 4), 2)]
    gathered = pieces
    ((first_bit, n),) = spread
    moved = [
        lax.ppermute(gathered, "dp", [(i, i ^ (k << first_bit)) for i in range(dp_size)])
        for k in range(1, 1 << n)
    ]

    def backward(saved, d_attended, spans):
        query, keys, values, attended, lse = saved
        return attend_backward(
            spans,
            clean_bounds,
            noisy_bounds,
            query,
            keys,
            values,
            attended,
            d_attended,
            lse,
            cosine,
            sine,
            normed1_t,
        )

    d_fields2, grad2 = backward(other, d_att2, spans)
    grad2 = grad2.reshape(-1, ROW_TILE, grad2.shape[2])
    low_bit, high_bit = (place >> 2) & 1, (place >> 3) & 1
    moved, _ = tie(moved, grad2)
    gathered = in_order(
        high_bit,
        in_order(low_bit, gathered, moved[0], 1),
        in_order(low_bit, moved[1], moved[2], 1),
        1,
    )
    half = ROW_TILE // 2
    part_of = lambda array, which: lax.dynamic_slice_in_dim(array, which * half, half, 1)
    got = sibling(part_of(grad2, 1 - core))
    crossing = (part_of(grad2, core).astype(f32) + got.astype(f32)).astype(bf16)
    (crossing, gathered), spans = tie((crossing, gathered), spans)
    crossed = across(crossing)
    moved = beside(gathered)
    d_fields1, grad1 = backward(mine, d_att, spans)
    grad1 = grad1.reshape(-1, ROW_TILE, grad1.shape[2])
    moved, grad1 = tie(moved, grad1)
    gathered = in_order(side, gathered, moved, 1)
    gathered, grad1 = tie(gathered, grad1)
    moved = sibling(gathered)
    lead = hidden // width
    bias2, bias1 = grad_bias.reshape(2, lead, width)
    shared = jnp.concatenate([norms[:3], jnp.zeros((2, width), f32)], axis=0)
    full, grad_tokens, sums = leave(
        bits,
        (grad1, grad_out.reshape(-1, ROW_TILE, grad_out.shape[1])),
        (crossed, crossed_out.reshape(-1, ROW_TILE, grad_out.shape[1])),
        (d_fields1, d_fields2),
        (qkv_mine, qkv_other),
        x_rows,
        context,
        vectors,
        d_mid,
        jnp.concatenate([bias1, shared], axis=0),
        jnp.concatenate([bias2, shared], axis=0),
    )
    moved, _ = tie(moved, full)
    gathered = in_order(core, gathered, moved, 1)
    count = hidden // HIDDEN_TILE
    grad_down = gathered[:count].reshape(hidden, width).astype(f32)
    grad_up = gathered[count:].reshape(count, PIECES, PIECES, width // HIDDEN_TILE, HIDDEN_TILE)
    grad_up = grad_up.transpose(1, 3, 2, 0, 4).reshape(width, hidden).astype(f32)
    split = 3 * width // ROW_TILE
    grad_qkv = full[:split].reshape(qkv_mine.shape).transpose(1, 0, 2).astype(f32)
    flat = full[split:].reshape(2, w_out.shape[0], width // 2)
    grad_out = jnp.concatenate([flat[0], flat[1]], axis=1).astype(f32)
    return (
        out.reshape(tokens.shape),
        grad_tokens.reshape(tokens.shape),
        sums[lead + 3],
        sums[lead + 4],
        grad_qkv,
        grad_out,
        sums[lead],
        sums[lead + 1],
        grad_up,
        sums[:lead].reshape(hidden),
        grad_down,
        sums[lead + 2],
    )


def solution(mesh):
    in_specs = (
        P(None, ("dp", "mp"), None),
        P("dp", None),
        P(),
        P(None, ("dp", "mp"), None),
        P(),
        P(),
        P(None, None, "mp"),
        P("mp", None),
        P(),
        P(),
        P(None, "mp"),
        P("mp"),
        P("mp", None),
        P(),
    )
    out_specs = (
        P(None, ("dp", "mp"), None),
        P(None, ("dp", "mp"), None),
        P(),
        P(),
        P(None, None, "mp"),
        P("mp", None),
        P(),
        P(),
        P(None, "mp"),
        P("mp"),
        P("mp", None),
        P(),
    )
    return jax.shard_map(
        functools.partial(local, mesh.shape["dp"]),
        mesh=mesh,
        in_specs=in_specs,
        out_specs=out_specs,
        check_vma=False,
    )
```

profile of v0, /device:TPU:0, one launch (start us, length us, event | category | flops | bytes accessed | tf_op | source)
XLA Modules:
  0.0 385.2 jit_solution(3296153702909047035)
XLA Ops:
  0.7 1.2 slice_bitcast_fusion
  1.9 0.8 select_bitcast_fusion
  2.8 3.0 collective-permute-start
  7.7 0.7 pad_add_fusion.1.span_ref
  8.3 0.6 add_add_fusion.clean_ref
  8.9 0.6 pad_add_fusion.noisy_ref
  9.5 1.1 dynamic-slice_bitcast_fusion
  10.6 1.1 constant_dynamic-slice_fusion.2
  11.7 0.9 constant_dynamic-slice_fusion.1
  12.6 0.6 stack.29.vectors_ref.refs_6_.refs_10_
  13.3 1.1 constant_dynamic-slice_fusion.3
  14.4 4.4 %fusion.2 = (f32[1584,128]{1,0:T(8,128)}, f32[1584,128]{1,0:T(8,128)}) fusion(f32[128]{0:T(128)S(1)} %get-tuple-element.197, f32[128]{0:T(128)S(1)} %get-tuple-element.198, f32[1584]{0:T(1024)S(1)} %get-tuple-element.191), kind=kLoop, calls=%fused_computation.20 | loop fusion | flops 405504 | bytes 1629376 | tf_op jit(solution)/shard_map/mul | solution.py:1453
  18.8 5.2 %collective-permute-done.context_ref.refs_9_ = bf16[528,768]{1,0:T(8,128)(2,1)} collective-permute-done((bf16[528,768]{1,0:T(8,128)(2,1)S(1)}, bf16[528,768]{1,0:T(8,128)(2,1)}, u32[]{:S(2)}, u32[]{:S(2)}) %collective-permute-start) | collective-permute-done | bytes 811040 | tf_op jit(solution)/shard_map/ppermute | solution.py:1491
  24.0 1.7 collective-permute-start.1
  25.7 0.3 collective-permute-start.5
  26.0 11.4 %enter.1 = (bf16[1584,768]{1,0:T(8,128)(2,1)}, bf16[768,1584]{1,0:T(8,128)(2,1)}, bf16[1584,384]{1,0:T(8,128)(2,1)}, bf16[1584,384]{1,0:T(8,128)(2,1)}, bf16[1584,384]{1,0:T(8,128)(2,1)}) custom-call(bf16[2,512,768]{2,1,0:T(8,128)(2,1)} %tokens_ref.1, bf16[528,768]{1,0:T(8,128)(2,1)} %collective-permute-done.context_ref.refs_9_, ...), custom_call_target="tpu_custom_call" | custom-call | flops 10000000000 | bytes 16000000 | tf_op jit(solution)/shard_map/enter/pallas_call | solution.py:157
  37.4 1.7 collective-permute-start.4
  39.1 15.7 %attend_forward.2 = (bf16[1024,384]{1,0:T(8,128)(2,1)}, f32[3,4,2,256]{3,2,1,0:T(2,128)}) custom-call(s32[4,2]{1,0:T(4,128)} %pad_add_fusion.1.span_ref, s32[4,2,256]{2,1,0:T(2,128)} %add_add_fusion.clean_ref, s32[4,2,128]{2,1,0:T(2,128)} %pad_add_fusion.noisy_ref, bf16[1584,384]{1,0:T(8,128)(2,1)} %get-tuple-element.92.q_ref, ...), custom_call_target="tpu_custom_call" | custom-call | flops 1610612736 | bytes 4866048 | tf_op jit(solution)/shard_map/attend_forward/pallas_call | solution.py:290
  55.0 6.9 %collective-permute-start.2 = (bf16[384,768]{1,0:T(8,128)(2,1)S(1)}, bf16[384,768]{1,0:T(8,128)(2,1)}, u32[]{:S(2)}, u32[]{:S(2)}) collective-permute-start(bf16[384,768]{1,0:T(8,128)(2,1)S(1)} %constant_dynamic-slice_fusion.2), channel_id=1, source_target_pairs={{0,1},{1,0},{2,3},{3,2},{4,5},{5,4},{6,7},{7,6},{8,9},{9,8},{10,11... | collective-permute-start | bytes 1769480 | tf_op jit(solution)/shard_map/ppermute | solution.py:1491
  62.0 0.3 broadcast_select_fusion.5
  62.3 1.4 pad_maximum_fusion.2.w_ref.refs_7_
  63.7 7.4 %project.1 = (bf16[1584,384]{1,0:T(8,128)(2,1)}, bf16[1584,384]{1,0:T(8,128)(2,1)}, bf16[1584,384]{1,0:T(8,128)(2,1)}) custom-call(bf16[1584,768]{1,0:T(8,128)(2,1)} %get-tuple-element.98.rows_ref, bf16[3,768,384]{2,1,0:T(8,128)(2,1)} %pad_maximum_fusion.2.w_ref.refs_7_, f32[1584,128]{1,0:T(8,128)} %get-tuple-element.87.cos_ref, ...), custom_call_target="tpu_custom_call" | custom-call | flops 2802843648 | bytes 7852032 | tf_op jit(solution)/shard_map/project/pallas_call | solution.py:78
  71.1 7.9 %collective-permute-done.3 = bf16[96,768]{1,0:T(8,128)(2,1)S(1)} collective-permute-done((bf16[96,768]{1,0:T(8,128)(2,1)S(1)}, bf16[96,768]{1,0:T(8,128)(2,1)S(1)}, u32[]{:S(2)}, u32[]{:S(2)}) %collective-permute-start.3) | collective-permute-done | bytes 147488 | tf_op jit(solution)/shard_map/ppermute | solution.py:1491
  79.0 1.8 collective-permute-start.10
  80.8 2.0 collective-permute-start.7
  82.8 15.6 %attend_forward.3 = (bf16[1024,384]{1,0:T(8,128)(2,1)}, f32[3,4,2,256]{3,2,1,0:T(2,128)}) custom-call(s32[4,2]{1,0:T(4,128)} %pad_add_fusion.1.span_ref, s32[4,2,256]{2,1,0:T(2,128)} %add_add_fusion.clean_ref, s32[4,2,128]{2,1,0:T(2,128)} %pad_add_fusion.noisy_ref, bf16[1584,384]{1,0:T(8,128)(2,1)} %get-tuple-element.106.q_ref, ...), custom_call_target="tpu_custom_call" | custom-call | flops 1610612736 | bytes 4866048 | tf_op jit(solution)/shard_map/attend_forward/pallas_call | solution.py:290
  98.6 0.6 pad.9.clone
  99.2 0.6 maximum_convert_fusion.1.refs_7_
  99.8 0.3 collective-permute-done.11
  100.3 0.9 pad_maximum_fusion.6.refs_4_
  101.1 99.5 %middle.1 = (bf16[1024,768]{1,0:T(8,128)(2,1)}, f32[1024,768]{1,0:T(8,128)}, bf16[1024,384]{1,0:T(8,128)(2,1)}, bf16[1024,384]{1,0:T(8,128)(2,1)}, bf16[768,384]...) custom-call(bf16[1024,768]{1,0:T(8,128)(2,1)} %bitcast.55, ...), custom_call_target="tpu_custom_call" | custom-call | flops 60000002048 | bytes 40000000 | tf_op jit(solution)/shard_map/middle/pallas_call | solution.py:1046
  200.6 0.4 collective-permute-start.13
  201.0 1.3 collective-permute-start.14
  202.3 2.7 collective-permute-start.15
  205.0 0.7 slice_reduce_fusion
  205.8 0.7 slice.71
  206.6 34.6 %attend_backward.2 = (bf16[3,1584,384]{2,1,0:T(8,128)(2,1)}, bf16[3,768,384]{2,1,0:T(8,128)(2,1)}) custom-call(s32[4,2]{1,0:T(4,128)} %pad_add_fusion.1.span_ref, s32[4,2,256]{2,1,0:T(2,128)} %add_add_fusion.clean_ref, s32[4,2,128]{2,1,0:T(2,128)} %pad_add_fusion.noisy_ref, bf16[1584,384]{1,0:T(8,128)(2,1)} %get-tuple-element.106.q_ref, ...), custom_call_target="tpu_custom_call" | custom-call | flops 35999997952 | bytes 36000000 | tf_op jit(solution)/shard_map/attend_backward/pallas_call | solution.py:471
  241.2 1.3 constant_dynamic-slice_fusion
  242.6 5.6 %collective-permute-start.18 = (bf16[768,384]{1,0:T(8,128)(2,1)}, bf16[768,384]{1,0:T(8,128)(2,1)}, u32[]{:S(2)}, u32[]{:S(2)}) collective-permute-start(bf16[768,384]{1,0:T(8,128)(2,1)} %get-tuple-element.139), channel_id=1, source_target_pairs={{0,1},{1,0},{2,3},{3,2},{4,5},{5,4},{6,7},{7,6},{8,9},{9,8},{10,11... | collective-permute-start | bytes 1769480 | tf_op jit(solution)/shard_map/ppermute | solution.py:1491
  248.1 0.7 fusion.6
  249.0 0.3 broadcast_select_fusion.7
  249.3 1.4 copy-done.1
  250.7 0.3 add_convert_fusion
  251.2 24.0 %attend_backward.3 = (bf16[3,1584,384]{2,1,0:T(8,128)(2,1)}, bf16[3,768,384]{2,1,0:T(8,128)(2,1)}) custom-call(s32[4,2]{1,0:T(4,128)} %pad_add_fusion.1.span_ref, s32[4,2,256]{2,1,0:T(2,128)} %add_add_fusion.clean_ref, s32[4,2,128]{2,1,0:T(2,128)} %pad_add_fusion.noisy_ref, bf16[1584,384]{1,0:T(8,128)(2,1)} %get-tuple-element.92.q_ref, ...), custom_call_target="tpu_custom_call" | custom-call | flops 35999997952 | bytes 36000000 | tf_op jit(solution)/shard_map/attend_backward/pallas_call | solution.py:471
  275.2 3.9 %collective-permute-done.16 = bf16[12,64,768]{2,1,0:T(8,128)(2,1)S(1)} collective-permute-done((bf16[12,64,768]{2,1,0:T(8,128)(2,1)S(1)}, bf16[12,64,768]{2,1,0:T(8,128)(2,1)S(1)}, u32[]{:S(2)}, u32[]{:S(2)}) %collective-permute-start.16) | collective-permute-done | bytes 1179680 | tf_op jit(solution)/shard_map/ppermute | solution.py:1497
  279.2 1.6 pad_maximum_fusion.1
  280.8 0.5 collective-permute-done.17.refs_2_
  281.3 62.9 %leave.1 = (bf16[12,256,384]{2,1,0:T(8,128)(2,1)}, f32[1024,768]{1,0:T(8,128)}, f32[16,768]{1,0:T(8,128)}) custom-call(bf16[9,256,384]{2,1,0:T(8,128)(2,1)} %bitcast.68, bf16[3,256,384]{2,1,0:T(8,128)(2,1)} %bitcast.69, bf16[9,128,384]{2,1,0:T(8,128)(2,1)} %collective-permute-done.17.refs_2_, bf16[3,256,384]{2,1,0:T(8,128)(2,1)} %bitcast.19.refs_3_, ...), custom_call_target="tpu_custom_call" | custom-call | flops 40000000000 | bytes 40000000 | tf_op jit(solution)/shard_map/leave/pallas_call | solution.py:1374
  344.2 1.1 slice.75
  345.4 1.7 slice.74
  347.0 0.7 slice.81
  347.8 0.6 reshape.382
  348.4 1.6 slice_reduce_fusion.2
  350.0 1.1 maximum_convert_fusion
  351.1 2.0 convert_bitcast_fusion
  353.2 2.7 broadcast_select_fusion
  355.8 3.4 pad_maximum_fusion
  359.2 8.3 %reshape.386 = f32[6,16,16,3,256]{4,3,2,1,0:T(4,128)} reshape(f32[6,256,768]{2,1,0:T(8,128)} %get-tuple-element.166) | data formatting | bytes 9437184 | tf_op jit(solution)/shard_map/convert_element_type | solution.py:1627
  367.5 6.2 %copy.47 = f32[16,3,16,6,256]{4,3,2,1,0:T(8,128)S(1)} copy(f32[16,3,16,6,256]{4,1,2,0,3:T(4,128)} %bitcast.46) | data formatting | bytes 9437184 | tf_op jit(solution)/shard_map/convert_element_type | solution.py:1627
  373.7 4.5 %copy.48 = f32[96,8,6,256]{3,1,2,0:T(8,128)} copy(f32[96,8,6,256]{3,2,1,0:T(8,128)S(1)} %bitcast.47) | data formatting | bytes 9437184
  378.2 2.7 bitcast_convert_fusion
  380.9 1.1 copy.52
  382.0 1.3 copy-done
  383.3 1.7 copy.53
  (83 shorter events, 2.6 us)
Async XLA Ops:
  0.6 5.2 %copy-start.11 = (s32[1,4]{1,0:T(1,128)S(1)}, s32[1,4]{1,0:T(1,128)}, u32[]{:S(2)}) copy-start(s32[1,4]{1,0:T(1,128)} %param.15) | copy-start | bytes 52
  0.7 6.9 %copy-start.4 = (f32[768]{0:T(1024)S(1)}, f32[768]{0:T(1024)}, u32[]{:S(2)}) copy-start(f32[768]{0:T(1024)} %param.18) | copy-start | bytes 9220
  0.7 6.9 %copy-start.5 = (f32[768]{0:T(1024)S(1)}, f32[768]{0:T(1024)}, u32[]{:S(2)}) copy-start(f32[768]{0:T(1024)} %param.19) | copy-start | bytes 9220
  0.7 6.9 %copy-start.6 = (f32[768]{0:T(1024)S(1)}, f32[768]{0:T(1024)}, u32[]{:S(2)}) copy-start(f32[768]{0:T(1024)} %param.22) | copy-start | bytes 9220
  0.7 6.9 %copy-start.7 = (f32[768]{0:T(1024)S(1)}, f32[768]{0:T(1024)}, u32[]{:S(2)}) copy-start(f32[768]{0:T(1024)} %param.23) | copy-start | bytes 9220
  0.7 6.9 %copy-start.8 = (f32[768]{0:T(1024)S(1)}, f32[768]{0:T(1024)}, u32[]{:S(2)}) copy-start(f32[768]{0:T(1024)} %param.27) | copy-start | bytes 9220
  2.8 21.2 %collective-permute-start = (bf16[528,768]{1,0:T(8,128)(2,1)S(1)}, bf16[528,768]{1,0:T(8,128)(2,1)}, u32[]{:S(2)}, u32[]{:S(2)}) collective-permute-start(bf16[528,768]{1,0:T(8,128)(2,1)S(1)} %pad_maximum_fusion.5), channel_id=1, source_target_pairs={{0,1},{1,0},{2,3},{3,2},{4,5},{5,4},{6,7},{7,6},{8,9},{9,8},{10,11... | collective-permute-start | bytes 2433032 | tf_op jit(solution)/shard_map/ppermute | solution.py:1491
  24.0 13.4 %collective-permute-start.1 = (bf16[3,192,384]{2,1,0:T(8,128)(2,1)S(1)}, bf16[3,192,384]{2,1,0:T(8,128)(2,1)S(1)}, u32[]{:S(2)}, u32[]{:S(2)}) collective-permute-start(bf16[3,192,384]{2,1,0:T(8,128)(2,1)S(1)} %dynamic-slice_bitcast_fusion), channel_id=1, source_target_pairs={{0,1},{1,0},{2,3},{3,2},{4,5},{5,4},{6,7},{7,6},{8,9},{9,8},{10,11... | collective-permute-start | bytes 1327112 | tf_op jit(solution)/shard_map/ppermute | solution.py:1491
  25.7 29.0 %collective-permute-start.5 = (bf16[192,1536]{1,0:T(8,128)(2,1)S(1)}, bf16[192,1536]{1,0:T(8,128)(2,1)}, u32[]{:S(2)}, u32[]{:S(2)}) collective-permute-start(bf16[192,1536]{1,0:T(8,128)(2,1)S(1)} %constant_dynamic-slice_fusion.3), channel_id=1, source_target_pairs={{0,1},{1,0},{2,3},{3,2},{4,5},{5,4},{6,7},{7,6},{8,9},{9,8},{10,11... | collective-permute-start | bytes 1769480 | tf_op jit(solution)/shard_map/ppermute | solution.py:1491
  37.4 17.4 %collective-permute-start.4 = (bf16[3,192,384]{2,1,0:T(8,128)(2,1)S(1)}, bf16[3,192,384]{2,1,0:T(8,128)(2,1)S(1)}, u32[]{:S(2)}, u32[]{:S(2)}) collective-permute-start(bf16[3,192,384]{2,1,0:T(8,128)(2,1)S(1)} %collective-permute-done.1), channel_id=1, source_target_pairs={{0,4},{2,6},{4,0},{6,2},{8,12},{10,14},{12,8},{14,10},{16,20},{18,... | collective-permute-start | bytes 1327112 | tf_op jit(solution)/shard_map/ppermute | solution.py:1497
  54.9 7.1 %collective-permute-start.6 = (bf16[3,384,384]{2,1,0:T(8,128)(2,1)S(1)}, bf16[3,384,384]{2,1,0:T(8,128)(2,1)S(1)}, u32[]{:S(2)}, u32[]{:S(2)}) collective-permute-start(bf16[3,384,384]{2,1,0:T(8,128)(2,1)S(1)} %pad_maximum_fusion.4), channel_id=1, source_target_pairs={{0,2},{2,0},{4,6},{6,4},{8,10},{10,8},{12,14},{14,12},{16,18},{18,... | collective-permute-start | bytes 2654216 | tf_op jit(solution)/shard_map/ppermute | solution.py:1494
  55.0 24.0 %collective-permute-start.2 = (bf16[384,768]{1,0:T(8,128)(2,1)S(1)}, bf16[384,768]{1,0:T(8,128)(2,1)}, u32[]{:S(2)}, u32[]{:S(2)}) collective-permute-start(bf16[384,768]{1,0:T(8,128)(2,1)S(1)} %constant_dynamic-slice_fusion.2), channel_id=1, source_target_pairs={{0,1},{1,0},{2,3},{3,2},{4,5},{5,4},{6,7},{7,6},{8,9},{9,8},{10,11... | collective-permute-start | bytes 1769480 | tf_op jit(solution)/shard_map/ppermute | solution.py:1491
  61.9 17.1 %collective-permute-start.3 = (bf16[96,768]{1,0:T(8,128)(2,1)S(1)}, bf16[96,768]{1,0:T(8,128)(2,1)S(1)}, u32[]{:S(2)}, u32[]{:S(2)}) collective-permute-start(bf16[96,768]{1,0:T(8,128)(2,1)S(1)} %constant_dynamic-slice_fusion.1), channel_id=1, source_target_pairs={{0,1},{1,0},{2,3},{3,2},{4,5},{5,4},{6,7},{7,6},{8,9},{9,8},{10,11... | collective-permute-start | bytes 442376 | tf_op jit(solution)/shard_map/ppermute | solution.py:1491
  62.0 36.4 %collective-permute-start.8 = (bf16[192,1536]{1,0:T(8,128)(2,1)}, bf16[192,1536]{1,0:T(8,128)(2,1)}, u32[]{:S(2)}, u32[]{:S(2)}) collective-permute-start(bf16[192,1536]{1,0:T(8,128)(2,1)} %collective-permute-done.5.refs_9_), channel_id=1, source_target_pairs={{0,4},{2,6},{4,0},{6,2},{8,12},{10,14},{12,8},{14,10},{16,20},{18,... | collective-permute-start | bytes 1769480 | tf_op jit(solution)/shard_map/ppermute | solution.py:1497
  63.7 15.3 %copy-start.9 = (bf16[1536]{0:T(1024)(128)(2,1)S(1)}, bf16[1536]{0:T(1024)(128)(2,1)}, u32[]{:S(2)}) copy-start(bf16[1536]{0:T(1024)(128)(2,1)} %param.25) | copy-start | bytes 9220
  79.0 19.4 %collective-permute-start.9 = (bf16[384,768]{1,0:T(8,128)(2,1)}, bf16[384,768]{1,0:T(8,128)(2,1)S(1)}, u32[]{:S(2)}, u32[]{:S(2)}) collective-permute-start(bf16[384,768]{1,0:T(8,128)(2,1)} %collective-permute-done.2.refs_12_), channel_id=1, source_target_pairs={{0,4},{2,6},{4,0},{6,2},{8,12},{10,14},{12,8},{14,10},{16,20},{18,... | collective-permute-start | bytes 1769480 | tf_op jit(solution)/shard_map/ppermute | solution.py:1497
  79.0 19.4 %collective-permute-start.10 = (bf16[1536]{0:T(1024)(128)(2,1)S(1)}, bf16[1536]{0:T(1024)(128)(2,1)S(1)}, u32[]{:S(2)}, u32[]{:S(2)}) collective-permute-start(bf16[1536]{0:T(1024)(128)(2,1)S(1)} %copy-done.9), channel_id=1, source_target_pairs={{0,1},{1,0},{2,3},{3,2},{4,5},{5,4},{6,7},{7,6},{8,9},{9,8},{10,11... | collective-permute-start | bytes 9224 | tf_op jit(solution)/shard_map/ppermute | solution.py:1491
  80.8 17.6 %collective-permute-start.7 = (bf16[96,768]{1,0:T(8,128)(2,1)S(1)}, bf16[96,768]{1,0:T(8,128)(2,1)S(1)}, u32[]{:S(2)}, u32[]{:S(2)}) collective-permute-start(bf16[96,768]{1,0:T(8,128)(2,1)S(1)} %collective-permute-done.3), channel_id=1, source_target_pairs={{0,4},{2,6},{4,0},{6,2},{8,12},{10,14},{12,8},{14,10},{16,20},{18,... | collective-permute-start | bytes 442376 | tf_op jit(solution)/shard_map/ppermute | solution.py:1497
  98.4 2.7 copy-start.12
  98.5 1.6 collective-permute-start.11
  200.6 48.3 %collective-permute-start.13 = (bf16[12,16,768]{2,1,0:T(8,128)(2,1)}, bf16[12,16,768]{2,1,0:T(8,128)(2,1)S(1)}, u32[]{:S(2)}, u32[]{:S(2)}) collective-permute-start(bf16[12,16,768]{2,1,0:T(8,128)(2,1)} %get-tuple-element.125), channel_id=1, source_target_pairs={{0,8},{2,10},{4,12},{6,14},{8,0},{10,2},{12,4},{14,6},{16,24},{18,... | collective-permute-start | bytes 884744 | tf_op jit(solution)/shard_map/ppermute | solution.py:1562
  201.0 47.8 %collective-permute-start.14 = (bf16[12,16,768]{2,1,0:T(8,128)(2,1)}, bf16[12,16,768]{2,1,0:T(8,128)(2,1)S(1)}, u32[]{:S(2)}, u32[]{:S(2)}) collective-permute-start(bf16[12,16,768]{2,1,0:T(8,128)(2,1)} %get-tuple-element.125), channel_id=1, source_target_pairs={{0,16},{2,18},{4,20},{6,22},{8,24},{10,26},{12,28},{14,30},{16,0},... | collective-permute-start | bytes 884744 | tf_op jit(solution)/shard_map/ppermute | solution.py:1562
  202.3 46.6 %collective-permute-start.15 = (bf16[12,16,768]{2,1,0:T(8,128)(2,1)}, bf16[12,16,768]{2,1,0:T(8,128)(2,1)S(1)}, u32[]{:S(2)}, u32[]{:S(2)}) collective-permute-start(bf16[12,16,768]{2,1,0:T(8,128)(2,1)} %get-tuple-element.125), channel_id=1, source_target_pairs={{0,24},{2,26},{4,28},{6,30},{8,16},{10,18},{12,20},{14,22},{16,8},... | collective-permute-start | bytes 884744 | tf_op jit(solution)/shard_map/ppermute | solution.py:1562
  241.2 7.0 %copy-start.10 = (f32[7]{0:T(128)S(1)}, f32[7]{0:T(128)}, u32[]{:S(2)}) copy-start(f32[7]{0:T(128)} %pad.9.clone) | copy-start | bytes 88
  241.2 7.7 %copy-start.3 = (bf16[12,16,768]{2,1,0:T(8,128)(2,1)S(1)}, bf16[12,16,768]{2,1,0:T(8,128)(2,1)}, u32[]{:S(2)}) copy-start(bf16[12,16,768]{2,1,0:T(8,128)(2,1)} %get-tuple-element.125) | copy-start | bytes 884740
  242.5 6.8 %collective-permute-start.12 = (bf16[9,128,384]{2,1,0:T(8,128)(2,1)S(1)}, bf16[9,128,384]{2,1,0:T(8,128)(2,1)S(1)}, u32[]{:S(2)}, u32[]{:S(2)}) collective-permute-start(bf16[9,128,384]{2,1,0:T(8,128)(2,1)S(1)} %constant_dynamic-slice_fusion), channel_id=1, source_target_pairs={{0,2},{2,0},{4,6},{6,4},{8,10},{10,8},{12,14},{14,12},{16,18},{18,... | collective-permute-start | bytes 2654216 | tf_op jit(solution)/shard_map/ppermute | solution.py:1494
  242.6 38.2 %collective-permute-start.18 = (bf16[768,384]{1,0:T(8,128)(2,1)}, bf16[768,384]{1,0:T(8,128)(2,1)}, u32[]{:S(2)}, u32[]{:S(2)}) collective-permute-start(bf16[768,384]{1,0:T(8,128)(2,1)} %get-tuple-element.139), channel_id=1, source_target_pairs={{0,1},{1,0},{2,3},{3,2},{4,5},{5,4},{6,7},{7,6},{8,9},{9,8},{10,11... | collective-permute-start | bytes 1769480 | tf_op jit(solution)/shard_map/ppermute | solution.py:1491
  249.2 1.5 copy-start.1
  251.0 28.1 %collective-permute-start.16 = (bf16[12,64,768]{2,1,0:T(8,128)(2,1)S(1)}, bf16[12,64,768]{2,1,0:T(8,128)(2,1)S(1)}, u32[]{:S(2)}, u32[]{:S(2)}) collective-permute-start(bf16[12,64,768]{2,1,0:T(8,128)(2,1)S(1)} %pad_maximum_fusion.3), channel_id=1, source_target_pairs={{0,4},{2,6},{4,0},{6,2},{8,12},{10,14},{12,8},{14,10},{16,20},{18,... | collective-permute-start | bytes 3538952 | tf_op jit(solution)/shard_map/ppermute | solution.py:1497
  251.2 30.1 %collective-permute-start.17 = (bf16[9,128,384]{2,1,0:T(8,128)(2,1)S(1)}, bf16[9,128,384]{2,1,0:T(8,128)(2,1)}, u32[]{:S(2)}, u32[]{:S(2)}) collective-permute-start(bf16[9,128,384]{2,1,0:T(8,128)(2,1)S(1)} %add_convert_fusion), channel_id=1, source_target_pairs={{0,1},{1,0},{2,3},{3,2},{4,5},{5,4},{6,7},{7,6},{8,9},{9,8},{10,11... | collective-permute-start | bytes 2654216 | tf_op jit(solution)/shard_map/ppermute | solution.py:1491
  280.8 72.3 %collective-permute-start.19 = (bf16[12,128,768]{2,1,0:T(8,128)(2,1)}, bf16[12,128,768]{2,1,0:T(8,128)(2,1)}, u32[]{:S(2)}, u32[]{:S(2)}) collective-permute-start(bf16[12,128,768]{2,1,0:T(8,128)(2,1)} %pad_maximum_fusion.1), channel_id=1, source_target_pairs={{0,2},{2,0},{4,6},{6,4},{8,10},{10,8},{12,14},{14,12},{16,18},{18,... | collective-permute-start | bytes 7077896 | tf_op jit(solution)/shard_map/ppermute | solution.py:1494
  378.2 2.7 copy-start.2
  380.9 2.5 copy-start
where the time goes:
time: 390 us; the launch traced here: 385 us
  Pallas kernels  271 us (69%)
  local copies, waits for them, and re-layouts  40 us (10%)
  starting transfers between devices  28 us (7%)
  other arithmetic  26.4 us (7%)
  waiting for transfers between devices  17.8 us (5%)
    pallas_call x1, Pallas kernels, middle(): pl.pallas_call(functools.partial(middle_kernel, exchanges, tiles), in_spe...  99.5 us
    pallas_call x1, Pallas kernels, leave(): pl.pallas_call(functools.partial(leave_kernel, exchange), in_specs=[vmem]...  62.9 us
    pallas_call x2, Pallas kernels, attend_backward(): pl.pallas_call(backward_kernel, in_specs=[pl.BlockSpec(memory_space=pltpu...  58.6 us
    pallas_call x2, Pallas kernels, attend_forward(): pl.pallas_call(forward_kernel, in_specs=[pl.BlockSpec(memory_space=pltpu....  31.3 us
    ppermute x8, starting transfers between devices, across(): return lax.ppermute(array, 'mp', [(0, 1), (1, 0)])  19.4 us
    convert_element_type x2, local copies, waits for them, and re-layouts, local(): grad_up.transpose(1, 3, 2, 0, 4).reshape(width, hidden).astype(f32)  14.5 us
    ppermute x8, waiting for transfers between devices, across(): return lax.ppermute(array, 'mp', [(0, 1), (1, 0)])  13.6 us
    pallas_call x1, Pallas kernels, enter(): pl.pallas_call(enter_kernel, in_specs=[vmem] * 6, out_specs=[vmem] * 5, o...  11.4 us
  transfers between devices with their start and end apart: 20, of which 5 were waited for; matrix products, arithmetic and copies ran while one was open for 8% of the time, Pallas kernels for 45%

commit v1 on v0

--- a/solution.py
+++ b/solution.py
@@ -318,13 +318,14 @@
     lse_ref,
     cos_ref,
     sin_ref,
-    rows_ref,
-    out_ref,
-    grad_ref,
-    dk_ref,
-    dv_ref,
-    bias_ref,
+    *refs,
 ):
+    rows_ref, out_ref, grad_ref, dk_ref, dv_ref, bias_ref = refs if len(refs) == 6 else (
+        None,
+        refs[0],
+        None,
+        *refs[1:],
+    )
     pairs = q_ref.shape[1] // LANES
     lanes = [slice(p * LANES, (p + 1) * LANES) for p in range(pairs)]
     dk_ref[...] = jnp.zeros_like(dk_ref)
@@ -448,7 +449,8 @@
             grad_ref[c, rows, :] = dot(rows_ref[rows, :], out_ref[c]).astype(bf16)
         return 0
 
-    lax.fori_loop(0, rows_ref.shape[0] // ROW_TILE, weight_rows, 0)
+    if rows_ref is not None:
+        lax.fori_loop(0, rows_ref.shape[0] // ROW_TILE, weight_rows, 0)
 
 
 def attend_backward(
@@ -463,15 +465,14 @@
     lse,
     cosine,
     sine,
-    rows_t,
+    *rows_t,
 ):
     count, cols = query.shape
-    width = rows_t.shape[0]
     vmem = pl.BlockSpec(memory_space=pltpu.VMEM)
     return pl.pallas_call(
         backward_kernel,
-        in_specs=[pl.BlockSpec(memory_space=pltpu.SMEM)] + [vmem] * 11,
-        out_specs=[vmem] * 2,
+        in_specs=[pl.BlockSpec(memory_space=pltpu.SMEM)] + [vmem] * (10 + len(rows_t)),
+        out_specs=[vmem] * (1 + len(rows_t)),
         scratch_shapes=[
             pltpu.VMEM((count, cols), f32),
             pltpu.VMEM((count, cols), f32),
@@ -479,7 +480,7 @@
         ],
         out_shape=[
             jax.ShapeDtypeStruct((3, count, cols), bf16),
-            jax.ShapeDtypeStruct((3, width, cols), bf16),
+            *[jax.ShapeDtypeStruct((3, rows.shape[0], cols), bf16) for rows in rows_t],
         ],
         name="attend_backward",
         cost_estimate=pl.CostEstimate(
@@ -497,7 +498,7 @@
         lse,
         cosine,
         sine,
-        rows_t,
+        *rows_t,
     )
 
 
@@ -738,6 +739,8 @@
         act_ref,
         dpre_ref,
         n2_t,
+        bup_other,
+        bias_sem,
         down_grad,
         up_grad,
         *rest,
@@ -867,6 +870,15 @@
             load_down(i, down_mine.at[:strip, :], h).wait()
 
     ex.greet()
+    bias_swap = pltpu.make_async_remote_copy(
+        src_ref=bup_ref,
+        dst_ref=bup_other,
+        send_sem=bias_sem.at[0],
+        recv_sem=bias_sem.at[1],
+        device_id=ex.across,
+        device_id_type=MESH,
+    )
+    bias_swap.start()
 
     def hand(k, _):
         hand_up(k, 0).start()
@@ -897,6 +909,8 @@
     for c in range(width // LANES):
         cols = slice(c * LANES, (c + 1) * LANES)
         n2_t[cols, :] = n2_ref[:, cols].T
+    n2_t[width:, :] = jnp.ones((PIECES, rows_all), bf16)
+    bias_swap.wait()
 
     def tile(i):
         other, k = which(i)
@@ -909,7 +923,9 @@
 
         up, down = up_buf.at[slot], down_buf.at[slot]
         bias_at = jnp.where(other, k, count + k)
-        bias_grad = jnp.zeros((1, HIDDEN_TILE), f32)
+        bias = jnp.where(other, bup_other[k], bup_ref[k])
+        linear = 0.7978845608028654
+        cubic = linear * 0.044715
         block = lambda r: slice(r * ROW_TILE, (r + 1) * ROW_TILE)
 
         def begin(r):
@@ -919,29 +935,28 @@
         for r in range(blocks):
             rows = block(r)
             ahead = begin(r + 1) if r + 1 < blocks else None
-            pre = ready[0] + bup_ref[bias_at]
+            pre = ready[0] + bias
             square = pre * pre
-            bend = jnp.tanh(0.7978845608028654 * (pre + 0.044715 * square * pre))
-            part_one = 0.5 * (1.0 + bend)
-            act = (pre * part_one).astype(bf16)
-            slope = part_one + (0.5 * pre) * (1.0 - bend * bend) * (
-                0.7978845608028654 * (1.0 + 3.0 * 0.044715 * square)
-            )
+            bend = jnp.tanh(pre * (square * cubic + linear))
+            gate = 0.5 * bend + 0.5
+            full_act = pre * gate
+            slope = gate + (full_act - full_act * gate) * (square * (6.0 * cubic) + 2.0 * linear)
+            act = full_act.astype(bf16)
             d_pre = (ready[1] * slope).astype(bf16)
             act_ref[rows, :] = act
             dpre_ref[rows, :] = d_pre
-            bias_grad = bias_grad + jnp.sum(d_pre.astype(f32), axis=0, keepdims=True)
             total_ref[rows, :] += dot(act, down[...])
             dn2_ref[rows, :] += dot(d_pre, up[...], NT)
             ready = ahead
-        gbup_ref[bias_at] = bias_grad
         down_grad[k] = dot(act_ref[...].T, dy_ref[...]).astype(bf16)
 
         def start(lane):
             for side, grad in sides:
                 side.start_a(k, lane, grad)
 
-        up_grad[k] = dot(n2_t[...], dpre_ref[...]).astype(bf16)
+        by_rows = dot(n2_t[...], dpre_ref[...])
+        up_grad[k] = by_rows[:width].astype(bf16)
+        gbup_ref[bias_at] = by_rows[width : width + 1]
         pl.when(other)(functools.partial(start, 0))
         pl.when(jnp.logical_not(other))(functools.partial(start, 1))
 
@@ -975,8 +990,7 @@
         each((i - 6) // 2, even, arrive)
         each((i - 5) // 2, odd, stage_d)
         each((i - 4) // 2, even, stage_c)
-        crossing = jnp.logical_or(i == 1, jnp.logical_and(even, i >= 2))
-        each(i // 2, crossing, stage_b)
+        each(i // 2, even, stage_b)
 
     def epilogue(r, _):
         rows = pl.ds(pl.multiple_of(r * ROW_TILE, ROW_TILE), ROW_TILE)
@@ -1071,7 +1085,9 @@
             pltpu.VMEM((rows, width), f32),
             pltpu.VMEM((rows, HIDDEN_TILE), bf16),
             pltpu.VMEM((rows, HIDDEN_TILE), bf16),
-            pltpu.VMEM((width, rows), bf16),
+            pltpu.VMEM((width + PIECES, rows), bf16),
+            pltpu.VMEM(bup.shape, f32),
+            pltpu.SemaphoreType.DMA((2,)),
             pltpu.VMEM((count, HIDDEN_TILE, width), bf16),
             pltpu.VMEM((count, width, HIDDEN_TILE), bf16),
         ]
@@ -1089,7 +1105,7 @@
 
 def leave_kernel(exchange, *refs):
     (
-        mine_ref,
+        rows_hbm,
         mine_out_ref,
         crossed_ref,
         crossed_out_ref,
@@ -1107,6 +1123,7 @@
         back_ref,
         sums_ref,
         out_buf,
+        rows_t_ref,
         d_ref,
         d2_ref,
         w_ref,
@@ -1127,11 +1144,18 @@
     place, part = lax.axis_index("dp"), lax.axis_index("mp")
     ex = exchange.bind(place, part, rest)
     count, bits = ex.count, ex.bits
-    first = mine_ref.shape[0]
+    first = mine_out_ref.shape[0]
     loads = [
         pltpu.make_async_copy(source, target, load_sem.at[n])
         for n, (source, target) in enumerate(
-            ((w_hbm, w_ref), (d_hbm, d_ref), (w2_hbm, w2_ref), (d2_hbm, d2_ref), (dmid_hbm, dmid_ref))
+            (
+                (w_hbm, w_ref),
+                (d_hbm, d_ref),
+                (w2_hbm, w2_ref),
+                (d2_hbm, d2_ref),
+                (rows_hbm, rows_t_ref),
+                (dmid_hbm, dmid_ref),
+            )
         )
     ]
     for load in loads:
@@ -1143,33 +1167,35 @@
     ex.partners += [near[j - 1] for j in (3, 5, 6, 7)]
     ex.greet()
 
-    def begin(k, _):
-        ex.start_a(k, 0, mine_ref)
-        return 0
-
-    lax.fori_loop(0, first, begin, 0)
-
     def begin_out(k, _):
         total = mine_out_ref[k].astype(f32) + crossed_out_ref[k].astype(f32)
-        out_buf[first + k] = total.astype(bf16)
-        ex.start_a(first + k, 0, out_buf)
+        out_buf[k] = total.astype(bf16)
+        ex.start_a(k, 0, out_buf)
         return 0
 
-    lax.fori_loop(0, count - first, begin_out, 0)
-
-    def back_of(rows):
+    lax.fori_loop(0, first, begin_out, 0)
+    step = KEY_ROWS // 3
+
+    def back_rows(n):
+        rows = pl.ds(pl.multiple_of(n * step, EDGE), step)
         total = 0.0
         for grads, weights in ((d_ref, w_ref), (d2_ref, w2_ref)):
             for c in range(3):
                 total = total + dot(grads[c, rows, :], weights[c], NT)
-        return total
+        rows_ref[rows, :] = total
+
+    def grad_chunk(j):
+        parts = rows_t_ref.shape[0] // ROW_TILE
+        rows = pl.ds(pl.multiple_of(j % parts * ROW_TILE, ROW_TILE), ROW_TILE)
+        out_buf[first + j] = dot(rows_t_ref[rows, :], d_ref[j // parts]).astype(bf16)
+        ex.start_a(first + j, 0, out_buf)
 
     def stage_c(k):
+        @pl.when(k >= first)
+        def _():
+            ex.stage_c(k, out_buf, lambda rows: crossed_ref[k - first, rows, :].astype(f32))
+
         @pl.when(k < first)
-        def _():
-            ex.stage_c(k, mine_ref, lambda rows: crossed_ref[k, rows, :].astype(f32))
-
-        @pl.when(k >= first)
         def _():
             ex.stage_c(k, out_buf)
 
@@ -1201,42 +1227,43 @@
     main = slice(0, HALF)
     edges = slice(HALF, HALF + 2 * EDGE)
     parts = tokens_ref.shape[0] // TILE
-    own = NOISY_OWN - 2 * HALF
     lead = small_ref.shape[0] - 2
     bias = lead - 3
     norm_ref[...] = jnp.zeros_like(norm_ref)
+    for load in loads[:4]:
+        load.wait()
+
+    def own_at(b):
+        start = jnp.where(b < TILES, NOISY_OWN + b * TILE, CLEAN_OWN + (b - TILES) * TILE)
+        return pl.ds(pl.multiple_of(start, EDGE), TILE)
+
+    def tokens_at(b):
+        return pl.ds(pl.multiple_of(b * TILE, TILE), TILE)
 
     def give_main():
-        for load in loads[:4]:
-            load.wait()
-        given = back_of(main)
-        give_ref[main, :] = given.astype(bf16)
-        rows_ref[:HALF, :] = given
+        give_ref[main, :] = rows_ref[main, :].astype(bf16)
         swap(main, 0).start()
+        loads[4].wait()
 
     def give_edges():
+        side = rows_ref[NOISY_BASE:NOISY_OWN, :] + rows_ref[NOISY_OWN + HALF :, :]
+        after = rows_ref[2 * HALF : NOISY_BASE, :]
+        give_ref[HALF : HALF + EDGE, :] = after.astype(bf16)
+        give_ref[HALF + EDGE :, :] = side.astype(bf16)
+        swap(edges, 1).start()
+        sums_of(after, normal(context_ref[:EDGE, :].astype(f32))[0])
+        sums_of(side, normal(context_ref[HALF:, :].astype(f32))[0])
+
+    def tell_near():
         def context_sums(b, _):
-            rows = pl.ds(pl.multiple_of(b * TILE, TILE), TILE)
+            rows = tokens_at(b)
             sums_of(rows_ref[rows, :], normal(context_ref[rows, :].astype(f32))[0])
             return 0
 
         lax.fori_loop(0, HALF // TILE, context_sums, 0)
-        tail = back_of(slice(2 * HALF, KEY_ROWS))
-        rows_ref[:HALF, :] = tail[own : own + HALF]
-        side = tail[EDGE:own] + tail[own + HALF :]
-        give_ref[HALF : HALF + EDGE, :] = tail[:EDGE].astype(bf16)
-        give_ref[HALF + EDGE :, :] = side.astype(bf16)
-        swap(edges, 1).start()
-        sums_of(tail[:EDGE], normal(context_ref[:EDGE, :].astype(f32))[0])
-        sums_of(side, normal(context_ref[HALF:, :].astype(f32))[0])
-
-    def own_clean():
-        rows_ref[HALF:, :] = back_of(slice(CLEAN_OWN, CLEAN_OWN + HALF))
-
-    def tell_near():
+
         def own_sums(b, _):
-            rows = pl.ds(pl.multiple_of(b * TILE, TILE), TILE)
-            sums_of(rows_ref[rows, :], normal(tokens_ref[rows, :].astype(f32))[0])
+            sums_of(rows_ref[own_at(b), :], normal(tokens_ref[tokens_at(b), :].astype(f32))[0])
             return 0
 
         lax.fori_loop(0, parts, own_sums, 0)
@@ -1299,18 +1326,20 @@
             far_copy(j, ex.z).start()
 
     def take_back():
-        loads[4].wait()
+        loads[5].wait()
         swap(main, 0).wait()
         swap(edges, 1).wait()
-        rows_ref[HALF:, :] += take_ref[main, :].astype(f32)
-        rows_ref[HALF : HALF + EDGE, :] += take_ref[HALF : HALF + EDGE, :].astype(f32)
-        edge = pl.ds(pl.multiple_of((1 - part) * (HALF - EDGE), EDGE), EDGE)
+        clean = slice(CLEAN_OWN, CLEAN_OWN + HALF)
+        rows_ref[clean, :] += take_ref[main, :].astype(f32)
+        begin = slice(CLEAN_OWN, CLEAN_OWN + EDGE)
+        rows_ref[begin, :] += take_ref[HALF : HALF + EDGE, :].astype(f32)
+        edge = pl.ds(pl.multiple_of(NOISY_OWN + (1 - part) * (HALF - EDGE), EDGE), EDGE)
         rows_ref[edge, :] += take_ref[HALF + EDGE :, :].astype(f32)
 
     def norm_back(b):
-        rows = pl.ds(pl.multiple_of(b * TILE, TILE), TILE)
+        rows = tokens_at(b)
         unit, scale = normal(tokens_ref[rows, :].astype(f32))
-        lean = rows_ref[rows, :] * vectors_ref[0:1, :]
+        lean = rows_ref[own_at(b), :] * vectors_ref[0:1, :]
         back_ref[rows, :] = dmid_ref[rows, :] + scale * (
             lean
             - jnp.mean(lean, axis=-1, keepdims=True)
@@ -1339,33 +1368,46 @@
             total = total + far_ref[5 + 2 * i]
         sums_ref[...] = total
 
-    actions = [give_main, give_edges, own_clean, tell_near, tell_far, take_back]
-    ticks = [0, 2, 5, 8, 12, 13]
+    chunks = count - first
+    begin_chunks, end_chunks = 1, 1 + chunks
+    actions = {
+        0: give_main,
+        end_chunks + 1: give_edges,
+        end_chunks + 2: tell_near,
+        end_chunks + 3: tell_far,
+        end_chunks + 4: take_back,
+    }
+    begin_back = end_chunks + 5
 
     def phase(p, _):
-        for n, action in enumerate(actions):
+        back = jnp.logical_or(p == 0, jnp.logical_or(p == end_chunks, p == end_chunks + 1))
+
+        @pl.when(back)
+        def _():
+            back_rows(jnp.where(p == 0, 0, p - end_chunks + 1))
+
+        @pl.when(jnp.logical_and(p >= begin_chunks, p < end_chunks))
+        def _():
+            grad_chunk(p - begin_chunks)
+
+        for n, action in actions.items():
             pl.when(p == n)(action)
-        block = p - len(actions)
+        block = p - begin_back
 
         @pl.when(jnp.logical_and(block >= 0, block < parts))
         def _():
             norm_back(block)
 
         pl.when(block == parts)(end_far)
-        low = jnp.maximum(block, 0) + ticks[-1]
-        high = low + 1
-        for n in reversed(range(len(actions))):
-            low = jnp.where(p == n, ticks[n], low)
-            high = jnp.where(p == n, ticks[n + 1] if n + 1 < len(ticks) else ticks[n], high)
-        lax.fori_loop(low, high, lambda i, _: (steps(i), 0)[1], 0)
+        steps(p - 1)
         return 0
 
-    lax.fori_loop(0, len(actions) + count + 10 - ticks[-1], phase, 0)
-
-
-def leave(bits, mine, crossed, d_fields, weights, tokens, context, vectors, d_mid, small, small2):
-    total = mine[0].shape[0] + mine[1].shape[0]
-    rows, cols = mine[0].shape[1:]
+    lax.fori_loop(0, max(begin_back + parts + 1, count + 11), phase, 0)
+
+
+def leave(bits, rows_t, mine, crossed, d_fields, weights, tokens, context, vectors, d_mid, small, small2):
+    total = mine.shape[0] + crossed[0].shape[0]
+    rows, cols = mine.shape[1:]
     exchange = Exchange(bits, total, rows, cols)
     count, width = tokens.shape
     vmem = pl.BlockSpec(memory_space=pltpu.VMEM)
@@ -1373,7 +1415,7 @@
     shape = jax.ShapeDtypeStruct
     return pl.pallas_call(
         functools.partial(leave_kernel, exchange),
-        in_specs=[vmem] * 4 + [hbm] * 4 + [vmem] * 3 + [hbm] + [vmem] * 2,
+        in_specs=[hbm] + [vmem] * 3 + [hbm] * 4 + [vmem] * 3 + [hbm] + [vmem] * 2,
         out_specs=[vmem] * 3,
         out_shape=[
             shape((total, rows, cols), bf16),
@@ -1382,13 +1424,14 @@
         ],
         scratch_shapes=[
             pltpu.VMEM((total, rows, cols), bf16),
+            pltpu.VMEM(rows_t.shape, bf16),
             pltpu.VMEM(d_fields[0].shape, bf16),
             pltpu.VMEM(d_fields[1].shape, bf16),
             pltpu.VMEM(weights[0].shape, bf16),
             pltpu.VMEM(weights[1].shape, bf16),
             pltpu.VMEM(d_mid.shape, f32),
-            pltpu.SemaphoreType.DMA((5,)),
-            pltpu.VMEM((count, width), f32),
+            pltpu.SemaphoreType.DMA((6,)),
+            pltpu.VMEM((KEY_ROWS, width), f32),
             pltpu.VMEM((HALF + 2 * EDGE, width), bf16),
             pltpu.VMEM((HALF + 2 * EDGE, width), bf16),
             pltpu.SemaphoreType.DMA((2, 2)),
@@ -1407,8 +1450,53 @@
             flops=40 * 10**9, bytes_accessed=40 * 10**6, transcendentals=0
         ),
     )(
-        *mine, *crossed, *d_fields, *weights, tokens, context, vectors, d_mid, small, small2
-    )
+        rows_t, mine, *crossed, *d_fields, *weights, tokens, context, vectors, d_mid, small, small2
+    )
+
+
+def assemble_kernel(core_ref, down_mine, up_mine, down_got, up_got, down_ref, up_ref):
+    core = core_ref[0]
+    block = down_mine.shape[1]
+    lanes = up_ref.shape[1]
+    parts = down_mine.shape[2] // lanes
+    deep = block * parts
+    for side, down, up in ((core, down_mine, up_mine), (1 - core, down_got, up_got)):
+        rows = pl.ds(pl.multiple_of(side * block, block), block)
+        down_ref[rows, :] = down[0].astype(f32)
+        for n in range(block // PIECES):
+            for c in range(parts):
+                at = side * deep + (n * parts + c) * PIECES
+                rows = pl.ds(pl.multiple_of(at, PIECES), PIECES)
+                piece = up[0, n * PIECES : (n + 1) * PIECES, c * lanes : (c + 1) * lanes]
+                up_ref[rows, :] = piece.astype(f32)
+
+
+def assemble(core, gathered, moved):
+    tiles, half, width = gathered.shape
+    count = tiles // 2
+    down_spec = pl.BlockSpec((1, half, width), lambda k, c: (k, 0, 0))
+    up_spec = pl.BlockSpec((1, half, width), lambda k, c: (count + k, 0, 0))
+    hidden = count * 2 * half
+    return pl.pallas_call(
+        assemble_kernel,
+        grid_spec=pltpu.PrefetchScalarGridSpec(
+            num_scalar_prefetch=1,
+            grid=(count,),
+            in_specs=[down_spec, up_spec, down_spec, up_spec],
+            out_specs=[
+                pl.BlockSpec((2 * half, width), lambda k, c: (k, 0)),
+                pl.BlockSpec((width, 2 * half), lambda k, c: (0, k)),
+            ],
+        ),
+        out_shape=[
+            jax.ShapeDtypeStruct((hidden, width), f32),
+            jax.ShapeDtypeStruct((width, hidden), f32),
+        ],
+        name="assemble",
+        cost_estimate=pl.CostEstimate(
+            flops=10**6, bytes_accessed=14 * 10**6, transcendentals=0
+        ),
+    )(core, gathered, gathered, moved, moved)
 
 
 def key_layout(seq_lengths, block_len, part):
@@ -1515,7 +1603,6 @@
     vectors = jnp.stack([ln1_gain, ln1_bias, ln2_gain, ln2_bias, b_down])
     context, (quarters, layout, vectors) = tie(context, (quarters, layout, vectors))
     qkv_here, up_here, down_here, out_here = [across(piece) for piece in quarters]
-    bias_other = across(b_up)
 
     spans, clean_bounds, noisy_bounds, cosine, sine = layout
     normed1, normed1_t, *fields = enter(tokens, context, vectors, qkv_mine, cosine, sine)
@@ -1531,12 +1618,12 @@
     out_beside = beside(out_here)
     down_beside = beside(down_here)
     other = [*fields, *attend_forward(spans, clean_bounds, noisy_bounds, *fields)]
-    (out_here, out_beside, up_here, up_beside, down_here, down_beside, bias_other), _ = tie(
-        (out_here, out_beside, up_here, up_beside, down_here, down_beside, bias_other), other[3]
+    (out_here, out_beside, up_here, up_beside, down_here, down_beside), _ = tie(
+        (out_here, out_beside, up_here, up_beside, down_here, down_beside), other[3]
     )
     out_half = in_order(side, out_here, out_beside)
     out_other = in_order(core, out_half, sibling(out_half))
-    bias_all = jnp.concatenate([bias_other, b_up]).astype(f32).reshape(-1, 1, HIDDEN_TILE)
+    bias_all = b_up.astype(f32).reshape(-1, 1, HIDDEN_TILE)
 
     x_rows = tokens.reshape(TOK_DEV, width)
     out, d_mid, d_att, d_att2, grad_out, grad_out2, grad_bias, norms, pieces = middle(
@@ -1563,7 +1650,7 @@
         for k in range(1, 1 << n)
     ]
 
-    def backward(saved, d_attended, spans):
+    def backward(saved, d_attended, spans, *rows_t):
         query, keys, values, attended, lse = saved
         return attend_backward(
             spans,
@@ -1577,10 +1664,10 @@
             lse,
             cosine,
             sine,
-            normed1_t,
+            *rows_t,
         )
 
-    d_fields2, grad2 = backward(other, d_att2, spans)
+    d_fields2, grad2 = backward(other, d_att2, spans, normed1_t)
     grad2 = grad2.reshape(-1, ROW_TILE, grad2.shape[2])
     low_bit, high_bit = (place >> 2) & 1, (place >> 3) & 1
     moved, _ = tie(moved, grad2)
@@ -1597,18 +1684,18 @@
     (crossing, gathered), spans = tie((crossing, gathered), spans)
     crossed = across(crossing)
     moved = beside(gathered)
-    d_fields1, grad1 = backward(mine, d_att, spans)
-    grad1 = grad1.reshape(-1, ROW_TILE, grad1.shape[2])
-    moved, grad1 = tie(moved, grad1)
+    (d_fields1,) = backward(mine, d_att, spans)
+    moved, d_fields1 = tie(moved, d_fields1)
     gathered = in_order(side, gathered, moved, 1)
-    gathered, grad1 = tie(gathered, grad1)
+    gathered, d_fields1 = tie(gathered, d_fields1)
     moved = sibling(gathered)
     lead = hidden // width
     bias2, bias1 = grad_bias.reshape(2, lead, width)
     shared = jnp.concatenate([norms[:3], jnp.zeros((2, width), f32)], axis=0)
     full, grad_tokens, sums = leave(
         bits,
-        (grad1, grad_out.reshape(-1, ROW_TILE, grad_out.shape[1])),
+        normed1_t,
+        grad_out.reshape(-1, ROW_TILE, grad_out.shape[1]),
         (crossed, crossed_out.reshape(-1, ROW_TILE, grad_out.shape[1])),
         (d_fields1, d_fields2),
         (qkv_mine, qkv_other),
@@ -1620,15 +1707,11 @@
         jnp.concatenate([bias2, shared], axis=0),
     )
     moved, _ = tie(moved, full)
-    gathered = in_order(core, gathered, moved, 1)
-    count = hidden // HIDDEN_TILE
-    grad_down = gathered[:count].reshape(hidden, width).astype(f32)
-    grad_up = gathered[count:].reshape(count, PIECES, PIECES, width // HIDDEN_TILE, HIDDEN_TILE)
-    grad_up = grad_up.transpose(1, 3, 2, 0, 4).reshape(width, hidden).astype(f32)
-    split = 3 * width // ROW_TILE
-    grad_qkv = full[:split].reshape(qkv_mine.shape).transpose(1, 0, 2).astype(f32)
-    flat = full[split:].reshape(2, w_out.shape[0], width // 2)
+    grad_down, grad_up = assemble(core.reshape(1), gathered, moved)
+    split = grad_out.shape[0] // ROW_TILE
+    flat = full[:split].reshape(2, w_out.shape[0], width // 2)
     grad_out = jnp.concatenate([flat[0], flat[1]], axis=1).astype(f32)
+    grad_qkv = full[split:].reshape(qkv_mine.shape).transpose(1, 0, 2).astype(f32)
     return (
         out.reshape(tokens.shape),
         grad_tokens.reshape(tokens.shape),

time: 390 us -> 355 us (0.910)
  local copies, waits for them, and re-layouts: 40 us -> 20.2 us
  other arithmetic: 26.4 us -> 17.1 us
  Pallas kernels: 271 us -> 267 us
    pallas_call x2, Pallas kernels: 58.6 us -> 43.5 us  [attend_backward(): pl.pallas_call(backward_kernel, in_specs=[pl.BlockSpec(memory_space=pltpu...]
    convert_element_type x2 -> x0, local copies, waits for them, and re-layouts: 14.5 us -> none  [local(): grad_up.transpose(1, 3, 2, 0, 4).reshape(width, hidden).astype(f32)]
    pallas_call x1 -> x2, Pallas kernels: 62.9 us -> 73.5 us  [the longest x1 66.4 us: leave(): pl.pallas_call(functools.partial(leave_kernel, exchange), in_specs=[hbm]...]
    ppermute x8 -> x7, starting transfers between devices: 19.4 us -> 14.6 us  [across(): return lax.ppermute(array, 'mp', [(0, 1), (1, 0)])]
    unnamed x29 -> x32, local copies, waits for them, and re-layouts: 10 us -> 5.54 us
    ppermute x8 -> x7, waiting for transfers between devices: 13.6 us -> 11.8 us  [across(): return lax.ppermute(array, 'mp', [(0, 1), (1, 0)])]
  transfers between devices with their start and end apart: 20 -> 19, of which waited for: 5 -> 6; matrix products, arithmetic and copies ran while one was open for 8% -> 8% of each run, Pallas kernels for 45% -> 45%
where the time goes in v1:
time: 355 us; the launch traced here: 352 us
  Pallas kernels  267 us (75%)
  starting transfers between devices  26.4 us (7%)
  local copies, waits for them, and re-layouts  20.2 us (6%)
  waiting for transfers between devices  19.7 us (6%)
  other arithmetic  17.1 us (5%)
    pallas_call x1, Pallas kernels, middle(): pl.pallas_call(functools.partial(middle_kernel, exchanges, tiles), in_spe...  99.7 us
    pallas_call x1, Pallas kernels, leave(): pl.pallas_call(functools.partial(leave_kernel, exchange), in_specs=[hbm]...  66.4 us
    pallas_call x2, Pallas kernels, attend_backward(): pl.pallas_call(backward_kernel, in_specs=[pl.BlockSpec(memory_space=pltpu...  43.5 us
    pallas_call x2, Pallas kernels, attend_forward(): pl.pallas_call(forward_kernel, in_specs=[pl.BlockSpec(memory_space=pltpu....  31.3 us
    ppermute x7, starting transfers between devices, across(): return lax.ppermute(array, 'mp', [(0, 1), (1, 0)])  14.6 us
    ppermute x7, waiting for transfers between devices, across(): return lax.ppermute(array, 'mp', [(0, 1), (1, 0)])  11.8 us
    pallas_call x1, Pallas kernels, enter(): pl.pallas_call(enter_kernel, in_specs=[vmem] * 6, out_specs=[vmem] * 5, o...  11.4 us
    ppermute x5, waiting for transfers between devices, beside(): return lax.ppermute(array, 'dp', [(i, i ^ 2) for i in range(dp_size)])  7.61 us
  transfers between devices with their start and end apart: 19, of which 6 were waited for; matrix products, arithmetic and copies ran while one was open for 8% of the time, Pallas kernels for 45%

profile of v1, /device:TPU:0, one launch (start us, length us, event | category | flops | bytes accessed | tf_op | source)
XLA Modules:
  0.0 352.0 jit_solution(8619560602162837717)
XLA Ops:
  0.7 1.2 slice_bitcast_fusion
  1.9 0.8 select_bitcast_fusion
  2.8 3.0 collective-permute-start
  5.8 0.2 reduce-window.8
  6.9 0.3 fusion.16
  7.3 0.2 reduce_min.21
  7.6 1.1 dynamic-slice_bitcast_fusion
  8.7 1.1 constant_dynamic-slice_fusion.2
  9.8 0.9 constant_dynamic-slice_fusion.1
  10.8 0.7 pad_add_fusion.1.span_ref
  11.4 0.6 add_add_fusion.clean_ref
  12.0 0.6 pad_add_fusion.noisy_ref
  12.6 0.6 stack.29.vectors_ref.refs_6_.refs_10_
  13.3 1.1 constant_dynamic-slice_fusion.3
  14.4 4.4 %fusion = (f32[1584,128]{1,0:T(8,128)}, f32[1584,128]{1,0:T(8,128)}) fusion(f32[128]{0:T(128)S(1)} %get-tuple-element.191, f32[128]{0:T(128)S(1)} %get-tuple-element.192, f32[1584]{0:T(1024)S(1)} %get-tuple-element.185), kind=kLoop, calls=%fused_computation.12 | loop fusion | flops 405504 | bytes 1629376 | tf_op jit(solution)/shard_map/mul | solution.py:1541
  18.8 5.2 %collective-permute-done.context_ref.refs_9_ = bf16[528,768]{1,0:T(8,128)(2,1)} collective-permute-done((bf16[528,768]{1,0:T(8,128)(2,1)S(1)}, bf16[528,768]{1,0:T(8,128)(2,1)}, u32[]{:S(2)}, u32[]{:S(2)}) %collective-permute-start) | collective-permute-done | bytes 811040 | tf_op jit(solution)/shard_map/ppermute | solution.py:1579
  24.0 1.7 collective-permute-start.1
  25.7 0.3 collective-permute-start.5
  26.0 11.4 %enter.1 = (bf16[1584,768]{1,0:T(8,128)(2,1)}, bf16[768,1584]{1,0:T(8,128)(2,1)}, bf16[1584,384]{1,0:T(8,128)(2,1)}, bf16[1584,384]{1,0:T(8,128)(2,1)}, bf16[1584,384]{1,0:T(8,128)(2,1)}) custom-call(bf16[2,512,768]{2,1,0:T(8,128)(2,1)} %tokens_ref.1, bf16[528,768]{1,0:T(8,128)(2,1)} %collective-permute-done.context_ref.refs_9_, ...), custom_call_target="tpu_custom_call" | custom-call | flops 10000000000 | bytes 16000000 | tf_op jit(solution)/shard_map/enter/pallas_call | solution.py:157
  37.4 1.7 collective-permute-start.4
  39.1 15.7 %attend_forward.2 = (bf16[1024,384]{1,0:T(8,128)(2,1)}, f32[3,4,2,256]{3,2,1,0:T(2,128)}) custom-call(s32[4,2]{1,0:T(4,128)} %pad_add_fusion.1.span_ref, s32[4,2,256]{2,1,0:T(2,128)} %add_add_fusion.clean_ref, s32[4,2,128]{2,1,0:T(2,128)} %pad_add_fusion.noisy_ref, bf16[1584,384]{1,0:T(8,128)(2,1)} %get-tuple-element.91.q_ref, ...), custom_call_target="tpu_custom_call" | custom-call | flops 1610612736 | bytes 4866048 | tf_op jit(solution)/shard_map/attend_forward/pallas_call | solution.py:290
  55.0 4.8 %collective-permute-start.2 = (bf16[384,768]{1,0:T(8,128)(2,1)S(1)}, bf16[384,768]{1,0:T(8,128)(2,1)}, u32[]{:S(2)}, u32[]{:S(2)}) collective-permute-start(bf16[384,768]{1,0:T(8,128)(2,1)S(1)} %constant_dynamic-slice_fusion.2), channel_id=1, source_target_pairs={{0,1},{1,0},{2,3},{3,2},{4,5},{5,4},{6,7},{7,6},{8,9},{9,8},{10,11... | collective-permute-start | bytes 1769480 | tf_op jit(solution)/shard_map/ppermute | solution.py:1579
  59.9 1.5 collective-permute-start.8
  61.4 0.3 broadcast_select_fusion.3
  61.7 1.4 pad_maximum_fusion.1.w_ref.refs_7_
  63.1 7.4 %project.1 = (bf16[1584,384]{1,0:T(8,128)(2,1)}, bf16[1584,384]{1,0:T(8,128)(2,1)}, bf16[1584,384]{1,0:T(8,128)(2,1)}) custom-call(bf16[1584,768]{1,0:T(8,128)(2,1)} %get-tuple-element.97.rows_ref, bf16[3,768,384]{2,1,0:T(8,128)(2,1)} %pad_maximum_fusion.1.w_ref.refs_7_, f32[1584,128]{1,0:T(8,128)} %get-tuple-element.86.cos_ref, ...), custom_call_target="tpu_custom_call" | custom-call | flops 2802843648 | bytes 7852032 | tf_op jit(solution)/shard_map/project/pallas_call | solution.py:78
  70.5 6.4 %collective-permute-done.3 = bf16[96,768]{1,0:T(8,128)(2,1)S(1)} collective-permute-done((bf16[96,768]{1,0:T(8,128)(2,1)S(1)}, bf16[96,768]{1,0:T(8,128)(2,1)S(1)}, u32[]{:S(2)}, u32[]{:S(2)}) %collective-permute-start.3) | collective-permute-done | bytes 147488 | tf_op jit(solution)/shard_map/ppermute | solution.py:1579
  76.9 1.5 collective-permute-start.9
  78.4 0.5 collective-permute-start.7
  78.9 15.7 %attend_forward.3 = (bf16[1024,384]{1,0:T(8,128)(2,1)}, f32[3,4,2,256]{3,2,1,0:T(2,128)}) custom-call(s32[4,2]{1,0:T(4,128)} %pad_add_fusion.1.span_ref, s32[4,2,256]{2,1,0:T(2,128)} %add_add_fusion.clean_ref, s32[4,2,128]{2,1,0:T(2,128)} %pad_add_fusion.noisy_ref, bf16[1584,384]{1,0:T(8,128)(2,1)} %get-tuple-element.105.q_ref, ...), custom_call_target="tpu_custom_call" | custom-call | flops 1610612736 | bytes 4866048 | tf_op jit(solution)/shard_map/attend_forward/pallas_call | solution.py:290
  94.6 0.8 collective-permute-done.7
  95.5 0.6 reshape.352.refs_7_
  96.1 0.6 pad.7.clone
  96.7 0.3 collective-permute-done.10
  97.1 0.9 pad_maximum_fusion.5.refs_4_
  98.0 99.7 %middle.1 = (bf16[1024,768]{1,0:T(8,128)(2,1)}, f32[1024,768]{1,0:T(8,128)}, bf16[1024,384]{1,0:T(8,128)(2,1)}, bf16[1024,384]{1,0:T(8,128)(2,1)}, bf16[768,384]...) custom-call(bf16[1024,768]{1,0:T(8,128)(2,1)} %bitcast.45, ...), custom_call_target="tpu_custom_call" | custom-call | flops 60000002048 | bytes 40000000 | tf_op jit(solution)/shard_map/middle/pallas_call | solution.py:1060
  197.7 0.4 collective-permute-start.12
  198.1 2.0 collective-permute-start.13
  200.1 2.0 collective-permute-start.14
  202.1 24.0 %attend_backward.2 = (bf16[3,1584,384]{2,1,0:T(8,128)(2,1)}, bf16[3,768,384]{2,1,0:T(8,128)(2,1)}) custom-call(s32[4,2]{1,0:T(4,128)} %pad_add_fusion.1.span_ref, s32[4,2,256]{2,1,0:T(2,128)} %add_add_fusion.clean_ref, s32[4,2,128]{2,1,0:T(2,128)} %pad_add_fusion.noisy_ref, bf16[1584,384]{1,0:T(8,128)(2,1)} %get-tuple-element.105.q_ref, ...), custom_call_target="tpu_custom_call" | custom-call | flops 35999997952 | bytes 36000000 | tf_op jit(solution)/shard_map/attend_backward/pallas_call | solution.py:472
  226.2 1.3 constant_dynamic-slice_fusion
  227.6 4.6 %collective-permute-start.16 = (bf16[768,384]{1,0:T(8,128)(2,1)}, bf16[768,384]{1,0:T(8,128)(2,1)}, u32[]{:S(2)}, u32[]{:S(2)}) collective-permute-start(bf16[768,384]{1,0:T(8,128)(2,1)} %get-tuple-element.129), channel_id=1, source_target_pairs={{0,1},{1,0},{2,3},{3,2},{4,5},{5,4},{6,7},{7,6},{8,9},{9,8},{10,11... | collective-permute-start | bytes 1769480 | tf_op jit(solution)/shard_map/ppermute | solution.py:1579
  232.3 0.7 fusion.4
  233.1 0.3 broadcast_select_fusion.5
  233.5 1.4 copy-done.1
  234.9 0.2 add_convert_fusion
  235.2 1.9 collective-permute-start.17
  237.1 19.4 %attend_backward.3.refs_4_ = bf16[3,1584,384]{2,1,0:T(8,128)(2,1)} custom-call(s32[4,2]{1,0:T(4,128)} %pad_add_fusion.1.span_ref, s32[4,2,256]{2,1,0:T(2,128)} %add_add_fusion.clean_ref, s32[4,2,128]{2,1,0:T(2,128)} %pad_add_fusion.noisy_ref, bf16[1584,384]{1,0:T(8,128)(2,1)} %get-tuple-element.91.q_ref, bf16[1584,384]{1,0:T(8,128)(2,1)} %get-tuple-element.92.k_ref, ...), custom_call_target="tpu_custom_call" | custom-call | flops 35999997952 | bytes 36000000 | tf_op jit(solution)/shard_map/attend_backward/pallas_call | solution.py:472
  256.6 6.9 %collective-permute-done.17 = bf16[12,64,768]{2,1,0:T(8,128)(2,1)S(1)} collective-permute-done((bf16[12,64,768]{2,1,0:T(8,128)(2,1)S(1)}, bf16[12,64,768]{2,1,0:T(8,128)(2,1)S(1)}, u32[]{:S(2)}, u32[]{:S(2)}) %collective-permute-start.17) | collective-permute-done | bytes 1179680 | tf_op jit(solution)/shard_map/ppermute | solution.py:1585
  263.4 0.2 broadcast_select_fusion.1
  263.6 1.6 pad_maximum_fusion.down_mine.up_mine
  265.2 0.2 collective-permute-done.15.refs_2_
  265.4 66.4 %leave.1 = (bf16[12,256,384]{2,1,0:T(8,128)(2,1)}, f32[1024,768]{1,0:T(8,128)}, f32[16,768]{1,0:T(8,128)}) custom-call(bf16[768,1584]{1,0:T(8,128)(2,1)} %get-tuple-element.119.refs_0_, bf16[3,256,384]{2,1,0:T(8,128)(2,1)} %bitcast.58, bf16[9,128,384]{2,1,0:T(8,128)(2,1)} %collective-permute-done.15.refs_2_, bf16[3,256,384]{2,1,0:T(8,128)(2,1)} %bitcast.18.refs_3_, ...), custom_call_target="tpu_custom_call" | custom-call | flops 40000000000 | bytes 40000000 | tf_op jit(solution)/shard_map/leave/pallas_call | solution.py:1416
  331.8 1.7 slice.68
  333.5 1.1 slice.69
  334.7 0.7 slice.74
  335.4 0.6 reshape.350
  336.0 1.6 slice_reduce_fusion.2
  337.7 1.1 maximum_convert_fusion
  338.8 2.0 convert_bitcast_fusion
  340.8 7.1 %assemble.1 = (f32[1536,768]{1,0:T(8,128)}, f32[768,1536]{1,0:T(8,128)}) custom-call(s32[1]{0:T(128)} %bitcast.25.core_ref, bf16[12,128,768]{2,1,0:T(8,128)(2,1)} %pad_maximum_fusion.down_mine.up_mine, bf16[12,128,768]{2,1,0:T(8,128)(2,1)} %pad_maximum_fusion.down_mine.up_mine, bf16[12,128,768]{2,1,0:T(8,128)(2,1)} %collective-permute-done.18.down_got.up_got, ...), custom_call_target="tpu_custom_call" | custom-call | flops 1000000 | bytes 14000000 | tf_op jit(solution)/shard_map/assemble/pallas_call | solution.py:1480
  347.9 1.1 copy.39
  349.1 1.3 copy-done
  350.4 1.7 copy.40
  (78 shorter events, 1.7 us)
Async XLA Ops:
  0.6 5.2 %copy-start.13 = (s32[1,4]{1,0:T(1,128)S(1)}, s32[1,4]{1,0:T(1,128)}, u32[]{:S(2)}) copy-start(s32[1,4]{1,0:T(1,128)} %param.15) | copy-start | bytes 52
  0.7 6.9 %copy-start.6 = (f32[768]{0:T(1024)S(1)}, f32[768]{0:T(1024)}, u32[]{:S(2)}) copy-start(f32[768]{0:T(1024)} %param.18) | copy-start | bytes 9220
  0.7 6.9 %copy-start.7 = (f32[768]{0:T(1024)S(1)}, f32[768]{0:T(1024)}, u32[]{:S(2)}) copy-start(f32[768]{0:T(1024)} %param.19) | copy-start | bytes 9220
  0.7 6.9 %copy-start.8 = (f32[768]{0:T(1024)S(1)}, f32[768]{0:T(1024)}, u32[]{:S(2)}) copy-start(f32[768]{0:T(1024)} %param.22) | copy-start | bytes 9220
  0.7 6.9 %copy-start.9 = (f32[768]{0:T(1024)S(1)}, f32[768]{0:T(1024)}, u32[]{:S(2)}) copy-start(f32[768]{0:T(1024)} %param.23) | copy-start | bytes 9220
  0.7 6.9 %copy-start.10 = (f32[768]{0:T(1024)S(1)}, f32[768]{0:T(1024)}, u32[]{:S(2)}) copy-start(f32[768]{0:T(1024)} %param.27) | copy-start | bytes 9220
  2.8 21.2 %collective-permute-start = (bf16[528,768]{1,0:T(8,128)(2,1)S(1)}, bf16[528,768]{1,0:T(8,128)(2,1)}, u32[]{:S(2)}, u32[]{:S(2)}) collective-permute-start(bf16[528,768]{1,0:T(8,128)(2,1)S(1)} %pad_maximum_fusion.4), channel_id=1, source_target_pairs={{0,1},{1,0},{2,3},{3,2},{4,5},{5,4},{6,7},{7,6},{8,9},{9,8},{10,11... | collective-permute-start | bytes 2433032 | tf_op jit(solution)/shard_map/ppermute | solution.py:1579
  24.0 13.4 %collective-permute-start.1 = (bf16[3,192,384]{2,1,0:T(8,128)(2,1)S(1)}, bf16[3,192,384]{2,1,0:T(8,128)(2,1)S(1)}, u32[]{:S(2)}, u32[]{:S(2)}) collective-permute-start(bf16[3,192,384]{2,1,0:T(8,128)(2,1)S(1)} %dynamic-slice_bitcast_fusion), channel_id=1, source_target_pairs={{0,1},{1,0},{2,3},{3,2},{4,5},{5,4},{6,7},{7,6},{8,9},{9,8},{10,11... | collective-permute-start | bytes 1327112 | tf_op jit(solution)/shard_map/ppermute | solution.py:1579
  25.7 29.0 %collective-permute-start.5 = (bf16[192,1536]{1,0:T(8,128)(2,1)S(1)}, bf16[192,1536]{1,0:T(8,128)(2,1)}, u32[]{:S(2)}, u32[]{:S(2)}) collective-permute-start(bf16[192,1536]{1,0:T(8,128)(2,1)S(1)} %constant_dynamic-slice_fusion.3), channel_id=1, source_target_pairs={{0,1},{1,0},{2,3},{3,2},{4,5},{5,4},{6,7},{7,6},{8,9},{9,8},{10,11... | collective-permute-start | bytes 1769480 | tf_op jit(solution)/shard_map/ppermute | solution.py:1579
  37.4 17.4 %collective-permute-start.4 = (bf16[3,192,384]{2,1,0:T(8,128)(2,1)S(1)}, bf16[3,192,384]{2,1,0:T(8,128)(2,1)S(1)}, u32[]{:S(2)}, u32[]{:S(2)}) collective-permute-start(bf16[3,192,384]{2,1,0:T(8,128)(2,1)S(1)} %collective-permute-done.1), channel_id=1, source_target_pairs={{0,4},{2,6},{4,0},{6,2},{8,12},{10,14},{12,8},{14,10},{16,20},{18,... | collective-permute-start | bytes 1327112 | tf_op jit(solution)/shard_map/ppermute | solution.py:1585
  54.9 6.5 %collective-permute-start.6 = (bf16[3,384,384]{2,1,0:T(8,128)(2,1)S(1)}, bf16[3,384,384]{2,1,0:T(8,128)(2,1)S(1)}, u32[]{:S(2)}, u32[]{:S(2)}) collective-permute-start(bf16[3,384,384]{2,1,0:T(8,128)(2,1)S(1)} %pad_maximum_fusion.3), channel_id=1, source_target_pairs={{0,2},{2,0},{4,6},{6,4},{8,10},{10,8},{12,14},{14,12},{16,18},{18,... | collective-permute-start | bytes 2654216 | tf_op jit(solution)/shard_map/ppermute | solution.py:1582
  55.0 21.8 %collective-permute-start.2 = (bf16[384,768]{1,0:T(8,128)(2,1)S(1)}, bf16[384,768]{1,0:T(8,128)(2,1)}, u32[]{:S(2)}, u32[]{:S(2)}) collective-permute-start(bf16[384,768]{1,0:T(8,128)(2,1)S(1)} %constant_dynamic-slice_fusion.2), channel_id=1, source_target_pairs={{0,1},{1,0},{2,3},{3,2},{4,5},{5,4},{6,7},{7,6},{8,9},{9,8},{10,11... | collective-permute-start | bytes 1769480 | tf_op jit(solution)/shard_map/ppermute | solution.py:1579
  59.8 17.1 %collective-permute-start.3 = (bf16[96,768]{1,0:T(8,128)(2,1)S(1)}, bf16[96,768]{1,0:T(8,128)(2,1)S(1)}, u32[]{:S(2)}, u32[]{:S(2)}) collective-permute-start(bf16[96,768]{1,0:T(8,128)(2,1)S(1)} %constant_dynamic-slice_fusion.1), channel_id=1, source_target_pairs={{0,1},{1,0},{2,3},{3,2},{4,5},{5,4},{6,7},{7,6},{8,9},{9,8},{10,11... | collective-permute-start | bytes 442376 | tf_op jit(solution)/shard_map/ppermute | solution.py:1579
  59.9 34.7 %collective-permute-start.8 = (bf16[192,1536]{1,0:T(8,128)(2,1)}, bf16[192,1536]{1,0:T(8,128)(2,1)}, u32[]{:S(2)}, u32[]{:S(2)}) collective-permute-start(bf16[192,1536]{1,0:T(8,128)(2,1)} %collective-permute-done.5.refs_9_), channel_id=1, source_target_pairs={{0,4},{2,6},{4,0},{6,2},{8,12},{10,14},{12,8},{14,10},{16,20},{18,... | collective-permute-start | bytes 1769480 | tf_op jit(solution)/shard_map/ppermute | solution.py:1585
  76.9 18.6 %copy-start.11 = (bf16[1536]{0:T(1024)(128)(2,1)S(1)}, bf16[1536]{0:T(1024)(128)(2,1)}, u32[]{:S(2)}) copy-start(bf16[1536]{0:T(1024)(128)(2,1)} %param.25) | copy-start | bytes 9220
  76.9 18.5 %collective-permute-start.9 = (bf16[384,768]{1,0:T(8,128)(2,1)}, bf16[384,768]{1,0:T(8,128)(2,1)S(1)}, u32[]{:S(2)}, u32[]{:S(2)}) collective-permute-start(bf16[384,768]{1,0:T(8,128)(2,1)} %collective-permute-done.2.refs_12_), channel_id=1, source_target_pairs={{0,4},{2,6},{4,0},{6,2},{8,12},{10,14},{12,8},{14,10},{16,20},{18,... | collective-permute-start | bytes 1769480 | tf_op jit(solution)/shard_map/ppermute | solution.py:1585
  78.4 16.9 %collective-permute-start.7 = (bf16[96,768]{1,0:T(8,128)(2,1)S(1)}, bf16[96,768]{1,0:T(8,128)(2,1)S(1)}, u32[]{:S(2)}, u32[]{:S(2)}) collective-permute-start(bf16[96,768]{1,0:T(8,128)(2,1)S(1)} %collective-permute-done.3), channel_id=1, source_target_pairs={{0,4},{2,6},{4,0},{6,2},{8,12},{10,14},{12,8},{14,10},{16,20},{18,... | collective-permute-start | bytes 442376 | tf_op jit(solution)/shard_map/ppermute | solution.py:1585
  95.3 2.7 copy-start.14
  95.4 1.6 collective-permute-start.10
  197.7 35.3 %collective-permute-start.12 = (bf16[12,16,768]{2,1,0:T(8,128)(2,1)}, bf16[12,16,768]{2,1,0:T(8,128)(2,1)S(1)}, u32[]{:S(2)}, u32[]{:S(2)}) collective-permute-start(bf16[12,16,768]{2,1,0:T(8,128)(2,1)} %get-tuple-element.124), channel_id=1, source_target_pairs={{0,8},{2,10},{4,12},{6,14},{8,0},{10,2},{12,4},{14,6},{16,24},{18,... | collective-permute-start | bytes 884744 | tf_op jit(solution)/shard_map/ppermute | solution.py:1649
  198.1 34.9 %collective-permute-start.13 = (bf16[12,16,768]{2,1,0:T(8,128)(2,1)}, bf16[12,16,768]{2,1,0:T(8,128)(2,1)S(1)}, u32[]{:S(2)}, u32[]{:S(2)}) collective-permute-start(bf16[12,16,768]{2,1,0:T(8,128)(2,1)} %get-tuple-element.124), channel_id=1, source_target_pairs={{0,16},{2,18},{4,20},{6,22},{8,24},{10,26},{12,28},{14,30},{16,0},... | collective-permute-start | bytes 884744 | tf_op jit(solution)/shard_map/ppermute | solution.py:1649
  200.1 32.9 %collective-permute-start.14 = (bf16[12,16,768]{2,1,0:T(8,128)(2,1)}, bf16[12,16,768]{2,1,0:T(8,128)(2,1)S(1)}, u32[]{:S(2)}, u32[]{:S(2)}) collective-permute-start(bf16[12,16,768]{2,1,0:T(8,128)(2,1)} %get-tuple-element.124), channel_id=1, source_target_pairs={{0,24},{2,26},{4,28},{6,30},{8,16},{10,18},{12,20},{14,22},{16,8},... | collective-permute-start | bytes 884744 | tf_op jit(solution)/shard_map/ppermute | solution.py:1649
  226.2 6.0 %copy-start.5 = (f32[8,768]{1,0:T(8,128)S(1)}, f32[8,768]{1,0:T(8,128)}, u32[]{:S(2)}) copy-start(f32[8,768]{1,0:T(8,128)} %get-tuple-element.140) | copy-start | bytes 73732
  226.2 6.0 %copy-start.4 = (f32[12,1,256]{2,1,0:T(1,128)S(1)}, f32[12,1,256]{2,1,0:T(1,128)}, u32[]{:S(2)}) copy-start(f32[12,1,256]{2,1,0:T(1,128)} %get-tuple-element.139) | copy-start | bytes 36868
  226.2 6.1 %copy-start.12 = (f32[7]{0:T(128)S(1)}, f32[7]{0:T(128)}, u32[]{:S(2)}) copy-start(f32[7]{0:T(128)} %pad.7.clone) | copy-start | bytes 88
  226.2 6.8 %copy-start.3 = (bf16[12,16,768]{2,1,0:T(8,128)(2,1)S(1)}, bf16[12,16,768]{2,1,0:T(8,128)(2,1)}, u32[]{:S(2)}) copy-start(bf16[12,16,768]{2,1,0:T(8,128)(2,1)} %get-tuple-element.124) | copy-start | bytes 884740
  227.5 5.9 %collective-permute-start.11 = (bf16[9,128,384]{2,1,0:T(8,128)(2,1)S(1)}, bf16[9,128,384]{2,1,0:T(8,128)(2,1)S(1)}, u32[]{:S(2)}, u32[]{:S(2)}) collective-permute-start(bf16[9,128,384]{2,1,0:T(8,128)(2,1)S(1)} %constant_dynamic-slice_fusion), channel_id=1, source_target_pairs={{0,2},{2,0},{4,6},{6,4},{8,10},{10,8},{12,14},{14,12},{16,18},{18,... | collective-permute-start | bytes 2654216 | tf_op jit(solution)/shard_map/ppermute | solution.py:1582
  227.6 37.6 %collective-permute-start.16 = (bf16[768,384]{1,0:T(8,128)(2,1)}, bf16[768,384]{1,0:T(8,128)(2,1)}, u32[]{:S(2)}, u32[]{:S(2)}) collective-permute-start(bf16[768,384]{1,0:T(8,128)(2,1)} %get-tuple-element.129), channel_id=1, source_target_pairs={{0,1},{1,0},{2,3},{3,2},{4,5},{5,4},{6,7},{7,6},{8,9},{9,8},{10,11... | collective-permute-start | bytes 1769480 | tf_op jit(solution)/shard_map/ppermute | solution.py:1579
  233.4 1.5 copy-start.1
  235.1 30.3 %collective-permute-start.15 = (bf16[9,128,384]{2,1,0:T(8,128)(2,1)S(1)}, bf16[9,128,384]{2,1,0:T(8,128)(2,1)}, u32[]{:S(2)}, u32[]{:S(2)}) collective-permute-start(bf16[9,128,384]{2,1,0:T(8,128)(2,1)S(1)} %add_convert_fusion), channel_id=1, source_target_pairs={{0,1},{1,0},{2,3},{3,2},{4,5},{5,4},{6,7},{7,6},{8,9},{9,8},{10,11... | collective-permute-start | bytes 2654216 | tf_op jit(solution)/shard_map/ppermute | solution.py:1579
  235.2 28.2 %collective-permute-start.17 = (bf16[12,64,768]{2,1,0:T(8,128)(2,1)S(1)}, bf16[12,64,768]{2,1,0:T(8,128)(2,1)S(1)}, u32[]{:S(2)}, u32[]{:S(2)}) collective-permute-start(bf16[12,64,768]{2,1,0:T(8,128)(2,1)S(1)} %pad_maximum_fusion.2), channel_id=1, source_target_pairs={{0,4},{2,6},{4,0},{6,2},{8,12},{10,14},{12,8},{14,10},{16,20},{18,... | collective-permute-start | bytes 3538952 | tf_op jit(solution)/shard_map/ppermute | solution.py:1585
  265.2 75.6 %collective-permute-start.18 = (bf16[12,128,768]{2,1,0:T(8,128)(2,1)}, bf16[12,128,768]{2,1,0:T(8,128)(2,1)}, u32[]{:S(2)}, u32[]{:S(2)}) collective-permute-start(bf16[12,128,768]{2,1,0:T(8,128)(2,1)} %pad_maximum_fusion.down_mine.up_mine), channel_id=1, source_target_pairs={{0,2},{2,0},{4,6},{6,4},{8,10},{10,8},{12,14},{14,12},{16,18},{18,... | collective-permute-start | bytes 7077896 | tf_op jit(solution)/shard_map/ppermute | solution.py:1582
  340.8 7.1 %copy-start.2 = (bf16[1024,768]{1,0:T(8,128)(2,1)S(1)}, bf16[1024,768]{1,0:T(8,128)(2,1)}, u32[]{:S(2)}) copy-start(bf16[1024,768]{1,0:T(8,128)(2,1)} %get-tuple-element.118) | copy-start | bytes 4718596
  347.9 2.5 copy-start

commit v2 on v1

--- a/solution.py
+++ b/solution.py
@@ -445,8 +445,10 @@
 
     def weight_rows(i, _):
         rows = pl.ds(pl.multiple_of(i * ROW_TILE, LANES), ROW_TILE)
+        cols = q_ref.shape[1]
+        spread = pl.ds(pl.multiple_of(i * cols, LANES), cols)
         for c in range(3):
-            grad_ref[c, rows, :] = dot(rows_ref[rows, :], out_ref[c]).astype(bf16)
+            grad_ref[c, :, spread] = dot(rows_ref[rows, :], out_ref[c]).astype(bf16)
         return 0
 
     if rows_ref is not None:
@@ -480,7 +482,10 @@
         ],
         out_shape=[
             jax.ShapeDtypeStruct((3, count, cols), bf16),
-            *[jax.ShapeDtypeStruct((3, rows.shape[0], cols), bf16) for rows in rows_t],
+            *[
+                jax.ShapeDtypeStruct((3, ROW_TILE, rows.shape[0] // ROW_TILE * cols), bf16)
+                for rows in rows_t
+            ],
         ],
         name="attend_backward",
         cost_estimate=pl.CostEstimate(
@@ -716,7 +721,6 @@
         up_beside,
         down_mine,
         down_here,
-        down_beside,
         out_ref,
         mid_ref,
         datt_ref,
@@ -787,35 +791,23 @@
             device_id_type=MESH,
         )
 
-    def hand_down(b, part_of):
-        side = ex.x if part_of == 0 else 1 - ex.x
+    def hand_down(b):
         return pltpu.make_async_remote_copy(
-            src_ref=(down_here, down_beside)[part_of].at[strip_rows(b)],
-            dst_ref=down_there.at[side * (count // 2) + b],
-            send_sem=pass_down.at[side * (count // 2) + b, 0],
-            recv_sem=pass_down.at[side * (count // 2) + b, 1],
+            src_ref=down_here.at[strip_rows(b)],
+            dst_ref=down_there.at[b],
+            send_sem=pass_down.at[b, 0],
+            recv_sem=pass_down.at[b, 1],
             device_id=ex.sibling,
             device_id_type=MESH,
         )
 
     def strip_rows(b):
         return pl.ds(pl.multiple_of(b * strip, strip), strip)
-
-    def got_down(slot):
-        return pltpu.make_async_remote_copy(
-            src_ref=down_there.at[slot],
-            dst_ref=down_there.at[slot],
-            send_sem=pass_down.at[slot, 0],
-            recv_sem=pass_down.at[slot, 1],
-            device_id=ex.sibling,
-            device_id_type=MESH,
-        )
 
     def start_loads(i):
         other, k = which(i)
         mine = jnp.logical_not(other)
         cols = pl.ds(pl.multiple_of(k * HIDDEN_TILE, HIDDEN_TILE), HIDDEN_TILE)
-        span = count // 2
 
         @pl.when(other)
         def _():
@@ -843,25 +835,20 @@
 
         for h in range(2):
             b = 2 * k + h
-            piece, inner = b // span, b % span
+            inner = b % count
 
             @pl.when(mine)
             def _():
                 load_down(i, down_mine.at[strip_rows(b), :], h).start()
 
-            @pl.when(jnp.logical_and(other, held == piece))
+            @pl.when(jnp.logical_and(other, core == b // count))
             def _():
                 load_down(i, down_here.at[strip_rows(inner), :], h).start()
 
-            @pl.when(jnp.logical_and(other, kept == piece))
+            @pl.when(jnp.logical_and(other, core != b // count))
             def _():
-                load_down(i, down_beside.at[strip_rows(inner), :], h).start()
-
-            @pl.when(jnp.logical_and(other, core != piece // 2))
-            def _():
-                slot = piece % 2 * span + inner
-                got_down(slot).wait_recv()
-                load_down(i, down_there.at[slot], h).start()
+                hand_down(inner).wait_recv()
+                load_down(i, down_there.at[inner], h).start()
 
     def wait_loads(i):
         for h in range(4):
@@ -883,12 +870,7 @@
     def hand(k, _):
         hand_up(k, 0).start()
         hand_up(k, 1).start()
-
-        @pl.when(k < count // 2)
-        def _():
-            hand_down(k, 0).start()
-            hand_down(k, 1).start()
-
+        hand_down(k).start()
         return 0
 
     lax.fori_loop(0, count, hand, 0)
@@ -926,28 +908,19 @@
         bias = jnp.where(other, bup_other[k], bup_ref[k])
         linear = 0.7978845608028654
         cubic = linear * 0.044715
-        block = lambda r: slice(r * ROW_TILE, (r + 1) * ROW_TILE)
-
-        def begin(r):
-            return dot(n2_ref[block(r), :], up[...]), dot(dy_ref[block(r), :], down[...], NT)
-
-        ready = begin(0)
         for r in range(blocks):
-            rows = block(r)
-            ahead = begin(r + 1) if r + 1 < blocks else None
-            pre = ready[0] + bias
+            rows = slice(r * ROW_TILE, (r + 1) * ROW_TILE)
+            pre = dot(n2_ref[rows, :], up[...]) + bias
+            d_act = dot(dy_ref[rows, :], down[...], NT)
             square = pre * pre
             bend = jnp.tanh(pre * (square * cubic + linear))
             gate = 0.5 * bend + 0.5
             full_act = pre * gate
             slope = gate + (full_act - full_act * gate) * (square * (6.0 * cubic) + 2.0 * linear)
-            act = full_act.astype(bf16)
-            d_pre = (ready[1] * slope).astype(bf16)
-            act_ref[rows, :] = act
-            dpre_ref[rows, :] = d_pre
-            total_ref[rows, :] += dot(act, down[...])
-            dn2_ref[rows, :] += dot(d_pre, up[...], NT)
-            ready = ahead
+            act_ref[rows, :] = full_act.astype(bf16)
+            dpre_ref[rows, :] = (d_act * slope).astype(bf16)
+        total_ref[...] += dot(act_ref[...], down[...])
+        dn2_ref[...] += dot(dpre_ref[...], up[...], NT)
         down_grad[k] = dot(act_ref[...].T, dy_ref[...]).astype(bf16)
 
         def start(lane):
@@ -1016,11 +989,14 @@
         return 0
 
     def out_grads():
-        depth = wout_ref.shape[0]
         for source, target in ((att_ref, gout_ref), (att2_ref, gout2_ref)):
             grad = dot(source[...].T, n2_ref[...]).astype(bf16)
-            target[:depth, :] = grad[:, :lanes]
-            target[depth:, :] = grad[:, lanes:]
+            for a in range(wout_ref.shape[0] // LANES):
+                for b in range(2):
+                    rows = slice(a * LANES, (a + 1) * LANES)
+                    cols = slice(b * lanes, (b + 1) * lanes)
+                    spread = slice(a * lanes, (a + 1) * lanes)
+                    target[b * LANES : (b + 1) * LANES, spread] = grad[rows, cols]
 
     def main(i, _):
         pl.when(i < tiles)(functools.partial(tile, i))
@@ -1038,7 +1014,7 @@
     lax.fori_loop(0, tiles + 5, main, 0)
 
     def handed(slot, _):
-        got_down(slot).wait_send()
+        hand_down(slot).wait_send()
         return 0
 
     lax.fori_loop(0, count, handed, 0)
@@ -1059,15 +1035,15 @@
     depth = wout.shape[0]
     return pl.pallas_call(
         functools.partial(middle_kernel, exchanges, tiles),
-        in_specs=[vmem] * 8 + [hbm] * 6,
+        in_specs=[vmem] * 8 + [hbm] * 5,
         out_specs=[vmem] * 9,
         out_shape=[
             shape((rows, width), bf16),
             shape((rows, width), f32),
             shape(att.shape, bf16),
             shape(att2.shape, bf16),
-            shape((2 * depth, width // 2), bf16),
-            shape((2 * depth, width // 2), bf16),
+            shape((2 * LANES, depth // LANES * width // 2), bf16),
+            shape((2 * LANES, depth // LANES * width // 2), bf16),
             shape((tiles, 1, HIDDEN_TILE), f32),
             shape((8, width), f32),
             shape((2 * count, PIECES, width), bf16),
@@ -1119,9 +1095,11 @@
         dmid_hbm,
         small_ref,
         small2_ref,
-        full_ref,
+        gqkv_ref,
+        gout_ref,
         back_ref,
         sums_ref,
+        full_ref,
         out_buf,
         rows_t_ref,
         d_ref,
@@ -1144,7 +1122,6 @@
     place, part = lax.axis_index("dp"), lax.axis_index("mp")
     ex = exchange.bind(place, part, rest)
     count, bits = ex.count, ex.bits
-    first = mine_out_ref.shape[0]
     loads = [
         pltpu.make_async_copy(source, target, load_sem.at[n])
         for n, (source, target) in enumerate(
@@ -1167,13 +1144,9 @@
     ex.partners += [near[j - 1] for j in (3, 5, 6, 7)]
     ex.greet()
 
-    def begin_out(k, _):
-        total = mine_out_ref[k].astype(f32) + crossed_out_ref[k].astype(f32)
-        out_buf[k] = total.astype(bf16)
-        ex.start_a(k, 0, out_buf)
-        return 0
-
-    lax.fori_loop(0, first, begin_out, 0)
+    total = mine_out_ref[...].astype(f32) + crossed_out_ref[...].astype(f32)
+    out_buf[0] = total.astype(bf16)
+    ex.start_a(0, 0, out_buf)
     step = KEY_ROWS // 3
 
     def back_rows(n):
@@ -1184,28 +1157,49 @@
                 total = total + dot(grads[c, rows, :], weights[c], NT)
         rows_ref[rows, :] = total
 
-    def grad_chunk(j):
-        parts = rows_t_ref.shape[0] // ROW_TILE
-        rows = pl.ds(pl.multiple_of(j % parts * ROW_TILE, ROW_TILE), ROW_TILE)
-        out_buf[first + j] = dot(rows_t_ref[rows, :], d_ref[j // parts]).astype(bf16)
-        ex.start_a(first + j, 0, out_buf)
+    lanes = d_ref.shape[2]
+
+    def grad_chunk(c):
+        for r in range(rows_t_ref.shape[0] // ROW_TILE):
+            rows = slice(r * ROW_TILE, (r + 1) * ROW_TILE)
+            grad = dot(rows_t_ref[rows, :], d_ref[c]).astype(bf16)
+            out_buf[c + 1, :, r * lanes : (r + 1) * lanes] = grad
+        ex.start_a(c + 1, 0, out_buf)
 
     def stage_c(k):
-        @pl.when(k >= first)
+        @pl.when(k >= 1)
         def _():
-            ex.stage_c(k, out_buf, lambda rows: crossed_ref[k - first, rows, :].astype(f32))
-
-        @pl.when(k < first)
+            ex.stage_c(k, out_buf, lambda rows: crossed_ref[k - 1, rows, :].astype(f32))
+
+        @pl.when(k == 0)
         def _():
             ex.stage_c(k, out_buf)
 
+    def arrive(k):
+        ex.stage_h(k, full_ref)
+
+        @pl.when(k == 0)
+        def _():
+            for a in range(gout_ref.shape[0] // LANES):
+                for b in range(2):
+                    spread = slice(a * lanes, (a + 1) * lanes)
+                    rows = slice(a * LANES, (a + 1) * LANES)
+                    piece = full_ref[0, b * LANES : (b + 1) * LANES, spread]
+                    gout_ref[rows, b * lanes : (b + 1) * lanes] = piece
+
+        @pl.when(k > 0)
+        def _():
+            for r in range(rows_t_ref.shape[0] // ROW_TILE):
+                rows = slice(r * ROW_TILE, (r + 1) * ROW_TILE)
+                gqkv_ref[k - 1, rows, :] = full_ref[k, :, r * lanes : (r + 1) * lanes]
+
     def steps(i):
-        at_step(i - 10, count, lambda k: ex.stage_h(k, full_ref))
-        at_step(i - 8, count, lambda k: ex.stage_g(k, full_ref))
-        at_step(i - 6, count, lambda k: ex.stage_f(k, full_ref))
-        at_step(i - 4, count, lambda k: ex.stage_e(k, full_ref))
+        at_step(i - 6, count, arrive)
+        at_step(i - 5, count, lambda k: ex.stage_g(k, full_ref))
+        at_step(i - 4, count, lambda k: ex.stage_f(k, full_ref))
+        at_step(i - 3, count, lambda k: ex.stage_e(k, full_ref))
         at_step(i - 2, count, lambda k: ex.stage_d(k))
-        at_step(i, count, stage_c)
+        at_step(i - 1, count, stage_c)
 
     width = tokens_ref.shape[1]
 
@@ -1368,46 +1362,45 @@
             total = total + far_ref[5 + 2 * i]
         sums_ref[...] = total
 
-    chunks = count - first
-    begin_chunks, end_chunks = 1, 1 + chunks
+    groups = count - 1
     actions = {
         0: give_main,
-        end_chunks + 1: give_edges,
-        end_chunks + 2: tell_near,
-        end_chunks + 3: tell_far,
-        end_chunks + 4: take_back,
+        groups + 2: give_edges,
+        groups + 3: tell_near,
+        groups + 4: tell_far,
+        groups + 5: take_back,
     }
-    begin_back = end_chunks + 5
+    begin_back = groups + 6
 
     def phase(p, _):
-        back = jnp.logical_or(p == 0, jnp.logical_or(p == end_chunks, p == end_chunks + 1))
-
-        @pl.when(back)
+        later = jnp.logical_or(p == groups + 1, p == groups + 2)
+
+        @pl.when(jnp.logical_or(p == 0, later))
         def _():
-            back_rows(jnp.where(p == 0, 0, p - end_chunks + 1))
-
-        @pl.when(jnp.logical_and(p >= begin_chunks, p < end_chunks))
+            back_rows(jnp.where(p == 0, 0, p - groups))
+
+        @pl.when(jnp.logical_and(p >= 1, p <= groups))
         def _():
-            grad_chunk(p - begin_chunks)
+            grad_chunk(p - 1)
 
         for n, action in actions.items():
             pl.when(p == n)(action)
-        block = p - begin_back
+        block = 2 * (p - begin_back)
 
         @pl.when(jnp.logical_and(block >= 0, block < parts))
         def _():
-            norm_back(block)
+            lax.fori_loop(block, block + 2, lambda b, _: (norm_back(b), 0)[1], 0)
 
         pl.when(block == parts)(end_far)
-        steps(p - 1)
+        steps(p)
         return 0
 
-    lax.fori_loop(0, max(begin_back + parts + 1, count + 11), phase, 0)
+    lax.fori_loop(0, begin_back + parts // 2 + 1, phase, 0)
 
 
 def leave(bits, rows_t, mine, crossed, d_fields, weights, tokens, context, vectors, d_mid, small, small2):
-    total = mine.shape[0] + crossed[0].shape[0]
-    rows, cols = mine.shape[1:]
+    total = 1 + crossed[0].shape[0]
+    rows, cols = mine.shape
     exchange = Exchange(bits, total, rows, cols)
     count, width = tokens.shape
     vmem = pl.BlockSpec(memory_space=pltpu.VMEM)
@@ -1416,13 +1409,15 @@
     return pl.pallas_call(
         functools.partial(leave_kernel, exchange),
         in_specs=[hbm] + [vmem] * 3 + [hbm] * 4 + [vmem] * 3 + [hbm] + [vmem] * 2,
-        out_specs=[vmem] * 3,
+        out_specs=[vmem] * 4,
         out_shape=[
-            shape((total, rows, cols), bf16),
+            shape(weights[0].shape, bf16),
+            shape((d_fields[0].shape[2], width), bf16),
             shape((count, width), f32),
             shape((16, width), f32),
         ],
         scratch_shapes=[
+            pltpu.VMEM((total, rows, cols), bf16),
             pltpu.VMEM((total, rows, cols), bf16),
             pltpu.VMEM(rows_t.shape, bf16),
             pltpu.VMEM(d_fields[0].shape, bf16),
@@ -1593,12 +1588,11 @@
         size = array.shape[axis] // 4
         return lax.dynamic_slice_in_dim(array, (2 * core + side) * size, size, axis)
 
-    quarters = [
-        quarter_of(qkv_mine, 1),
-        quarter_of(w_up),
-        quarter_of(w_down),
-        quarter_of(w_out),
-    ]
+    def half_of(array):
+        size = array.shape[0] // 2
+        return lax.dynamic_slice_in_dim(array, core * size, size, 0)
+
+    quarters = [quarter_of(qkv_mine, 1), quarter_of(w_up), half_of(w_down), half_of(w_out)]
     layout = key_layout(lengths[0], block_size[0], part)
     vectors = jnp.stack([ln1_gain, ln1_bias, ln2_gain, ln2_bias, b_down])
     context, (quarters, layout, vectors) = tie(context, (quarters, layout, vectors))
@@ -1614,15 +1608,11 @@
     qkv_other = in_order(core, qkv_half, sibling(qkv_half), axis=1)
     up_beside = beside(up_here)
     fields = project(normed1, qkv_other, cosine, sine)
-    (down_here, out_here), fields = tie((down_here, out_here), fields)
-    out_beside = beside(out_here)
-    down_beside = beside(down_here)
     other = [*fields, *attend_forward(spans, clean_bounds, noisy_bounds, *fields)]
-    (out_here, out_beside, up_here, up_beside, down_here, down_beside), _ = tie(
-        (out_here, out_beside, up_here, up_beside, down_here, down_beside), other[3]
-    )
-    out_half = in_order(side, out_here, out_beside)
-    out_other = in_order(core, out_half, sibling(out_half))
+    (out_here, up_here, up_beside, down_here), _ = tie(
+        (out_here, up_here, up_beside, down_here), other[3]
+    )
+    out_other = in_order(core, out_here, sibling(out_here))
     bias_all = b_up.astype(f32).reshape(-1, 1, HIDDEN_TILE)
 
     x_rows = tokens.reshape(TOK_DEV, width)
@@ -1637,7 +1627,7 @@
         vectors,
         bias_all,
         (w_up, up_here, up_beside),
-        (w_down, down_here, down_beside),
+        (w_down, down_here),
     )
     hidden = b_up.shape[0]
 
@@ -1668,7 +1658,6 @@
         )
 
     d_fields2, grad2 = backward(other, d_att2, spans, normed1_t)
-    grad2 = grad2.reshape(-1, ROW_TILE, grad2.shape[2])
     low_bit, high_bit = (place >> 2) & 1, (place >> 3) & 1
     moved, _ = tie(moved, grad2)
     gathered = in_order(
@@ -1692,11 +1681,11 @@
     lead = hidden // width
     bias2, bias1 = grad_bias.reshape(2, lead, width)
     shared = jnp.concatenate([norms[:3], jnp.zeros((2, width), f32)], axis=0)
-    full, grad_tokens, sums = leave(
+    grad_qkv, grad_out, grad_tokens, sums = leave(
         bits,
         normed1_t,
-        grad_out.reshape(-1, ROW_TILE, grad_out.shape[1]),
-        (crossed, crossed_out.reshape(-1, ROW_TILE, grad_out.shape[1])),
+        grad_out,
+        (crossed, crossed_out),
         (d_fields1, d_fields2),
         (qkv_mine, qkv_other),
         x_rows,
@@ -1706,19 +1695,15 @@
         jnp.concatenate([bias1, shared], axis=0),
         jnp.concatenate([bias2, shared], axis=0),
     )
-    moved, _ = tie(moved, full)
+    moved, _ = tie(moved, grad_qkv)
     grad_down, grad_up = assemble(core.reshape(1), gathered, moved)
-    split = grad_out.shape[0] // ROW_TILE
-    flat = full[:split].reshape(2, w_out.shape[0], width // 2)
-    grad_out = jnp.concatenate([flat[0], flat[1]], axis=1).astype(f32)
-    grad_qkv = full[split:].reshape(qkv_mine.shape).transpose(1, 0, 2).astype(f32)
     return (
         out.reshape(tokens.shape),
         grad_tokens.reshape(tokens.shape),
         sums[lead + 3],
         sums[lead + 4],
-        grad_qkv,
-        grad_out,
+        grad_qkv.transpose(1, 0, 2).astype(f32),
+        grad_out.astype(f32),
         sums[lead],
         sums[lead + 1],
         grad_up,

time: 355 us -> 339 us (0.955)
  Pallas kernels: 267 us -> 246 us
  waiting for transfers between devices: 19.7 us -> 24.8 us
    pallas_call x1, Pallas kernels: 99.7 us -> 93.2 us  [middle(): pl.pallas_call(functools.partial(middle_kernel, exchanges, tiles), in_spe...]
    ppermute x7, starting transfers between devices: 14.6 us -> 20.8 us  [across(): return lax.ppermute(array, 'mp', [(0, 1), (1, 0)])]
    pallas_call x1, Pallas kernels: 66.4 us -> 60.3 us  [leave(): pl.pallas_call(functools.partial(leave_kernel, exchange), in_specs=[hbm]...]
    ppermute x5 -> x3, starting transfers between devices: 7.17 us -> 1.77 us  [beside(): return lax.ppermute(array, 'dp', [(i, i ^ 2) for i in range(dp_size)])]
    pallas_call x2, Pallas kernels: 31.3 us -> 27.1 us  [attend_forward(): pl.pallas_call(forward_kernel, in_specs=[pl.BlockSpec(memory_space=pltpu....]
    pallas_call x2, Pallas kernels: 43.5 us -> 39.7 us  [attend_backward(): pl.pallas_call(backward_kernel, in_specs=[pl.BlockSpec(memory_space=pltpu...]
    ppermute x5 -> x3, waiting for transfers between devices: 7.61 us -> 10.5 us  [beside(): return lax.ppermute(array, 'dp', [(i, i ^ 2) for i in range(dp_size)])]
  transfers between devices with their start and end apart: 19 -> 17, of which waited for: 6 -> 5; matrix products, arithmetic and copies ran while one was open for 8% -> 8% of each run, Pallas kernels for 45% -> 43%
where the time goes in v2:
time: 339 us; the launch traced here: 337 us
  Pallas kernels  246 us (73%)
  starting transfers between devices  27.4 us (8%)
  waiting for transfers between devices  24.8 us (7%)
  other arithmetic  19.4 us (6%)
  local copies, waits for them, and re-layouts  17.4 us (5%)
    pallas_call x1, Pallas kernels, middle(): pl.pallas_call(functools.partial(middle_kernel, exchanges, tiles), in_spe...  93.2 us
    pallas_call x1, Pallas kernels, leave(): pl.pallas_call(functools.partial(leave_kernel, exchange), in_specs=[hbm]...  60.3 us
    pallas_call x2, Pallas kernels, attend_backward(): pl.pallas_call(backward_kernel, in_specs=[pl.BlockSpec(memory_space=pltpu...  39.7 us
    pallas_call x2, Pallas kernels, attend_forward(): pl.pallas_call(forward_kernel, in_specs=[pl.BlockSpec(memory_space=pltpu....  27.1 us
    ppermute x7, starting transfers between devices, across(): return lax.ppermute(array, 'mp', [(0, 1), (1, 0)])  20.8 us
    ppermute x7, waiting for transfers between devices, across(): return lax.ppermute(array, 'mp', [(0, 1), (1, 0)])  13.9 us
    pallas_call x1, Pallas kernels, enter(): pl.pallas_call(enter_kernel, in_specs=[vmem] * 6, out_specs=[vmem] * 5, o...  11.4 us
    ppermute x3, waiting for transfers between devices, beside(): return lax.ppermute(array, 'dp', [(i, i ^ 2) for i in range(dp_size)])  10.5 us
  transfers between devices with their start and end apart: 17, of which 5 were waited for; matrix products, arithmetic and copies ran while one was open for 8% of the time, Pallas kernels for 43%

profile of v2, /device:TPU:0, one launch (start us, length us, event | category | flops | bytes accessed | tf_op | source)
XLA Modules:
  0.0 336.8 jit_solution(167532307100323463)
XLA Ops:
  0.7 1.2 slice_bitcast_fusion
  1.9 0.8 select_bitcast_fusion
  2.8 3.0 collective-permute-start
  5.8 0.2 reduce-window.8
  6.7 0.1 fusion.2
  6.8 0.1 subtract_convert_fusion
  6.9 0.3 fusion.16
  7.2 0.1 copy.35
  7.3 0.2 reduce_min.21
  7.5 0.1 copy.31
  7.7 1.1 dynamic-slice_bitcast_fusion
  8.7 1.4 constant_dynamic-slice_fusion.2
  10.1 0.7 constant_dynamic-slice_fusion.1
  10.9 0.7 pad_add_fusion.1.span_ref
  11.5 0.6 add_add_fusion.clean_ref
  12.1 0.6 pad_add_fusion.noisy_ref
  12.7 0.6 stack.29.vectors_ref.refs_6_.refs_10_
  13.4 1.1 constant_dynamic-slice_fusion.3
  14.5 4.4 %fusion = (f32[1584,128]{1,0:T(8,128)}, f32[1584,128]{1,0:T(8,128)}) fusion(f32[128]{0:T(128)S(1)} %get-tuple-element.175, f32[128]{0:T(128)S(1)} %get-tuple-element.176, f32[1584]{0:T(1024)S(1)} %get-tuple-element.169), kind=kLoop, calls=%fused_computation.12 | loop fusion | flops 405504 | bytes 1629376 | tf_op jit(solution)/shard_map/mul | solution.py:1536
  18.9 5.1 %collective-permute-done.context_ref.refs_9_ = bf16[528,768]{1,0:T(8,128)(2,1)} collective-permute-done((bf16[528,768]{1,0:T(8,128)(2,1)S(1)}, bf16[528,768]{1,0:T(8,128)(2,1)}, u32[]{:S(2)}, u32[]{:S(2)}) %collective-permute-start) | collective-permute-done | bytes 811040 | tf_op jit(solution)/shard_map/ppermute | solution.py:1574
  24.0 1.7 collective-permute-start.1
  25.7 0.3 collective-permute-start.3
  26.0 11.4 %enter.1 = (bf16[1584,768]{1,0:T(8,128)(2,1)}, bf16[768,1584]{1,0:T(8,128)(2,1)}, bf16[1584,384]{1,0:T(8,128)(2,1)}, bf16[1584,384]{1,0:T(8,128)(2,1)}, bf16[1584,384]{1,0:T(8,128)(2,1)}) custom-call(bf16[2,512,768]{2,1,0:T(8,128)(2,1)} %tokens_ref.1, bf16[528,768]{1,0:T(8,128)(2,1)} %collective-permute-done.context_ref.refs_9_, ...), custom_call_target="tpu_custom_call" | custom-call | flops 10000000000 | bytes 16000000 | tf_op jit(solution)/shard_map/enter/pallas_call | solution.py:157
  37.4 1.7 collective-permute-start.2
  39.1 13.5 %attend_forward.2 = (bf16[1024,384]{1,0:T(8,128)(2,1)}, f32[3,4,2,256]{3,2,1,0:T(2,128)}) custom-call(s32[4,2]{1,0:T(4,128)} %pad_add_fusion.1.span_ref, s32[4,2,256]{2,1,0:T(2,128)} %add_add_fusion.clean_ref, s32[4,2,128]{2,1,0:T(2,128)} %pad_add_fusion.noisy_ref, bf16[1584,384]{1,0:T(8,128)(2,1)} %get-tuple-element.85.q_ref, ...), custom_call_target="tpu_custom_call" | custom-call | flops 1610612736 | bytes 4866048 | tf_op jit(solution)/shard_map/attend_forward/pallas_call | solution.py:290
  52.7 0.1 pad_maximum_fusion.3
  52.8 0.3 collective-permute-start.4
  53.1 7.7 %collective-permute-start.7 = (bf16[768,768]{1,0:T(8,128)(2,1)S(1)}, bf16[768,768]{1,0:T(8,128)(2,1)}, u32[]{:S(2)}, u32[]{:S(2)}) collective-permute-start(bf16[768,768]{1,0:T(8,128)(2,1)S(1)} %constant_dynamic-slice_fusion.2), channel_id=1, source_target_pairs={{0,1},{1,0},{2,3},{3,2},{4,5},{5,4},{6,7},{7,6},{8,9},{9,8},{10,11... | collective-permute-start | bytes 3538952 | tf_op jit(solution)/shard_map/ppermute | solution.py:1574
  60.9 0.6 collective-permute-start.5
  61.5 1.5 broadcast_select_fusion.3
  63.0 1.4 pad_maximum_fusion.1.w_ref.refs_7_
  64.4 7.3 %project.1 = (bf16[1584,384]{1,0:T(8,128)(2,1)}, bf16[1584,384]{1,0:T(8,128)(2,1)}, bf16[1584,384]{1,0:T(8,128)(2,1)}) custom-call(bf16[1584,768]{1,0:T(8,128)(2,1)} %get-tuple-element.89.rows_ref, bf16[3,768,384]{2,1,0:T(8,128)(2,1)} %pad_maximum_fusion.1.w_ref.refs_7_, f32[1584,128]{1,0:T(8,128)} %get-tuple-element.80.cos_ref, ...), custom_call_target="tpu_custom_call" | custom-call | flops 2802843648 | bytes 7852032 | tf_op jit(solution)/shard_map/project/pallas_call | solution.py:78
  71.8 13.6 %attend_forward.3 = (bf16[1024,384]{1,0:T(8,128)(2,1)}, f32[3,4,2,256]{3,2,1,0:T(2,128)}) custom-call(s32[4,2]{1,0:T(4,128)} %pad_add_fusion.1.span_ref, s32[4,2,256]{2,1,0:T(2,128)} %add_add_fusion.clean_ref, s32[4,2,128]{2,1,0:T(2,128)} %pad_add_fusion.noisy_ref, bf16[1584,384]{1,0:T(8,128)(2,1)} %get-tuple-element.94.q_ref, ...), custom_call_target="tpu_custom_call" | custom-call | flops 1610612736 | bytes 4866048 | tf_op jit(solution)/shard_map/attend_forward/pallas_call | solution.py:290
  85.3 8.4 %collective-permute-done.5 = bf16[192,768]{1,0:T(8,128)(2,1)S(1)} collective-permute-done((bf16[192,768]{1,0:T(8,128)(2,1)S(1)}, bf16[192,768]{1,0:T(8,128)(2,1)S(1)}, u32[]{:S(2)}, u32[]{:S(2)}) %collective-permute-start.5) | collective-permute-done | bytes 294944 | tf_op jit(solution)/shard_map/ppermute | solution.py:1574
  93.8 0.6 reshape.333.refs_7_
  94.4 0.6 pad.5.clone
  95.0 0.4 collective-permute-done.8
  95.4 0.9 pad_maximum_fusion.5.refs_4_
  96.2 93.2 %middle.1 = (bf16[1024,768]{1,0:T(8,128)(2,1)}, f32[1024,768]{1,0:T(8,128)}, bf16[1024,384]{1,0:T(8,128)(2,1)}, bf16[1024,384]{1,0:T(8,128)(2,1)}, bf16[256,1152...) custom-call(bf16[1024,768]{1,0:T(8,128)(2,1)} %bitcast.29, ...), custom_call_target="tpu_custom_call" | custom-call | flops 60000002048 | bytes 40000000 | tf_op jit(solution)/shard_map/middle/pallas_call | solution.py:1036
  189.5 1.5 collective-permute-start.11
  190.9 2.9 collective-permute-start.12
  193.8 22.2 %attend_backward.2 = (bf16[3,1584,384]{2,1,0:T(8,128)(2,1)}, bf16[3,256,1152]{2,1,0:T(8,128)(2,1)}) custom-call(s32[4,2]{1,0:T(4,128)} %pad_add_fusion.1.span_ref, s32[4,2,256]{2,1,0:T(2,128)} %add_add_fusion.clean_ref, s32[4,2,128]{2,1,0:T(2,128)} %pad_add_fusion.noisy_ref, bf16[1584,384]{1,0:T(8,128)(2,1)} %get-tuple-element.94.q_ref, ...), custom_call_target="tpu_custom_call" | custom-call | flops 35999997952 | bytes 36000000 | tf_op jit(solution)/shard_map/attend_backward/pallas_call | solution.py:474
  216.0 1.3 constant_dynamic-slice_fusion
  217.4 7.3 %collective-permute-start.14 = (bf16[256,1152]{1,0:T(8,128)(2,1)}, bf16[256,1152]{1,0:T(8,128)(2,1)}, u32[]{:S(2)}, u32[]{:S(2)}) collective-permute-start(bf16[256,1152]{1,0:T(8,128)(2,1)} %get-tuple-element.116), channel_id=1, source_target_pairs={{0,1},{1,0},{2,3},{3,2},{4,5},{5,4},{6,7},{7,6},{8,9},{9,8},{10,11... | collective-permute-start | bytes 1769480 | tf_op jit(solution)/shard_map/ppermute | solution.py:1574
  224.8 0.7 fusion.4
  225.6 0.3 broadcast_select_fusion.5
  226.0 1.4 copy-done.1
  227.4 0.2 add_convert_fusion
  227.6 0.1 collective-permute-start.13
  227.8 17.5 %attend_backward.3.refs_4_ = bf16[3,1584,384]{2,1,0:T(8,128)(2,1)} custom-call(s32[4,2]{1,0:T(4,128)} %pad_add_fusion.1.span_ref, s32[4,2,256]{2,1,0:T(2,128)} %add_add_fusion.clean_ref, s32[4,2,128]{2,1,0:T(2,128)} %pad_add_fusion.noisy_ref, bf16[1584,384]{1,0:T(8,128)(2,1)} %get-tuple-element.85.q_ref, bf16[1584,384]{1,0:T(8,128)(2,1)} %get-tuple-element.86.k_ref, ...), custom_call_target="tpu_custom_call" | custom-call | flops 35999997952 | bytes 36000000 | tf_op jit(solution)/shard_map/attend_backward/pallas_call | solution.py:474
  245.3 10.5 %collective-permute-done.15 = bf16[12,64,768]{2,1,0:T(8,128)(2,1)S(1)} collective-permute-done((bf16[12,64,768]{2,1,0:T(8,128)(2,1)S(1)}, bf16[12,64,768]{2,1,0:T(8,128)(2,1)S(1)}, u32[]{:S(2)}, u32[]{:S(2)}) %collective-permute-start.15) | collective-permute-done | bytes 1179680 | tf_op jit(solution)/shard_map/ppermute | solution.py:1580
  255.8 0.2 broadcast_select_fusion.1
  255.9 1.7 pad_maximum_fusion.down_mine.up_mine
  257.6 0.3 collective-permute-done.13.refs_2_
  257.9 60.3 %leave.1 = (bf16[3,768,384]{2,1,0:T(8,128)(2,1)}, bf16[384,768]{1,0:T(8,128)(2,1)}, f32[1024,768]{1,0:T(8,128)}, f32[16,768]{1,0:T(8,128)}) custom-call(bf16[768,1584]{1,0:T(8,128)(2,1)} %get-tuple-element.106.refs_0_, bf16[256,1152]{1,0:T(8,128)(2,1)} %get-tuple-element.107.refs_1_, bf16[3,128,1152]{2,1,0:T(8,128)(2,1)} %collective-permute-done.13.refs_2_, ...), custom_call_target="tpu_custom_call" | custom-call | flops 40000000000 | bytes 40000000 | tf_op jit(solution)/shard_map/leave/pallas_call | solution.py:1409
  318.3 2.3 convert_element_type.40
  320.5 0.7 slice.58
  321.3 0.6 reshape.331
  321.9 1.6 slice_reduce_fusion.2
  323.5 2.0 convert_bitcast_fusion
  325.5 7.1 %assemble.1 = (f32[1536,768]{1,0:T(8,128)}, f32[768,1536]{1,0:T(8,128)}) custom-call(s32[1]{0:T(128)} %bitcast.18.core_ref, bf16[12,128,768]{2,1,0:T(8,128)(2,1)} %pad_maximum_fusion.down_mine.up_mine, bf16[12,128,768]{2,1,0:T(8,128)(2,1)} %pad_maximum_fusion.down_mine.up_mine, bf16[12,128,768]{2,1,0:T(8,128)(2,1)} %collective-permute-done.16.down_got.up_got, ...), custom_call_target="tpu_custom_call" | custom-call | flops 1000000 | bytes 14000000 | tf_op jit(solution)/shard_map/assemble/pallas_call | solution.py:1475
  332.6 1.1 copy.39
  333.8 1.3 copy-done
  335.1 1.7 copy.40
  (73 shorter events, 0.8 us)
Async XLA Ops:
  0.6 5.2 %copy-start.16 = (s32[1,4]{1,0:T(1,128)S(1)}, s32[1,4]{1,0:T(1,128)}, u32[]{:S(2)}) copy-start(s32[1,4]{1,0:T(1,128)} %param.15) | copy-start | bytes 52
  0.7 6.9 %copy-start.9 = (f32[768]{0:T(1024)S(1)}, f32[768]{0:T(1024)}, u32[]{:S(2)}) copy-start(f32[768]{0:T(1024)} %param.18) | copy-start | bytes 9220
  0.7 6.9 %copy-start.10 = (f32[768]{0:T(1024)S(1)}, f32[768]{0:T(1024)}, u32[]{:S(2)}) copy-start(f32[768]{0:T(1024)} %param.19) | copy-start | bytes 9220
  0.7 6.9 %copy-start.11 = (f32[768]{0:T(1024)S(1)}, f32[768]{0:T(1024)}, u32[]{:S(2)}) copy-start(f32[768]{0:T(1024)} %param.22) | copy-start | bytes 9220
  0.7 6.9 %copy-start.12 = (f32[768]{0:T(1024)S(1)}, f32[768]{0:T(1024)}, u32[]{:S(2)}) copy-start(f32[768]{0:T(1024)} %param.23) | copy-start | bytes 9220
  0.7 6.9 %copy-start.13 = (f32[768]{0:T(1024)S(1)}, f32[768]{0:T(1024)}, u32[]{:S(2)}) copy-start(f32[768]{0:T(1024)} %param.27) | copy-start | bytes 9220
  2.8 7.3 %copy-start.6 = (bf16[384,768]{1,0:T(8,128)(2,1)S(1)}, bf16[384,768]{1,0:T(8,128)(2,1)}, u32[]{:S(2)}) copy-start(bf16[384,768]{1,0:T(8,128)(2,1)} %refs_3_.1) | copy-start | bytes 1769476
  2.8 21.2 %collective-permute-start = (bf16[528,768]{1,0:T(8,128)(2,1)S(1)}, bf16[528,768]{1,0:T(8,128)(2,1)}, u32[]{:S(2)}, u32[]{:S(2)}) collective-permute-start(bf16[528,768]{1,0:T(8,128)(2,1)S(1)} %pad_maximum_fusion.4), channel_id=1, source_target_pairs={{0,1},{1,0},{2,3},{3,2},{4,5},{5,4},{6,7},{7,6},{8,9},{9,8},{10,11... | collective-permute-start | bytes 2433032 | tf_op jit(solution)/shard_map/ppermute | solution.py:1574
  24.0 13.4 %collective-permute-start.1 = (bf16[3,192,384]{2,1,0:T(8,128)(2,1)S(1)}, bf16[3,192,384]{2,1,0:T(8,128)(2,1)S(1)}, u32[]{:S(2)}, u32[]{:S(2)}) collective-permute-start(bf16[3,192,384]{2,1,0:T(8,128)(2,1)S(1)} %dynamic-slice_bitcast_fusion), channel_id=1, source_target_pairs={{0,1},{1,0},{2,3},{3,2},{4,5},{5,4},{6,7},{7,6},{8,9},{9,8},{10,11... | collective-permute-start | bytes 1327112 | tf_op jit(solution)/shard_map/ppermute | solution.py:1574
  25.7 26.9 %collective-permute-start.3 = (bf16[192,1536]{1,0:T(8,128)(2,1)S(1)}, bf16[192,1536]{1,0:T(8,128)(2,1)}, u32[]{:S(2)}, u32[]{:S(2)}) collective-permute-start(bf16[192,1536]{1,0:T(8,128)(2,1)S(1)} %constant_dynamic-slice_fusion.3), channel_id=1, source_target_pairs={{0,1},{1,0},{2,3},{3,2},{4,5},{5,4},{6,7},{7,6},{8,9},{9,8},{10,11... | collective-permute-start | bytes 1769480 | tf_op jit(solution)/shard_map/ppermute | solution.py:1574
  37.4 15.2 %collective-permute-start.2 = (bf16[3,192,384]{2,1,0:T(8,128)(2,1)S(1)}, bf16[3,192,384]{2,1,0:T(8,128)(2,1)S(1)}, u32[]{:S(2)}, u32[]{:S(2)}) collective-permute-start(bf16[3,192,384]{2,1,0:T(8,128)(2,1)S(1)} %collective-permute-done.1), channel_id=1, source_target_pairs={{0,4},{2,6},{4,0},{6,2},{8,12},{10,14},{12,8},{14,10},{16,20},{18,... | collective-permute-start | bytes 1327112 | tf_op jit(solution)/shard_map/ppermute | solution.py:1580
  52.6 8.2 %copy-start.4 = (bf16[192,768]{1,0:T(8,128)(2,1)S(1)}, bf16[192,768]{1,0:T(8,128)(2,1)}, u32[]{:S(2)}) copy-start(bf16[192,768]{1,0:T(8,128)(2,1)} %constant_dynamic-slice_fusion.1) | copy-start | bytes 884740
  52.8 8.6 %collective-permute-start.4 = (bf16[3,384,384]{2,1,0:T(8,128)(2,1)S(1)}, bf16[3,384,384]{2,1,0:T(8,128)(2,1)}, u32[]{:S(2)}, u32[]{:S(2)}) collective-permute-start(bf16[3,384,384]{2,1,0:T(8,128)(2,1)S(1)} %pad_maximum_fusion.3), channel_id=1, source_target_pairs={{0,2},{2,0},{4,6},{6,4},{8,10},{10,8},{12,14},{14,12},{16,18},{18,... | collective-permute-start | bytes 2654216 | tf_op jit(solution)/shard_map/ppermute | solution.py:1577
  53.1 40.6 %collective-permute-start.7 = (bf16[768,768]{1,0:T(8,128)(2,1)S(1)}, bf16[768,768]{1,0:T(8,128)(2,1)}, u32[]{:S(2)}, u32[]{:S(2)}) collective-permute-start(bf16[768,768]{1,0:T(8,128)(2,1)S(1)} %constant_dynamic-slice_fusion.2), channel_id=1, source_target_pairs={{0,1},{1,0},{2,3},{3,2},{4,5},{5,4},{6,7},{7,6},{8,9},{9,8},{10,11... | collective-permute-start | bytes 3538952 | tf_op jit(solution)/shard_map/ppermute | solution.py:1574
  60.9 32.9 %collective-permute-start.5 = (bf16[192,768]{1,0:T(8,128)(2,1)S(1)}, bf16[192,768]{1,0:T(8,128)(2,1)S(1)}, u32[]{:S(2)}, u32[]{:S(2)}) collective-permute-start(bf16[192,768]{1,0:T(8,128)(2,1)S(1)} %copy-done.4), channel_id=1, source_target_pairs={{0,1},{1,0},{2,3},{3,2},{4,5},{5,4},{6,7},{7,6},{8,9},{9,8},{10,11... | collective-permute-start | bytes 884744 | tf_op jit(solution)/shard_map/ppermute | solution.py:1574
  61.5 32.3 %collective-permute-start.6 = (bf16[192,1536]{1,0:T(8,128)(2,1)}, bf16[192,1536]{1,0:T(8,128)(2,1)}, u32[]{:S(2)}, u32[]{:S(2)}) collective-permute-start(bf16[192,1536]{1,0:T(8,128)(2,1)} %collective-permute-done.3.refs_9_), channel_id=1, source_target_pairs={{0,4},{2,6},{4,0},{6,2},{8,12},{10,14},{12,8},{14,10},{16,20},{18,... | collective-permute-start | bytes 1769480 | tf_op jit(solution)/shard_map/ppermute | solution.py:1580
  71.8 22.0 %copy-start.14 = (bf16[1536]{0:T(1024)(128)(2,1)S(1)}, bf16[1536]{0:T(1024)(128)(2,1)}, u32[]{:S(2)}) copy-start(bf16[1536]{0:T(1024)(128)(2,1)} %param.25) | copy-start | bytes 9220
  93.7 1.6 collective-permute-start.8
  189.4 36.1 %collective-permute-start.10 = (bf16[12,16,768]{2,1,0:T(8,128)(2,1)}, bf16[12,16,768]{2,1,0:T(8,128)(2,1)S(1)}, u32[]{:S(2)}, u32[]{:S(2)}) collective-permute-start(bf16[12,16,768]{2,1,0:T(8,128)(2,1)} %get-tuple-element.111), channel_id=1, source_target_pairs={{0,8},{2,10},{4,12},{6,14},{8,0},{10,2},{12,4},{14,6},{16,24},{18,... | collective-permute-start | bytes 884744 | tf_op jit(solution)/shard_map/ppermute | solution.py:1639
  189.5 36.0 %collective-permute-start.11 = (bf16[12,16,768]{2,1,0:T(8,128)(2,1)}, bf16[12,16,768]{2,1,0:T(8,128)(2,1)S(1)}, u32[]{:S(2)}, u32[]{:S(2)}) collective-permute-start(bf16[12,16,768]{2,1,0:T(8,128)(2,1)} %get-tuple-element.111), channel_id=1, source_target_pairs={{0,16},{2,18},{4,20},{6,22},{8,24},{10,26},{12,28},{14,30},{16,0},... | collective-permute-start | bytes 884744 | tf_op jit(solution)/shard_map/ppermute | solution.py:1639
  190.9 34.6 %collective-permute-start.12 = (bf16[12,16,768]{2,1,0:T(8,128)(2,1)}, bf16[12,16,768]{2,1,0:T(8,128)(2,1)S(1)}, u32[]{:S(2)}, u32[]{:S(2)}) collective-permute-start(bf16[12,16,768]{2,1,0:T(8,128)(2,1)} %get-tuple-element.111), channel_id=1, source_target_pairs={{0,24},{2,26},{4,28},{6,30},{8,16},{10,18},{12,20},{14,22},{16,8},... | collective-permute-start | bytes 884744 | tf_op jit(solution)/shard_map/ppermute | solution.py:1639
  216.0 8.7 %copy-start.8 = (f32[8,768]{1,0:T(8,128)S(1)}, f32[8,768]{1,0:T(8,128)}, u32[]{:S(2)}) copy-start(f32[8,768]{1,0:T(8,128)} %get-tuple-element.127) | copy-start | bytes 73732
  216.0 8.7 %copy-start.7 = (f32[12,1,256]{2,1,0:T(1,128)S(1)}, f32[12,1,256]{2,1,0:T(1,128)}, u32[]{:S(2)}) copy-start(f32[12,1,256]{2,1,0:T(1,128)} %get-tuple-element.126) | copy-start | bytes 36868
  216.0 8.8 %copy-start.15 = (f32[7]{0:T(128)S(1)}, f32[7]{0:T(128)}, u32[]{:S(2)}) copy-start(f32[7]{0:T(128)} %pad.5.clone) | copy-start | bytes 88
  216.0 9.5 %copy-start.5 = (bf16[12,16,768]{2,1,0:T(8,128)(2,1)S(1)}, bf16[12,16,768]{2,1,0:T(8,128)(2,1)}, u32[]{:S(2)}) copy-start(bf16[12,16,768]{2,1,0:T(8,128)(2,1)} %get-tuple-element.111) | copy-start | bytes 884740
  217.3 8.6 %collective-permute-start.9 = (bf16[3,128,1152]{2,1,0:T(8,128)(2,1)S(1)}, bf16[3,128,1152]{2,1,0:T(8,128)(2,1)S(1)}, u32[]{:S(2)}, u32[]{:S(2)}) collective-permute-start(bf16[3,128,1152]{2,1,0:T(8,128)(2,1)S(1)} %constant_dynamic-slice_fusion), channel_id=1, source_target_pairs={{0,2},{2,0},{4,6},{6,4},{8,10},{10,8},{12,14},{14,12},{16,18},{18,... | collective-permute-start | bytes 2654216 | tf_op jit(solution)/shard_map/ppermute | solution.py:1577
  217.4 40.2 %collective-permute-start.14 = (bf16[256,1152]{1,0:T(8,128)(2,1)}, bf16[256,1152]{1,0:T(8,128)(2,1)}, u32[]{:S(2)}, u32[]{:S(2)}) collective-permute-start(bf16[256,1152]{1,0:T(8,128)(2,1)} %get-tuple-element.116), channel_id=1, source_target_pairs={{0,1},{1,0},{2,3},{3,2},{4,5},{5,4},{6,7},{7,6},{8,9},{9,8},{10,11... | collective-permute-start | bytes 1769480 | tf_op jit(solution)/shard_map/ppermute | solution.py:1574
  225.9 1.5 copy-start.1
  227.6 30.3 %collective-permute-start.13 = (bf16[3,128,1152]{2,1,0:T(8,128)(2,1)S(1)}, bf16[3,128,1152]{2,1,0:T(8,128)(2,1)}, u32[]{:S(2)}, u32[]{:S(2)}) collective-permute-start(bf16[3,128,1152]{2,1,0:T(8,128)(2,1)S(1)} %add_convert_fusion), channel_id=1, source_target_pairs={{0,1},{1,0},{2,3},{3,2},{4,5},{5,4},{6,7},{7,6},{8,9},{9,8},{10,11... | collective-permute-start | bytes 2654216 | tf_op jit(solution)/shard_map/ppermute | solution.py:1574
  227.7 28.1 %collective-permute-start.15 = (bf16[12,64,768]{2,1,0:T(8,128)(2,1)S(1)}, bf16[12,64,768]{2,1,0:T(8,128)(2,1)S(1)}, u32[]{:S(2)}, u32[]{:S(2)}) collective-permute-start(bf16[12,64,768]{2,1,0:T(8,128)(2,1)S(1)} %pad_maximum_fusion.2), channel_id=1, source_target_pairs={{0,4},{2,6},{4,0},{6,2},{8,12},{10,14},{12,8},{14,10},{16,20},{18,... | collective-permute-start | bytes 3538952 | tf_op jit(solution)/shard_map/ppermute | solution.py:1580
  257.6 67.9 %collective-permute-start.16 = (bf16[12,128,768]{2,1,0:T(8,128)(2,1)}, bf16[12,128,768]{2,1,0:T(8,128)(2,1)}, u32[]{:S(2)}, u32[]{:S(2)}) collective-permute-start(bf16[12,128,768]{2,1,0:T(8,128)(2,1)} %pad_maximum_fusion.down_mine.up_mine), channel_id=1, source_target_pairs={{0,2},{2,0},{4,6},{6,4},{8,10},{10,8},{12,14},{14,12},{16,18},{18,... | collective-permute-start | bytes 7077896 | tf_op jit(solution)/shard_map/ppermute | solution.py:1577
  318.2 5.3 %copy-start.2 = (bf16[3,768,384]{2,1,0:T(8,128)(2,1)S(1)}, bf16[3,768,384]{2,1,0:T(8,128)(2,1)}, u32[]{:S(2)}) copy-start(bf16[3,768,384]{2,1,0:T(8,128)(2,1)} %get-tuple-element.130) | copy-start | bytes 5308420
  325.5 7.1 %copy-start.3 = (bf16[1024,768]{1,0:T(8,128)(2,1)S(1)}, bf16[1024,768]{1,0:T(8,128)(2,1)}, u32[]{:S(2)}) copy-start(bf16[1024,768]{1,0:T(8,128)(2,1)} %get-tuple-element.105) | copy-start | bytes 4718596
  332.6 2.5 copy-start

commit v3 on v2

--- a/solution.py
+++ b/solution.py
@@ -445,10 +445,8 @@
 
     def weight_rows(i, _):
         rows = pl.ds(pl.multiple_of(i * ROW_TILE, LANES), ROW_TILE)
-        cols = q_ref.shape[1]
-        spread = pl.ds(pl.multiple_of(i * cols, LANES), cols)
         for c in range(3):
-            grad_ref[c, :, spread] = dot(rows_ref[rows, :], out_ref[c]).astype(bf16)
+            grad_ref[c, rows, :] = dot(rows_ref[rows, :], out_ref[c]).astype(bf16)
         return 0
 
     if rows_ref is not None:
@@ -482,10 +480,7 @@
         ],
         out_shape=[
             jax.ShapeDtypeStruct((3, count, cols), bf16),
-            *[
-                jax.ShapeDtypeStruct((3, ROW_TILE, rows.shape[0] // ROW_TILE * cols), bf16)
-                for rows in rows_t
-            ],
+            *[jax.ShapeDtypeStruct((3, rows.shape[0], cols), bf16) for rows in rows_t],
         ],
         name="attend_backward",
         cost_estimate=pl.CostEstimate(
@@ -721,10 +716,10 @@
         up_beside,
         down_mine,
         down_here,
-        out_ref,
-        mid_ref,
-        datt_ref,
-        datt2_ref,
+        out_hbm,
+        mid_hbm,
+        datt_hbm,
+        datt2_hbm,
         gout_ref,
         gout2_ref,
         gbup_ref,
@@ -745,6 +740,11 @@
         n2_t,
         bup_other,
         bias_sem,
+        out_ref,
+        mid_ref,
+        datt_ref,
+        datt2_ref,
+        store_sem,
         down_grad,
         up_grad,
         *rest,
@@ -960,9 +960,9 @@
     def steps(i):
         even = i % 2 == 0
         odd = jnp.logical_not(even)
-        each((i - 6) // 2, even, arrive)
-        each((i - 5) // 2, odd, stage_d)
-        each((i - 4) // 2, even, stage_c)
+        each((i - 5) // 2, odd, arrive)
+        each((i - 4) // 2, even, stage_d)
+        each((i - 3) // 2, odd, stage_c)
         each(i // 2, even, stage_b)
 
     def epilogue(r, _):
@@ -1006,12 +1006,30 @@
             first = (i - tiles) * (blocks // 2)
             lax.fori_loop(first, first + blocks // 2, epilogue, 0)
 
-        pl.when(i == tiles + 2)(out_grads)
+        @pl.when(i == tiles + 2)
+        def _():
+            for store in stores:
+                store.start()
+            out_grads()
+
         steps(i)
         return 0
 
     small_ref[...] = jnp.zeros_like(small_ref)
-    lax.fori_loop(0, tiles + 5, main, 0)
+    stores = [
+        pltpu.make_async_copy(source, target, store_sem.at[n])
+        for n, (source, target) in enumerate(
+            (
+                (datt2_ref, datt2_hbm),
+                (out_ref, out_hbm),
+                (mid_ref, mid_hbm),
+                (datt_ref, datt_hbm),
+            )
+        )
+    ]
+    lax.fori_loop(0, tiles + 4, main, 0)
+    for store in stores:
+        store.wait()
 
     def handed(slot, _):
         hand_down(slot).wait_send()
@@ -1036,7 +1054,7 @@
     return pl.pallas_call(
         functools.partial(middle_kernel, exchanges, tiles),
         in_specs=[vmem] * 8 + [hbm] * 5,
-        out_specs=[vmem] * 9,
+        out_specs=[hbm] * 4 + [vmem] * 5,
         out_shape=[
             shape((rows, width), bf16),
             shape((rows, width), f32),
@@ -1064,6 +1082,11 @@
             pltpu.VMEM((width + PIECES, rows), bf16),
             pltpu.VMEM(bup.shape, f32),
             pltpu.SemaphoreType.DMA((2,)),
+            pltpu.VMEM((rows, width), bf16),
+            pltpu.VMEM((rows, width), f32),
+            pltpu.VMEM(att.shape, bf16),
+            pltpu.VMEM(att2.shape, bf16),
+            pltpu.SemaphoreType.DMA((4,)),
             pltpu.VMEM((count, HIDDEN_TILE, width), bf16),
             pltpu.VMEM((count, width, HIDDEN_TILE), bf16),
         ]
@@ -1126,11 +1149,11 @@
         pltpu.make_async_copy(source, target, load_sem.at[n])
         for n, (source, target) in enumerate(
             (
+                (d_hbm, d_ref),
+                (rows_hbm, rows_t_ref),
                 (w_hbm, w_ref),
-                (d_hbm, d_ref),
                 (w2_hbm, w2_ref),
                 (d2_hbm, d2_ref),
-                (rows_hbm, rows_t_ref),
                 (dmid_hbm, dmid_ref),
             )
         )
@@ -1144,9 +1167,13 @@
     ex.partners += [near[j - 1] for j in (3, 5, 6, 7)]
     ex.greet()
 
-    total = mine_out_ref[...].astype(f32) + crossed_out_ref[...].astype(f32)
-    out_buf[0] = total.astype(bf16)
-    ex.start_a(0, 0, out_buf)
+    lanes = d_ref.shape[2]
+    split = mine_out_ref.shape[1] // lanes
+    for r in range(split):
+        cols = slice(r * lanes, (r + 1) * lanes)
+        total = mine_out_ref[:, cols].astype(f32) + crossed_out_ref[:, cols].astype(f32)
+        out_buf[r] = total.astype(bf16)
+        ex.start_a(r, 0, out_buf)
     step = KEY_ROWS // 3
 
     def back_rows(n):
@@ -1157,49 +1184,50 @@
                 total = total + dot(grads[c, rows, :], weights[c], NT)
         rows_ref[rows, :] = total
 
-    lanes = d_ref.shape[2]
-
     def grad_chunk(c):
-        for r in range(rows_t_ref.shape[0] // ROW_TILE):
+        for r in range(split):
             rows = slice(r * ROW_TILE, (r + 1) * ROW_TILE)
-            grad = dot(rows_t_ref[rows, :], d_ref[c]).astype(bf16)
-            out_buf[c + 1, :, r * lanes : (r + 1) * lanes] = grad
-        ex.start_a(c + 1, 0, out_buf)
+            k = (c + 1) * split + r
+            out_buf[k] = dot(rows_t_ref[rows, :], d_ref[c]).astype(bf16)
+            ex.start_a(k, 0, out_buf)
 
     def stage_c(k):
-        @pl.when(k >= 1)
+        @pl.when(k >= split)
         def _():
-            ex.stage_c(k, out_buf, lambda rows: crossed_ref[k - 1, rows, :].astype(f32))
-
-        @pl.when(k == 0)
+            ex.stage_c(k, out_buf, lambda rows: crossed_ref[k - split, rows, :].astype(f32))
+
+        @pl.when(k < split)
         def _():
             ex.stage_c(k, out_buf)
 
     def arrive(k):
         ex.stage_h(k, full_ref)
 
-        @pl.when(k == 0)
+        @pl.when(k < split)
         def _():
-            for a in range(gout_ref.shape[0] // LANES):
-                for b in range(2):
-                    spread = slice(a * lanes, (a + 1) * lanes)
-                    rows = slice(a * LANES, (a + 1) * LANES)
-                    piece = full_ref[0, b * LANES : (b + 1) * LANES, spread]
-                    gout_ref[rows, b * lanes : (b + 1) * lanes] = piece
-
-        @pl.when(k > 0)
+            rows = pl.ds(pl.multiple_of(k * LANES, LANES), LANES)
+            for b in range(2):
+                piece = full_ref[k, b * LANES : (b + 1) * LANES, :]
+                gout_ref[rows, b * lanes : (b + 1) * lanes] = piece
+
+        @pl.when(k >= split)
         def _():
-            for r in range(rows_t_ref.shape[0] // ROW_TILE):
-                rows = slice(r * ROW_TILE, (r + 1) * ROW_TILE)
-                gqkv_ref[k - 1, rows, :] = full_ref[k, :, r * lanes : (r + 1) * lanes]
+            n = k - split
+            rows = pl.ds(pl.multiple_of(n % split * ROW_TILE, ROW_TILE), ROW_TILE)
+            gqkv_ref[n // split, rows, :] = full_ref[k]
+
+    def group(g, action):
+        @pl.when(jnp.logical_and(g >= 0, g < count // split))
+        def _():
+            lax.fori_loop(g * split, (g + 1) * split, lambda k, _: (action(k), 0)[1], 0)
 
     def steps(i):
-        at_step(i - 6, count, arrive)
-        at_step(i - 5, count, lambda k: ex.stage_g(k, full_ref))
-        at_step(i - 4, count, lambda k: ex.stage_f(k, full_ref))
-        at_step(i - 3, count, lambda k: ex.stage_e(k, full_ref))
-        at_step(i - 2, count, lambda k: ex.stage_d(k))
-        at_step(i - 1, count, stage_c)
+        group(i - 5, arrive)
+        group(i - 4, lambda k: ex.stage_g(k, full_ref))
+        group(i - 3, lambda k: ex.stage_f(k, full_ref))
+        group(i - 2, lambda k: ex.stage_e(k, full_ref))
+        group(i - 1, lambda k: ex.stage_d(k))
+        group(i, stage_c)
 
     width = tokens_ref.shape[1]
 
@@ -1224,7 +1252,7 @@
     lead = small_ref.shape[0] - 2
     bias = lead - 3
     norm_ref[...] = jnp.zeros_like(norm_ref)
-    for load in loads[:4]:
+    for load in loads[:2]:
         load.wait()
 
     def own_at(b):
@@ -1234,10 +1262,13 @@
     def tokens_at(b):
         return pl.ds(pl.multiple_of(b * TILE, TILE), TILE)
 
+    def ready():
+        for load in loads[2:5]:
+            load.wait()
+
     def give_main():
         give_ref[main, :] = rows_ref[main, :].astype(bf16)
         swap(main, 0).start()
-        loads[4].wait()
 
     def give_edges():
         side = rows_ref[NOISY_BASE:NOISY_OWN, :] + rows_ref[NOISY_OWN + HALF :, :]
@@ -1362,9 +1393,9 @@
             total = total + far_ref[5 + 2 * i]
         sums_ref[...] = total
 
-    groups = count - 1
+    groups = count // split - 1
     actions = {
-        0: give_main,
+        groups: give_main,
         groups + 2: give_edges,
         groups + 3: tell_near,
         groups + 4: tell_far,
@@ -1373,15 +1404,15 @@
     begin_back = groups + 6
 
     def phase(p, _):
-        later = jnp.logical_or(p == groups + 1, p == groups + 2)
-
-        @pl.when(jnp.logical_or(p == 0, later))
+        @pl.when(p < groups)
         def _():
-            back_rows(jnp.where(p == 0, 0, p - groups))
-
-        @pl.when(jnp.logical_and(p >= 1, p <= groups))
+            grad_chunk(p)
+
+        pl.when(p == groups)(ready)
+
+        @pl.when(jnp.logical_and(p >= groups, p < groups + 3))
         def _():
-            grad_chunk(p - 1)
+            back_rows(p - groups)
 
         for n, action in actions.items():
             pl.when(p == n)(action)
@@ -1399,8 +1430,8 @@
 
 
 def leave(bits, rows_t, mine, crossed, d_fields, weights, tokens, context, vectors, d_mid, small, small2):
-    total = 1 + crossed[0].shape[0]
-    rows, cols = mine.shape
+    rows, cols = ROW_TILE, d_fields[0].shape[2]
+    total = mine.shape[1] // cols + crossed[0].shape[0]
     exchange = Exchange(bits, total, rows, cols)
     count, width = tokens.shape
     vmem = pl.BlockSpec(memory_space=pltpu.VMEM)
@@ -1658,6 +1689,7 @@
         )
 
     d_fields2, grad2 = backward(other, d_att2, spans, normed1_t)
+    grad2 = grad2.reshape(-1, ROW_TILE, grad2.shape[2])
     low_bit, high_bit = (place >> 2) & 1, (place >> 3) & 1
     moved, _ = tie(moved, grad2)
     gathered = in_order(

time: 339 us -> 331 us (0.976)
  waiting for transfers between devices: 24.8 us -> 17.2 us
    ppermute x7, starting transfers between devices: 20.8 us -> 14.6 us  [across(): return lax.ppermute(array, 'mp', [(0, 1), (1, 0)])]
    pallas_call x2, Pallas kernels: 27.1 us -> 31.3 us  [attend_forward(): pl.pallas_call(forward_kernel, in_specs=[pl.BlockSpec(memory_space=pltpu....]
    ppermute x7, waiting for transfers between devices: 13.9 us -> 9.88 us  [across(): return lax.ppermute(array, 'mp', [(0, 1), (1, 0)])]
    pallas_call x1, Pallas kernels: 93.2 us -> 89.3 us  [middle(): pl.pallas_call(functools.partial(middle_kernel, exchanges, tiles), in_spe...]
    pallas_call x2, Pallas kernels: 39.7 us -> 43.3 us  [attend_backward(): pl.pallas_call(backward_kernel, in_specs=[pl.BlockSpec(memory_space=pltpu...]
    ppermute x3, starting transfers between devices: 1.77 us -> 5.38 us  [beside(): return lax.ppermute(array, 'dp', [(i, i ^ 2) for i in range(dp_size)])]
    ppermute x3, waiting for transfers between devices: 10.5 us -> 6.97 us  [beside(): return lax.ppermute(array, 'dp', [(i, i ^ 2) for i in range(dp_size)])]
  transfers between devices with their start and end apart: 17 -> 17, of which waited for: 5 -> 5; matrix products, arithmetic and copies ran while one was open for 8% -> 9% of each run, Pallas kernels for 43% -> 46%
where the time goes in v3:
time: 331 us; the launch traced here: 330 us
  Pallas kernels  249 us (75%)
  starting transfers between devices  24.5 us (7%)
  other arithmetic  19.4 us (6%)
  local copies, waits for them, and re-layouts  17.4 us (5%)
  waiting for transfers between devices  17.2 us (5%)
    pallas_call x1, Pallas kernels, middle(): pl.pallas_call(functools.partial(middle_kernel, exchanges, tiles), in_spe...  89.3 us
    pallas_call x1, Pallas kernels, leave(): pl.pallas_call(functools.partial(leave_kernel, exchange), in_specs=[hbm]...  59.7 us
    pallas_call x2, Pallas kernels, attend_backward(): pl.pallas_call(backward_kernel, in_specs=[pl.BlockSpec(memory_space=pltpu...  43.3 us
    pallas_call x2, Pallas kernels, attend_forward(): pl.pallas_call(forward_kernel, in_specs=[pl.BlockSpec(memory_space=pltpu....  31.3 us
    ppermute x7, starting transfers between devices, across(): return lax.ppermute(array, 'mp', [(0, 1), (1, 0)])  14.6 us
    pallas_call x1, Pallas kernels, enter(): pl.pallas_call(enter_kernel, in_specs=[vmem] * 6, out_specs=[vmem] * 5, o...  11.4 us
    ppermute x7, waiting for transfers between devices, across(): return lax.ppermute(array, 'mp', [(0, 1), (1, 0)])  9.88 us
    pallas_call x1, Pallas kernels, project(): pl.pallas_call(project_kernel, grid=(3,), in_specs=[row_spec, pl.BlockSpe...  7.34 us
  transfers between devices with their start and end apart: 17, of which 5 were waited for; matrix products, arithmetic and copies ran while one was open for 9% of the time, Pallas kernels for 46%

profile of v3, /device:TPU:0, one launch (start us, length us, event | category | flops | bytes accessed | tf_op | source)
XLA Modules:
  0.0 329.8 jit_solution(13072214289169482943)
XLA Ops:
  0.7 1.2 slice_bitcast_fusion
  1.9 0.8 select_bitcast_fusion
  2.8 3.0 collective-permute-start
  5.8 0.2 reduce-window.8
  6.7 0.1 fusion.2
  6.8 0.1 subtract_convert_fusion
  6.9 0.3 fusion.16
  7.2 0.1 copy.35
  7.3 0.2 reduce_min.21
  7.5 0.1 copy.31
  7.7 1.1 dynamic-slice_bitcast_fusion
  8.7 1.4 constant_dynamic-slice_fusion.2
  10.1 0.7 constant_dynamic-slice_fusion.1
  10.9 0.7 pad_add_fusion.1.span_ref
  11.5 0.6 add_add_fusion.clean_ref
  12.1 0.6 pad_add_fusion.noisy_ref
  12.7 0.6 stack.29.vectors_ref.refs_6_.refs_10_
  13.4 1.1 constant_dynamic-slice_fusion.3
  14.5 4.4 %fusion = (f32[1584,128]{1,0:T(8,128)}, f32[1584,128]{1,0:T(8,128)}) fusion(f32[128]{0:T(128)S(1)} %get-tuple-element.175, f32[128]{0:T(128)S(1)} %get-tuple-element.176, f32[1584]{0:T(1024)S(1)} %get-tuple-element.169), kind=kLoop, calls=%fused_computation.12 | loop fusion | flops 405504 | bytes 1629376 | tf_op jit(solution)/shard_map/mul | solution.py:1567
  18.9 5.1 %collective-permute-done.context_ref.refs_9_ = bf16[528,768]{1,0:T(8,128)(2,1)} collective-permute-done((bf16[528,768]{1,0:T(8,128)(2,1)S(1)}, bf16[528,768]{1,0:T(8,128)(2,1)}, u32[]{:S(2)}, u32[]{:S(2)}) %collective-permute-start) | collective-permute-done | bytes 811040 | tf_op jit(solution)/shard_map/ppermute | solution.py:1605
  24.0 1.7 collective-permute-start.1
  25.7 0.3 collective-permute-start.3
  26.0 11.4 %enter.1 = (bf16[1584,768]{1,0:T(8,128)(2,1)}, bf16[768,1584]{1,0:T(8,128)(2,1)}, bf16[1584,384]{1,0:T(8,128)(2,1)}, bf16[1584,384]{1,0:T(8,128)(2,1)}, bf16[1584,384]{1,0:T(8,128)(2,1)}) custom-call(bf16[2,512,768]{2,1,0:T(8,128)(2,1)} %tokens_ref.1, bf16[528,768]{1,0:T(8,128)(2,1)} %collective-permute-done.context_ref.refs_9_, ...), custom_call_target="tpu_custom_call" | custom-call | flops 10000000000 | bytes 16000000 | tf_op jit(solution)/shard_map/enter/pallas_call | solution.py:157
  37.4 1.7 collective-permute-start.2
  39.1 15.6 %attend_forward.2 = (bf16[1024,384]{1,0:T(8,128)(2,1)}, f32[3,4,2,256]{3,2,1,0:T(2,128)}) custom-call(s32[4,2]{1,0:T(4,128)} %pad_add_fusion.1.span_ref, s32[4,2,256]{2,1,0:T(2,128)} %add_add_fusion.clean_ref, s32[4,2,128]{2,1,0:T(2,128)} %pad_add_fusion.noisy_ref, bf16[1584,384]{1,0:T(8,128)(2,1)} %get-tuple-element.85.q_ref, ...), custom_call_target="tpu_custom_call" | custom-call | flops 1610612736 | bytes 4866048 | tf_op jit(solution)/shard_map/attend_forward/pallas_call | solution.py:290
  54.8 0.1 pad_maximum_fusion.3
  55.0 4.7 %collective-permute-start.7 = (bf16[768,768]{1,0:T(8,128)(2,1)S(1)}, bf16[768,768]{1,0:T(8,128)(2,1)}, u32[]{:S(2)}, u32[]{:S(2)}) collective-permute-start(bf16[768,768]{1,0:T(8,128)(2,1)S(1)} %constant_dynamic-slice_fusion.2), channel_id=1, source_target_pairs={{0,1},{1,0},{2,3},{3,2},{4,5},{5,4},{6,7},{7,6},{8,9},{9,8},{10,11... | collective-permute-start | bytes 3538952 | tf_op jit(solution)/shard_map/ppermute | solution.py:1605
  59.8 0.6 collective-permute-start.5
  60.4 1.6 collective-permute-start.6
  62.0 1.5 broadcast_select_fusion.3
  63.5 1.4 pad_maximum_fusion.1.w_ref.refs_7_
  64.9 7.3 %project.1 = (bf16[1584,384]{1,0:T(8,128)(2,1)}, bf16[1584,384]{1,0:T(8,128)(2,1)}, bf16[1584,384]{1,0:T(8,128)(2,1)}) custom-call(bf16[1584,768]{1,0:T(8,128)(2,1)} %get-tuple-element.89.rows_ref, bf16[3,768,384]{2,1,0:T(8,128)(2,1)} %pad_maximum_fusion.1.w_ref.refs_7_, f32[1584,128]{1,0:T(8,128)} %get-tuple-element.80.cos_ref, ...), custom_call_target="tpu_custom_call" | custom-call | flops 2802843648 | bytes 7852032 | tf_op jit(solution)/shard_map/project/pallas_call | solution.py:78
  72.3 15.6 %attend_forward.3 = (bf16[1024,384]{1,0:T(8,128)(2,1)}, f32[3,4,2,256]{3,2,1,0:T(2,128)}) custom-call(s32[4,2]{1,0:T(4,128)} %pad_add_fusion.1.span_ref, s32[4,2,256]{2,1,0:T(2,128)} %add_add_fusion.clean_ref, s32[4,2,128]{2,1,0:T(2,128)} %pad_add_fusion.noisy_ref, bf16[1584,384]{1,0:T(8,128)(2,1)} %get-tuple-element.94.q_ref, ...), custom_call_target="tpu_custom_call" | custom-call | flops 1610612736 | bytes 4866048 | tf_op jit(solution)/shard_map/attend_forward/pallas_call | solution.py:290
  87.9 4.7 %collective-permute-done.5 = bf16[192,768]{1,0:T(8,128)(2,1)S(1)} collective-permute-done((bf16[192,768]{1,0:T(8,128)(2,1)S(1)}, bf16[192,768]{1,0:T(8,128)(2,1)S(1)}, u32[]{:S(2)}, u32[]{:S(2)}) %collective-permute-start.5) | collective-permute-done | bytes 294944 | tf_op jit(solution)/shard_map/ppermute | solution.py:1605
  92.7 0.6 reshape.337.refs_7_
  93.3 0.6 pad.5.clone
  93.9 0.4 collective-permute-done.8
  94.3 0.9 pad_maximum_fusion.5.refs_4_
  95.1 89.3 %middle.1 = (bf16[1024,768]{1,0:T(8,128)(2,1)}, f32[1024,768]{1,0:T(8,128)}, bf16[1024,384]{1,0:T(8,128)(2,1)}, bf16[1024,384]{1,0:T(8,128)(2,1)}, bf16[256,1152...) custom-call(bf16[1024,768]{1,0:T(8,128)(2,1)} %bitcast.32, ...), custom_call_target="tpu_custom_call" | custom-call | flops 60000002048 | bytes 40000000 | tf_op jit(solution)/shard_map/middle/pallas_call | solution.py:1054
  184.5 2.6 collective-permute-start.11
  187.1 1.8 collective-permute-start.12
  188.9 24.0 %attend_backward.2 = (bf16[3,1584,384]{2,1,0:T(8,128)(2,1)}, bf16[3,768,384]{2,1,0:T(8,128)(2,1)}) custom-call(s32[4,2]{1,0:T(4,128)} %pad_add_fusion.1.span_ref, s32[4,2,256]{2,1,0:T(2,128)} %add_add_fusion.clean_ref, s32[4,2,128]{2,1,0:T(2,128)} %pad_add_fusion.noisy_ref, bf16[1584,384]{1,0:T(8,128)(2,1)} %get-tuple-element.94.q_ref, ...), custom_call_target="tpu_custom_call" | custom-call | flops 35999997952 | bytes 36000000 | tf_op jit(solution)/shard_map/attend_backward/pallas_call | solution.py:472
  212.9 1.3 constant_dynamic-slice_fusion
  214.3 4.1 %collective-permute-start.14 = (bf16[256,1152]{1,0:T(8,128)(2,1)}, bf16[256,1152]{1,0:T(8,128)(2,1)}, u32[]{:S(2)}, u32[]{:S(2)}) collective-permute-start(bf16[256,1152]{1,0:T(8,128)(2,1)} %get-tuple-element.116), channel_id=1, source_target_pairs={{0,1},{1,0},{2,3},{3,2},{4,5},{5,4},{6,7},{7,6},{8,9},{9,8},{10,11... | collective-permute-start | bytes 1769480 | tf_op jit(solution)/shard_map/ppermute | solution.py:1605
  218.5 0.7 fusion.4
  219.3 0.3 broadcast_select_fusion.5
  219.7 1.4 copy-done.1
  221.0 0.2 add_convert_fusion
  221.3 0.1 collective-permute-start.13
  221.4 2.0 collective-permute-start.15
  223.4 19.3 %attend_backward.3.refs_4_ = bf16[3,1584,384]{2,1,0:T(8,128)(2,1)} custom-call(s32[4,2]{1,0:T(4,128)} %pad_add_fusion.1.span_ref, s32[4,2,256]{2,1,0:T(2,128)} %add_add_fusion.clean_ref, s32[4,2,128]{2,1,0:T(2,128)} %pad_add_fusion.noisy_ref, bf16[1584,384]{1,0:T(8,128)(2,1)} %get-tuple-element.85.q_ref, bf16[1584,384]{1,0:T(8,128)(2,1)} %get-tuple-element.86.k_ref, ...), custom_call_target="tpu_custom_call" | custom-call | flops 35999997952 | bytes 36000000 | tf_op jit(solution)/shard_map/attend_backward/pallas_call | solution.py:472
  242.8 7.0 %collective-permute-done.15 = bf16[12,64,768]{2,1,0:T(8,128)(2,1)S(1)} collective-permute-done((bf16[12,64,768]{2,1,0:T(8,128)(2,1)S(1)}, bf16[12,64,768]{2,1,0:T(8,128)(2,1)S(1)}, u32[]{:S(2)}, u32[]{:S(2)}) %collective-permute-start.15) | collective-permute-done | bytes 1179680 | tf_op jit(solution)/shard_map/ppermute | solution.py:1611
  249.7 0.2 broadcast_select_fusion.1
  249.9 1.7 pad_maximum_fusion.down_mine.up_mine
  251.6 59.7 %leave.1 = (bf16[3,768,384]{2,1,0:T(8,128)(2,1)}, bf16[384,768]{1,0:T(8,128)(2,1)}, f32[1024,768]{1,0:T(8,128)}, f32[16,768]{1,0:T(8,128)}) custom-call(bf16[768,1584]{1,0:T(8,128)(2,1)} %get-tuple-element.106.refs_0_, bf16[256,1152]{1,0:T(8,128)(2,1)} %get-tuple-element.107.refs_1_, bf16[9,128,384]{2,1,0:T(8,128)(2,1)} %collective-permute-done.13.refs_2_, ...), custom_call_target="tpu_custom_call" | custom-call | flops 40000000000 | bytes 40000000 | tf_op jit(solution)/shard_map/leave/pallas_call | solution.py:1440
  311.3 2.3 convert_element_type.40
  313.6 0.7 slice.58
  314.3 0.6 reshape.335
  314.9 1.6 slice_reduce_fusion.2
  316.5 2.0 convert_bitcast_fusion
  318.6 7.1 %assemble.1 = (f32[1536,768]{1,0:T(8,128)}, f32[768,1536]{1,0:T(8,128)}) custom-call(s32[1]{0:T(128)} %bitcast.19.core_ref, bf16[12,128,768]{2,1,0:T(8,128)(2,1)} %pad_maximum_fusion.down_mine.up_mine, bf16[12,128,768]{2,1,0:T(8,128)(2,1)} %pad_maximum_fusion.down_mine.up_mine, bf16[12,128,768]{2,1,0:T(8,128)(2,1)} %collective-permute-done.16.down_got.up_got, ...), custom_call_target="tpu_custom_call" | custom-call | flops 1000000 | bytes 14000000 | tf_op jit(solution)/shard_map/assemble/pallas_call | solution.py:1506
  325.7 1.1 copy.39
  326.8 1.3 copy-done
  328.1 1.7 copy.40
  (73 shorter events, 0.9 us)
Async XLA Ops:
  0.6 5.2 %copy-start.16 = (s32[1,4]{1,0:T(1,128)S(1)}, s32[1,4]{1,0:T(1,128)}, u32[]{:S(2)}) copy-start(s32[1,4]{1,0:T(1,128)} %param.15) | copy-start | bytes 52
  0.7 6.9 %copy-start.9 = (f32[768]{0:T(1024)S(1)}, f32[768]{0:T(1024)}, u32[]{:S(2)}) copy-start(f32[768]{0:T(1024)} %param.18) | copy-start | bytes 9220
  0.7 6.9 %copy-start.10 = (f32[768]{0:T(1024)S(1)}, f32[768]{0:T(1024)}, u32[]{:S(2)}) copy-start(f32[768]{0:T(1024)} %param.19) | copy-start | bytes 9220
  0.7 6.9 %copy-start.11 = (f32[768]{0:T(1024)S(1)}, f32[768]{0:T(1024)}, u32[]{:S(2)}) copy-start(f32[768]{0:T(1024)} %param.22) | copy-start | bytes 9220
  0.7 6.9 %copy-start.12 = (f32[768]{0:T(1024)S(1)}, f32[768]{0:T(1024)}, u32[]{:S(2)}) copy-start(f32[768]{0:T(1024)} %param.23) | copy-start | bytes 9220
  0.7 6.9 %copy-start.13 = (f32[768]{0:T(1024)S(1)}, f32[768]{0:T(1024)}, u32[]{:S(2)}) copy-start(f32[768]{0:T(1024)} %param.27) | copy-start | bytes 9220
  2.8 7.3 %copy-start.6 = (bf16[384,768]{1,0:T(8,128)(2,1)S(1)}, bf16[384,768]{1,0:T(8,128)(2,1)}, u32[]{:S(2)}) copy-start(bf16[384,768]{1,0:T(8,128)(2,1)} %refs_3_.1) | copy-start | bytes 1769476
  2.8 21.2 %collective-permute-start = (bf16[528,768]{1,0:T(8,128)(2,1)S(1)}, bf16[528,768]{1,0:T(8,128)(2,1)}, u32[]{:S(2)}, u32[]{:S(2)}) collective-permute-start(bf16[528,768]{1,0:T(8,128)(2,1)S(1)} %pad_maximum_fusion.4), channel_id=1, source_target_pairs={{0,1},{1,0},{2,3},{3,2},{4,5},{5,4},{6,7},{7,6},{8,9},{9,8},{10,11... | collective-permute-start | bytes 2433032 | tf_op jit(solution)/shard_map/ppermute | solution.py:1605
  24.0 13.4 %collective-permute-start.1 = (bf16[3,192,384]{2,1,0:T(8,128)(2,1)S(1)}, bf16[3,192,384]{2,1,0:T(8,128)(2,1)S(1)}, u32[]{:S(2)}, u32[]{:S(2)}) collective-permute-start(bf16[3,192,384]{2,1,0:T(8,128)(2,1)S(1)} %dynamic-slice_bitcast_fusion), channel_id=1, source_target_pairs={{0,1},{1,0},{2,3},{3,2},{4,5},{5,4},{6,7},{7,6},{8,9},{9,8},{10,11... | collective-permute-start | bytes 1327112 | tf_op jit(solution)/shard_map/ppermute | solution.py:1605
  25.7 29.0 %collective-permute-start.3 = (bf16[192,1536]{1,0:T(8,128)(2,1)S(1)}, bf16[192,1536]{1,0:T(8,128)(2,1)}, u32[]{:S(2)}, u32[]{:S(2)}) collective-permute-start(bf16[192,1536]{1,0:T(8,128)(2,1)S(1)} %constant_dynamic-slice_fusion.3), channel_id=1, source_target_pairs={{0,1},{1,0},{2,3},{3,2},{4,5},{5,4},{6,7},{7,6},{8,9},{9,8},{10,11... | collective-permute-start | bytes 1769480 | tf_op jit(solution)/shard_map/ppermute | solution.py:1605
  37.4 17.3 %collective-permute-start.2 = (bf16[3,192,384]{2,1,0:T(8,128)(2,1)S(1)}, bf16[3,192,384]{2,1,0:T(8,128)(2,1)S(1)}, u32[]{:S(2)}, u32[]{:S(2)}) collective-permute-start(bf16[3,192,384]{2,1,0:T(8,128)(2,1)S(1)} %collective-permute-done.1), channel_id=1, source_target_pairs={{0,4},{2,6},{4,0},{6,2},{8,12},{10,14},{12,8},{14,10},{16,20},{18,... | collective-permute-start | bytes 1327112 | tf_op jit(solution)/shard_map/ppermute | solution.py:1611
  54.7 5.0 %copy-start.4 = (bf16[192,768]{1,0:T(8,128)(2,1)S(1)}, bf16[192,768]{1,0:T(8,128)(2,1)}, u32[]{:S(2)}) copy-start(bf16[192,768]{1,0:T(8,128)(2,1)} %constant_dynamic-slice_fusion.1) | copy-start | bytes 884740
  54.9 7.1 %collective-permute-start.4 = (bf16[3,384,384]{2,1,0:T(8,128)(2,1)S(1)}, bf16[3,384,384]{2,1,0:T(8,128)(2,1)}, u32[]{:S(2)}, u32[]{:S(2)}) collective-permute-start(bf16[3,384,384]{2,1,0:T(8,128)(2,1)S(1)} %pad_maximum_fusion.3), channel_id=1, source_target_pairs={{0,2},{2,0},{4,6},{6,4},{8,10},{10,8},{12,14},{14,12},{16,18},{18,... | collective-permute-start | bytes 2654216 | tf_op jit(solution)/shard_map/ppermute | solution.py:1608
  55.0 37.6 %collective-permute-start.7 = (bf16[768,768]{1,0:T(8,128)(2,1)S(1)}, bf16[768,768]{1,0:T(8,128)(2,1)}, u32[]{:S(2)}, u32[]{:S(2)}) collective-permute-start(bf16[768,768]{1,0:T(8,128)(2,1)S(1)} %constant_dynamic-slice_fusion.2), channel_id=1, source_target_pairs={{0,1},{1,0},{2,3},{3,2},{4,5},{5,4},{6,7},{7,6},{8,9},{9,8},{10,11... | collective-permute-start | bytes 3538952 | tf_op jit(solution)/shard_map/ppermute | solution.py:1605
  59.8 32.9 %collective-permute-start.5 = (bf16[192,768]{1,0:T(8,128)(2,1)S(1)}, bf16[192,768]{1,0:T(8,128)(2,1)S(1)}, u32[]{:S(2)}, u32[]{:S(2)}) collective-permute-start(bf16[192,768]{1,0:T(8,128)(2,1)S(1)} %copy-done.4), channel_id=1, source_target_pairs={{0,1},{1,0},{2,3},{3,2},{4,5},{5,4},{6,7},{7,6},{8,9},{9,8},{10,11... | collective-permute-start | bytes 884744 | tf_op jit(solution)/shard_map/ppermute | solution.py:1605
  60.4 32.3 %collective-permute-start.6 = (bf16[192,1536]{1,0:T(8,128)(2,1)}, bf16[192,1536]{1,0:T(8,128)(2,1)}, u32[]{:S(2)}, u32[]{:S(2)}) collective-permute-start(bf16[192,1536]{1,0:T(8,128)(2,1)} %collective-permute-done.3.refs_9_), channel_id=1, source_target_pairs={{0,4},{2,6},{4,0},{6,2},{8,12},{10,14},{12,8},{14,10},{16,20},{18,... | collective-permute-start | bytes 1769480 | tf_op jit(solution)/shard_map/ppermute | solution.py:1611
  72.3 20.4 %copy-start.14 = (bf16[1536]{0:T(1024)(128)(2,1)S(1)}, bf16[1536]{0:T(1024)(128)(2,1)}, u32[]{:S(2)}) copy-start(bf16[1536]{0:T(1024)(128)(2,1)} %param.25) | copy-start | bytes 9220
  92.6 1.6 collective-permute-start.8
  184.5 34.7 %collective-permute-start.10 = (bf16[12,16,768]{2,1,0:T(8,128)(2,1)}, bf16[12,16,768]{2,1,0:T(8,128)(2,1)S(1)}, u32[]{:S(2)}, u32[]{:S(2)}) collective-permute-start(bf16[12,16,768]{2,1,0:T(8,128)(2,1)} %get-tuple-element.111), channel_id=1, source_target_pairs={{0,8},{2,10},{4,12},{6,14},{8,0},{10,2},{12,4},{14,6},{16,24},{18,... | collective-permute-start | bytes 884744 | tf_op jit(solution)/shard_map/ppermute | solution.py:1670
  184.5 34.6 %collective-permute-start.11 = (bf16[12,16,768]{2,1,0:T(8,128)(2,1)}, bf16[12,16,768]{2,1,0:T(8,128)(2,1)S(1)}, u32[]{:S(2)}, u32[]{:S(2)}) collective-permute-start(bf16[12,16,768]{2,1,0:T(8,128)(2,1)} %get-tuple-element.111), channel_id=1, source_target_pairs={{0,16},{2,18},{4,20},{6,22},{8,24},{10,26},{12,28},{14,30},{16,0},... | collective-permute-start | bytes 884744 | tf_op jit(solution)/shard_map/ppermute | solution.py:1670
  187.1 32.1 %collective-permute-start.12 = (bf16[12,16,768]{2,1,0:T(8,128)(2,1)}, bf16[12,16,768]{2,1,0:T(8,128)(2,1)S(1)}, u32[]{:S(2)}, u32[]{:S(2)}) collective-permute-start(bf16[12,16,768]{2,1,0:T(8,128)(2,1)} %get-tuple-element.111), channel_id=1, source_target_pairs={{0,24},{2,26},{4,28},{6,30},{8,16},{10,18},{12,20},{14,22},{16,8},... | collective-permute-start | bytes 884744 | tf_op jit(solution)/shard_map/ppermute | solution.py:1670
  212.9 5.5 %copy-start.8 = (f32[8,768]{1,0:T(8,128)S(1)}, f32[8,768]{1,0:T(8,128)}, u32[]{:S(2)}) copy-start(f32[8,768]{1,0:T(8,128)} %get-tuple-element.127) | copy-start | bytes 73732
  212.9 5.5 %copy-start.7 = (f32[12,1,256]{2,1,0:T(1,128)S(1)}, f32[12,1,256]{2,1,0:T(1,128)}, u32[]{:S(2)}) copy-start(f32[12,1,256]{2,1,0:T(1,128)} %get-tuple-element.126) | copy-start | bytes 36868
  212.9 5.6 %copy-start.15 = (f32[7]{0:T(128)S(1)}, f32[7]{0:T(128)}, u32[]{:S(2)}) copy-start(f32[7]{0:T(128)} %pad.5.clone) | copy-start | bytes 88
  212.9 6.3 %copy-start.5 = (bf16[12,16,768]{2,1,0:T(8,128)(2,1)S(1)}, bf16[12,16,768]{2,1,0:T(8,128)(2,1)}, u32[]{:S(2)}) copy-start(bf16[12,16,768]{2,1,0:T(8,128)(2,1)} %get-tuple-element.111) | copy-start | bytes 884740
  214.3 5.4 %collective-permute-start.9 = (bf16[9,128,384]{2,1,0:T(8,128)(2,1)S(1)}, bf16[9,128,384]{2,1,0:T(8,128)(2,1)S(1)}, u32[]{:S(2)}, u32[]{:S(2)}) collective-permute-start(bf16[9,128,384]{2,1,0:T(8,128)(2,1)S(1)} %constant_dynamic-slice_fusion), channel_id=1, source_target_pairs={{0,2},{2,0},{4,6},{6,4},{8,10},{10,8},{12,14},{14,12},{16,18},{18,... | collective-permute-start | bytes 2654216 | tf_op jit(solution)/shard_map/ppermute | solution.py:1608
  214.3 37.2 %collective-permute-start.14 = (bf16[256,1152]{1,0:T(8,128)(2,1)}, bf16[256,1152]{1,0:T(8,128)(2,1)}, u32[]{:S(2)}, u32[]{:S(2)}) collective-permute-start(bf16[256,1152]{1,0:T(8,128)(2,1)} %get-tuple-element.116), channel_id=1, source_target_pairs={{0,1},{1,0},{2,3},{3,2},{4,5},{5,4},{6,7},{7,6},{8,9},{9,8},{10,11... | collective-permute-start | bytes 1769480 | tf_op jit(solution)/shard_map/ppermute | solution.py:1605
  219.6 1.5 copy-start.1
  221.3 30.3 %collective-permute-start.13 = (bf16[9,128,384]{2,1,0:T(8,128)(2,1)S(1)}, bf16[9,128,384]{2,1,0:T(8,128)(2,1)}, u32[]{:S(2)}, u32[]{:S(2)}) collective-permute-start(bf16[9,128,384]{2,1,0:T(8,128)(2,1)S(1)} %add_convert_fusion), channel_id=1, source_target_pairs={{0,1},{1,0},{2,3},{3,2},{4,5},{5,4},{6,7},{7,6},{8,9},{9,8},{10,11... | collective-permute-start | bytes 2654216 | tf_op jit(solution)/shard_map/ppermute | solution.py:1605
  221.4 28.3 %collective-permute-start.15 = (bf16[12,64,768]{2,1,0:T(8,128)(2,1)S(1)}, bf16[12,64,768]{2,1,0:T(8,128)(2,1)S(1)}, u32[]{:S(2)}, u32[]{:S(2)}) collective-permute-start(bf16[12,64,768]{2,1,0:T(8,128)(2,1)S(1)} %pad_maximum_fusion.2), channel_id=1, source_target_pairs={{0,4},{2,6},{4,0},{6,2},{8,12},{10,14},{12,8},{14,10},{16,20},{18,... | collective-permute-start | bytes 3538952 | tf_op jit(solution)/shard_map/ppermute | solution.py:1611
  251.5 67.0 %collective-permute-start.16 = (bf16[12,128,768]{2,1,0:T(8,128)(2,1)}, bf16[12,128,768]{2,1,0:T(8,128)(2,1)}, u32[]{:S(2)}, u32[]{:S(2)}) collective-permute-start(bf16[12,128,768]{2,1,0:T(8,128)(2,1)} %pad_maximum_fusion.down_mine.up_mine), channel_id=1, source_target_pairs={{0,2},{2,0},{4,6},{6,4},{8,10},{10,8},{12,14},{14,12},{16,18},{18,... | collective-permute-start | bytes 7077896 | tf_op jit(solution)/shard_map/ppermute | solution.py:1608
  311.3 5.3 %copy-start.2 = (bf16[3,768,384]{2,1,0:T(8,128)(2,1)S(1)}, bf16[3,768,384]{2,1,0:T(8,128)(2,1)}, u32[]{:S(2)}) copy-start(bf16[3,768,384]{2,1,0:T(8,128)(2,1)} %get-tuple-element.130) | copy-start | bytes 5308420
  318.6 7.1 %copy-start.3 = (bf16[1024,768]{1,0:T(8,128)(2,1)S(1)}, bf16[1024,768]{1,0:T(8,128)(2,1)}, u32[]{:S(2)}) copy-start(bf16[1024,768]{1,0:T(8,128)(2,1)} %get-tuple-element.105) | copy-start | bytes 4718596
  325.7 2.5 copy-start

commit v4 on v3

--- a/solution.py
+++ b/solution.py
@@ -307,6 +307,7 @@
 
 
 def backward_kernel(
+    giving,
     span_ref,
     clean_ref,
     noisy_ref,
@@ -320,12 +321,19 @@
     sin_ref,
     *refs,
 ):
-    rows_ref, out_ref, grad_ref, dk_ref, dv_ref, bias_ref = refs if len(refs) == 6 else (
-        None,
-        refs[0],
-        None,
-        *refs[1:],
-    )
+    if giving:
+        d2_hbm, w_hbm, w2_hbm, out_ref, give_ref, *refs = refs
+        dk_ref, dv_ref, bias_ref, d2_ref, w_ref, w2_ref, load_sem = refs
+        loads = [(w_hbm, w_ref), (w2_hbm, w2_ref)]
+        loads += [(d2_hbm.at[c, :HALF], d2_ref.at[c]) for c in range(3)]
+        loads = [
+            pltpu.make_async_copy(source, target, load_sem.at[n])
+            for n, (source, target) in enumerate(loads)
+        ]
+        for load in loads:
+            load.start()
+    else:
+        rows_ref, out_ref, grad_ref, dk_ref, dv_ref, bias_ref = refs
     pairs = q_ref.shape[1] // LANES
     lanes = [slice(p * LANES, (p + 1) * LANES) for p in range(pairs)]
     dk_ref[...] = jnp.zeros_like(dk_ref)
@@ -449,7 +457,14 @@
             grad_ref[c, rows, :] = dot(rows_ref[rows, :], out_ref[c]).astype(bf16)
         return 0
 
-    if rows_ref is not None:
+    if giving:
+        for load in loads:
+            load.wait()
+        total = 0.0
+        for c in range(3):
+            total = total + dot(out_ref[c, :HALF, :], w_ref[c], NT) + dot(d2_ref[c], w2_ref[c], NT)
+        give_ref[...] = total
+    else:
         lax.fori_loop(0, rows_ref.shape[0] // ROW_TILE, weight_rows, 0)
 
 
@@ -465,23 +480,38 @@
     lse,
     cosine,
     sine,
-    *rows_t,
+    rest,
 ):
     count, cols = query.shape
     vmem = pl.BlockSpec(memory_space=pltpu.VMEM)
+    hbm = pl.BlockSpec(memory_space=pl.ANY)
+    shape = jax.ShapeDtypeStruct
+    giving = len(rest) > 1
+    if giving:
+        width = rest[1].shape[1]
+        second = shape((HALF, width), f32)
+        scratch = [
+            pltpu.VMEM((3, HALF, cols), bf16),
+            pltpu.VMEM(rest[1].shape, bf16),
+            pltpu.VMEM(rest[2].shape, bf16),
+            pltpu.SemaphoreType.DMA((5,)),
+        ]
+    else:
+        second = shape((3, rest[0].shape[0], cols), bf16)
+        scratch = []
     return pl.pallas_call(
-        backward_kernel,
-        in_specs=[pl.BlockSpec(memory_space=pltpu.SMEM)] + [vmem] * (10 + len(rows_t)),
-        out_specs=[vmem] * (1 + len(rows_t)),
+        functools.partial(backward_kernel, giving),
+        in_specs=[pl.BlockSpec(memory_space=pltpu.SMEM)]
+        + [vmem] * 10
+        + [hbm if giving else vmem] * len(rest),
+        out_specs=[vmem] * 2,
         scratch_shapes=[
             pltpu.VMEM((count, cols), f32),
             pltpu.VMEM((count, cols), f32),
             pltpu.VMEM((max(KEY_TILE, WINDOW), 2 * TILE), f32),
-        ],
-        out_shape=[
-            jax.ShapeDtypeStruct((3, count, cols), bf16),
-            *[jax.ShapeDtypeStruct((3, rows.shape[0], cols), bf16) for rows in rows_t],
-        ],
+        ]
+        + scratch,
+        out_shape=[shape((3, count, cols), bf16), second],
         name="attend_backward",
         cost_estimate=pl.CostEstimate(
             flops=36 * 10**9, bytes_accessed=36 * 10**6, transcendentals=6 * 10**6
@@ -498,7 +528,7 @@
         lse,
         cosine,
         sine,
-        *rows_t,
+        *rest,
     )
 
 
@@ -875,7 +905,12 @@
 
     lax.fori_loop(0, count, hand, 0)
 
-    def prologue(r, _):
+    def prologue(n, _):
+        prologue_block(2 * n)
+        prologue_block(2 * n + 1)
+        return 0
+
+    def prologue_block(r):
         rows = pl.ds(pl.multiple_of(r * ROW_TILE, ROW_TILE), ROW_TILE)
         branch = dot(att_ref[rows, :], wout_ref[...]) + dot(att2_ref[rows, :], wout2_ref[...])
         mid = x_ref[rows, :].astype(f32) + branch
@@ -884,9 +919,8 @@
         n2_ref[rows, :] = (unit * vectors_ref[2:3, :] + vectors_ref[3:4, :]).astype(bf16)
         total_ref[rows, :] = mid + vectors_ref[4:5, :]
         dn2_ref[rows, :] = jnp.zeros((ROW_TILE, width), f32)
-        return 0
-
-    lax.fori_loop(0, blocks, prologue, 0)
+
+    lax.fori_loop(0, blocks // 2, prologue, 0)
     start_loads(0)
     for c in range(width // LANES):
         cols = slice(c * LANES, (c + 1) * LANES)
@@ -1114,6 +1148,7 @@
         w2_hbm,
         tokens_ref,
         context_ref,
+        given_ref,
         vectors_ref,
         dmid_hbm,
         small_ref,
@@ -1174,10 +1209,11 @@
         total = mine_out_ref[:, cols].astype(f32) + crossed_out_ref[:, cols].astype(f32)
         out_buf[r] = total.astype(bf16)
         ex.start_a(r, 0, out_buf)
-    step = KEY_ROWS // 3
+    step = HALF + 2 * EDGE
 
     def back_rows(n):
-        rows = pl.ds(pl.multiple_of(n * step, EDGE), step)
+        start = CLEAN_OWN + n * (KEY_ROWS - step - CLEAN_OWN)
+        rows = pl.ds(pl.multiple_of(start, EDGE), step)
         total = 0.0
         for grads, weights in ((d_ref, w_ref), (d2_ref, w2_ref)):
             for c in range(3):
@@ -1266,9 +1302,8 @@
         for load in loads[2:5]:
             load.wait()
 
-    def give_main():
-        give_ref[main, :] = rows_ref[main, :].astype(bf16)
-        swap(main, 0).start()
+    give_ref[main, :] = given_ref[...].astype(bf16)
+    swap(main, 0).start()
 
     def give_edges():
         side = rows_ref[NOISY_BASE:NOISY_OWN, :] + rows_ref[NOISY_OWN + HALF :, :]
@@ -1282,7 +1317,7 @@
     def tell_near():
         def context_sums(b, _):
             rows = tokens_at(b)
-            sums_of(rows_ref[rows, :], normal(context_ref[rows, :].astype(f32))[0])
+            sums_of(given_ref[rows, :], normal(context_ref[rows, :].astype(f32))[0])
             return 0
 
         lax.fori_loop(0, HALF // TILE, context_sums, 0)
@@ -1395,13 +1430,12 @@
 
     groups = count // split - 1
     actions = {
-        groups: give_main,
-        groups + 2: give_edges,
-        groups + 3: tell_near,
-        groups + 4: tell_far,
-        groups + 5: take_back,
+        groups + 1: give_edges,
+        groups + 2: tell_near,
+        groups + 3: tell_far,
+        groups + 4: take_back,
     }
-    begin_back = groups + 6
+    begin_back = groups + 5
 
     def phase(p, _):
         @pl.when(p < groups)
@@ -1410,7 +1444,7 @@
 
         pl.when(p == groups)(ready)
 
-        @pl.when(jnp.logical_and(p >= groups, p < groups + 3))
+        @pl.when(jnp.logical_and(p >= groups, p < groups + 2))
         def _():
             back_rows(p - groups)
 
@@ -1429,7 +1463,7 @@
     lax.fori_loop(0, begin_back + parts // 2 + 1, phase, 0)
 
 
-def leave(bits, rows_t, mine, crossed, d_fields, weights, tokens, context, vectors, d_mid, small, small2):
+def leave(bits, rows_t, mine, crossed, d_fields, weights, tokens, context, given, vectors, d_mid, small, small2):
     rows, cols = ROW_TILE, d_fields[0].shape[2]
     total = mine.shape[1] // cols + crossed[0].shape[0]
     exchange = Exchange(bits, total, rows, cols)
@@ -1439,7 +1473,7 @@
     shape = jax.ShapeDtypeStruct
     return pl.pallas_call(
         functools.partial(leave_kernel, exchange),
-        in_specs=[hbm] + [vmem] * 3 + [hbm] * 4 + [vmem] * 3 + [hbm] + [vmem] * 2,
+        in_specs=[hbm] + [vmem] * 3 + [hbm] * 4 + [vmem] * 4 + [hbm] + [vmem] * 2,
         out_specs=[vmem] * 4,
         out_shape=[
             shape(weights[0].shape, bf16),
@@ -1476,7 +1510,7 @@
             flops=40 * 10**9, bytes_accessed=40 * 10**6, transcendentals=0
         ),
     )(
-        rows_t, mine, *crossed, *d_fields, *weights, tokens, context, vectors, d_mid, small, small2
+        rows_t, mine, *crossed, *d_fields, *weights, tokens, context, given, vectors, d_mid, small, small2
     )
 
 
@@ -1671,7 +1705,7 @@
         for k in range(1, 1 << n)
     ]
 
-    def backward(saved, d_attended, spans, *rows_t):
+    def backward(saved, d_attended, spans, *rest):
         query, keys, values, attended, lse = saved
         return attend_backward(
             spans,
@@ -1685,7 +1719,7 @@
             lse,
             cosine,
             sine,
-            *rows_t,
+            rest,
         )
 
     d_fields2, grad2 = backward(other, d_att2, spans, normed1_t)
@@ -1705,7 +1739,7 @@
     (crossing, gathered), spans = tie((crossing, gathered), spans)
     crossed = across(crossing)
     moved = beside(gathered)
-    (d_fields1,) = backward(mine, d_att, spans)
+    d_fields1, given = backward(mine, d_att, spans, d_fields2, qkv_mine, qkv_other)
     moved, d_fields1 = tie(moved, d_fields1)
     gathered = in_order(side, gathered, moved, 1)
     gathered, d_fields1 = tie(gathered, d_fields1)
@@ -1722,6 +1756,7 @@
         (qkv_mine, qkv_other),
         x_rows,
         context,
+        given,
         vectors,
         d_mid,
         jnp.concatenate([bias1, shared], axis=0),

time: 331 us -> 330 us (level)
  Pallas kernels: 249 us -> 240 us
  starting transfers between devices: 24.5 us -> 30.3 us
    ppermute x7, starting transfers between devices: 14.6 us -> 20.4 us  [across(): return lax.ppermute(array, 'mp', [(0, 1), (1, 0)])]
    pallas_call x2, Pallas kernels: 31.3 us -> 27.1 us  [attend_forward(): pl.pallas_call(forward_kernel, in_specs=[pl.BlockSpec(memory_space=pltpu....]
  transfers between devices with their start and end apart: 17 -> 17, of which waited for: 5 -> 5; matrix products, arithmetic and copies ran while one was open for 9% -> 9% of each run, Pallas kernels for 46% -> 43%
where the time goes in v4:
time: 330 us; the launch traced here: 332 us
  Pallas kernels  240 us (73%)
  starting transfers between devices  30.3 us (9%)
  other arithmetic  20.4 us (6%)
  waiting for transfers between devices  19.8 us (6%)
  local copies, waits for them, and re-layouts  19.6 us (6%)
    pallas_call x1, Pallas kernels, middle(): pl.pallas_call(functools.partial(middle_kernel, exchanges, tiles), in_spe...  88.6 us
    pallas_call x1, Pallas kernels, leave(): pl.pallas_call(functools.partial(leave_kernel, exchange), in_specs=[hbm]...  56.8 us
    pallas_call x2, Pallas kernels, attend_backward(): pl.pallas_call(functools.partial(backward_kernel, giving), in_specs=[pl.B...  41.7 us
    pallas_call x2, Pallas kernels, attend_forward(): pl.pallas_call(forward_kernel, in_specs=[pl.BlockSpec(memory_space=pltpu....  27.1 us
    ppermute x7, starting transfers between devices, across(): return lax.ppermute(array, 'mp', [(0, 1), (1, 0)])  20.4 us
    ppermute x7, waiting for transfers between devices, across(): return lax.ppermute(array, 'mp', [(0, 1), (1, 0)])  12.4 us
    pallas_call x1, Pallas kernels, enter(): pl.pallas_call(enter_kernel, in_specs=[vmem] * 6, out_specs=[vmem] * 5, o...  11.4 us
    pallas_call x1, Pallas kernels, project(): pl.pallas_call(project_kernel, grid=(3,), in_specs=[row_spec, pl.BlockSpe...  7.34 us
  transfers between devices with their start and end apart: 17, of which 5 were waited for; matrix products, arithmetic and copies ran while one was open for 9% of the time, Pallas kernels for 43%

profile of v4, /device:TPU:0, one launch (start us, length us, event | category | flops | bytes accessed | tf_op | source)
XLA Modules:
  0.0 331.8 jit_solution(5821676185495852021)
XLA Ops:
  0.7 1.2 slice_bitcast_fusion
  1.9 0.8 select_bitcast_fusion
  2.8 3.0 collective-permute-start
  5.8 0.2 reduce-window.8
  6.8 0.1 subtract_convert_fusion
  6.9 0.3 fusion.16
  7.3 0.2 reduce_min.21
  7.7 0.7 pad_add_fusion.1.span_ref
  8.3 0.6 add_add_fusion.clean_ref
  8.9 0.6 pad_add_fusion.noisy_ref
  9.5 1.1 dynamic-slice_bitcast_fusion
  10.6 1.4 constant_dynamic-slice_fusion.2
  12.0 0.7 constant_dynamic-slice_fusion.1
  12.7 0.6 stack.29.vectors_ref.refs_6_.refs_11_
  13.3 1.1 constant_dynamic-slice_fusion.3
  14.5 4.4 %fusion = (f32[1584,128]{1,0:T(8,128)}, f32[1584,128]{1,0:T(8,128)}) fusion(f32[128]{0:T(128)S(1)} %get-tuple-element.179, f32[128]{0:T(128)S(1)} %get-tuple-element.180, f32[1584]{0:T(1024)S(1)} %get-tuple-element.173), kind=kLoop, calls=%fused_computation.12 | loop fusion | flops 405504 | bytes 1629376 | tf_op jit(solution)/shard_map/mul | solution.py:1601
  18.8 5.1 %collective-permute-done.context_ref.refs_9_ = bf16[528,768]{1,0:T(8,128)(2,1)} collective-permute-done((bf16[528,768]{1,0:T(8,128)(2,1)S(1)}, bf16[528,768]{1,0:T(8,128)(2,1)}, u32[]{:S(2)}, u32[]{:S(2)}) %collective-permute-start) | collective-permute-done | bytes 811040 | tf_op jit(solution)/shard_map/ppermute | solution.py:1639
  24.0 1.7 collective-permute-start.1
  25.7 0.3 collective-permute-start.3
  26.0 11.4 %enter.1 = (bf16[1584,768]{1,0:T(8,128)(2,1)}, bf16[768,1584]{1,0:T(8,128)(2,1)}, bf16[1584,384]{1,0:T(8,128)(2,1)}, bf16[1584,384]{1,0:T(8,128)(2,1)}, bf16[1584,384]{1,0:T(8,128)(2,1)}) custom-call(bf16[2,512,768]{2,1,0:T(8,128)(2,1)} %tokens_ref.1, bf16[528,768]{1,0:T(8,128)(2,1)} %collective-permute-done.context_ref.refs_9_, ...), custom_call_target="tpu_custom_call" | custom-call | flops 10000000000 | bytes 16000000 | tf_op jit(solution)/shard_map/enter/pallas_call | solution.py:157
  37.4 1.7 collective-permute-start.2
  39.1 13.5 %attend_forward.2 = (bf16[1024,384]{1,0:T(8,128)(2,1)}, f32[3,4,2,256]{3,2,1,0:T(2,128)}) custom-call(s32[4,2]{1,0:T(4,128)} %pad_add_fusion.1.span_ref, s32[4,2,256]{2,1,0:T(2,128)} %add_add_fusion.clean_ref, s32[4,2,128]{2,1,0:T(2,128)} %pad_add_fusion.noisy_ref, bf16[1584,384]{1,0:T(8,128)(2,1)} %get-tuple-element.87.q_ref, ...), custom_call_target="tpu_custom_call" | custom-call | flops 1610612736 | bytes 4866048 | tf_op jit(solution)/shard_map/attend_forward/pallas_call | solution.py:290
  52.6 0.8 copy-done.15
  53.7 7.9 %collective-permute-start.7 = (bf16[768,768]{1,0:T(8,128)(2,1)S(1)}, bf16[768,768]{1,0:T(8,128)(2,1)}, u32[]{:S(2)}, u32[]{:S(2)}) collective-permute-start(bf16[768,768]{1,0:T(8,128)(2,1)S(1)} %constant_dynamic-slice_fusion.2), channel_id=1, source_target_pairs={{0,1},{1,0},{2,3},{3,2},{4,5},{5,4},{6,7},{7,6},{8,9},{9,8},{10,11... | collective-permute-start | bytes 3538952 | tf_op jit(solution)/shard_map/ppermute | solution.py:1639
  61.7 0.6 collective-permute-start.5
  62.3 1.5 collective-permute-start.6
  63.8 1.5 broadcast_select_fusion.3
  65.3 1.4 pad_maximum_fusion.1.w_ref.refs_2_.refs_7_
  66.8 7.3 %project.1 = (bf16[1584,384]{1,0:T(8,128)(2,1)}, bf16[1584,384]{1,0:T(8,128)(2,1)}, bf16[1584,384]{1,0:T(8,128)(2,1)}) custom-call(bf16[1584,768]{1,0:T(8,128)(2,1)} %get-tuple-element.91.rows_ref, bf16[3,768,384]{2,1,0:T(8,128)(2,1)} %pad_maximum_fusion.1.w_ref.refs_2_.refs_7_, f32[1584,128]{1,0:T(8,128)} %get-tuple-element.82.cos_ref, ...), custom_call_target="tpu_custom_call" | custom-call | flops 2802843648 | bytes 7852032 | tf_op jit(solution)/shard_map/project/pallas_call | solution.py:78
  74.1 13.6 %attend_forward.3 = (bf16[1024,384]{1,0:T(8,128)(2,1)}, f32[3,4,2,256]{3,2,1,0:T(2,128)}) custom-call(s32[4,2]{1,0:T(4,128)} %pad_add_fusion.1.span_ref, s32[4,2,256]{2,1,0:T(2,128)} %add_add_fusion.clean_ref, s32[4,2,128]{2,1,0:T(2,128)} %pad_add_fusion.noisy_ref, bf16[1584,384]{1,0:T(8,128)(2,1)} %get-tuple-element.96.q_ref, ...), custom_call_target="tpu_custom_call" | custom-call | flops 1610612736 | bytes 4866048 | tf_op jit(solution)/shard_map/attend_forward/pallas_call | solution.py:290
  87.7 7.0 %collective-permute-done.5 = bf16[192,768]{1,0:T(8,128)(2,1)} collective-permute-done((bf16[192,768]{1,0:T(8,128)(2,1)S(1)}, bf16[192,768]{1,0:T(8,128)(2,1)}, u32[]{:S(2)}, u32[]{:S(2)}) %collective-permute-start.5) | collective-permute-done | bytes 294944 | tf_op jit(solution)/shard_map/ppermute | solution.py:1639
  94.7 0.6 reshape.337.refs_7_
  95.3 0.6 pad.5.clone
  95.9 0.6 collective-permute-done.8
  96.4 1.0 broadcast_select_fusion.13
  97.5 0.9 pad_maximum_fusion.5.refs_4_
  98.3 88.6 %middle.1 = (bf16[1024,768]{1,0:T(8,128)(2,1)}, f32[1024,768]{1,0:T(8,128)}, bf16[1024,384]{1,0:T(8,128)(2,1)}, bf16[1024,384]{1,0:T(8,128)(2,1)}, bf16[256,1152...) custom-call(bf16[1024,768]{1,0:T(8,128)(2,1)} %bitcast.32, ...), custom_call_target="tpu_custom_call" | custom-call | flops 60000002048 | bytes 40000000 | tf_op jit(solution)/shard_map/middle/pallas_call | solution.py:1088
  187.0 2.6 collective-permute-start.11
  189.6 1.7 collective-permute-start.12
  191.3 0.7 slice_reduce_fusion
  192.1 0.7 slice.53
  192.9 22.2 %attend_backward.2 = (bf16[3,1584,384]{2,1,0:T(8,128)(2,1)}, bf16[3,768,384]{2,1,0:T(8,128)(2,1)}) custom-call(s32[4,2]{1,0:T(4,128)} %pad_add_fusion.1.span_ref, s32[4,2,256]{2,1,0:T(2,128)} %add_add_fusion.clean_ref, s32[4,2,128]{2,1,0:T(2,128)} %pad_add_fusion.noisy_ref, bf16[1584,384]{1,0:T(8,128)(2,1)} %get-tuple-element.96.q_ref, ...), custom_call_target="tpu_custom_call" | custom-call | flops 35999997952 | bytes 36000000 | tf_op jit(solution)/shard_map/attend_backward/pallas_call | solution.py:502
  215.0 1.3 constant_dynamic-slice_fusion
  216.4 6.8 %collective-permute-start.14 = (bf16[256,1152]{1,0:T(8,128)(2,1)}, bf16[256,1152]{1,0:T(8,128)(2,1)}, u32[]{:S(2)}, u32[]{:S(2)}) collective-permute-start(bf16[256,1152]{1,0:T(8,128)(2,1)} %get-tuple-element.118), channel_id=1, source_target_pairs={{0,1},{1,0},{2,3},{3,2},{4,5},{5,4},{6,7},{7,6},{8,9},{9,8},{10,11... | collective-permute-start | bytes 1769480 | tf_op jit(solution)/shard_map/ppermute | solution.py:1639
  223.2 0.7 fusion.4
  224.1 0.3 broadcast_select_fusion.5
  224.5 1.4 copy-done.1
  225.8 0.3 add_convert_fusion
  226.1 2.0 collective-permute-start.15
  228.1 19.5 %attend_backward.3 = (bf16[3,1584,384]{2,1,0:T(8,128)(2,1)}, f32[512,768]{1,0:T(8,128)}) custom-call(s32[4,2]{1,0:T(4,128)} %pad_add_fusion.1.span_ref, s32[4,2,256]{2,1,0:T(2,128)} %add_add_fusion.clean_ref, s32[4,2,128]{2,1,0:T(2,128)} %pad_add_fusion.noisy_ref, bf16[1584,384]{1,0:T(8,128)(2,1)} %get-tuple-element.87.q_ref, ...), custom_call_target="tpu_custom_call" | custom-call | flops 35999997952 | bytes 36000000 | tf_op jit(solution)/shard_map/attend_backward/pallas_call | solution.py:502
  247.6 6.8 %collective-permute-done.15 = bf16[12,64,768]{2,1,0:T(8,128)(2,1)S(1)} collective-permute-done((bf16[12,64,768]{2,1,0:T(8,128)(2,1)S(1)}, bf16[12,64,768]{2,1,0:T(8,128)(2,1)S(1)}, u32[]{:S(2)}, u32[]{:S(2)}) %collective-permute-start.15) | collective-permute-done | bytes 1179680 | tf_op jit(solution)/shard_map/ppermute | solution.py:1645
  254.3 0.2 broadcast_select_fusion.1
  254.5 1.7 pad_maximum_fusion.down_mine.up_mine
  256.2 0.3 collective-permute-done.13.refs_2_
  256.4 56.8 %leave.1 = (bf16[3,768,384]{2,1,0:T(8,128)(2,1)}, bf16[384,768]{1,0:T(8,128)(2,1)}, f32[1024,768]{1,0:T(8,128)}, f32[16,768]{1,0:T(8,128)}) custom-call(bf16[768,1584]{1,0:T(8,128)(2,1)} %get-tuple-element.108.refs_0_, bf16[256,1152]{1,0:T(8,128)(2,1)} %get-tuple-element.109.refs_1_, bf16[9,128,384]{2,1,0:T(8,128)(2,1)} %collective-permute-done.13.refs_2_, ...), custom_call_target="tpu_custom_call" | custom-call | flops 40000000000 | bytes 40000000 | tf_op jit(solution)/shard_map/leave/pallas_call | solution.py:1474
  313.3 2.3 convert_element_type.40
  315.6 0.7 slice.58
  316.3 0.6 reshape.335
  316.9 1.6 slice_reduce_fusion.2
  318.5 2.0 convert_bitcast_fusion
  320.6 7.1 %assemble.1 = (f32[1536,768]{1,0:T(8,128)}, f32[768,1536]{1,0:T(8,128)}) custom-call(s32[1]{0:T(128)} %bitcast.19.core_ref, bf16[12,128,768]{2,1,0:T(8,128)(2,1)} %pad_maximum_fusion.down_mine.up_mine, bf16[12,128,768]{2,1,0:T(8,128)(2,1)} %pad_maximum_fusion.down_mine.up_mine, bf16[12,128,768]{2,1,0:T(8,128)(2,1)} %collective-permute-done.16.down_got.up_got, ...), custom_call_target="tpu_custom_call" | custom-call | flops 1000000 | bytes 14000000 | tf_op jit(solution)/shard_map/assemble/pallas_call | solution.py:1540
  327.7 1.1 copy.39
  328.8 1.3 copy-done
  330.1 1.7 copy.40
  (71 shorter events, 1.2 us)
Async XLA Ops:
  0.6 5.2 %copy-start.14 = (s32[1,4]{1,0:T(1,128)S(1)}, s32[1,4]{1,0:T(1,128)}, u32[]{:S(2)}) copy-start(s32[1,4]{1,0:T(1,128)} %param.15) | copy-start | bytes 52
  0.7 6.9 %copy-start.7 = (f32[768]{0:T(1024)S(1)}, f32[768]{0:T(1024)}, u32[]{:S(2)}) copy-start(f32[768]{0:T(1024)} %param.18) | copy-start | bytes 9220
  0.7 6.9 %copy-start.8 = (f32[768]{0:T(1024)S(1)}, f32[768]{0:T(1024)}, u32[]{:S(2)}) copy-start(f32[768]{0:T(1024)} %param.19) | copy-start | bytes 9220
  0.7 6.9 %copy-start.9 = (f32[768]{0:T(1024)S(1)}, f32[768]{0:T(1024)}, u32[]{:S(2)}) copy-start(f32[768]{0:T(1024)} %param.22) | copy-start | bytes 9220
  0.7 6.9 %copy-start.10 = (f32[768]{0:T(1024)S(1)}, f32[768]{0:T(1024)}, u32[]{:S(2)}) copy-start(f32[768]{0:T(1024)} %param.23) | copy-start | bytes 9220
  0.7 6.9 %copy-start.11 = (f32[768]{0:T(1024)S(1)}, f32[768]{0:T(1024)}, u32[]{:S(2)}) copy-start(f32[768]{0:T(1024)} %param.27) | copy-start | bytes 9220
  2.8 9.2 %copy-start.6 = (bf16[384,768]{1,0:T(8,128)(2,1)S(1)}, bf16[384,768]{1,0:T(8,128)(2,1)}, u32[]{:S(2)}) copy-start(bf16[384,768]{1,0:T(8,128)(2,1)} %refs_3_.1) | copy-start | bytes 1769476
  2.8 21.2 %collective-permute-start = (bf16[528,768]{1,0:T(8,128)(2,1)S(1)}, bf16[528,768]{1,0:T(8,128)(2,1)}, u32[]{:S(2)}, u32[]{:S(2)}) collective-permute-start(bf16[528,768]{1,0:T(8,128)(2,1)S(1)} %pad_maximum_fusion.4), channel_id=1, source_target_pairs={{0,1},{1,0},{2,3},{3,2},{4,5},{5,4},{6,7},{7,6},{8,9},{9,8},{10,11... | collective-permute-start | bytes 2433032 | tf_op jit(solution)/shard_map/ppermute | solution.py:1639
  24.0 13.4 %collective-permute-start.1 = (bf16[3,192,384]{2,1,0:T(8,128)(2,1)S(1)}, bf16[3,192,384]{2,1,0:T(8,128)(2,1)S(1)}, u32[]{:S(2)}, u32[]{:S(2)}) collective-permute-start(bf16[3,192,384]{2,1,0:T(8,128)(2,1)S(1)} %dynamic-slice_bitcast_fusion), channel_id=1, source_target_pairs={{0,1},{1,0},{2,3},{3,2},{4,5},{5,4},{6,7},{7,6},{8,9},{9,8},{10,11... | collective-permute-start | bytes 1327112 | tf_op jit(solution)/shard_map/ppermute | solution.py:1639
  25.7 26.9 %collective-permute-start.3 = (bf16[192,1536]{1,0:T(8,128)(2,1)S(1)}, bf16[192,1536]{1,0:T(8,128)(2,1)S(1)}, u32[]{:S(2)}, u32[]{:S(2)}) collective-permute-start(bf16[192,1536]{1,0:T(8,128)(2,1)S(1)} %constant_dynamic-slice_fusion.3), channel_id=1, source_target_pairs={{0,1},{1,0},{2,3},{3,2},{4,5},{5,4},{6,7},{7,6},{8,9},{9,8},{10,11... | collective-permute-start | bytes 1769480 | tf_op jit(solution)/shard_map/ppermute | solution.py:1639
  37.4 15.3 %collective-permute-start.2 = (bf16[3,192,384]{2,1,0:T(8,128)(2,1)S(1)}, bf16[3,192,384]{2,1,0:T(8,128)(2,1)S(1)}, u32[]{:S(2)}, u32[]{:S(2)}) collective-permute-start(bf16[3,192,384]{2,1,0:T(8,128)(2,1)S(1)} %collective-permute-done.1), channel_id=1, source_target_pairs={{0,4},{2,6},{4,0},{6,2},{8,12},{10,14},{12,8},{14,10},{16,20},{18,... | collective-permute-start | bytes 1327112 | tf_op jit(solution)/shard_map/ppermute | solution.py:1645
  52.6 0.8 copy-start.15
  53.4 8.2 %copy-start.4 = (bf16[192,768]{1,0:T(8,128)(2,1)S(1)}, bf16[192,768]{1,0:T(8,128)(2,1)}, u32[]{:S(2)}) copy-start(bf16[192,768]{1,0:T(8,128)(2,1)} %constant_dynamic-slice_fusion.1) | copy-start | bytes 884740
  53.6 10.2 %collective-permute-start.4 = (bf16[3,384,384]{2,1,0:T(8,128)(2,1)S(1)}, bf16[3,384,384]{2,1,0:T(8,128)(2,1)}, u32[]{:S(2)}, u32[]{:S(2)}) collective-permute-start(bf16[3,384,384]{2,1,0:T(8,128)(2,1)S(1)} %pad_maximum_fusion.3), channel_id=1, source_target_pairs={{0,2},{2,0},{4,6},{6,4},{8,10},{10,8},{12,14},{14,12},{16,18},{18,... | collective-permute-start | bytes 2654216 | tf_op jit(solution)/shard_map/ppermute | solution.py:1642
  53.7 40.9 %collective-permute-start.7 = (bf16[768,768]{1,0:T(8,128)(2,1)S(1)}, bf16[768,768]{1,0:T(8,128)(2,1)}, u32[]{:S(2)}, u32[]{:S(2)}) collective-permute-start(bf16[768,768]{1,0:T(8,128)(2,1)S(1)} %constant_dynamic-slice_fusion.2), channel_id=1, source_target_pairs={{0,1},{1,0},{2,3},{3,2},{4,5},{5,4},{6,7},{7,6},{8,9},{9,8},{10,11... | collective-permute-start | bytes 3538952 | tf_op jit(solution)/shard_map/ppermute | solution.py:1639
  61.7 33.0 %collective-permute-start.5 = (bf16[192,768]{1,0:T(8,128)(2,1)S(1)}, bf16[192,768]{1,0:T(8,128)(2,1)}, u32[]{:S(2)}, u32[]{:S(2)}) collective-permute-start(bf16[192,768]{1,0:T(8,128)(2,1)S(1)} %copy-done.4), channel_id=1, source_target_pairs={{0,1},{1,0},{2,3},{3,2},{4,5},{5,4},{6,7},{7,6},{8,9},{9,8},{10,11... | collective-permute-start | bytes 884744 | tf_op jit(solution)/shard_map/ppermute | solution.py:1639
  62.3 32.4 %collective-permute-start.6 = (bf16[192,1536]{1,0:T(8,128)(2,1)}, bf16[192,1536]{1,0:T(8,128)(2,1)}, u32[]{:S(2)}, u32[]{:S(2)}) collective-permute-start(bf16[192,1536]{1,0:T(8,128)(2,1)} %copy-done.15), channel_id=1, source_target_pairs={{0,4},{2,6},{4,0},{6,2},{8,12},{10,14},{12,8},{14,10},{16,20},{18,... | collective-permute-start | bytes 1769480 | tf_op jit(solution)/shard_map/ppermute | solution.py:1645
  74.1 20.6 %copy-start.12 = (bf16[1536]{0:T(1024)(128)(2,1)S(1)}, bf16[1536]{0:T(1024)(128)(2,1)}, u32[]{:S(2)}) copy-start(bf16[1536]{0:T(1024)(128)(2,1)} %param.25) | copy-start | bytes 9220
  94.7 1.8 collective-permute-start.8
  186.9 37.0 %collective-permute-start.10 = (bf16[12,16,768]{2,1,0:T(8,128)(2,1)}, bf16[12,16,768]{2,1,0:T(8,128)(2,1)S(1)}, u32[]{:S(2)}, u32[]{:S(2)}) collective-permute-start(bf16[12,16,768]{2,1,0:T(8,128)(2,1)} %get-tuple-element.113), channel_id=1, source_target_pairs={{0,8},{2,10},{4,12},{6,14},{8,0},{10,2},{12,4},{14,6},{16,24},{18,... | collective-permute-start | bytes 884744 | tf_op jit(solution)/shard_map/ppermute | solution.py:1704
  187.0 37.0 %collective-permute-start.11 = (bf16[12,16,768]{2,1,0:T(8,128)(2,1)}, bf16[12,16,768]{2,1,0:T(8,128)(2,1)S(1)}, u32[]{:S(2)}, u32[]{:S(2)}) collective-permute-start(bf16[12,16,768]{2,1,0:T(8,128)(2,1)} %get-tuple-element.113), channel_id=1, source_target_pairs={{0,16},{2,18},{4,20},{6,22},{8,24},{10,26},{12,28},{14,30},{16,0},... | collective-permute-start | bytes 884744 | tf_op jit(solution)/shard_map/ppermute | solution.py:1704
  189.6 34.3 %collective-permute-start.12 = (bf16[12,16,768]{2,1,0:T(8,128)(2,1)}, bf16[12,16,768]{2,1,0:T(8,128)(2,1)S(1)}, u32[]{:S(2)}, u32[]{:S(2)}) collective-permute-start(bf16[12,16,768]{2,1,0:T(8,128)(2,1)} %get-tuple-element.113), channel_id=1, source_target_pairs={{0,24},{2,26},{4,28},{6,30},{8,16},{10,18},{12,20},{14,22},{16,8},... | collective-permute-start | bytes 884744 | tf_op jit(solution)/shard_map/ppermute | solution.py:1704
  215.0 8.2 %copy-start.13 = (f32[7]{0:T(128)S(1)}, f32[7]{0:T(128)}, u32[]{:S(2)}) copy-start(f32[7]{0:T(128)} %pad.5.clone) | copy-start | bytes 88
  215.0 8.9 %copy-start.5 = (bf16[12,16,768]{2,1,0:T(8,128)(2,1)S(1)}, bf16[12,16,768]{2,1,0:T(8,128)(2,1)}, u32[]{:S(2)}) copy-start(bf16[12,16,768]{2,1,0:T(8,128)(2,1)} %get-tuple-element.113) | copy-start | bytes 884740
  216.4 8.1 %collective-permute-start.9 = (bf16[9,128,384]{2,1,0:T(8,128)(2,1)S(1)}, bf16[9,128,384]{2,1,0:T(8,128)(2,1)S(1)}, u32[]{:S(2)}, u32[]{:S(2)}) collective-permute-start(bf16[9,128,384]{2,1,0:T(8,128)(2,1)S(1)} %constant_dynamic-slice_fusion), channel_id=1, source_target_pairs={{0,2},{2,0},{4,6},{6,4},{8,10},{10,8},{12,14},{14,12},{16,18},{18,... | collective-permute-start | bytes 2654216 | tf_op jit(solution)/shard_map/ppermute | solution.py:1642
  216.4 39.7 %collective-permute-start.14 = (bf16[256,1152]{1,0:T(8,128)(2,1)}, bf16[256,1152]{1,0:T(8,128)(2,1)}, u32[]{:S(2)}, u32[]{:S(2)}) collective-permute-start(bf16[256,1152]{1,0:T(8,128)(2,1)} %get-tuple-element.118), channel_id=1, source_target_pairs={{0,1},{1,0},{2,3},{3,2},{4,5},{5,4},{6,7},{7,6},{8,9},{9,8},{10,11... | collective-permute-start | bytes 1769480 | tf_op jit(solution)/shard_map/ppermute | solution.py:1639
  224.3 1.5 copy-start.1
  226.1 28.3 %collective-permute-start.15 = (bf16[12,64,768]{2,1,0:T(8,128)(2,1)S(1)}, bf16[12,64,768]{2,1,0:T(8,128)(2,1)S(1)}, u32[]{:S(2)}, u32[]{:S(2)}) collective-permute-start(bf16[12,64,768]{2,1,0:T(8,128)(2,1)S(1)} %pad_maximum_fusion.2), channel_id=1, source_target_pairs={{0,4},{2,6},{4,0},{6,2},{8,12},{10,14},{12,8},{14,10},{16,20},{18,... | collective-permute-start | bytes 3538952 | tf_op jit(solution)/shard_map/ppermute | solution.py:1645
  228.0 28.4 %collective-permute-start.13 = (bf16[9,128,384]{2,1,0:T(8,128)(2,1)S(1)}, bf16[9,128,384]{2,1,0:T(8,128)(2,1)}, u32[]{:S(2)}, u32[]{:S(2)}) collective-permute-start(bf16[9,128,384]{2,1,0:T(8,128)(2,1)S(1)} %add_convert_fusion), channel_id=1, source_target_pairs={{0,1},{1,0},{2,3},{3,2},{4,5},{5,4},{6,7},{7,6},{8,9},{9,8},{10,11... | collective-permute-start | bytes 2654216 | tf_op jit(solution)/shard_map/ppermute | solution.py:1639
  256.2 64.4 %collective-permute-start.16 = (bf16[12,128,768]{2,1,0:T(8,128)(2,1)}, bf16[12,128,768]{2,1,0:T(8,128)(2,1)}, u32[]{:S(2)}, u32[]{:S(2)}) collective-permute-start(bf16[12,128,768]{2,1,0:T(8,128)(2,1)} %pad_maximum_fusion.down_mine.up_mine), channel_id=1, source_target_pairs={{0,2},{2,0},{4,6},{6,4},{8,10},{10,8},{12,14},{14,12},{16,18},{18,... | collective-permute-start | bytes 7077896 | tf_op jit(solution)/shard_map/ppermute | solution.py:1642
  313.3 5.3 %copy-start.2 = (bf16[3,768,384]{2,1,0:T(8,128)(2,1)S(1)}, bf16[3,768,384]{2,1,0:T(8,128)(2,1)}, u32[]{:S(2)}) copy-start(bf16[3,768,384]{2,1,0:T(8,128)(2,1)} %get-tuple-element.134) | copy-start | bytes 5308420
  320.6 7.1 %copy-start.3 = (bf16[1024,768]{1,0:T(8,128)(2,1)S(1)}, bf16[1024,768]{1,0:T(8,128)(2,1)}, u32[]{:S(2)}) copy-start(bf16[1024,768]{1,0:T(8,128)(2,1)} %get-tuple-element.107) | copy-start | bytes 4718596
  327.7 2.5 copy-start

commit v5 on v4

--- a/solution.py
+++ b/solution.py
@@ -1171,12 +1171,9 @@
         take_ref,
         swap_sem,
         norm_ref,
-        near_ref,
-        far_ref,
-        near_sem,
-        far_sem,
         *rest,
     ) = refs
+    early, late, rest = rest[:4], rest[4:8], rest[8:]
     place, part = lax.axis_index("dp"), lax.axis_index("mp")
     ex = exchange.bind(place, part, rest)
     count, bits = ex.count, ex.bits
@@ -1327,37 +1324,23 @@
             return 0
 
         lax.fori_loop(0, parts, own_sums, 0)
-        mine = near_ref.at[near_id]
-        mine[:lead, :] = small_ref[:lead, :]
-        mine[lead : lead + 2, :] = norm_ref[:2, :]
-        mine[lead + 2 : lead + 2 + bias, :] = small2_ref[:bias, :]
-        rest_rows = 16 - lead - 2 - bias
-        mine[16 - rest_rows :, :] = jnp.zeros((rest_rows, width), f32)
-        for j in range(1, 8):
-            near_copy(j).start()
-
-    def near_copy(j):
+        mine = late[0].at[near_id]
+        mine[...] = norm_ref[...]
+        start_near(late)
+
+    def near_copy(group, j, at):
+        near_ref, _, near_sem, _ = group
         return pltpu.make_async_remote_copy(
-            src_ref=near_ref.at[near_id],
-            dst_ref=near_ref.at[near_id],
+            src_ref=near_ref.at[at],
+            dst_ref=near_ref.at[at],
             send_sem=near_sem.at[j, 0],
             recv_sem=near_sem.at[j, 1],
             device_id=near[j - 1],
             device_id_type=MESH,
         )
 
-    def near_got(j):
-        came = (part + j // 4) % 2 * 4 + flip(place % 4, j % 4)
-        return pltpu.make_async_remote_copy(
-            src_ref=near_ref.at[came],
-            dst_ref=near_ref.at[came],
-            send_sem=near_sem.at[j, 0],
-            recv_sem=near_sem.at[j, 1],
-            device_id=near[j - 1],
-            device_id_type=MESH,
-        )
-
-    def far_copy(j, at):
+    def far_copy(group, j, at):
+        _, far_ref, _, far_sem = group
         return pltpu.make_async_remote_copy(
             src_ref=far_ref.at[at],
             dst_ref=far_ref.at[at],
@@ -1367,49 +1350,31 @@
             device_id_type=MESH,
         )
 
-    def tell_far():
+    def start_near(group):
         for j in range(1, 8):
-            near_copy(j).wait_send()
-            near_got(j).wait_recv()
-        total = near_ref[0]
+            near_copy(group, j, near_id).start()
+
+    def near_sum(group, places):
+        total = group[0][places[0]]
+        for at in places[1:]:
+            total = total + group[0][at]
+        return total
+
+    def wait_near(group):
         for j in range(1, 8):
-            total = total + near_ref[j]
-        plane = near_ref[part * 4]
-        other = near_ref[(1 - part) * 4]
+            near_copy(group, j, near_id).wait_send()
+            came = (part + j // 4) % 2 * 4 + flip(place % 4, j % 4)
+            near_copy(group, j, came).wait_recv()
+
+    def start_far(group):
         for j in range(1, 4):
-            plane = plane + near_ref[part * 4 + j]
-            other = other + near_ref[(1 - part) * 4 + j]
-        spot = far_ref.at[ex.z]
-        spot[...] = total
-        spot[:bias, :] = plane[:bias] + other[lead + 2 : lead + 2 + bias]
+            far_copy(group, j, ex.z).start()
+
+    def far_sum(group):
+        far_ref, far_sem = group[1], group[3]
         for j in range(1, 4):
-            far_copy(j, ex.z).start()
-
-    def take_back():
-        loads[5].wait()
-        swap(main, 0).wait()
-        swap(edges, 1).wait()
-        clean = slice(CLEAN_OWN, CLEAN_OWN + HALF)
-        rows_ref[clean, :] += take_ref[main, :].astype(f32)
-        begin = slice(CLEAN_OWN, CLEAN_OWN + EDGE)
-        rows_ref[begin, :] += take_ref[HALF : HALF + EDGE, :].astype(f32)
-        edge = pl.ds(pl.multiple_of(NOISY_OWN + (1 - part) * (HALF - EDGE), EDGE), EDGE)
-        rows_ref[edge, :] += take_ref[HALF + EDGE :, :].astype(f32)
-
-    def norm_back(b):
-        rows = tokens_at(b)
-        unit, scale = normal(tokens_ref[rows, :].astype(f32))
-        lean = rows_ref[own_at(b), :] * vectors_ref[0:1, :]
-        back_ref[rows, :] = dmid_ref[rows, :] + scale * (
-            lean
-            - jnp.mean(lean, axis=-1, keepdims=True)
-            - unit * jnp.mean(lean * unit, axis=-1, keepdims=True)
-        )
-
-    def end_far():
-        for j in range(1, 4):
-            far_copy(j, ex.z).wait_send()
-            far_copy(j, flip(ex.z, j)).wait_recv()
+            far_copy(group, j, ex.z).wait_send()
+            far_copy(group, j, flip(ex.z, j)).wait_recv()
         total = far_ref[0]
         for j in range(1, 4):
             total = total + far_ref[j]
@@ -1426,16 +1391,73 @@
             trade.start()
             trade.wait()
             total = total + far_ref[5 + 2 * i]
-        sums_ref[...] = total
+        return total
+
+    def early_near():
+        mine = early[0].at[near_id]
+        mine[:lead, :] = small_ref[:lead, :]
+        mine[lead : lead + bias, :] = small2_ref[:bias, :]
+        mine[lead + bias :, :] = jnp.zeros((16 - lead - bias, width), f32)
+        start_near(early)
+
+    def early_far():
+        wait_near(early)
+        spot = early[1].at[ex.z]
+        spot[...] = near_sum(early, range(8))
+        plane = near_sum(early, [part * 4 + j for j in range(4)])
+        other = near_sum(early, [(1 - part) * 4 + j for j in range(4)])
+        spot[:bias, :] = plane[:bias] + other[lead : lead + bias]
+        start_far(early)
+
+    def early_end():
+        sums_ref[...] = far_sum(early)
+
+    def late_far():
+        wait_near(late)
+        late[1][ex.z] = near_sum(late, range(8))
+        start_far(late)
+
+    def late_end():
+        sums_ref[lead : lead + 2, :] = far_sum(late)[:2]
+
+    def take_back():
+        loads[5].wait()
+        swap(main, 0).wait()
+        swap(edges, 1).wait()
+        clean = slice(CLEAN_OWN, CLEAN_OWN + HALF)
+        rows_ref[clean, :] += take_ref[main, :].astype(f32)
+        begin = slice(CLEAN_OWN, CLEAN_OWN + EDGE)
+        rows_ref[begin, :] += take_ref[HALF : HALF + EDGE, :].astype(f32)
+        edge = pl.ds(pl.multiple_of(NOISY_OWN + (1 - part) * (HALF - EDGE), EDGE), EDGE)
+        rows_ref[edge, :] += take_ref[HALF + EDGE :, :].astype(f32)
+
+    def norm_back(b):
+        rows = tokens_at(b)
+        unit, scale = normal(tokens_ref[rows, :].astype(f32))
+        lean = rows_ref[own_at(b), :] * vectors_ref[0:1, :]
+        back_ref[rows, :] = dmid_ref[rows, :] + scale * (
+            lean
+            - jnp.mean(lean, axis=-1, keepdims=True)
+            - unit * jnp.mean(lean * unit, axis=-1, keepdims=True)
+        )
+
+    def middle_step():
+        take_back()
+        early_far()
+
+    def last_step():
+        late_far()
+        early_end()
 
     groups = count // split - 1
     actions = {
+        0: early_near,
         groups + 1: give_edges,
         groups + 2: tell_near,
-        groups + 3: tell_far,
-        groups + 4: take_back,
+        groups + 3: middle_step,
+        groups + 6: last_step,
     }
-    begin_back = groups + 5
+    begin_back = groups + 4
 
     def phase(p, _):
         @pl.when(p < groups)
@@ -1456,7 +1478,7 @@
         def _():
             lax.fori_loop(block, block + 2, lambda b, _: (norm_back(b), 0)[1], 0)
 
-        pl.when(block == parts)(end_far)
+        pl.when(block == parts)(late_end)
         steps(p)
         return 0
 
@@ -1496,10 +1518,16 @@
             pltpu.VMEM((HALF + 2 * EDGE, width), bf16),
             pltpu.SemaphoreType.DMA((2, 2)),
             pltpu.VMEM((8, width), f32),
-            pltpu.VMEM((8, 16, width), f32),
-            pltpu.VMEM((4 + 2 * len(exchange.extra), 16, width), f32),
-            pltpu.SemaphoreType.DMA((8, 2)),
-            pltpu.SemaphoreType.DMA((4 + len(exchange.extra), 2)),
+        ]
+        + [
+            spec
+            for depth in (16, 8)
+            for spec in (
+                pltpu.VMEM((8, depth, width), f32),
+                pltpu.VMEM((4 + 2 * len(exchange.extra), depth, width), f32),
+                pltpu.SemaphoreType.DMA((8, 2)),
+                pltpu.SemaphoreType.DMA((4 + len(exchange.extra), 2)),
+            )
         ]
         + exchange.scratch(),
         compiler_params=pltpu.CompilerParams(

time: 330 us -> 336 us (1.018)
  waiting for transfers between devices: 19.8 us -> 23.5 us
    pallas_call x1, Pallas kernels: 56.8 us -> 62.6 us  [leave(): pl.pallas_call(functools.partial(leave_kernel, exchange), in_specs=[hbm]...]
  transfers between devices with their start and end apart: 17 -> 17, of which waited for: 5 -> 5; matrix products, arithmetic and copies ran while one was open for 9% -> 9% of each run, Pallas kernels for 43% -> 44%
where the time goes in v5:
time: 336 us; the launch traced here: 335 us
  Pallas kernels  241 us (72%)
  starting transfers between devices  29.6 us (9%)
  waiting for transfers between devices  23.5 us (7%)
  other arithmetic  20.4 us (6%)
  local copies, waits for them, and re-layouts  19.6 us (6%)
    pallas_call x1, Pallas kernels, middle(): pl.pallas_call(functools.partial(middle_kernel, exchanges, tiles), in_spe...  87.2 us
    pallas_call x1, Pallas kernels, leave(): pl.pallas_call(functools.partial(leave_kernel, exchange), in_specs=[hbm]...  62.6 us
    pallas_call x2, Pallas kernels, attend_backward(): pl.pallas_call(functools.partial(backward_kernel, giving), in_specs=[pl.B...  39.9 us
    pallas_call x2, Pallas kernels, attend_forward(): pl.pallas_call(forward_kernel, in_specs=[pl.BlockSpec(memory_space=pltpu....  25 us
    ppermute x7, starting transfers between devices, across(): return lax.ppermute(array, 'mp', [(0, 1), (1, 0)])  20.4 us
    ppermute x7, waiting for transfers between devices, across(): return lax.ppermute(array, 'mp', [(0, 1), (1, 0)])  14.6 us
    pallas_call x1, Pallas kernels, enter(): pl.pallas_call(enter_kernel, in_specs=[vmem] * 6, out_specs=[vmem] * 5, o...  11.4 us
    ppermute x3, waiting for transfers between devices, beside(): return lax.ppermute(array, 'dp', [(i, i ^ 2) for i in range(dp_size)])  8.31 us
  transfers between devices with their start and end apart: 17, of which 5 were waited for; matrix products, arithmetic and copies ran while one was open for 9% of the time, Pallas kernels for 44%

profile of v5, /device:TPU:0, one launch (start us, length us, event | category | flops | bytes accessed | tf_op | source)
XLA Modules:
  0.0 335.5 jit_solution(12338338870163572606)
XLA Ops:
  0.7 1.2 slice_bitcast_fusion
  1.9 0.8 select_bitcast_fusion
  2.8 3.0 collective-permute-start
  5.8 0.2 reduce-window.8
  6.9 0.3 fusion.16
  7.3 0.2 reduce_min.21
  7.7 0.7 pad_add_fusion.1.span_ref
  8.3 0.6 add_add_fusion.clean_ref
  8.9 0.6 pad_add_fusion.noisy_ref
  9.5 1.1 dynamic-slice_bitcast_fusion
  10.6 1.4 constant_dynamic-slice_fusion.2
  12.0 0.7 constant_dynamic-slice_fusion.1
  12.7 0.6 stack.29.vectors_ref.refs_6_.refs_11_
  13.3 1.1 constant_dynamic-slice_fusion.3
  14.5 4.4 %fusion = (f32[1584,128]{1,0:T(8,128)}, f32[1584,128]{1,0:T(8,128)}) fusion(f32[128]{0:T(128)S(1)} %get-tuple-element.179, f32[128]{0:T(128)S(1)} %get-tuple-element.180, f32[1584]{0:T(1024)S(1)} %get-tuple-element.173), kind=kLoop, calls=%fused_computation.12 | loop fusion | flops 405504 | bytes 1629376 | tf_op jit(solution)/shard_map/mul | solution.py:1629
  18.8 5.1 %collective-permute-done.context_ref.refs_9_ = bf16[528,768]{1,0:T(8,128)(2,1)} collective-permute-done((bf16[528,768]{1,0:T(8,128)(2,1)S(1)}, bf16[528,768]{1,0:T(8,128)(2,1)}, u32[]{:S(2)}, u32[]{:S(2)}) %collective-permute-start) | collective-permute-done | bytes 811040 | tf_op jit(solution)/shard_map/ppermute | solution.py:1667
  24.0 1.7 collective-permute-start.1
  25.7 0.3 collective-permute-start.3
  26.0 11.4 %enter.1 = (bf16[1584,768]{1,0:T(8,128)(2,1)}, bf16[768,1584]{1,0:T(8,128)(2,1)}, bf16[1584,384]{1,0:T(8,128)(2,1)}, bf16[1584,384]{1,0:T(8,128)(2,1)}, bf16[1584,384]{1,0:T(8,128)(2,1)}) custom-call(bf16[2,512,768]{2,1,0:T(8,128)(2,1)} %tokens_ref.1, bf16[528,768]{1,0:T(8,128)(2,1)} %collective-permute-done.context_ref.refs_9_, ...), custom_call_target="tpu_custom_call" | custom-call | flops 10000000000 | bytes 16000000 | tf_op jit(solution)/shard_map/enter/pallas_call | solution.py:157
  37.4 1.7 collective-permute-start.2
  39.1 12.5 %attend_forward.2 = (bf16[1024,384]{1,0:T(8,128)(2,1)}, f32[3,4,2,256]{3,2,1,0:T(2,128)}) custom-call(s32[4,2]{1,0:T(4,128)} %pad_add_fusion.1.span_ref, s32[4,2,256]{2,1,0:T(2,128)} %add_add_fusion.clean_ref, s32[4,2,128]{2,1,0:T(2,128)} %pad_add_fusion.noisy_ref, bf16[1584,384]{1,0:T(8,128)(2,1)} %get-tuple-element.87.q_ref, ...), custom_call_target="tpu_custom_call" | custom-call | flops 1610612736 | bytes 4866048 | tf_op jit(solution)/shard_map/attend_forward/pallas_call | solution.py:290
  51.6 0.8 copy-done.15
  52.6 1.3 collective-permute-start.4
  53.9 7.8 %collective-permute-start.7 = (bf16[768,768]{1,0:T(8,128)(2,1)S(1)}, bf16[768,768]{1,0:T(8,128)(2,1)}, u32[]{:S(2)}, u32[]{:S(2)}) collective-permute-start(bf16[768,768]{1,0:T(8,128)(2,1)S(1)} %constant_dynamic-slice_fusion.2), channel_id=1, source_target_pairs={{0,1},{1,0},{2,3},{3,2},{4,5},{5,4},{6,7},{7,6},{8,9},{9,8},{10,11... | collective-permute-start | bytes 3538952 | tf_op jit(solution)/shard_map/ppermute | solution.py:1667
  61.7 0.6 collective-permute-start.5
  62.3 0.5 collective-permute-start.6
  62.8 1.5 broadcast_select_fusion.3
  64.3 1.4 pad_maximum_fusion.1.w_ref.refs_2_.refs_7_
  65.7 7.3 %project.1 = (bf16[1584,384]{1,0:T(8,128)(2,1)}, bf16[1584,384]{1,0:T(8,128)(2,1)}, bf16[1584,384]{1,0:T(8,128)(2,1)}) custom-call(bf16[1584,768]{1,0:T(8,128)(2,1)} %get-tuple-element.91.rows_ref, bf16[3,768,384]{2,1,0:T(8,128)(2,1)} %pad_maximum_fusion.1.w_ref.refs_2_.refs_7_, f32[1584,128]{1,0:T(8,128)} %get-tuple-element.82.cos_ref, ...), custom_call_target="tpu_custom_call" | custom-call | flops 2802843648 | bytes 7852032 | tf_op jit(solution)/shard_map/project/pallas_call | solution.py:78
  73.0 12.5 %attend_forward.3 = (bf16[1024,384]{1,0:T(8,128)(2,1)}, f32[3,4,2,256]{3,2,1,0:T(2,128)}) custom-call(s32[4,2]{1,0:T(4,128)} %pad_add_fusion.1.span_ref, s32[4,2,256]{2,1,0:T(2,128)} %add_add_fusion.clean_ref, s32[4,2,128]{2,1,0:T(2,128)} %pad_add_fusion.noisy_ref, bf16[1584,384]{1,0:T(8,128)(2,1)} %get-tuple-element.96.q_ref, ...), custom_call_target="tpu_custom_call" | custom-call | flops 1610612736 | bytes 4866048 | tf_op jit(solution)/shard_map/attend_forward/pallas_call | solution.py:290
  85.6 9.1 %collective-permute-done.5 = bf16[192,768]{1,0:T(8,128)(2,1)} collective-permute-done((bf16[192,768]{1,0:T(8,128)(2,1)S(1)}, bf16[192,768]{1,0:T(8,128)(2,1)}, u32[]{:S(2)}, u32[]{:S(2)}) %collective-permute-start.5) | collective-permute-done | bytes 294944 | tf_op jit(solution)/shard_map/ppermute | solution.py:1667
  94.7 0.6 reshape.337.refs_7_
  95.3 0.6 pad.5.clone
  95.9 0.6 collective-permute-done.8
  96.4 1.0 broadcast_select_fusion.13
  97.5 0.9 pad_maximum_fusion.5.refs_4_
  98.3 87.2 %middle.1 = (bf16[1024,768]{1,0:T(8,128)(2,1)}, f32[1024,768]{1,0:T(8,128)}, bf16[1024,384]{1,0:T(8,128)(2,1)}, bf16[1024,384]{1,0:T(8,128)(2,1)}, bf16[256,1152...) custom-call(bf16[1024,768]{1,0:T(8,128)(2,1)} %bitcast.32, ...), custom_call_target="tpu_custom_call" | custom-call | flops 60000002048 | bytes 40000000 | tf_op jit(solution)/shard_map/middle/pallas_call | solution.py:1088
  185.6 1.2 collective-permute-start.11
  186.8 3.2 collective-permute-start.12
  190.0 0.7 slice_reduce_fusion
  190.8 0.7 slice.53
  191.5 21.3 %attend_backward.2 = (bf16[3,1584,384]{2,1,0:T(8,128)(2,1)}, bf16[3,768,384]{2,1,0:T(8,128)(2,1)}) custom-call(s32[4,2]{1,0:T(4,128)} %pad_add_fusion.1.span_ref, s32[4,2,256]{2,1,0:T(2,128)} %add_add_fusion.clean_ref, s32[4,2,128]{2,1,0:T(2,128)} %pad_add_fusion.noisy_ref, bf16[1584,384]{1,0:T(8,128)(2,1)} %get-tuple-element.96.q_ref, ...), custom_call_target="tpu_custom_call" | custom-call | flops 35999997952 | bytes 36000000 | tf_op jit(solution)/shard_map/attend_backward/pallas_call | solution.py:502
  212.8 1.3 constant_dynamic-slice_fusion
  214.2 6.9 %collective-permute-start.14 = (bf16[256,1152]{1,0:T(8,128)(2,1)}, bf16[256,1152]{1,0:T(8,128)(2,1)}, u32[]{:S(2)}, u32[]{:S(2)}) collective-permute-start(bf16[256,1152]{1,0:T(8,128)(2,1)} %get-tuple-element.118), channel_id=1, source_target_pairs={{0,1},{1,0},{2,3},{3,2},{4,5},{5,4},{6,7},{7,6},{8,9},{9,8},{10,11... | collective-permute-start | bytes 1769480 | tf_op jit(solution)/shard_map/ppermute | solution.py:1667
  221.1 0.7 fusion.4
  221.9 0.3 broadcast_select_fusion.5
  222.3 1.4 copy-done.1
  223.7 0.3 add_convert_fusion
  223.9 1.2 collective-permute-start.15
  225.1 18.6 %attend_backward.3 = (bf16[3,1584,384]{2,1,0:T(8,128)(2,1)}, f32[512,768]{1,0:T(8,128)}) custom-call(s32[4,2]{1,0:T(4,128)} %pad_add_fusion.1.span_ref, s32[4,2,256]{2,1,0:T(2,128)} %add_add_fusion.clean_ref, s32[4,2,128]{2,1,0:T(2,128)} %pad_add_fusion.noisy_ref, bf16[1584,384]{1,0:T(8,128)(2,1)} %get-tuple-element.87.q_ref, ...), custom_call_target="tpu_custom_call" | custom-call | flops 35999997952 | bytes 36000000 | tf_op jit(solution)/shard_map/attend_backward/pallas_call | solution.py:502
  243.7 8.3 %collective-permute-done.15 = bf16[12,64,768]{2,1,0:T(8,128)(2,1)S(1)} collective-permute-done((bf16[12,64,768]{2,1,0:T(8,128)(2,1)S(1)}, bf16[12,64,768]{2,1,0:T(8,128)(2,1)S(1)}, u32[]{:S(2)}, u32[]{:S(2)}) %collective-permute-start.15) | collective-permute-done | bytes 1179680 | tf_op jit(solution)/shard_map/ppermute | solution.py:1673
  252.0 0.2 broadcast_select_fusion.1
  252.2 1.7 pad_maximum_fusion.down_mine.up_mine
  253.9 0.4 collective-permute-done.13.refs_2_
  254.3 62.6 %leave.1 = (bf16[3,768,384]{2,1,0:T(8,128)(2,1)}, bf16[384,768]{1,0:T(8,128)(2,1)}, f32[1024,768]{1,0:T(8,128)}, f32[16,768]{1,0:T(8,128)}) custom-call(bf16[768,1584]{1,0:T(8,128)(2,1)} %get-tuple-element.108.refs_0_, bf16[256,1152]{1,0:T(8,128)(2,1)} %get-tuple-element.109.refs_1_, bf16[9,128,384]{2,1,0:T(8,128)(2,1)} %collective-permute-done.13.refs_2_, ...), custom_call_target="tpu_custom_call" | custom-call | flops 40000000000 | bytes 40000000 | tf_op jit(solution)/shard_map/leave/pallas_call | solution.py:1496
  316.9 2.3 convert_element_type.40
  319.2 0.7 slice.58
  320.0 0.6 reshape.335
  320.6 1.6 slice_reduce_fusion.2
  322.2 2.0 convert_bitcast_fusion
  324.2 7.1 %assemble.1 = (f32[1536,768]{1,0:T(8,128)}, f32[768,1536]{1,0:T(8,128)}) custom-call(s32[1]{0:T(128)} %bitcast.19.core_ref, bf16[12,128,768]{2,1,0:T(8,128)(2,1)} %pad_maximum_fusion.down_mine.up_mine, bf16[12,128,768]{2,1,0:T(8,128)(2,1)} %pad_maximum_fusion.down_mine.up_mine, bf16[12,128,768]{2,1,0:T(8,128)(2,1)} %collective-permute-done.16.down_got.up_got, ...), custom_call_target="tpu_custom_call" | custom-call | flops 1000000 | bytes 14000000 | tf_op jit(solution)/shard_map/assemble/pallas_call | solution.py:1568
  331.3 1.1 copy.39
  332.5 1.3 copy-done
  333.8 1.7 copy.40
  (71 shorter events, 1.3 us)
Async XLA Ops:
  0.6 5.2 %copy-start.14 = (s32[1,4]{1,0:T(1,128)S(1)}, s32[1,4]{1,0:T(1,128)}, u32[]{:S(2)}) copy-start(s32[1,4]{1,0:T(1,128)} %param.15) | copy-start | bytes 52
  0.7 6.9 %copy-start.7 = (f32[768]{0:T(1024)S(1)}, f32[768]{0:T(1024)}, u32[]{:S(2)}) copy-start(f32[768]{0:T(1024)} %param.18) | copy-start | bytes 9220
  0.7 6.9 %copy-start.8 = (f32[768]{0:T(1024)S(1)}, f32[768]{0:T(1024)}, u32[]{:S(2)}) copy-start(f32[768]{0:T(1024)} %param.19) | copy-start | bytes 9220
  0.7 6.9 %copy-start.9 = (f32[768]{0:T(1024)S(1)}, f32[768]{0:T(1024)}, u32[]{:S(2)}) copy-start(f32[768]{0:T(1024)} %param.22) | copy-start | bytes 9220
  0.7 6.9 %copy-start.10 = (f32[768]{0:T(1024)S(1)}, f32[768]{0:T(1024)}, u32[]{:S(2)}) copy-start(f32[768]{0:T(1024)} %param.23) | copy-start | bytes 9220
  0.7 6.9 %copy-start.11 = (f32[768]{0:T(1024)S(1)}, f32[768]{0:T(1024)}, u32[]{:S(2)}) copy-start(f32[768]{0:T(1024)} %param.27) | copy-start | bytes 9220
  2.8 9.2 %copy-start.6 = (bf16[384,768]{1,0:T(8,128)(2,1)S(1)}, bf16[384,768]{1,0:T(8,128)(2,1)}, u32[]{:S(2)}) copy-start(bf16[384,768]{1,0:T(8,128)(2,1)} %refs_3_.1) | copy-start | bytes 1769476
  2.8 21.2 %collective-permute-start = (bf16[528,768]{1,0:T(8,128)(2,1)S(1)}, bf16[528,768]{1,0:T(8,128)(2,1)}, u32[]{:S(2)}, u32[]{:S(2)}) collective-permute-start(bf16[528,768]{1,0:T(8,128)(2,1)S(1)} %pad_maximum_fusion.4), channel_id=1, source_target_pairs={{0,1},{1,0},{2,3},{3,2},{4,5},{5,4},{6,7},{7,6},{8,9},{9,8},{10,11... | collective-permute-start | bytes 2433032 | tf_op jit(solution)/shard_map/ppermute | solution.py:1667
  24.0 13.4 %collective-permute-start.1 = (bf16[3,192,384]{2,1,0:T(8,128)(2,1)S(1)}, bf16[3,192,384]{2,1,0:T(8,128)(2,1)S(1)}, u32[]{:S(2)}, u32[]{:S(2)}) collective-permute-start(bf16[3,192,384]{2,1,0:T(8,128)(2,1)S(1)} %dynamic-slice_bitcast_fusion), channel_id=1, source_target_pairs={{0,1},{1,0},{2,3},{3,2},{4,5},{5,4},{6,7},{7,6},{8,9},{9,8},{10,11... | collective-permute-start | bytes 1327112 | tf_op jit(solution)/shard_map/ppermute | solution.py:1667
  25.7 25.9 %collective-permute-start.3 = (bf16[192,1536]{1,0:T(8,128)(2,1)S(1)}, bf16[192,1536]{1,0:T(8,128)(2,1)S(1)}, u32[]{:S(2)}, u32[]{:S(2)}) collective-permute-start(bf16[192,1536]{1,0:T(8,128)(2,1)S(1)} %constant_dynamic-slice_fusion.3), channel_id=1, source_target_pairs={{0,1},{1,0},{2,3},{3,2},{4,5},{5,4},{6,7},{7,6},{8,9},{9,8},{10,11... | collective-permute-start | bytes 1769480 | tf_op jit(solution)/shard_map/ppermute | solution.py:1667
  37.4 14.2 %collective-permute-start.2 = (bf16[3,192,384]{2,1,0:T(8,128)(2,1)S(1)}, bf16[3,192,384]{2,1,0:T(8,128)(2,1)S(1)}, u32[]{:S(2)}, u32[]{:S(2)}) collective-permute-start(bf16[3,192,384]{2,1,0:T(8,128)(2,1)S(1)} %collective-permute-done.1), channel_id=1, source_target_pairs={{0,4},{2,6},{4,0},{6,2},{8,12},{10,14},{12,8},{14,10},{16,20},{18,... | collective-permute-start | bytes 1327112 | tf_op jit(solution)/shard_map/ppermute | solution.py:1673
  51.6 0.8 copy-start.15
  52.4 9.3 %copy-start.4 = (bf16[192,768]{1,0:T(8,128)(2,1)S(1)}, bf16[192,768]{1,0:T(8,128)(2,1)}, u32[]{:S(2)}) copy-start(bf16[192,768]{1,0:T(8,128)(2,1)} %constant_dynamic-slice_fusion.1) | copy-start | bytes 884740
  52.6 10.2 %collective-permute-start.4 = (bf16[3,384,384]{2,1,0:T(8,128)(2,1)S(1)}, bf16[3,384,384]{2,1,0:T(8,128)(2,1)}, u32[]{:S(2)}, u32[]{:S(2)}) collective-permute-start(bf16[3,384,384]{2,1,0:T(8,128)(2,1)S(1)} %pad_maximum_fusion.3), channel_id=1, source_target_pairs={{0,2},{2,0},{4,6},{6,4},{8,10},{10,8},{12,14},{14,12},{16,18},{18,... | collective-permute-start | bytes 2654216 | tf_op jit(solution)/shard_map/ppermute | solution.py:1670
  53.9 40.7 %collective-permute-start.7 = (bf16[768,768]{1,0:T(8,128)(2,1)S(1)}, bf16[768,768]{1,0:T(8,128)(2,1)}, u32[]{:S(2)}, u32[]{:S(2)}) collective-permute-start(bf16[768,768]{1,0:T(8,128)(2,1)S(1)} %constant_dynamic-slice_fusion.2), channel_id=1, source_target_pairs={{0,1},{1,0},{2,3},{3,2},{4,5},{5,4},{6,7},{7,6},{8,9},{9,8},{10,11... | collective-permute-start | bytes 3538952 | tf_op jit(solution)/shard_map/ppermute | solution.py:1667
  61.7 33.0 %collective-permute-start.5 = (bf16[192,768]{1,0:T(8,128)(2,1)S(1)}, bf16[192,768]{1,0:T(8,128)(2,1)}, u32[]{:S(2)}, u32[]{:S(2)}) collective-permute-start(bf16[192,768]{1,0:T(8,128)(2,1)S(1)} %copy-done.4), channel_id=1, source_target_pairs={{0,1},{1,0},{2,3},{3,2},{4,5},{5,4},{6,7},{7,6},{8,9},{9,8},{10,11... | collective-permute-start | bytes 884744 | tf_op jit(solution)/shard_map/ppermute | solution.py:1667
  62.3 32.4 %collective-permute-start.6 = (bf16[192,1536]{1,0:T(8,128)(2,1)}, bf16[192,1536]{1,0:T(8,128)(2,1)}, u32[]{:S(2)}, u32[]{:S(2)}) collective-permute-start(bf16[192,1536]{1,0:T(8,128)(2,1)} %copy-done.15), channel_id=1, source_target_pairs={{0,4},{2,6},{4,0},{6,2},{8,12},{10,14},{12,8},{14,10},{16,20},{18,... | collective-permute-start | bytes 1769480 | tf_op jit(solution)/shard_map/ppermute | solution.py:1673
  73.0 21.6 %copy-start.12 = (bf16[1536]{0:T(1024)(128)(2,1)S(1)}, bf16[1536]{0:T(1024)(128)(2,1)}, u32[]{:S(2)}) copy-start(bf16[1536]{0:T(1024)(128)(2,1)} %param.25) | copy-start | bytes 9220
  94.7 1.8 collective-permute-start.8
  185.5 36.3 %collective-permute-start.10 = (bf16[12,16,768]{2,1,0:T(8,128)(2,1)}, bf16[12,16,768]{2,1,0:T(8,128)(2,1)S(1)}, u32[]{:S(2)}, u32[]{:S(2)}) collective-permute-start(bf16[12,16,768]{2,1,0:T(8,128)(2,1)} %get-tuple-element.113), channel_id=1, source_target_pairs={{0,8},{2,10},{4,12},{6,14},{8,0},{10,2},{12,4},{14,6},{16,24},{18,... | collective-permute-start | bytes 884744 | tf_op jit(solution)/shard_map/ppermute | solution.py:1732
  185.6 36.2 %collective-permute-start.11 = (bf16[12,16,768]{2,1,0:T(8,128)(2,1)}, bf16[12,16,768]{2,1,0:T(8,128)(2,1)S(1)}, u32[]{:S(2)}, u32[]{:S(2)}) collective-permute-start(bf16[12,16,768]{2,1,0:T(8,128)(2,1)} %get-tuple-element.113), channel_id=1, source_target_pairs={{0,16},{2,18},{4,20},{6,22},{8,24},{10,26},{12,28},{14,30},{16,0},... | collective-permute-start | bytes 884744 | tf_op jit(solution)/shard_map/ppermute | solution.py:1732
  186.8 35.0 %collective-permute-start.12 = (bf16[12,16,768]{2,1,0:T(8,128)(2,1)}, bf16[12,16,768]{2,1,0:T(8,128)(2,1)S(1)}, u32[]{:S(2)}, u32[]{:S(2)}) collective-permute-start(bf16[12,16,768]{2,1,0:T(8,128)(2,1)} %get-tuple-element.113), channel_id=1, source_target_pairs={{0,24},{2,26},{4,28},{6,30},{8,16},{10,18},{12,20},{14,22},{16,8},... | collective-permute-start | bytes 884744 | tf_op jit(solution)/shard_map/ppermute | solution.py:1732
  212.8 8.3 %copy-start.13 = (f32[7]{0:T(128)S(1)}, f32[7]{0:T(128)}, u32[]{:S(2)}) copy-start(f32[7]{0:T(128)} %pad.5.clone) | copy-start | bytes 88
  212.8 9.0 %copy-start.5 = (bf16[12,16,768]{2,1,0:T(8,128)(2,1)S(1)}, bf16[12,16,768]{2,1,0:T(8,128)(2,1)}, u32[]{:S(2)}) copy-start(bf16[12,16,768]{2,1,0:T(8,128)(2,1)} %get-tuple-element.113) | copy-start | bytes 884740
  214.1 8.2 %collective-permute-start.9 = (bf16[9,128,384]{2,1,0:T(8,128)(2,1)S(1)}, bf16[9,128,384]{2,1,0:T(8,128)(2,1)S(1)}, u32[]{:S(2)}, u32[]{:S(2)}) collective-permute-start(bf16[9,128,384]{2,1,0:T(8,128)(2,1)S(1)} %constant_dynamic-slice_fusion), channel_id=1, source_target_pairs={{0,2},{2,0},{4,6},{6,4},{8,10},{10,8},{12,14},{14,12},{16,18},{18,... | collective-permute-start | bytes 2654216 | tf_op jit(solution)/shard_map/ppermute | solution.py:1670
  214.2 39.7 %collective-permute-start.14 = (bf16[256,1152]{1,0:T(8,128)(2,1)}, bf16[256,1152]{1,0:T(8,128)(2,1)}, u32[]{:S(2)}, u32[]{:S(2)}) collective-permute-start(bf16[256,1152]{1,0:T(8,128)(2,1)} %get-tuple-element.118), channel_id=1, source_target_pairs={{0,1},{1,0},{2,3},{3,2},{4,5},{5,4},{6,7},{7,6},{8,9},{9,8},{10,11... | collective-permute-start | bytes 1769480 | tf_op jit(solution)/shard_map/ppermute | solution.py:1667
  222.2 1.5 copy-start.1
  223.9 28.1 %collective-permute-start.15 = (bf16[12,64,768]{2,1,0:T(8,128)(2,1)S(1)}, bf16[12,64,768]{2,1,0:T(8,128)(2,1)S(1)}, u32[]{:S(2)}, u32[]{:S(2)}) collective-permute-start(bf16[12,64,768]{2,1,0:T(8,128)(2,1)S(1)} %pad_maximum_fusion.2), channel_id=1, source_target_pairs={{0,4},{2,6},{4,0},{6,2},{8,12},{10,14},{12,8},{14,10},{16,20},{18,... | collective-permute-start | bytes 3538952 | tf_op jit(solution)/shard_map/ppermute | solution.py:1673
  225.1 29.2 %collective-permute-start.13 = (bf16[9,128,384]{2,1,0:T(8,128)(2,1)S(1)}, bf16[9,128,384]{2,1,0:T(8,128)(2,1)}, u32[]{:S(2)}, u32[]{:S(2)}) collective-permute-start(bf16[9,128,384]{2,1,0:T(8,128)(2,1)S(1)} %add_convert_fusion), channel_id=1, source_target_pairs={{0,1},{1,0},{2,3},{3,2},{4,5},{5,4},{6,7},{7,6},{8,9},{9,8},{10,11... | collective-permute-start | bytes 2654216 | tf_op jit(solution)/shard_map/ppermute | solution.py:1667
  253.9 70.4 %collective-permute-start.16 = (bf16[12,128,768]{2,1,0:T(8,128)(2,1)}, bf16[12,128,768]{2,1,0:T(8,128)(2,1)}, u32[]{:S(2)}, u32[]{:S(2)}) collective-permute-start(bf16[12,128,768]{2,1,0:T(8,128)(2,1)} %pad_maximum_fusion.down_mine.up_mine), channel_id=1, source_target_pairs={{0,2},{2,0},{4,6},{6,4},{8,10},{10,8},{12,14},{14,12},{16,18},{18,... | collective-permute-start | bytes 7077896 | tf_op jit(solution)/shard_map/ppermute | solution.py:1670
  316.9 5.3 %copy-start.2 = (bf16[3,768,384]{2,1,0:T(8,128)(2,1)S(1)}, bf16[3,768,384]{2,1,0:T(8,128)(2,1)}, u32[]{:S(2)}) copy-start(bf16[3,768,384]{2,1,0:T(8,128)(2,1)} %get-tuple-element.134) | copy-start | bytes 5308420
  324.2 7.1 %copy-start.3 = (bf16[1024,768]{1,0:T(8,128)(2,1)S(1)}, bf16[1024,768]{1,0:T(8,128)(2,1)}, u32[]{:S(2)}) copy-start(bf16[1024,768]{1,0:T(8,128)(2,1)} %get-tuple-element.107) | copy-start | bytes 4718596
  331.3 2.5 copy-start

commit v6 on v4

--- a/solution.py
+++ b/solution.py
@@ -1327,12 +1327,10 @@
             return 0
 
         lax.fori_loop(0, parts, own_sums, 0)
-        mine = near_ref.at[near_id]
-        mine[:lead, :] = small_ref[:lead, :]
-        mine[lead : lead + 2, :] = norm_ref[:2, :]
-        mine[lead + 2 : lead + 2 + bias, :] = small2_ref[:bias, :]
-        rest_rows = 16 - lead - 2 - bias
-        mine[16 - rest_rows :, :] = jnp.zeros((rest_rows, width), f32)
+        blank = jnp.zeros((16 - lead - 2 - bias, width), f32)
+        near_ref[near_id] = jnp.concatenate(
+            [small_ref[:lead, :], norm_ref[:2, :], small2_ref[:bias, :], blank], axis=0
+        ).astype(bf16)
         for j in range(1, 8):
             near_copy(j).start()
 
@@ -1371,17 +1369,13 @@
         for j in range(1, 8):
             near_copy(j).wait_send()
             near_got(j).wait_recv()
-        total = near_ref[0]
-        for j in range(1, 8):
-            total = total + near_ref[j]
-        plane = near_ref[part * 4]
-        other = near_ref[(1 - part) * 4]
-        for j in range(1, 4):
-            plane = plane + near_ref[part * 4 + j]
-            other = other + near_ref[(1 - part) * 4 + j]
-        spot = far_ref.at[ex.z]
-        spot[...] = total
-        spot[:bias, :] = plane[:bias] + other[lead + 2 : lead + 2 + bias]
+        near_sum = lambda at: sum(near_ref[at + j].astype(f32) for j in range(1, 4)) + near_ref[
+            at
+        ].astype(f32)
+        plane, other = near_sum(part * 4), near_sum((1 - part) * 4)
+        total = near_sum(0) + near_sum(4)
+        mixed = plane[:bias] + other[lead + 2 : lead + 2 + bias]
+        far_ref[ex.z] = jnp.concatenate([mixed, total[bias:]], axis=0).astype(bf16)
         for j in range(1, 4):
             far_copy(j, ex.z).start()
 
@@ -1410,11 +1404,12 @@
         for j in range(1, 4):
             far_copy(j, ex.z).wait_send()
             far_copy(j, flip(ex.z, j)).wait_recv()
-        total = far_ref[0]
+        total = far_ref[0].astype(f32)
         for j in range(1, 4):
-            total = total + far_ref[j]
+            total = total + far_ref[j].astype(f32)
         for i, b in enumerate(ex.extra):
-            far_ref[4 + 2 * i] = total
+            total = total.astype(bf16).astype(f32)
+            far_ref[4 + 2 * i] = total.astype(bf16)
             trade = pltpu.make_async_remote_copy(
                 src_ref=far_ref.at[4 + 2 * i],
                 dst_ref=far_ref.at[5 + 2 * i],
@@ -1425,17 +1420,17 @@
             )
             trade.start()
             trade.wait()
-            total = total + far_ref[5 + 2 * i]
+            total = total + far_ref[5 + 2 * i].astype(f32)
         sums_ref[...] = total
 
     groups = count // split - 1
     actions = {
         groups + 1: give_edges,
         groups + 2: tell_near,
-        groups + 3: tell_far,
-        groups + 4: take_back,
+        groups + 3: take_back,
+        groups + 6: tell_far,
     }
-    begin_back = groups + 5
+    begin_back = groups + 4
 
     def phase(p, _):
         @pl.when(p < groups)
@@ -1496,8 +1491,8 @@
             pltpu.VMEM((HALF + 2 * EDGE, width), bf16),
             pltpu.SemaphoreType.DMA((2, 2)),
             pltpu.VMEM((8, width), f32),
-            pltpu.VMEM((8, 16, width), f32),
-            pltpu.VMEM((4 + 2 * len(exchange.extra), 16, width), f32),
+            pltpu.VMEM((8, 16, width), bf16),
+            pltpu.VMEM((4 + 2 * len(exchange.extra), 16, width), bf16),
             pltpu.SemaphoreType.DMA((8, 2)),
             pltpu.SemaphoreType.DMA((4 + len(exchange.extra), 2)),
         ]

time: 330 us -> 333 us (level); the launches traced: 332 us -> 331 us
    pallas_call x1, Pallas kernels: 88.6 us -> 83.8 us  [middle(): pl.pallas_call(functools.partial(middle_kernel, exchanges, tiles), in_spe...]
  transfers between devices with their start and end apart: 17 -> 17, of which waited for: 5 -> 5; matrix products, arithmetic and copies ran while one was open for 9% -> 9% of each run, Pallas kernels for 43% -> 45%
where the time goes in v6:
time: 333 us; the launch traced here: 331 us
  Pallas kernels  239 us (72%)
  starting transfers between devices  31.2 us (9%)
  other arithmetic  20.4 us (6%)
  local copies, waits for them, and re-layouts  19.6 us (6%)
  waiting for transfers between devices  19 us (6%)
    pallas_call x1, Pallas kernels, middle(): pl.pallas_call(functools.partial(middle_kernel, exchanges, tiles), in_spe...  83.8 us
    pallas_call x1, Pallas kernels, leave(): pl.pallas_call(functools.partial(leave_kernel, exchange), in_specs=[hbm]...  56.4 us
    pallas_call x2, Pallas kernels, attend_backward(): pl.pallas_call(functools.partial(backward_kernel, giving), in_specs=[pl.B...  43.5 us
    pallas_call x2, Pallas kernels, attend_forward(): pl.pallas_call(forward_kernel, in_specs=[pl.BlockSpec(memory_space=pltpu....  29.3 us
    ppermute x7, starting transfers between devices, across(): return lax.ppermute(array, 'mp', [(0, 1), (1, 0)])  22.7 us
    ppermute x7, waiting for transfers between devices, across(): return lax.ppermute(array, 'mp', [(0, 1), (1, 0)])  12.5 us
    pallas_call x1, Pallas kernels, enter(): pl.pallas_call(enter_kernel, in_specs=[vmem] * 6, out_specs=[vmem] * 5, o...  11.4 us
    pallas_call x1, Pallas kernels, project(): pl.pallas_call(project_kernel, grid=(3,), in_specs=[row_spec, pl.BlockSpe...  7.35 us
  transfers between devices with their start and end apart: 17, of which 5 were waited for; matrix products, arithmetic and copies ran while one was open for 9% of the time, Pallas kernels for 45%

profile of v6, /device:TPU:0, one launch (start us, length us, event | category | flops | bytes accessed | tf_op | source)
XLA Modules:
  0.0 330.8 jit_solution(2223638118269653949)
XLA Ops:
  0.7 1.2 slice_bitcast_fusion
  1.9 0.8 select_bitcast_fusion
  2.8 3.0 collective-permute-start
  5.8 0.2 reduce-window.8
  6.8 0.1 subtract_convert_fusion
  6.9 0.3 fusion.16
  7.3 0.2 reduce_min.21
  7.7 0.7 pad_add_fusion.1.span_ref
  8.3 0.6 add_add_fusion.clean_ref
  8.9 0.6 pad_add_fusion.noisy_ref
  9.5 1.1 dynamic-slice_bitcast_fusion
  10.6 1.4 constant_dynamic-slice_fusion.2
  12.0 0.7 constant_dynamic-slice_fusion.1
  12.7 0.6 stack.29.vectors_ref.refs_6_.refs_11_
  13.3 1.1 constant_dynamic-slice_fusion.3
  14.5 4.4 %fusion = (f32[1584,128]{1,0:T(8,128)}, f32[1584,128]{1,0:T(8,128)}) fusion(f32[128]{0:T(128)S(1)} %get-tuple-element.179, f32[128]{0:T(128)S(1)} %get-tuple-element.180, f32[1584]{0:T(1024)S(1)} %get-tuple-element.173), kind=kLoop, calls=%fused_computation.12 | loop fusion | flops 405504 | bytes 1629376 | tf_op jit(solution)/shard_map/mul | solution.py:1596
  18.8 5.1 %collective-permute-done.context_ref.refs_9_ = bf16[528,768]{1,0:T(8,128)(2,1)} collective-permute-done((bf16[528,768]{1,0:T(8,128)(2,1)S(1)}, bf16[528,768]{1,0:T(8,128)(2,1)}, u32[]{:S(2)}, u32[]{:S(2)}) %collective-permute-start) | collective-permute-done | bytes 811040 | tf_op jit(solution)/shard_map/ppermute | solution.py:1634
  24.0 1.7 collective-permute-start.1
  25.7 0.3 collective-permute-start.3
  26.0 11.4 %enter.1 = (bf16[1584,768]{1,0:T(8,128)(2,1)}, bf16[768,1584]{1,0:T(8,128)(2,1)}, bf16[1584,384]{1,0:T(8,128)(2,1)}, bf16[1584,384]{1,0:T(8,128)(2,1)}, bf16[1584,384]{1,0:T(8,128)(2,1)}) custom-call(bf16[2,512,768]{2,1,0:T(8,128)(2,1)} %tokens_ref.1, bf16[528,768]{1,0:T(8,128)(2,1)} %collective-permute-done.context_ref.refs_9_, ...), custom_call_target="tpu_custom_call" | custom-call | flops 10000000000 | bytes 16000000 | tf_op jit(solution)/shard_map/enter/pallas_call | solution.py:157
  37.4 1.7 collective-permute-start.2
  39.1 14.6 %attend_forward.2 = (bf16[1024,384]{1,0:T(8,128)(2,1)}, f32[3,4,2,256]{3,2,1,0:T(2,128)}) custom-call(s32[4,2]{1,0:T(4,128)} %pad_add_fusion.1.span_ref, s32[4,2,256]{2,1,0:T(2,128)} %add_add_fusion.clean_ref, s32[4,2,128]{2,1,0:T(2,128)} %pad_add_fusion.noisy_ref, bf16[1584,384]{1,0:T(8,128)(2,1)} %get-tuple-element.87.q_ref, ...), custom_call_target="tpu_custom_call" | custom-call | flops 1610612736 | bytes 4866048 | tf_op jit(solution)/shard_map/attend_forward/pallas_call | solution.py:290
  53.7 0.8 copy-done.15
  54.8 9.0 %collective-permute-start.7 = (bf16[768,768]{1,0:T(8,128)(2,1)S(1)}, bf16[768,768]{1,0:T(8,128)(2,1)}, u32[]{:S(2)}, u32[]{:S(2)}) collective-permute-start(bf16[768,768]{1,0:T(8,128)(2,1)S(1)} %constant_dynamic-slice_fusion.2), channel_id=1, source_target_pairs={{0,1},{1,0},{2,3},{3,2},{4,5},{5,4},{6,7},{7,6},{8,9},{9,8},{10,11... | collective-permute-start | bytes 3538952 | tf_op jit(solution)/shard_map/ppermute | solution.py:1634
  63.8 0.6 collective-permute-start.5
  64.4 0.5 collective-permute-start.6
  64.9 1.5 broadcast_select_fusion.3
  66.4 1.4 pad_maximum_fusion.1.w_ref.refs_2_.refs_7_
  67.8 7.3 %project.1 = (bf16[1584,384]{1,0:T(8,128)(2,1)}, bf16[1584,384]{1,0:T(8,128)(2,1)}, bf16[1584,384]{1,0:T(8,128)(2,1)}) custom-call(bf16[1584,768]{1,0:T(8,128)(2,1)} %get-tuple-element.91.rows_ref, bf16[3,768,384]{2,1,0:T(8,128)(2,1)} %pad_maximum_fusion.1.w_ref.refs_2_.refs_7_, f32[1584,128]{1,0:T(8,128)} %get-tuple-element.82.cos_ref, ...), custom_call_target="tpu_custom_call" | custom-call | flops 2802843648 | bytes 7852032 | tf_op jit(solution)/shard_map/project/pallas_call | solution.py:78
  75.2 14.6 %attend_forward.3 = (bf16[1024,384]{1,0:T(8,128)(2,1)}, f32[3,4,2,256]{3,2,1,0:T(2,128)}) custom-call(s32[4,2]{1,0:T(4,128)} %pad_add_fusion.1.span_ref, s32[4,2,256]{2,1,0:T(2,128)} %add_add_fusion.clean_ref, s32[4,2,128]{2,1,0:T(2,128)} %pad_add_fusion.noisy_ref, bf16[1584,384]{1,0:T(8,128)(2,1)} %get-tuple-element.96.q_ref, ...), custom_call_target="tpu_custom_call" | custom-call | flops 1610612736 | bytes 4866048 | tf_op jit(solution)/shard_map/attend_forward/pallas_call | solution.py:290
  89.8 7.0 %collective-permute-done.5 = bf16[192,768]{1,0:T(8,128)(2,1)} collective-permute-done((bf16[192,768]{1,0:T(8,128)(2,1)S(1)}, bf16[192,768]{1,0:T(8,128)(2,1)}, u32[]{:S(2)}, u32[]{:S(2)}) %collective-permute-start.5) | collective-permute-done | bytes 294944 | tf_op jit(solution)/shard_map/ppermute | solution.py:1634
  96.8 0.6 reshape.337.refs_7_
  97.4 0.6 pad.5.clone
  98.0 0.6 collective-permute-done.8
  98.6 1.0 broadcast_select_fusion.13
  99.6 0.9 pad_maximum_fusion.5.refs_4_
  100.4 83.8 %middle.1 = (bf16[1024,768]{1,0:T(8,128)(2,1)}, f32[1024,768]{1,0:T(8,128)}, bf16[1024,384]{1,0:T(8,128)(2,1)}, bf16[1024,384]{1,0:T(8,128)(2,1)}, bf16[256,1152...) custom-call(bf16[1024,768]{1,0:T(8,128)(2,1)} %bitcast.32, ...), custom_call_target="tpu_custom_call" | custom-call | flops 60000002048 | bytes 40000000 | tf_op jit(solution)/shard_map/middle/pallas_call | solution.py:1088
  184.3 2.3 collective-permute-start.11
  186.6 2.1 collective-permute-start.12
  188.7 0.7 slice_reduce_fusion
  189.4 0.7 slice.53
  190.2 23.1 %attend_backward.2 = (bf16[3,1584,384]{2,1,0:T(8,128)(2,1)}, bf16[3,768,384]{2,1,0:T(8,128)(2,1)}) custom-call(s32[4,2]{1,0:T(4,128)} %pad_add_fusion.1.span_ref, s32[4,2,256]{2,1,0:T(2,128)} %add_add_fusion.clean_ref, s32[4,2,128]{2,1,0:T(2,128)} %pad_add_fusion.noisy_ref, bf16[1584,384]{1,0:T(8,128)(2,1)} %get-tuple-element.96.q_ref, ...), custom_call_target="tpu_custom_call" | custom-call | flops 35999997952 | bytes 36000000 | tf_op jit(solution)/shard_map/attend_backward/pallas_call | solution.py:502
  213.3 1.3 constant_dynamic-slice_fusion
  214.7 8.0 %collective-permute-start.14 = (bf16[256,1152]{1,0:T(8,128)(2,1)}, bf16[256,1152]{1,0:T(8,128)(2,1)}, u32[]{:S(2)}, u32[]{:S(2)}) collective-permute-start(bf16[256,1152]{1,0:T(8,128)(2,1)} %get-tuple-element.118), channel_id=1, source_target_pairs={{0,1},{1,0},{2,3},{3,2},{4,5},{5,4},{6,7},{7,6},{8,9},{9,8},{10,11... | collective-permute-start | bytes 1769480 | tf_op jit(solution)/shard_map/ppermute | solution.py:1634
  222.7 0.7 fusion.4
  223.5 0.3 broadcast_select_fusion.5
  223.9 1.4 copy-done.1
  225.3 0.3 add_convert_fusion
  225.5 1.8 collective-permute-start.15
  227.3 20.4 %attend_backward.3 = (bf16[3,1584,384]{2,1,0:T(8,128)(2,1)}, f32[512,768]{1,0:T(8,128)}) custom-call(s32[4,2]{1,0:T(4,128)} %pad_add_fusion.1.span_ref, s32[4,2,256]{2,1,0:T(2,128)} %add_add_fusion.clean_ref, s32[4,2,128]{2,1,0:T(2,128)} %pad_add_fusion.noisy_ref, bf16[1584,384]{1,0:T(8,128)(2,1)} %get-tuple-element.87.q_ref, ...), custom_call_target="tpu_custom_call" | custom-call | flops 35999997952 | bytes 36000000 | tf_op jit(solution)/shard_map/attend_backward/pallas_call | solution.py:502
  247.7 5.9 %collective-permute-done.15 = bf16[12,64,768]{2,1,0:T(8,128)(2,1)S(1)} collective-permute-done((bf16[12,64,768]{2,1,0:T(8,128)(2,1)S(1)}, bf16[12,64,768]{2,1,0:T(8,128)(2,1)S(1)}, u32[]{:S(2)}, u32[]{:S(2)}) %collective-permute-start.15) | collective-permute-done | bytes 1179680 | tf_op jit(solution)/shard_map/ppermute | solution.py:1640
  253.6 0.2 broadcast_select_fusion.1
  253.8 1.7 pad_maximum_fusion.down_mine.up_mine
  255.4 0.4 collective-permute-done.13.refs_2_
  255.9 56.4 %leave.1 = (bf16[3,768,384]{2,1,0:T(8,128)(2,1)}, bf16[384,768]{1,0:T(8,128)(2,1)}, f32[1024,768]{1,0:T(8,128)}, f32[16,768]{1,0:T(8,128)}) custom-call(bf16[768,1584]{1,0:T(8,128)(2,1)} %get-tuple-element.108.refs_0_, bf16[256,1152]{1,0:T(8,128)(2,1)} %get-tuple-element.109.refs_1_, bf16[9,128,384]{2,1,0:T(8,128)(2,1)} %collective-permute-done.13.refs_2_, ...), custom_call_target="tpu_custom_call" | custom-call | flops 40000000000 | bytes 40000000 | tf_op jit(solution)/shard_map/leave/pallas_call | solution.py:1469
  312.3 2.3 convert_element_type.40
  314.6 0.7 slice.58
  315.3 0.6 reshape.335
  315.9 1.6 slice_reduce_fusion.2
  317.6 2.0 convert_bitcast_fusion
  319.6 7.1 %assemble.1 = (f32[1536,768]{1,0:T(8,128)}, f32[768,1536]{1,0:T(8,128)}) custom-call(s32[1]{0:T(128)} %bitcast.19.core_ref, bf16[12,128,768]{2,1,0:T(8,128)(2,1)} %pad_maximum_fusion.down_mine.up_mine, bf16[12,128,768]{2,1,0:T(8,128)(2,1)} %pad_maximum_fusion.down_mine.up_mine, bf16[12,128,768]{2,1,0:T(8,128)(2,1)} %collective-permute-done.16.down_got.up_got, ...), custom_call_target="tpu_custom_call" | custom-call | flops 1000000 | bytes 14000000 | tf_op jit(solution)/shard_map/assemble/pallas_call | solution.py:1535
  326.7 1.1 copy.39
  327.8 1.3 copy-done
  329.1 1.7 copy.40
  (71 shorter events, 1.2 us)
Async XLA Ops:
  0.6 5.2 %copy-start.14 = (s32[1,4]{1,0:T(1,128)S(1)}, s32[1,4]{1,0:T(1,128)}, u32[]{:S(2)}) copy-start(s32[1,4]{1,0:T(1,128)} %param.15) | copy-start | bytes 52
  0.7 6.9 %copy-start.7 = (f32[768]{0:T(1024)S(1)}, f32[768]{0:T(1024)}, u32[]{:S(2)}) copy-start(f32[768]{0:T(1024)} %param.18) | copy-start | bytes 9220
  0.7 6.9 %copy-start.8 = (f32[768]{0:T(1024)S(1)}, f32[768]{0:T(1024)}, u32[]{:S(2)}) copy-start(f32[768]{0:T(1024)} %param.19) | copy-start | bytes 9220
  0.7 6.9 %copy-start.9 = (f32[768]{0:T(1024)S(1)}, f32[768]{0:T(1024)}, u32[]{:S(2)}) copy-start(f32[768]{0:T(1024)} %param.22) | copy-start | bytes 9220
  0.7 6.9 %copy-start.10 = (f32[768]{0:T(1024)S(1)}, f32[768]{0:T(1024)}, u32[]{:S(2)}) copy-start(f32[768]{0:T(1024)} %param.23) | copy-start | bytes 9220
  0.7 6.9 %copy-start.11 = (f32[768]{0:T(1024)S(1)}, f32[768]{0:T(1024)}, u32[]{:S(2)}) copy-start(f32[768]{0:T(1024)} %param.27) | copy-start | bytes 9220
  2.8 9.2 %copy-start.6 = (bf16[384,768]{1,0:T(8,128)(2,1)S(1)}, bf16[384,768]{1,0:T(8,128)(2,1)}, u32[]{:S(2)}) copy-start(bf16[384,768]{1,0:T(8,128)(2,1)} %refs_3_.1) | copy-start | bytes 1769476
  2.8 21.2 %collective-permute-start = (bf16[528,768]{1,0:T(8,128)(2,1)S(1)}, bf16[528,768]{1,0:T(8,128)(2,1)}, u32[]{:S(2)}, u32[]{:S(2)}) collective-permute-start(bf16[528,768]{1,0:T(8,128)(2,1)S(1)} %pad_maximum_fusion.4), channel_id=1, source_target_pairs={{0,1},{1,0},{2,3},{3,2},{4,5},{5,4},{6,7},{7,6},{8,9},{9,8},{10,11... | collective-permute-start | bytes 2433032 | tf_op jit(solution)/shard_map/ppermute | solution.py:1634
  24.0 13.4 %collective-permute-start.1 = (bf16[3,192,384]{2,1,0:T(8,128)(2,1)S(1)}, bf16[3,192,384]{2,1,0:T(8,128)(2,1)S(1)}, u32[]{:S(2)}, u32[]{:S(2)}) collective-permute-start(bf16[3,192,384]{2,1,0:T(8,128)(2,1)S(1)} %dynamic-slice_bitcast_fusion), channel_id=1, source_target_pairs={{0,1},{1,0},{2,3},{3,2},{4,5},{5,4},{6,7},{7,6},{8,9},{9,8},{10,11... | collective-permute-start | bytes 1327112 | tf_op jit(solution)/shard_map/ppermute | solution.py:1634
  25.7 28.0 %collective-permute-start.3 = (bf16[192,1536]{1,0:T(8,128)(2,1)S(1)}, bf16[192,1536]{1,0:T(8,128)(2,1)S(1)}, u32[]{:S(2)}, u32[]{:S(2)}) collective-permute-start(bf16[192,1536]{1,0:T(8,128)(2,1)S(1)} %constant_dynamic-slice_fusion.3), channel_id=1, source_target_pairs={{0,1},{1,0},{2,3},{3,2},{4,5},{5,4},{6,7},{7,6},{8,9},{9,8},{10,11... | collective-permute-start | bytes 1769480 | tf_op jit(solution)/shard_map/ppermute | solution.py:1634
  37.4 16.3 %collective-permute-start.2 = (bf16[3,192,384]{2,1,0:T(8,128)(2,1)S(1)}, bf16[3,192,384]{2,1,0:T(8,128)(2,1)S(1)}, u32[]{:S(2)}, u32[]{:S(2)}) collective-permute-start(bf16[3,192,384]{2,1,0:T(8,128)(2,1)S(1)} %collective-permute-done.1), channel_id=1, source_target_pairs={{0,4},{2,6},{4,0},{6,2},{8,12},{10,14},{12,8},{14,10},{16,20},{18,... | collective-permute-start | bytes 1327112 | tf_op jit(solution)/shard_map/ppermute | solution.py:1640
  53.7 0.8 copy-start.15
  54.5 9.3 %copy-start.4 = (bf16[192,768]{1,0:T(8,128)(2,1)S(1)}, bf16[192,768]{1,0:T(8,128)(2,1)}, u32[]{:S(2)}) copy-start(bf16[192,768]{1,0:T(8,128)(2,1)} %constant_dynamic-slice_fusion.1) | copy-start | bytes 884740
  54.7 10.2 %collective-permute-start.4 = (bf16[3,384,384]{2,1,0:T(8,128)(2,1)S(1)}, bf16[3,384,384]{2,1,0:T(8,128)(2,1)}, u32[]{:S(2)}, u32[]{:S(2)}) collective-permute-start(bf16[3,384,384]{2,1,0:T(8,128)(2,1)S(1)} %pad_maximum_fusion.3), channel_id=1, source_target_pairs={{0,2},{2,0},{4,6},{6,4},{8,10},{10,8},{12,14},{14,12},{16,18},{18,... | collective-permute-start | bytes 2654216 | tf_op jit(solution)/shard_map/ppermute | solution.py:1637
  54.8 42.0 %collective-permute-start.7 = (bf16[768,768]{1,0:T(8,128)(2,1)S(1)}, bf16[768,768]{1,0:T(8,128)(2,1)}, u32[]{:S(2)}, u32[]{:S(2)}) collective-permute-start(bf16[768,768]{1,0:T(8,128)(2,1)S(1)} %constant_dynamic-slice_fusion.2), channel_id=1, source_target_pairs={{0,1},{1,0},{2,3},{3,2},{4,5},{5,4},{6,7},{7,6},{8,9},{9,8},{10,11... | collective-permute-start | bytes 3538952 | tf_op jit(solution)/shard_map/ppermute | solution.py:1634
  63.8 33.0 %collective-permute-start.5 = (bf16[192,768]{1,0:T(8,128)(2,1)S(1)}, bf16[192,768]{1,0:T(8,128)(2,1)}, u32[]{:S(2)}, u32[]{:S(2)}) collective-permute-start(bf16[192,768]{1,0:T(8,128)(2,1)S(1)} %copy-done.4), channel_id=1, source_target_pairs={{0,1},{1,0},{2,3},{3,2},{4,5},{5,4},{6,7},{7,6},{8,9},{9,8},{10,11... | collective-permute-start | bytes 884744 | tf_op jit(solution)/shard_map/ppermute | solution.py:1634
  64.4 32.4 %collective-permute-start.6 = (bf16[192,1536]{1,0:T(8,128)(2,1)}, bf16[192,1536]{1,0:T(8,128)(2,1)}, u32[]{:S(2)}, u32[]{:S(2)}) collective-permute-start(bf16[192,1536]{1,0:T(8,128)(2,1)} %copy-done.15), channel_id=1, source_target_pairs={{0,4},{2,6},{4,0},{6,2},{8,12},{10,14},{12,8},{14,10},{16,20},{18,... | collective-permute-start | bytes 1769480 | tf_op jit(solution)/shard_map/ppermute | solution.py:1640
  75.2 21.6 %copy-start.12 = (bf16[1536]{0:T(1024)(128)(2,1)S(1)}, bf16[1536]{0:T(1024)(128)(2,1)}, u32[]{:S(2)}) copy-start(bf16[1536]{0:T(1024)(128)(2,1)} %param.25) | copy-start | bytes 9220
  96.8 1.8 collective-permute-start.8
  184.2 39.2 %collective-permute-start.10 = (bf16[12,16,768]{2,1,0:T(8,128)(2,1)}, bf16[12,16,768]{2,1,0:T(8,128)(2,1)S(1)}, u32[]{:S(2)}, u32[]{:S(2)}) collective-permute-start(bf16[12,16,768]{2,1,0:T(8,128)(2,1)} %get-tuple-element.113), channel_id=1, source_target_pairs={{0,8},{2,10},{4,12},{6,14},{8,0},{10,2},{12,4},{14,6},{16,24},{18,... | collective-permute-start | bytes 884744 | tf_op jit(solution)/shard_map/ppermute | solution.py:1699
  184.3 39.1 %collective-permute-start.11 = (bf16[12,16,768]{2,1,0:T(8,128)(2,1)}, bf16[12,16,768]{2,1,0:T(8,128)(2,1)S(1)}, u32[]{:S(2)}, u32[]{:S(2)}) collective-permute-start(bf16[12,16,768]{2,1,0:T(8,128)(2,1)} %get-tuple-element.113), channel_id=1, source_target_pairs={{0,16},{2,18},{4,20},{6,22},{8,24},{10,26},{12,28},{14,30},{16,0},... | collective-permute-start | bytes 884744 | tf_op jit(solution)/shard_map/ppermute | solution.py:1699
  186.6 36.8 %collective-permute-start.12 = (bf16[12,16,768]{2,1,0:T(8,128)(2,1)}, bf16[12,16,768]{2,1,0:T(8,128)(2,1)S(1)}, u32[]{:S(2)}, u32[]{:S(2)}) collective-permute-start(bf16[12,16,768]{2,1,0:T(8,128)(2,1)} %get-tuple-element.113), channel_id=1, source_target_pairs={{0,24},{2,26},{4,28},{6,30},{8,16},{10,18},{12,20},{14,22},{16,8},... | collective-permute-start | bytes 884744 | tf_op jit(solution)/shard_map/ppermute | solution.py:1699
  213.3 9.4 %copy-start.13 = (f32[7]{0:T(128)S(1)}, f32[7]{0:T(128)}, u32[]{:S(2)}) copy-start(f32[7]{0:T(128)} %pad.5.clone) | copy-start | bytes 88
  213.3 10.1 %copy-start.5 = (bf16[12,16,768]{2,1,0:T(8,128)(2,1)S(1)}, bf16[12,16,768]{2,1,0:T(8,128)(2,1)}, u32[]{:S(2)}) copy-start(bf16[12,16,768]{2,1,0:T(8,128)(2,1)} %get-tuple-element.113) | copy-start | bytes 884740
  214.6 9.3 %collective-permute-start.9 = (bf16[9,128,384]{2,1,0:T(8,128)(2,1)S(1)}, bf16[9,128,384]{2,1,0:T(8,128)(2,1)S(1)}, u32[]{:S(2)}, u32[]{:S(2)}) collective-permute-start(bf16[9,128,384]{2,1,0:T(8,128)(2,1)S(1)} %constant_dynamic-slice_fusion), channel_id=1, source_target_pairs={{0,2},{2,0},{4,6},{6,4},{8,10},{10,8},{12,14},{14,12},{16,18},{18,... | collective-permute-start | bytes 2654216 | tf_op jit(solution)/shard_map/ppermute | solution.py:1637
  214.7 40.7 %collective-permute-start.14 = (bf16[256,1152]{1,0:T(8,128)(2,1)}, bf16[256,1152]{1,0:T(8,128)(2,1)}, u32[]{:S(2)}, u32[]{:S(2)}) collective-permute-start(bf16[256,1152]{1,0:T(8,128)(2,1)} %get-tuple-element.118), channel_id=1, source_target_pairs={{0,1},{1,0},{2,3},{3,2},{4,5},{5,4},{6,7},{7,6},{8,9},{9,8},{10,11... | collective-permute-start | bytes 1769480 | tf_op jit(solution)/shard_map/ppermute | solution.py:1634
  223.8 1.5 copy-start.1
  225.5 28.1 %collective-permute-start.15 = (bf16[12,64,768]{2,1,0:T(8,128)(2,1)S(1)}, bf16[12,64,768]{2,1,0:T(8,128)(2,1)S(1)}, u32[]{:S(2)}, u32[]{:S(2)}) collective-permute-start(bf16[12,64,768]{2,1,0:T(8,128)(2,1)S(1)} %pad_maximum_fusion.2), channel_id=1, source_target_pairs={{0,4},{2,6},{4,0},{6,2},{8,12},{10,14},{12,8},{14,10},{16,20},{18,... | collective-permute-start | bytes 3538952 | tf_op jit(solution)/shard_map/ppermute | solution.py:1640
  227.3 28.6 %collective-permute-start.13 = (bf16[9,128,384]{2,1,0:T(8,128)(2,1)S(1)}, bf16[9,128,384]{2,1,0:T(8,128)(2,1)}, u32[]{:S(2)}, u32[]{:S(2)}) collective-permute-start(bf16[9,128,384]{2,1,0:T(8,128)(2,1)S(1)} %add_convert_fusion), channel_id=1, source_target_pairs={{0,1},{1,0},{2,3},{3,2},{4,5},{5,4},{6,7},{7,6},{8,9},{9,8},{10,11... | collective-permute-start | bytes 2654216 | tf_op jit(solution)/shard_map/ppermute | solution.py:1634
  255.4 64.1 %collective-permute-start.16 = (bf16[12,128,768]{2,1,0:T(8,128)(2,1)}, bf16[12,128,768]{2,1,0:T(8,128)(2,1)}, u32[]{:S(2)}, u32[]{:S(2)}) collective-permute-start(bf16[12,128,768]{2,1,0:T(8,128)(2,1)} %pad_maximum_fusion.down_mine.up_mine), channel_id=1, source_target_pairs={{0,2},{2,0},{4,6},{6,4},{8,10},{10,8},{12,14},{14,12},{16,18},{18,... | collective-permute-start | bytes 7077896 | tf_op jit(solution)/shard_map/ppermute | solution.py:1637
  312.3 5.3 %copy-start.2 = (bf16[3,768,384]{2,1,0:T(8,128)(2,1)S(1)}, bf16[3,768,384]{2,1,0:T(8,128)(2,1)}, u32[]{:S(2)}) copy-start(bf16[3,768,384]{2,1,0:T(8,128)(2,1)} %get-tuple-element.134) | copy-start | bytes 5308420
  319.6 7.1 %copy-start.3 = (bf16[1024,768]{1,0:T(8,128)(2,1)S(1)}, bf16[1024,768]{1,0:T(8,128)(2,1)}, u32[]{:S(2)}) copy-start(bf16[1024,768]{1,0:T(8,128)(2,1)} %get-tuple-element.107) | copy-start | bytes 4718596
  326.7 2.5 copy-start

commit v7 on v6

--- a/solution.py
+++ b/solution.py
@@ -322,7 +322,7 @@
     *refs,
 ):
     if giving:
-        d2_hbm, w_hbm, w2_hbm, out_ref, give_ref, *refs = refs
+        d2_hbm, w_hbm, w2_hbm, out_ref, give_ref, low_ref, *refs = refs
         dk_ref, dv_ref, bias_ref, d2_ref, w_ref, w2_ref, load_sem = refs
         loads = [(w_hbm, w_ref), (w2_hbm, w2_ref)]
         loads += [(d2_hbm.at[c, :HALF], d2_ref.at[c]) for c in range(3)]
@@ -464,6 +464,7 @@
         for c in range(3):
             total = total + dot(out_ref[c, :HALF, :], w_ref[c], NT) + dot(d2_ref[c], w2_ref[c], NT)
         give_ref[...] = total
+        low_ref[...] = total.astype(bf16)
     else:
         lax.fori_loop(0, rows_ref.shape[0] // ROW_TILE, weight_rows, 0)
 
@@ -489,7 +490,7 @@
     giving = len(rest) > 1
     if giving:
         width = rest[1].shape[1]
-        second = shape((HALF, width), f32)
+        second = [shape((HALF, width), f32), shape((HALF, width), bf16)]
         scratch = [
             pltpu.VMEM((3, HALF, cols), bf16),
             pltpu.VMEM(rest[1].shape, bf16),
@@ -497,21 +498,21 @@
             pltpu.SemaphoreType.DMA((5,)),
         ]
     else:
-        second = shape((3, rest[0].shape[0], cols), bf16)
+        second = [shape((3, rest[0].shape[0], cols), bf16)]
         scratch = []
     return pl.pallas_call(
         functools.partial(backward_kernel, giving),
         in_specs=[pl.BlockSpec(memory_space=pltpu.SMEM)]
         + [vmem] * 10
         + [hbm if giving else vmem] * len(rest),
-        out_specs=[vmem] * 2,
+        out_specs=[vmem] * (1 + len(second)),
         scratch_shapes=[
             pltpu.VMEM((count, cols), f32),
             pltpu.VMEM((count, cols), f32),
             pltpu.VMEM((max(KEY_TILE, WINDOW), 2 * TILE), f32),
         ]
         + scratch,
-        out_shape=[shape((3, count, cols), bf16), second],
+        out_shape=[shape((3, count, cols), bf16)] + second,
         name="attend_backward",
         cost_estimate=pl.CostEstimate(
             flops=36 * 10**9, bytes_accessed=36 * 10**6, transcendentals=6 * 10**6
@@ -1149,13 +1150,11 @@
         tokens_ref,
         context_ref,
         given_ref,
-        vectors_ref,
-        dmid_hbm,
         small_ref,
         small2_ref,
         gqkv_ref,
         gout_ref,
-        back_ref,
+        back_hbm,
         sums_ref,
         full_ref,
         out_buf,
@@ -1164,12 +1163,12 @@
         d2_ref,
         w_ref,
         w2_ref,
-        dmid_ref,
         load_sem,
         rows_ref,
         give_ref,
         take_ref,
         swap_sem,
+        back_sem,
         norm_ref,
         near_ref,
         far_ref,
@@ -1189,7 +1188,6 @@
                 (w_hbm, w_ref),
                 (w2_hbm, w2_ref),
                 (d2_hbm, d2_ref),
-                (dmid_hbm, dmid_ref),
             )
         )
     ]
@@ -1267,12 +1265,12 @@
 
     width = tokens_ref.shape[1]
 
-    def swap(rows, lane):
+    def swap():
         return pltpu.make_async_remote_copy(
-            src_ref=give_ref.at[rows],
-            dst_ref=take_ref.at[rows],
-            send_sem=swap_sem.at[lane, 0],
-            recv_sem=swap_sem.at[lane, 1],
+            src_ref=give_ref,
+            dst_ref=take_ref,
+            send_sem=swap_sem.at[0],
+            recv_sem=swap_sem.at[1],
             device_id=ex.across,
             device_id_type=MESH,
         )
@@ -1282,8 +1280,6 @@
         norm_ref[0:1, :] += add(d_rows * units)
         norm_ref[1:2, :] += add(d_rows)
 
-    main = slice(0, HALF)
-    edges = slice(HALF, HALF + 2 * EDGE)
     parts = tokens_ref.shape[0] // TILE
     lead = small_ref.shape[0] - 2
     bias = lead - 3
@@ -1302,15 +1298,12 @@
         for load in loads[2:5]:
             load.wait()
 
-    give_ref[main, :] = given_ref[...].astype(bf16)
-    swap(main, 0).start()
-
     def give_edges():
         side = rows_ref[NOISY_BASE:NOISY_OWN, :] + rows_ref[NOISY_OWN + HALF :, :]
         after = rows_ref[2 * HALF : NOISY_BASE, :]
-        give_ref[HALF : HALF + EDGE, :] = after.astype(bf16)
-        give_ref[HALF + EDGE :, :] = side.astype(bf16)
-        swap(edges, 1).start()
+        give_ref[:EDGE, :] = after.astype(bf16)
+        give_ref[EDGE:, :] = side.astype(bf16)
+        swap().start()
         sums_of(after, normal(context_ref[:EDGE, :].astype(f32))[0])
         sums_of(side, normal(context_ref[HALF:, :].astype(f32))[0])
 
@@ -1379,26 +1372,23 @@
         for j in range(1, 4):
             far_copy(j, ex.z).start()
 
+    halves = [
+        pltpu.make_async_copy(
+            rows_ref.at[start : start + HALF],
+            back_hbm.at[n * HALF : (n + 1) * HALF],
+            back_sem.at[n],
+        )
+        for n, start in enumerate((NOISY_OWN, CLEAN_OWN))
+    ]
+
     def take_back():
-        loads[5].wait()
-        swap(main, 0).wait()
-        swap(edges, 1).wait()
-        clean = slice(CLEAN_OWN, CLEAN_OWN + HALF)
-        rows_ref[clean, :] += take_ref[main, :].astype(f32)
+        swap().wait()
         begin = slice(CLEAN_OWN, CLEAN_OWN + EDGE)
-        rows_ref[begin, :] += take_ref[HALF : HALF + EDGE, :].astype(f32)
+        rows_ref[begin, :] += take_ref[:EDGE, :].astype(f32)
         edge = pl.ds(pl.multiple_of(NOISY_OWN + (1 - part) * (HALF - EDGE), EDGE), EDGE)
-        rows_ref[edge, :] += take_ref[HALF + EDGE :, :].astype(f32)
-
-    def norm_back(b):
-        rows = tokens_at(b)
-        unit, scale = normal(tokens_ref[rows, :].astype(f32))
-        lean = rows_ref[own_at(b), :] * vectors_ref[0:1, :]
-        back_ref[rows, :] = dmid_ref[rows, :] + scale * (
-            lean
-            - jnp.mean(lean, axis=-1, keepdims=True)
-            - unit * jnp.mean(lean * unit, axis=-1, keepdims=True)
-        )
+        rows_ref[edge, :] += take_ref[EDGE:, :].astype(f32)
+        for half in halves:
+            half.start()
 
     def end_far():
         for j in range(1, 4):
@@ -1428,9 +1418,9 @@
         groups + 1: give_edges,
         groups + 2: tell_near,
         groups + 3: take_back,
-        groups + 6: tell_far,
+        groups + 4: tell_far,
+        groups + 6: end_far,
     }
-    begin_back = groups + 4
 
     def phase(p, _):
         @pl.when(p < groups)
@@ -1445,20 +1435,15 @@
 
         for n, action in actions.items():
             pl.when(p == n)(action)
-        block = 2 * (p - begin_back)
-
-        @pl.when(jnp.logical_and(block >= 0, block < parts))
-        def _():
-            lax.fori_loop(block, block + 2, lambda b, _: (norm_back(b), 0)[1], 0)
-
-        pl.when(block == parts)(end_far)
         steps(p)
         return 0
 
-    lax.fori_loop(0, begin_back + parts // 2 + 1, phase, 0)
-
-
-def leave(bits, rows_t, mine, crossed, d_fields, weights, tokens, context, given, vectors, d_mid, small, small2):
+    lax.fori_loop(0, groups + 7, phase, 0)
+    for half in halves:
+        half.wait()
+
+
+def leave(bits, rows_t, mine, crossed, d_fields, weights, tokens, context, given, small, small2):
     rows, cols = ROW_TILE, d_fields[0].shape[2]
     total = mine.shape[1] // cols + crossed[0].shape[0]
     exchange = Exchange(bits, total, rows, cols)
@@ -1468,8 +1453,8 @@
     shape = jax.ShapeDtypeStruct
     return pl.pallas_call(
         functools.partial(leave_kernel, exchange),
-        in_specs=[hbm] + [vmem] * 3 + [hbm] * 4 + [vmem] * 4 + [hbm] + [vmem] * 2,
-        out_specs=[vmem] * 4,
+        in_specs=[hbm] + [vmem] * 3 + [hbm] * 4 + [vmem] * 5,
+        out_specs=[vmem] * 2 + [hbm, vmem],
         out_shape=[
             shape(weights[0].shape, bf16),
             shape((d_fields[0].shape[2], width), bf16),
@@ -1484,12 +1469,12 @@
             pltpu.VMEM(d_fields[1].shape, bf16),
             pltpu.VMEM(weights[0].shape, bf16),
             pltpu.VMEM(weights[1].shape, bf16),
-            pltpu.VMEM(d_mid.shape, f32),
-            pltpu.SemaphoreType.DMA((6,)),
+            pltpu.SemaphoreType.DMA((5,)),
             pltpu.VMEM((KEY_ROWS, width), f32),
-            pltpu.VMEM((HALF + 2 * EDGE, width), bf16),
-            pltpu.VMEM((HALF + 2 * EDGE, width), bf16),
-            pltpu.SemaphoreType.DMA((2, 2)),
+            pltpu.VMEM((2 * EDGE, width), bf16),
+            pltpu.VMEM((2 * EDGE, width), bf16),
+            pltpu.SemaphoreType.DMA((2,)),
+            pltpu.SemaphoreType.DMA((2,)),
             pltpu.VMEM((8, width), f32),
             pltpu.VMEM((8, 16, width), bf16),
             pltpu.VMEM((4 + 2 * len(exchange.extra), 16, width), bf16),
@@ -1505,8 +1490,43 @@
             flops=40 * 10**9, bytes_accessed=40 * 10**6, transcendentals=0
         ),
     )(
-        rows_t, mine, *crossed, *d_fields, *weights, tokens, context, given, vectors, d_mid, small, small2
+        rows_t, mine, *crossed, *d_fields, *weights, tokens, context, given, small, small2
     )
+
+
+def finish_kernel(rows_ref, got_ref, tokens_ref, vectors_ref, dmid_ref, out_ref):
+    clean = pl.program_id(0) >= pl.num_programs(0) // 2
+    got = jnp.where(clean, got_ref[...].astype(f32), 0.0)
+    unit, scale = normal(tokens_ref[...].astype(f32))
+    lean = (rows_ref[...] + got) * vectors_ref[0:1, :]
+    out_ref[...] = dmid_ref[...] + scale * (
+        lean
+        - jnp.mean(lean, axis=-1, keepdims=True)
+        - unit * jnp.mean(lean * unit, axis=-1, keepdims=True)
+    )
+
+
+def finish(rows, got, tokens, vectors, d_mid):
+    count, width = rows.shape
+    spec = pl.BlockSpec((ROW_TILE, width), lambda b: (b, 0))
+    half = count // ROW_TILE // 2
+    return pl.pallas_call(
+        finish_kernel,
+        grid=(count // ROW_TILE,),
+        in_specs=[
+            spec,
+            pl.BlockSpec((ROW_TILE, width), lambda b: (jnp.maximum(b - half, 0), 0)),
+            spec,
+            pl.BlockSpec(vectors.shape, lambda b: (0, 0)),
+            spec,
+        ],
+        out_specs=spec,
+        out_shape=jax.ShapeDtypeStruct((count, width), f32),
+        name="finish",
+        cost_estimate=pl.CostEstimate(
+            flops=10**7, bytes_accessed=12 * 10**6, transcendentals=0
+        ),
+    )(rows, got, tokens, vectors, d_mid)
 
 
 def assemble_kernel(core_ref, down_mine, up_mine, down_got, up_got, down_ref, up_ref):
@@ -1734,7 +1754,8 @@
     (crossing, gathered), spans = tie((crossing, gathered), spans)
     crossed = across(crossing)
     moved = beside(gathered)
-    d_fields1, given = backward(mine, d_att, spans, d_fields2, qkv_mine, qkv_other)
+    d_fields1, given, give = backward(mine, d_att, spans, d_fields2, qkv_mine, qkv_other)
+    took = across(give)
     moved, d_fields1 = tie(moved, d_fields1)
     gathered = in_order(side, gathered, moved, 1)
     gathered, d_fields1 = tie(gathered, d_fields1)
@@ -1742,7 +1763,7 @@
     lead = hidden // width
     bias2, bias1 = grad_bias.reshape(2, lead, width)
     shared = jnp.concatenate([norms[:3], jnp.zeros((2, width), f32)], axis=0)
-    grad_qkv, grad_out, grad_tokens, sums = leave(
+    grad_qkv, grad_out, d_rows, sums = leave(
         bits,
         normed1_t,
         grad_out,
@@ -1752,12 +1773,11 @@
         x_rows,
         context,
         given,
-        vectors,
-        d_mid,
         jnp.concatenate([bias1, shared], axis=0),
         jnp.concatenate([bias2, shared], axis=0),
     )
-    moved, _ = tie(moved, grad_qkv)
+    (moved, took), grad_qkv = tie((moved, took), grad_qkv)
+    grad_tokens = finish(d_rows, took, x_rows, vectors, d_mid)
     grad_down, grad_up = assemble(core.reshape(1), gathered, moved)
     return (
         out.reshape(tokens.shape),

time: 333 us -> 329 us (0.988)
  starting transfers between devices: 31.2 us -> 41.7 us
  waiting for transfers between devices: 19 us -> 13.5 us
  local copies, waits for them, and re-layouts: 19.6 us -> 15.8 us
    ppermute x7 -> x8, starting transfers between devices: 22.7 us -> 30.7 us  [across(): return lax.ppermute(array, 'mp', [(0, 1), (1, 0)])]
    pallas_call x0 -> x1, Pallas kernels: none -> 6.67 us  [finish(): pl.pallas_call(finish_kernel, grid=(count // ROW_TILE,), in_specs=[spec,...]
    ppermute x3, waiting for transfers between devices: 5.87 us -> 0.01 us  [beside(): return lax.ppermute(array, 'dp', [(i, i ^ 2) for i in range(dp_size)])]
    pallas_call x1, Pallas kernels: 56.4 us -> 51.5 us  [leave(): pl.pallas_call(functools.partial(leave_kernel, exchange), in_specs=[hbm]...]
    pallas_call x2, Pallas kernels: 29.3 us -> 25 us  [attend_forward(): pl.pallas_call(forward_kernel, in_specs=[pl.BlockSpec(memory_space=pltpu....]
    pallas_call x1, Pallas kernels: 83.8 us -> 87.6 us  [middle(): pl.pallas_call(functools.partial(middle_kernel, exchanges, tiles), in_spe...]
    unnamed x34 -> x29, local copies, waits for them, and re-layouts: 6.35 us -> 2.57 us
    pallas_call x2, Pallas kernels: 43.5 us -> 40.1 us  [attend_backward(): pl.pallas_call(functools.partial(backward_kernel, giving), in_specs=[pl.B...]
  transfers between devices with their start and end apart: 17 -> 18, of which waited for: 5 -> 3; matrix products, arithmetic and copies ran while one was open for 9% -> 8% of each run, Pallas kernels for 45% -> 41%
where the time goes in v7:
time: 329 us
  Pallas kernels  237 us (72%)
  starting transfers between devices  41.7 us (13%)
  other arithmetic  19.4 us (6%)
  local copies, waits for them, and re-layouts  15.8 us (5%)
  waiting for transfers between devices  13.5 us (4%)
    pallas_call x1, Pallas kernels, middle(): pl.pallas_call(functools.partial(middle_kernel, exchanges, tiles), in_spe...  87.6 us
    pallas_call x1, Pallas kernels, leave(): pl.pallas_call(functools.partial(leave_kernel, exchange), in_specs=[hbm]...  51.5 us
    pallas_call x2, Pallas kernels, attend_backward(): pl.pallas_call(functools.partial(backward_kernel, giving), in_specs=[pl.B...  40.1 us
    ppermute x8, starting transfers between devices, across(): return lax.ppermute(array, 'mp', [(0, 1), (1, 0)])  30.7 us
    pallas_call x2, Pallas kernels, attend_forward(): pl.pallas_call(forward_kernel, in_specs=[pl.BlockSpec(memory_space=pltpu....  25 us
    ppermute x8, waiting for transfers between devices, across(): return lax.ppermute(array, 'mp', [(0, 1), (1, 0)])  13.1 us
    pallas_call x1, Pallas kernels, enter(): pl.pallas_call(enter_kernel, in_specs=[vmem] * 6, out_specs=[vmem] * 5, o...  11.4 us
    pallas_call x1, Pallas kernels, project(): pl.pallas_call(project_kernel, grid=(3,), in_specs=[row_spec, pl.BlockSpe...  7.35 us
  transfers between devices with their start and end apart: 18, of which 3 were waited for; matrix products, arithmetic and copies ran while one was open for 8% of the time, Pallas kernels for 41%

profile of v7, /device:TPU:0, one launch (start us, length us, event | category | flops | bytes accessed | tf_op | source)
XLA Modules:
  0.0 328.8 jit_solution(6526376288925139907)
XLA Ops:
  0.7 1.2 slice_bitcast_fusion
  1.9 0.8 select_bitcast_fusion
  2.8 3.0 collective-permute-start
  5.8 0.2 reduce-window.8
  6.7 0.1 fusion.2
  6.8 0.1 subtract_convert_fusion
  6.9 0.3 fusion.16
  7.3 0.2 reduce_min.21
  7.5 0.1 copy.31
  7.7 0.7 pad_add_fusion.1.span_ref
  8.3 0.6 add_add_fusion.clean_ref
  8.9 0.6 pad_add_fusion.noisy_ref
  9.5 1.1 dynamic-slice_bitcast_fusion
  10.6 1.4 constant_dynamic-slice_fusion.2
  12.0 0.7 constant_dynamic-slice_fusion.1
  12.7 0.6 stack.29.vectors_ref.refs_6_
  13.4 1.1 constant_dynamic-slice_fusion.3
  14.5 4.4 %fusion = (f32[1584,128]{1,0:T(8,128)}, f32[1584,128]{1,0:T(8,128)}) fusion(f32[128]{0:T(128)S(1)} %get-tuple-element.185, f32[128]{0:T(128)S(1)} %get-tuple-element.186, f32[1584]{0:T(1024)S(1)} %get-tuple-element.179), kind=kLoop, calls=%fused_computation.12 | loop fusion | flops 405504 | bytes 1629376 | tf_op jit(solution)/shard_map/mul | solution.py:1616
  18.8 5.1 %collective-permute-done.context_ref.refs_9_ = bf16[528,768]{1,0:T(8,128)(2,1)} collective-permute-done((bf16[528,768]{1,0:T(8,128)(2,1)S(1)}, bf16[528,768]{1,0:T(8,128)(2,1)}, u32[]{:S(2)}, u32[]{:S(2)}) %collective-permute-start) | collective-permute-done | bytes 811040 | tf_op jit(solution)/shard_map/ppermute | solution.py:1654
  24.0 1.7 collective-permute-start.1
  25.7 0.3 collective-permute-start.3
  26.0 11.4 %enter.1 = (bf16[1584,768]{1,0:T(8,128)(2,1)}, bf16[768,1584]{1,0:T(8,128)(2,1)}, bf16[1584,384]{1,0:T(8,128)(2,1)}, bf16[1584,384]{1,0:T(8,128)(2,1)}, bf16[1584,384]{1,0:T(8,128)(2,1)}) custom-call(bf16[2,512,768]{2,1,0:T(8,128)(2,1)} %tokens_ref.1, bf16[528,768]{1,0:T(8,128)(2,1)} %collective-permute-done.context_ref.refs_9_, ...), custom_call_target="tpu_custom_call" | custom-call | flops 10000000000 | bytes 16000000 | tf_op jit(solution)/shard_map/enter/pallas_call | solution.py:157
  37.4 1.7 collective-permute-start.2
  39.1 12.5 %attend_forward.2 = (bf16[1024,384]{1,0:T(8,128)(2,1)}, f32[3,4,2,256]{3,2,1,0:T(2,128)}) custom-call(s32[4,2]{1,0:T(4,128)} %pad_add_fusion.1.span_ref, s32[4,2,256]{2,1,0:T(2,128)} %add_add_fusion.clean_ref, s32[4,2,128]{2,1,0:T(2,128)} %pad_add_fusion.noisy_ref, bf16[1584,384]{1,0:T(8,128)(2,1)} %get-tuple-element.90.q_ref, ...), custom_call_target="tpu_custom_call" | custom-call | flops 1610612736 | bytes 4866048 | tf_op jit(solution)/shard_map/attend_forward/pallas_call | solution.py:290
  51.9 9.1 %collective-permute-start.7 = (bf16[768,768]{1,0:T(8,128)(2,1)S(1)}, bf16[768,768]{1,0:T(8,128)(2,1)}, u32[]{:S(2)}, u32[]{:S(2)}) collective-permute-start(bf16[768,768]{1,0:T(8,128)(2,1)S(1)} %constant_dynamic-slice_fusion.2), channel_id=1, source_target_pairs={{0,1},{1,0},{2,3},{3,2},{4,5},{5,4},{6,7},{7,6},{8,9},{9,8},{10,11... | collective-permute-start | bytes 3538952 | tf_op jit(solution)/shard_map/ppermute | solution.py:1654
  61.0 0.5 collective-permute-start.5
  61.5 1.5 collective-permute-start.6
  63.0 1.5 broadcast_select_fusion.3
  64.5 1.4 pad_maximum_fusion.1.w_ref.refs_2_.refs_7_
  66.0 7.3 %project.1 = (bf16[1584,384]{1,0:T(8,128)(2,1)}, bf16[1584,384]{1,0:T(8,128)(2,1)}, bf16[1584,384]{1,0:T(8,128)(2,1)}) custom-call(bf16[1584,768]{1,0:T(8,128)(2,1)} %get-tuple-element.94.rows_ref, bf16[3,768,384]{2,1,0:T(8,128)(2,1)} %pad_maximum_fusion.1.w_ref.refs_2_.refs_7_, f32[1584,128]{1,0:T(8,128)} %get-tuple-element.85.cos_ref, ...), custom_call_target="tpu_custom_call" | custom-call | flops 2802843648 | bytes 7852032 | tf_op jit(solution)/shard_map/project/pallas_call | solution.py:78
  73.3 12.5 %attend_forward.3 = (bf16[1024,384]{1,0:T(8,128)(2,1)}, f32[3,4,2,256]{3,2,1,0:T(2,128)}) custom-call(s32[4,2]{1,0:T(4,128)} %pad_add_fusion.1.span_ref, s32[4,2,256]{2,1,0:T(2,128)} %add_add_fusion.clean_ref, s32[4,2,128]{2,1,0:T(2,128)} %pad_add_fusion.noisy_ref, bf16[1584,384]{1,0:T(8,128)(2,1)} %get-tuple-element.99.q_ref, ...), custom_call_target="tpu_custom_call" | custom-call | flops 1610612736 | bytes 4866048 | tf_op jit(solution)/shard_map/attend_forward/pallas_call | solution.py:290
  85.8 7.9 %collective-permute-done.5 = bf16[192,768]{1,0:T(8,128)(2,1)S(1)} collective-permute-done((bf16[192,768]{1,0:T(8,128)(2,1)S(1)}, bf16[192,768]{1,0:T(8,128)(2,1)S(1)}, u32[]{:S(2)}, u32[]{:S(2)}) %collective-permute-start.5) | collective-permute-done | bytes 294944 | tf_op jit(solution)/shard_map/ppermute | solution.py:1654
  93.8 0.6 reshape.337.refs_7_
  94.4 0.6 pad.5.clone
  95.0 0.4 collective-permute-done.8
  95.4 0.9 pad_maximum_fusion.5.refs_4_
  96.3 87.6 %middle.1 = (bf16[1024,768]{1,0:T(8,128)(2,1)}, f32[1024,768]{1,0:T(8,128)}, bf16[1024,384]{1,0:T(8,128)(2,1)}, bf16[1024,384]{1,0:T(8,128)(2,1)}, bf16[256,1152...) custom-call(bf16[1024,768]{1,0:T(8,128)(2,1)} %bitcast.28, ...), custom_call_target="tpu_custom_call" | custom-call | flops 60000002048 | bytes 40000000 | tf_op jit(solution)/shard_map/middle/pallas_call | solution.py:1089
  183.8 0.1 collective-permute-start.10
  184.0 2.6 collective-permute-start.11
  186.6 1.7 collective-permute-start.12
  188.3 0.7 slice_reduce_fusion
  189.1 0.7 slice.53
  189.8 21.3 %attend_backward.2 = (bf16[3,1584,384]{2,1,0:T(8,128)(2,1)}, bf16[3,768,384]{2,1,0:T(8,128)(2,1)}) custom-call(s32[4,2]{1,0:T(4,128)} %pad_add_fusion.1.span_ref, s32[4,2,256]{2,1,0:T(2,128)} %add_add_fusion.clean_ref, s32[4,2,128]{2,1,0:T(2,128)} %pad_add_fusion.noisy_ref, bf16[1584,384]{1,0:T(8,128)(2,1)} %get-tuple-element.99.q_ref, ...), custom_call_target="tpu_custom_call" | custom-call | flops 35999997952 | bytes 36000000 | tf_op jit(solution)/shard_map/attend_backward/pallas_call | solution.py:503
  211.1 1.3 constant_dynamic-slice_fusion
  212.5 7.6 %collective-permute-start.14 = (bf16[256,1152]{1,0:T(8,128)(2,1)}, bf16[256,1152]{1,0:T(8,128)(2,1)}, u32[]{:S(2)}, u32[]{:S(2)}) collective-permute-start(bf16[256,1152]{1,0:T(8,128)(2,1)} %get-tuple-element.121), channel_id=1, source_target_pairs={{0,1},{1,0},{2,3},{3,2},{4,5},{5,4},{6,7},{7,6},{8,9},{9,8},{10,11... | collective-permute-start | bytes 1769480 | tf_op jit(solution)/shard_map/ppermute | solution.py:1654
  220.0 0.7 fusion.4
  220.9 0.3 broadcast_select_fusion.5
  221.2 1.4 copy-done
  222.6 0.2 add_convert_fusion
  222.9 2.2 collective-permute-start.15
  225.1 18.9 %attend_backward.3 = (bf16[3,1584,384]{2,1,0:T(8,128)(2,1)}, f32[512,768]{1,0:T(8,128)}, bf16[512,768]{1,0:T(8,128)(2,1)}) custom-call(s32[4,2]{1,0:T(4,128)} %pad_add_fusion.1.span_ref, s32[4,2,256]{2,1,0:T(2,128)} %add_add_fusion.clean_ref, s32[4,2,128]{2,1,0:T(2,128)} %pad_add_fusion.noisy_ref, bf16[1584,384]{1,0:T(8,128)(2,1)} %get-tuple-element.90.q_ref, ...), custom_call_target="tpu_custom_call" | custom-call | flops 35999997952 | bytes 36000000 | tf_op jit(solution)/shard_map/attend_backward/pallas_call | solution.py:503
  244.0 8.4 %collective-permute-start.17 = (bf16[512,768]{1,0:T(8,128)(2,1)}, bf16[512,768]{1,0:T(8,128)(2,1)}, u32[]{:S(2)}, u32[]{:S(2)}) collective-permute-start(bf16[512,768]{1,0:T(8,128)(2,1)} %get-tuple-element.136), channel_id=1, source_target_pairs={{0,1},{1,0},{2,3},{3,2},{4,5},{5,4},{6,7},{7,6},{8,9},{9,8},{10,11... | collective-permute-start | bytes 2359304 | tf_op jit(solution)/shard_map/ppermute | solution.py:1654
  252.4 0.2 broadcast_select_fusion.1
  252.6 1.6 pad_maximum_fusion.down_mine.up_mine
  254.2 0.9 collective-permute-start.16
  255.2 51.5 %leave.1 = (bf16[3,768,384]{2,1,0:T(8,128)(2,1)}, bf16[384,768]{1,0:T(8,128)(2,1)}, f32[1024,768]{1,0:T(8,128)}, f32[16,768]{1,0:T(8,128)}) custom-call(bf16[768,1584]{1,0:T(8,128)(2,1)} %get-tuple-element.111.refs_0_, bf16[256,1152]{1,0:T(8,128)(2,1)} %get-tuple-element.112.refs_1_, bf16[9,128,384]{2,1,0:T(8,128)(2,1)} %collective-permute-done.13.refs_2_, ...), custom_call_target="tpu_custom_call" | custom-call | flops 40000000000 | bytes 40000000 | tf_op jit(solution)/shard_map/leave/pallas_call | solution.py:1454
  306.7 2.3 convert_element_type.40
  309.0 0.7 slice.58
  309.7 0.6 reshape.335
  310.3 1.6 slice_reduce_fusion.2
  311.9 2.0 convert_bitcast_fusion
  314.0 7.0 %assemble.1 = (f32[1536,768]{1,0:T(8,128)}, f32[768,1536]{1,0:T(8,128)}) custom-call(s32[1]{0:T(128)} %bitcast.19.core_ref, bf16[12,128,768]{2,1,0:T(8,128)(2,1)} %pad_maximum_fusion.down_mine.up_mine, bf16[12,128,768]{2,1,0:T(8,128)(2,1)} %pad_maximum_fusion.down_mine.up_mine, bf16[12,128,768]{2,1,0:T(8,128)(2,1)} %collective-permute-done.16.down_got.up_got, ...), custom_call_target="tpu_custom_call" | custom-call | flops 1000000 | bytes 14000000 | tf_op jit(solution)/shard_map/assemble/pallas_call | solution.py:1555
  320.9 6.7 %finish.1 = f32[1024,768]{1,0:T(8,128)} custom-call(f32[1024,768]{1,0:T(8,128)} %get-tuple-element.134.rows_ref, bf16[512,768]{1,0:T(8,128)(2,1)} %collective-permute-done.17.got_ref, bf16[1024,768]{1,0:T(8,128)(2,1)} %bitcast.30, f32[5,768]{1,0:T(8,128)} %stack.29.vectors_ref.refs_6_, f32[1024,768]{1,0:T(8,128)} %get-tuple-element.139.dmid_ref), custom_call_target="tpu_custom_call" | custom-call | flops 10000000 | bytes 12000000 | tf_op jit(solution)/shard_map/finish/pallas_call | solution.py:1513
  327.6 1.1 copy.38
  (69 shorter events, 0.9 us)
Async XLA Ops:
  0.6 5.2 %copy-start.13 = (s32[1,4]{1,0:T(1,128)S(1)}, s32[1,4]{1,0:T(1,128)}, u32[]{:S(2)}) copy-start(s32[1,4]{1,0:T(1,128)} %param.15) | copy-start | bytes 52
  0.7 6.9 %copy-start.6 = (f32[768]{0:T(1024)S(1)}, f32[768]{0:T(1024)}, u32[]{:S(2)}) copy-start(f32[768]{0:T(1024)} %param.18) | copy-start | bytes 9220
  0.7 6.9 %copy-start.7 = (f32[768]{0:T(1024)S(1)}, f32[768]{0:T(1024)}, u32[]{:S(2)}) copy-start(f32[768]{0:T(1024)} %param.19) | copy-start | bytes 9220
  0.7 6.9 %copy-start.8 = (f32[768]{0:T(1024)S(1)}, f32[768]{0:T(1024)}, u32[]{:S(2)}) copy-start(f32[768]{0:T(1024)} %param.22) | copy-start | bytes 9220
  0.7 6.9 %copy-start.9 = (f32[768]{0:T(1024)S(1)}, f32[768]{0:T(1024)}, u32[]{:S(2)}) copy-start(f32[768]{0:T(1024)} %param.23) | copy-start | bytes 9220
  0.7 6.9 %copy-start.10 = (f32[768]{0:T(1024)S(1)}, f32[768]{0:T(1024)}, u32[]{:S(2)}) copy-start(f32[768]{0:T(1024)} %param.27) | copy-start | bytes 9220
  2.8 9.2 %copy-start.5 = (bf16[384,768]{1,0:T(8,128)(2,1)S(1)}, bf16[384,768]{1,0:T(8,128)(2,1)}, u32[]{:S(2)}) copy-start(bf16[384,768]{1,0:T(8,128)(2,1)} %refs_3_.1) | copy-start | bytes 1769476
  2.8 21.2 %collective-permute-start = (bf16[528,768]{1,0:T(8,128)(2,1)S(1)}, bf16[528,768]{1,0:T(8,128)(2,1)}, u32[]{:S(2)}, u32[]{:S(2)}) collective-permute-start(bf16[528,768]{1,0:T(8,128)(2,1)S(1)} %pad_maximum_fusion.4), channel_id=1, source_target_pairs={{0,1},{1,0},{2,3},{3,2},{4,5},{5,4},{6,7},{7,6},{8,9},{9,8},{10,11... | collective-permute-start | bytes 2433032 | tf_op jit(solution)/shard_map/ppermute | solution.py:1654
  24.0 13.4 %collective-permute-start.1 = (bf16[3,192,384]{2,1,0:T(8,128)(2,1)S(1)}, bf16[3,192,384]{2,1,0:T(8,128)(2,1)S(1)}, u32[]{:S(2)}, u32[]{:S(2)}) collective-permute-start(bf16[3,192,384]{2,1,0:T(8,128)(2,1)S(1)} %dynamic-slice_bitcast_fusion), channel_id=1, source_target_pairs={{0,1},{1,0},{2,3},{3,2},{4,5},{5,4},{6,7},{7,6},{8,9},{9,8},{10,11... | collective-permute-start | bytes 1327112 | tf_op jit(solution)/shard_map/ppermute | solution.py:1654
  25.7 25.9 %collective-permute-start.3 = (bf16[192,1536]{1,0:T(8,128)(2,1)S(1)}, bf16[192,1536]{1,0:T(8,128)(2,1)}, u32[]{:S(2)}, u32[]{:S(2)}) collective-permute-start(bf16[192,1536]{1,0:T(8,128)(2,1)S(1)} %constant_dynamic-slice_fusion.3), channel_id=1, source_target_pairs={{0,1},{1,0},{2,3},{3,2},{4,5},{5,4},{6,7},{7,6},{8,9},{9,8},{10,11... | collective-permute-start | bytes 1769480 | tf_op jit(solution)/shard_map/ppermute | solution.py:1654
  37.4 14.2 %collective-permute-start.2 = (bf16[3,192,384]{2,1,0:T(8,128)(2,1)S(1)}, bf16[3,192,384]{2,1,0:T(8,128)(2,1)S(1)}, u32[]{:S(2)}, u32[]{:S(2)}) collective-permute-start(bf16[3,192,384]{2,1,0:T(8,128)(2,1)S(1)} %collective-permute-done.1), channel_id=1, source_target_pairs={{0,4},{2,6},{4,0},{6,2},{8,12},{10,14},{12,8},{14,10},{16,20},{18,... | collective-permute-start | bytes 1327112 | tf_op jit(solution)/shard_map/ppermute | solution.py:1660
  51.6 9.3 %copy-start.3 = (bf16[192,768]{1,0:T(8,128)(2,1)S(1)}, bf16[192,768]{1,0:T(8,128)(2,1)}, u32[]{:S(2)}) copy-start(bf16[192,768]{1,0:T(8,128)(2,1)} %constant_dynamic-slice_fusion.1) | copy-start | bytes 884740
  51.8 11.2 %collective-permute-start.4 = (bf16[3,384,384]{2,1,0:T(8,128)(2,1)S(1)}, bf16[3,384,384]{2,1,0:T(8,128)(2,1)}, u32[]{:S(2)}, u32[]{:S(2)}) collective-permute-start(bf16[3,384,384]{2,1,0:T(8,128)(2,1)S(1)} %pad_maximum_fusion.3), channel_id=1, source_target_pairs={{0,2},{2,0},{4,6},{6,4},{8,10},{10,8},{12,14},{14,12},{16,18},{18,... | collective-permute-start | bytes 2654216 | tf_op jit(solution)/shard_map/ppermute | solution.py:1657
  51.9 41.9 %collective-permute-start.7 = (bf16[768,768]{1,0:T(8,128)(2,1)S(1)}, bf16[768,768]{1,0:T(8,128)(2,1)}, u32[]{:S(2)}, u32[]{:S(2)}) collective-permute-start(bf16[768,768]{1,0:T(8,128)(2,1)S(1)} %constant_dynamic-slice_fusion.2), channel_id=1, source_target_pairs={{0,1},{1,0},{2,3},{3,2},{4,5},{5,4},{6,7},{7,6},{8,9},{9,8},{10,11... | collective-permute-start | bytes 3538952 | tf_op jit(solution)/shard_map/ppermute | solution.py:1654
  61.0 32.8 %collective-permute-start.5 = (bf16[192,768]{1,0:T(8,128)(2,1)S(1)}, bf16[192,768]{1,0:T(8,128)(2,1)S(1)}, u32[]{:S(2)}, u32[]{:S(2)}) collective-permute-start(bf16[192,768]{1,0:T(8,128)(2,1)S(1)} %copy-done.3), channel_id=1, source_target_pairs={{0,1},{1,0},{2,3},{3,2},{4,5},{5,4},{6,7},{7,6},{8,9},{9,8},{10,11... | collective-permute-start | bytes 884744 | tf_op jit(solution)/shard_map/ppermute | solution.py:1654
  61.5 32.3 %collective-permute-start.6 = (bf16[192,1536]{1,0:T(8,128)(2,1)}, bf16[192,1536]{1,0:T(8,128)(2,1)}, u32[]{:S(2)}, u32[]{:S(2)}) collective-permute-start(bf16[192,1536]{1,0:T(8,128)(2,1)} %collective-permute-done.3.refs_9_), channel_id=1, source_target_pairs={{0,4},{2,6},{4,0},{6,2},{8,12},{10,14},{12,8},{14,10},{16,20},{18,... | collective-permute-start | bytes 1769480 | tf_op jit(solution)/shard_map/ppermute | solution.py:1660
  73.3 20.5 %copy-start.11 = (bf16[1536]{0:T(1024)(128)(2,1)S(1)}, bf16[1536]{0:T(1024)(128)(2,1)}, u32[]{:S(2)}) copy-start(bf16[1536]{0:T(1024)(128)(2,1)} %param.25) | copy-start | bytes 9220
  93.8 1.6 collective-permute-start.8
  183.8 36.9 %collective-permute-start.10 = (bf16[12,16,768]{2,1,0:T(8,128)(2,1)}, bf16[12,16,768]{2,1,0:T(8,128)(2,1)S(1)}, u32[]{:S(2)}, u32[]{:S(2)}) collective-permute-start(bf16[12,16,768]{2,1,0:T(8,128)(2,1)} %get-tuple-element.116), channel_id=1, source_target_pairs={{0,8},{2,10},{4,12},{6,14},{8,0},{10,2},{12,4},{14,6},{16,24},{18,... | collective-permute-start | bytes 884744 | tf_op jit(solution)/shard_map/ppermute | solution.py:1719
  184.0 36.8 %collective-permute-start.11 = (bf16[12,16,768]{2,1,0:T(8,128)(2,1)}, bf16[12,16,768]{2,1,0:T(8,128)(2,1)S(1)}, u32[]{:S(2)}, u32[]{:S(2)}) collective-permute-start(bf16[12,16,768]{2,1,0:T(8,128)(2,1)} %get-tuple-element.116), channel_id=1, source_target_pairs={{0,16},{2,18},{4,20},{6,22},{8,24},{10,26},{12,28},{14,30},{16,0},... | collective-permute-start | bytes 884744 | tf_op jit(solution)/shard_map/ppermute | solution.py:1719
  186.6 34.2 %collective-permute-start.12 = (bf16[12,16,768]{2,1,0:T(8,128)(2,1)}, bf16[12,16,768]{2,1,0:T(8,128)(2,1)S(1)}, u32[]{:S(2)}, u32[]{:S(2)}) collective-permute-start(bf16[12,16,768]{2,1,0:T(8,128)(2,1)} %get-tuple-element.116), channel_id=1, source_target_pairs={{0,24},{2,26},{4,28},{6,30},{8,16},{10,18},{12,20},{14,22},{16,8},... | collective-permute-start | bytes 884744 | tf_op jit(solution)/shard_map/ppermute | solution.py:1719
  211.1 9.0 %copy-start.12 = (f32[7]{0:T(128)S(1)}, f32[7]{0:T(128)}, u32[]{:S(2)}) copy-start(f32[7]{0:T(128)} %pad.5.clone) | copy-start | bytes 88
  211.1 9.7 %copy-start.4 = (bf16[12,16,768]{2,1,0:T(8,128)(2,1)S(1)}, bf16[12,16,768]{2,1,0:T(8,128)(2,1)}, u32[]{:S(2)}) copy-start(bf16[12,16,768]{2,1,0:T(8,128)(2,1)} %get-tuple-element.116) | copy-start | bytes 884740
  212.4 8.8 %collective-permute-start.9 = (bf16[9,128,384]{2,1,0:T(8,128)(2,1)S(1)}, bf16[9,128,384]{2,1,0:T(8,128)(2,1)S(1)}, u32[]{:S(2)}, u32[]{:S(2)}) collective-permute-start(bf16[9,128,384]{2,1,0:T(8,128)(2,1)S(1)} %constant_dynamic-slice_fusion), channel_id=1, source_target_pairs={{0,2},{2,0},{4,6},{6,4},{8,10},{10,8},{12,14},{14,12},{16,18},{18,... | collective-permute-start | bytes 2654216 | tf_op jit(solution)/shard_map/ppermute | solution.py:1657
  212.5 42.7 %collective-permute-start.14 = (bf16[256,1152]{1,0:T(8,128)(2,1)}, bf16[256,1152]{1,0:T(8,128)(2,1)}, u32[]{:S(2)}, u32[]{:S(2)}) collective-permute-start(bf16[256,1152]{1,0:T(8,128)(2,1)} %get-tuple-element.121), channel_id=1, source_target_pairs={{0,1},{1,0},{2,3},{3,2},{4,5},{5,4},{6,7},{7,6},{8,9},{9,8},{10,11... | collective-permute-start | bytes 1769480 | tf_op jit(solution)/shard_map/ppermute | solution.py:1654
  221.1 1.5 copy-start
  222.9 29.6 %collective-permute-start.15 = (bf16[12,64,768]{2,1,0:T(8,128)(2,1)S(1)}, bf16[12,64,768]{2,1,0:T(8,128)(2,1)S(1)}, u32[]{:S(2)}, u32[]{:S(2)}) collective-permute-start(bf16[12,64,768]{2,1,0:T(8,128)(2,1)S(1)} %pad_maximum_fusion.2), channel_id=1, source_target_pairs={{0,4},{2,6},{4,0},{6,2},{8,12},{10,14},{12,8},{14,10},{16,20},{18,... | collective-permute-start | bytes 3538952 | tf_op jit(solution)/shard_map/ppermute | solution.py:1660
  225.1 30.1 %collective-permute-start.13 = (bf16[9,128,384]{2,1,0:T(8,128)(2,1)S(1)}, bf16[9,128,384]{2,1,0:T(8,128)(2,1)}, u32[]{:S(2)}, u32[]{:S(2)}) collective-permute-start(bf16[9,128,384]{2,1,0:T(8,128)(2,1)S(1)} %add_convert_fusion), channel_id=1, source_target_pairs={{0,1},{1,0},{2,3},{3,2},{4,5},{5,4},{6,7},{7,6},{8,9},{9,8},{10,11... | collective-permute-start | bytes 2654216 | tf_op jit(solution)/shard_map/ppermute | solution.py:1654
  244.0 67.9 %collective-permute-start.17 = (bf16[512,768]{1,0:T(8,128)(2,1)}, bf16[512,768]{1,0:T(8,128)(2,1)}, u32[]{:S(2)}, u32[]{:S(2)}) collective-permute-start(bf16[512,768]{1,0:T(8,128)(2,1)} %get-tuple-element.136), channel_id=1, source_target_pairs={{0,1},{1,0},{2,3},{3,2},{4,5},{5,4},{6,7},{7,6},{8,9},{9,8},{10,11... | collective-permute-start | bytes 2359304 | tf_op jit(solution)/shard_map/ppermute | solution.py:1654
  254.2 57.7 %collective-permute-start.16 = (bf16[12,128,768]{2,1,0:T(8,128)(2,1)}, bf16[12,128,768]{2,1,0:T(8,128)(2,1)}, u32[]{:S(2)}, u32[]{:S(2)}) collective-permute-start(bf16[12,128,768]{2,1,0:T(8,128)(2,1)} %pad_maximum_fusion.down_mine.up_mine), channel_id=1, source_target_pairs={{0,2},{2,0},{4,6},{6,4},{8,10},{10,8},{12,14},{14,12},{16,18},{18,... | collective-permute-start | bytes 7077896 | tf_op jit(solution)/shard_map/ppermute | solution.py:1657
  306.7 5.2 %copy-start.1 = (bf16[3,768,384]{2,1,0:T(8,128)(2,1)S(1)}, bf16[3,768,384]{2,1,0:T(8,128)(2,1)}, u32[]{:S(2)}) copy-start(bf16[3,768,384]{2,1,0:T(8,128)(2,1)} %get-tuple-element.141) | copy-start | bytes 5308420
  320.9 6.7 %copy-start.2 = (bf16[1024,768]{1,0:T(8,128)(2,1)S(1)}, bf16[1024,768]{1,0:T(8,128)(2,1)}, u32[]{:S(2)}) copy-start(bf16[1024,768]{1,0:T(8,128)(2,1)} %get-tuple-element.110) | copy-start | bytes 4718596

commit v8 on v7

--- a/solution.py
+++ b/solution.py
@@ -1508,14 +1508,14 @@
 
 def finish(rows, got, tokens, vectors, d_mid):
     count, width = rows.shape
-    spec = pl.BlockSpec((ROW_TILE, width), lambda b: (b, 0))
-    half = count // ROW_TILE // 2
+    spec = pl.BlockSpec((TILE, width), lambda b: (b, 0))
+    half = count // TILE // 2
     return pl.pallas_call(
         finish_kernel,
-        grid=(count // ROW_TILE,),
+        grid=(count // TILE,),
         in_specs=[
             spec,
-            pl.BlockSpec((ROW_TILE, width), lambda b: (jnp.maximum(b - half, 0), 0)),
+            pl.BlockSpec((TILE, width), lambda b: (jnp.maximum(b - half, 0), 0)),
             spec,
             pl.BlockSpec(vectors.shape, lambda b: (0, 0)),
             spec,
@@ -1529,7 +1529,11 @@
     )(rows, got, tokens, vectors, d_mid)
 
 
-def assemble_kernel(core_ref, down_mine, up_mine, down_got, up_got, down_ref, up_ref):
+def assemble_kernel(
+    core_ref, down_mine, up_mine, down_got, up_got, qkv_low, out_low, down_ref, up_ref, qkv_ref, out_ref
+):
+    qkv_ref[...] = qkv_low[...].astype(f32)
+    out_ref[...] = out_low[...].astype(f32)
     core = core_ref[0]
     block = down_mine.shape[1]
     lanes = up_ref.shape[1]
@@ -1546,32 +1550,38 @@
                 up_ref[rows, :] = piece.astype(f32)
 
 
-def assemble(core, gathered, moved):
+def assemble(core, gathered, moved, qkv, out):
     tiles, half, width = gathered.shape
     count = tiles // 2
     down_spec = pl.BlockSpec((1, half, width), lambda k, c: (k, 0, 0))
     up_spec = pl.BlockSpec((1, half, width), lambda k, c: (count + k, 0, 0))
     hidden = count * 2 * half
+    qkv_spec = pl.BlockSpec((qkv.shape[0] // count, qkv.shape[1]), lambda k, c: (k, 0))
+    out_spec = pl.BlockSpec((out.shape[0] // count, out.shape[1]), lambda k, c: (k, 0))
     return pl.pallas_call(
         assemble_kernel,
         grid_spec=pltpu.PrefetchScalarGridSpec(
             num_scalar_prefetch=1,
             grid=(count,),
-            in_specs=[down_spec, up_spec, down_spec, up_spec],
+            in_specs=[down_spec, up_spec, down_spec, up_spec, qkv_spec, out_spec],
             out_specs=[
                 pl.BlockSpec((2 * half, width), lambda k, c: (k, 0)),
                 pl.BlockSpec((width, 2 * half), lambda k, c: (0, k)),
+                qkv_spec,
+                out_spec,
             ],
         ),
         out_shape=[
             jax.ShapeDtypeStruct((hidden, width), f32),
             jax.ShapeDtypeStruct((width, hidden), f32),
+            jax.ShapeDtypeStruct(qkv.shape, f32),
+            jax.ShapeDtypeStruct(out.shape, f32),
         ],
         name="assemble",
         cost_estimate=pl.CostEstimate(
             flops=10**6, bytes_accessed=14 * 10**6, transcendentals=0
         ),
-    )(core, gathered, gathered, moved, moved)
+    )(core, gathered, gathered, moved, moved, qkv, out)
 
 
 def key_layout(seq_lengths, block_len, part):
@@ -1683,16 +1693,19 @@
     qkv_here, fields = tie(qkv_here, fields)
     qkv_beside = beside(qkv_here)
     mine = [*fields, *attend_forward(spans, clean_bounds, noisy_bounds, *fields)]
-    (qkv_here, qkv_beside, up_here), _ = tie((qkv_here, qkv_beside, up_here), mine[3])
+    (qkv_here, qkv_beside, up_here, out_here), _ = tie(
+        (qkv_here, qkv_beside, up_here, out_here), mine[3]
+    )
+    out_there = sibling(out_here)
     qkv_half = in_order(side, qkv_here, qkv_beside, axis=1)
     qkv_other = in_order(core, qkv_half, sibling(qkv_half), axis=1)
     up_beside = beside(up_here)
     fields = project(normed1, qkv_other, cosine, sine)
+    (out_here, out_there), fields = tie((out_here, out_there), fields)
+    out_other = in_order(core, out_here, out_there)
+    out_other, fields = tie(out_other, fields)
     other = [*fields, *attend_forward(spans, clean_bounds, noisy_bounds, *fields)]
-    (out_here, up_here, up_beside, down_here), _ = tie(
-        (out_here, up_here, up_beside, down_here), other[3]
-    )
-    out_other = in_order(core, out_here, sibling(out_here))
+    (up_here, up_beside, down_here), _ = tie((up_here, up_beside, down_here), other[3])
     bias_all = b_up.astype(f32).reshape(-1, 1, HIDDEN_TILE)
 
     x_rows = tokens.reshape(TOK_DEV, width)
@@ -1778,14 +1791,16 @@
     )
     (moved, took), grad_qkv = tie((moved, took), grad_qkv)
     grad_tokens = finish(d_rows, took, x_rows, vectors, d_mid)
-    grad_down, grad_up = assemble(core.reshape(1), gathered, moved)
+    grad_down, grad_up, grad_qkv, grad_out = assemble(
+        core.reshape(1), gathered, moved, grad_qkv.reshape(-1, grad_qkv.shape[2]), grad_out
+    )
     return (
         out.reshape(tokens.shape),
         grad_tokens.reshape(tokens.shape),
         sums[lead + 3],
         sums[lead + 4],
-        grad_qkv.transpose(1, 0, 2).astype(f32),
-        grad_out.astype(f32),
+        grad_qkv.reshape(qkv_mine.shape).transpose(1, 0, 2),
+        grad_out,
         sums[lead],
         sums[lead + 1],
         grad_up,

time: 329 us -> 329 us (level); the launches traced: 329 us -> 324 us
  Pallas kernels: 237 us -> 250 us
  starting transfers between devices: 41.7 us -> 33.6 us
  waiting for transfers between devices: 13.5 us -> 8.35 us
  other arithmetic: 19.4 us -> 16.1 us
    ppermute x8, waiting for transfers between devices: 13.1 us -> 5.22 us  [across(): return lax.ppermute(array, 'mp', [(0, 1), (1, 0)])]
    ppermute x8, starting transfers between devices: 30.7 us -> 23.1 us  [across(): return lax.ppermute(array, 'mp', [(0, 1), (1, 0)])]
    convert_element_type x2 -> x0, other arithmetic: 4.31 us -> none  [the longest x1 2.28 us: local(): grad_out.astype(f32)]
    pallas_call x1, Pallas kernels: 87.6 us -> 91.9 us  [middle(): pl.pallas_call(functools.partial(middle_kernel, exchanges, tiles), in_spe...]
  transfers between devices with their start and end apart: 18 -> 18, of which waited for: 3 -> 4; matrix products, arithmetic and copies ran while one was open for 8% -> 8% of each run, Pallas kernels for 41% -> 43%
where the time goes in v8:
time: 329 us; the launch traced here: 324 us
  Pallas kernels  250 us (76%)
  starting transfers between devices  33.6 us (10%)
  other arithmetic  16.1 us (5%)
  local copies, waits for them, and re-layouts  14.6 us (4%)
  waiting for transfers between devices  8.35 us (3%)
    pallas_call x1, Pallas kernels, middle(): pl.pallas_call(functools.partial(middle_kernel, exchanges, tiles), in_spe...  91.9 us
    pallas_call x1, Pallas kernels, leave(): pl.pallas_call(functools.partial(leave_kernel, exchange), in_specs=[hbm]...  52.5 us
    pallas_call x2, Pallas kernels, attend_backward(): pl.pallas_call(functools.partial(backward_kernel, giving), in_specs=[pl.B...  41.9 us
    pallas_call x2, Pallas kernels, attend_forward(): pl.pallas_call(forward_kernel, in_specs=[pl.BlockSpec(memory_space=pltpu....  27.1 us
    ppermute x8, starting transfers between devices, across(): return lax.ppermute(array, 'mp', [(0, 1), (1, 0)])  23.1 us
    pallas_call x1, Pallas kernels, enter(): pl.pallas_call(enter_kernel, in_specs=[vmem] * 6, out_specs=[vmem] * 5, o...  11.4 us
    pallas_call x1, Pallas kernels, assemble(): pl.pallas_call(assemble_kernel, grid_spec=pltpu.PrefetchScalarGridSpec(nu...  9 us
    pallas_call x1, Pallas kernels, finish(): pl.pallas_call(finish_kernel, grid=(count // TILE,), in_specs=[spec, pl.B...  8.44 us
  transfers between devices with their start and end apart: 18, of which 4 were waited for; matrix products, arithmetic and copies ran while one was open for 8% of the time, Pallas kernels for 43%

profile of v8, /device:TPU:0, one launch (start us, length us, event | category | flops | bytes accessed | tf_op | source)
XLA Modules:
  0.0 324.0 jit_solution(9439418864654854006)
XLA Ops:
  0.7 1.3 slice_bitcast_fusion
  2.0 0.8 select_bitcast_fusion
  2.8 3.0 collective-permute-start
  6.5 0.2 reduce-window.8
  6.8 0.1 fusion.2
  6.9 0.2 reduce_min.21
  7.1 0.1 copy.31
  7.2 0.1 subtract_convert_fusion
  7.3 0.3 fusion.16
  7.6 0.1 copy.35
  7.7 0.7 pad_add_fusion.1.span_ref
  8.4 0.6 pad_add_fusion.noisy_ref
  9.0 0.6 add_add_fusion.clean_ref
  9.6 0.7 constant_dynamic-slice_fusion.1
  10.3 1.1 dynamic-slice_bitcast_fusion
  11.4 1.4 constant_dynamic-slice_fusion.2
  12.7 0.6 stack.29.vectors_ref.refs_6_
  13.4 1.1 constant_dynamic-slice_fusion.3
  14.5 4.4 %fusion = (f32[1584,128]{1,0:T(8,128)}, f32[1584,128]{1,0:T(8,128)}) fusion(f32[128]{0:T(128)S(1)} %get-tuple-element.207, f32[128]{0:T(128)S(1)} %get-tuple-element.208, f32[1584]{0:T(1024)S(1)} %get-tuple-element.201), kind=kLoop, calls=%fused_computation.11 | loop fusion | flops 405504 | bytes 1629376 | tf_op jit(solution)/shard_map/mul | solution.py:1626
  18.9 5.1 %collective-permute-done.context_ref.refs_9_ = bf16[528,768]{1,0:T(8,128)(2,1)} collective-permute-done((bf16[528,768]{1,0:T(8,128)(2,1)S(1)}, bf16[528,768]{1,0:T(8,128)(2,1)}, u32[]{:S(2)}, u32[]{:S(2)}) %collective-permute-start) | collective-permute-done | bytes 811040 | tf_op jit(solution)/shard_map/ppermute | solution.py:1664
  24.0 1.7 collective-permute-start.1
  25.7 0.3 collective-permute-start.3
  26.0 11.4 %enter.1 = (bf16[1584,768]{1,0:T(8,128)(2,1)}, bf16[768,1584]{1,0:T(8,128)(2,1)}, bf16[1584,384]{1,0:T(8,128)(2,1)}, bf16[1584,384]{1,0:T(8,128)(2,1)}, bf16[1584,384]{1,0:T(8,128)(2,1)}) custom-call(bf16[2,512,768]{2,1,0:T(8,128)(2,1)} %tokens_ref.1, bf16[528,768]{1,0:T(8,128)(2,1)} %collective-permute-done.context_ref.refs_9_, ...), custom_call_target="tpu_custom_call" | custom-call | flops 10000000000 | bytes 16000000 | tf_op jit(solution)/shard_map/enter/pallas_call | solution.py:157
  37.5 1.7 collective-permute-start.2
  39.2 1.5 collective-permute-start.4
  40.7 13.6 %attend_forward.2 = (bf16[1024,384]{1,0:T(8,128)(2,1)}, f32[3,4,2,256]{3,2,1,0:T(2,128)}) custom-call(s32[4,2]{1,0:T(4,128)} %pad_add_fusion.1.span_ref, s32[4,2,256]{2,1,0:T(2,128)} %add_add_fusion.clean_ref, s32[4,2,128]{2,1,0:T(2,128)} %pad_add_fusion.noisy_ref, bf16[1584,384]{1,0:T(8,128)(2,1)} %get-tuple-element.101.q_ref, ...), custom_call_target="tpu_custom_call" | custom-call | flops 1610612736 | bytes 4866048 | tf_op jit(solution)/shard_map/attend_forward/pallas_call | solution.py:290
  54.5 1.0 collective-permute-start.6
  55.5 0.6 reshape.345.refs_7_
  56.1 0.6 pad.5.clone
  56.7 5.2 %collective-permute-start.8 = (bf16[768,768]{1,0:T(8,128)(2,1)S(1)}, bf16[768,768]{1,0:T(8,128)(2,1)}, u32[]{:S(2)}, u32[]{:S(2)}) collective-permute-start(bf16[768,768]{1,0:T(8,128)(2,1)S(1)} %constant_dynamic-slice_fusion.2), channel_id=1, source_target_pairs={{0,1},{1,0},{2,3},{3,2},{4,5},{5,4},{6,7},{7,6},{8,9},{9,8},{10,11... | collective-permute-start | bytes 3538952 | tf_op jit(solution)/shard_map/ppermute | solution.py:1664
  61.9 1.4 collective-permute-start.7
  63.3 1.5 broadcast_select_fusion.3
  64.8 1.4 pad_maximum_fusion.1.w_ref.refs_2_.refs_7_
  66.3 7.4 %project.1 = (bf16[1584,384]{1,0:T(8,128)(2,1)}, bf16[1584,384]{1,0:T(8,128)(2,1)}, bf16[1584,384]{1,0:T(8,128)(2,1)}) custom-call(bf16[1584,768]{1,0:T(8,128)(2,1)} %get-tuple-element.109.rows_ref, bf16[3,768,384]{2,1,0:T(8,128)(2,1)} %pad_maximum_fusion.1.w_ref.refs_2_.refs_7_, f32[1584,128]{1,0:T(8,128)} %get-tuple-element.96.cos_ref, ...), custom_call_target="tpu_custom_call" | custom-call | flops 2802843648 | bytes 7852032 | tf_op jit(solution)/shard_map/project/pallas_call | solution.py:78
  73.6 1.0 broadcast_select_fusion.13
  74.6 0.9 pad_maximum_fusion.5.refs_4_
  75.5 13.5 %attend_forward.3 = (bf16[1024,384]{1,0:T(8,128)(2,1)}, f32[3,4,2,256]{3,2,1,0:T(2,128)}) custom-call(s32[4,2]{1,0:T(4,128)} %pad_add_fusion.1.span_ref, s32[4,2,256]{2,1,0:T(2,128)} %add_add_fusion.clean_ref, s32[4,2,128]{2,1,0:T(2,128)} %pad_add_fusion.noisy_ref, bf16[1584,384]{1,0:T(8,128)(2,1)} %get-tuple-element.120.q_ref, ...), custom_call_target="tpu_custom_call" | custom-call | flops 1610612736 | bytes 4866048 | tf_op jit(solution)/shard_map/attend_forward/pallas_call | solution.py:290
  89.0 91.9 %middle.1 = (bf16[1024,768]{1,0:T(8,128)(2,1)}, f32[1024,768]{1,0:T(8,128)}, bf16[1024,384]{1,0:T(8,128)(2,1)}, bf16[1024,384]{1,0:T(8,128)(2,1)}, bf16[256,1152...) custom-call(bf16[1024,768]{1,0:T(8,128)(2,1)} %bitcast.30, ...), custom_call_target="tpu_custom_call" | custom-call | flops 60000002048 | bytes 40000000 | tf_op jit(solution)/shard_map/middle/pallas_call | solution.py:1089
  180.9 2.2 collective-permute-start.12
  183.1 2.3 collective-permute-start.10
  185.4 0.7 slice.53
  186.1 0.7 slice_reduce_fusion
  186.9 2.1 collective-permute-start.14
  189.0 22.2 %attend_backward.2 = (bf16[3,1584,384]{2,1,0:T(8,128)(2,1)}, bf16[3,768,384]{2,1,0:T(8,128)(2,1)}) custom-call(s32[4,2]{1,0:T(4,128)} %pad_add_fusion.1.span_ref, s32[4,2,256]{2,1,0:T(2,128)} %add_add_fusion.clean_ref, s32[4,2,128]{2,1,0:T(2,128)} %pad_add_fusion.noisy_ref, bf16[1584,384]{1,0:T(8,128)(2,1)} %get-tuple-element.120.q_ref, ...), custom_call_target="tpu_custom_call" | custom-call | flops 35999997952 | bytes 36000000 | tf_op jit(solution)/shard_map/attend_backward/pallas_call | solution.py:503
  211.1 1.3 constant_dynamic-slice_fusion
  212.6 0.7 fusion.4
  213.4 0.3 broadcast_select_fusion.5
  213.7 1.2 collective-permute-done.9
  215.0 0.2 copy-done
  215.1 0.3 add_convert_fusion
  215.4 4.5 %collective-permute-start.13 = (bf16[9,128,384]{2,1,0:T(8,128)(2,1)S(1)}, bf16[9,128,384]{2,1,0:T(8,128)(2,1)}, u32[]{:S(2)}, u32[]{:S(2)}) collective-permute-start(bf16[9,128,384]{2,1,0:T(8,128)(2,1)S(1)} %add_convert_fusion), channel_id=1, source_target_pairs={{0,1},{1,0},{2,3},{3,2},{4,5},{5,4},{6,7},{7,6},{8,9},{9,8},{10,11... | collective-permute-start | bytes 2654216 | tf_op jit(solution)/shard_map/ppermute | solution.py:1664
  219.9 1.9 collective-permute-start.15
  221.8 19.8 %attend_backward.3 = (bf16[3,1584,384]{2,1,0:T(8,128)(2,1)}, f32[512,768]{1,0:T(8,128)}, bf16[512,768]{1,0:T(8,128)(2,1)}) custom-call(s32[4,2]{1,0:T(4,128)} %pad_add_fusion.1.span_ref, s32[4,2,256]{2,1,0:T(2,128)} %add_add_fusion.clean_ref, s32[4,2,128]{2,1,0:T(2,128)} %pad_add_fusion.noisy_ref, bf16[1584,384]{1,0:T(8,128)(2,1)} %get-tuple-element.101.q_ref, ...), custom_call_target="tpu_custom_call" | custom-call | flops 35999997952 | bytes 36000000 | tf_op jit(solution)/shard_map/attend_backward/pallas_call | solution.py:503
  241.6 4.7 %collective-permute-start.17 = (bf16[512,768]{1,0:T(8,128)(2,1)}, bf16[512,768]{1,0:T(8,128)(2,1)}, u32[]{:S(2)}, u32[]{:S(2)}) collective-permute-start(bf16[512,768]{1,0:T(8,128)(2,1)} %get-tuple-element.156), channel_id=1, source_target_pairs={{0,1},{1,0},{2,3},{3,2},{4,5},{5,4},{6,7},{7,6},{8,9},{9,8},{10,11... | collective-permute-start | bytes 2359304 | tf_op jit(solution)/shard_map/ppermute | solution.py:1664
  246.3 1.9 collective-permute-done.15
  248.1 0.2 broadcast_select_fusion.1
  248.3 1.6 pad_maximum_fusion.down_mine.up_mine
  250.0 52.5 %leave.1 = (bf16[3,768,384]{2,1,0:T(8,128)(2,1)}, bf16[384,768]{1,0:T(8,128)(2,1)}, f32[1024,768]{1,0:T(8,128)}, f32[16,768]{1,0:T(8,128)}) custom-call(bf16[768,1584]{1,0:T(8,128)(2,1)} %get-tuple-element.131.refs_0_, bf16[256,1152]{1,0:T(8,128)(2,1)} %get-tuple-element.132.refs_1_, bf16[9,128,384]{2,1,0:T(8,128)(2,1)} %collective-permute-done.13.refs_2_, ...), custom_call_target="tpu_custom_call" | custom-call | flops 40000000000 | bytes 40000000 | tf_op jit(solution)/shard_map/leave/pallas_call | solution.py:1454
  302.4 0.7 slice.58
  303.2 0.6 reshape.343
  303.8 1.6 slice_reduce_fusion.2
  305.4 8.4 %finish.1 = f32[1024,768]{1,0:T(8,128)} custom-call(f32[1024,768]{1,0:T(8,128)} %get-tuple-element.154.rows_ref, bf16[512,768]{1,0:T(8,128)(2,1)} %collective-permute-done.17.got_ref, bf16[1024,768]{1,0:T(8,128)(2,1)} %bitcast.32, f32[5,768]{1,0:T(8,128)} %stack.29.vectors_ref.refs_6_, f32[1024,768]{1,0:T(8,128)} %get-tuple-element.159.dmid_ref), custom_call_target="tpu_custom_call" | custom-call | flops 10000000 | bytes 12000000 | tf_op jit(solution)/shard_map/finish/pallas_call | solution.py:1513
  313.8 9.0 %assemble.1 = (f32[1536,768]{1,0:T(8,128)}, f32[768,1536]{1,0:T(8,128)}, f32[2304,384]{1,0:T(8,128)}, f32[384,768]{1,0:T(8,128)}) custom-call(s32[1]{0:T(128)} %bitcast.18.core_ref, bf16[12,128,768]{2,1,0:T(8,128)(2,1)} %pad_maximum_fusion.down_mine.up_mine, bf16[12,128,768]{2,1,0:T(8,128)(2,1)} %pad_maximum_fusion.down_mine.up_mine, ...), custom_call_target="tpu_custom_call" | custom-call | flops 1000000 | bytes 14000000 | tf_op jit(solution)/shard_map/assemble/pallas_call | solution.py:1561
  322.8 1.1 copy.38
  (65 shorter events, 0.7 us)
Async XLA Ops:
  0.6 5.8 %copy-start.12 = (s32[1,4]{1,0:T(1,128)S(1)}, s32[1,4]{1,0:T(1,128)}, u32[]{:S(2)}) copy-start(s32[1,4]{1,0:T(1,128)} %param.15) | copy-start | bytes 52
  0.7 6.0 %copy-start.5 = (f32[768]{0:T(1024)S(1)}, f32[768]{0:T(1024)}, u32[]{:S(2)}) copy-start(f32[768]{0:T(1024)} %param.18) | copy-start | bytes 9220
  0.7 6.0 %copy-start.6 = (f32[768]{0:T(1024)S(1)}, f32[768]{0:T(1024)}, u32[]{:S(2)}) copy-start(f32[768]{0:T(1024)} %param.19) | copy-start | bytes 9220
  0.7 6.0 %copy-start.7 = (f32[768]{0:T(1024)S(1)}, f32[768]{0:T(1024)}, u32[]{:S(2)}) copy-start(f32[768]{0:T(1024)} %param.22) | copy-start | bytes 9220
  0.7 6.1 %copy-start.8 = (f32[768]{0:T(1024)S(1)}, f32[768]{0:T(1024)}, u32[]{:S(2)}) copy-start(f32[768]{0:T(1024)} %param.23) | copy-start | bytes 9220
  0.7 6.1 %copy-start.9 = (f32[768]{0:T(1024)S(1)}, f32[768]{0:T(1024)}, u32[]{:S(2)}) copy-start(f32[768]{0:T(1024)} %param.27) | copy-start | bytes 9220
  0.7 8.9 %copy-start.4 = (bf16[384,768]{1,0:T(8,128)(2,1)S(1)}, bf16[384,768]{1,0:T(8,128)(2,1)}, u32[]{:S(2)}) copy-start(bf16[384,768]{1,0:T(8,128)(2,1)} %refs_3_.1) | copy-start | bytes 1769476
  2.8 21.2 %collective-permute-start = (bf16[528,768]{1,0:T(8,128)(2,1)S(1)}, bf16[528,768]{1,0:T(8,128)(2,1)}, u32[]{:S(2)}, u32[]{:S(2)}) collective-permute-start(bf16[528,768]{1,0:T(8,128)(2,1)S(1)} %pad_maximum_fusion.4), channel_id=1, source_target_pairs={{0,1},{1,0},{2,3},{3,2},{4,5},{5,4},{6,7},{7,6},{8,9},{9,8},{10,11... | collective-permute-start | bytes 2433032 | tf_op jit(solution)/shard_map/ppermute | solution.py:1664
  24.0 13.5 %collective-permute-start.1 = (bf16[3,192,384]{2,1,0:T(8,128)(2,1)S(1)}, bf16[3,192,384]{2,1,0:T(8,128)(2,1)S(1)}, u32[]{:S(2)}, u32[]{:S(2)}) collective-permute-start(bf16[3,192,384]{2,1,0:T(8,128)(2,1)S(1)} %dynamic-slice_bitcast_fusion), channel_id=1, source_target_pairs={{0,1},{1,0},{2,3},{3,2},{4,5},{5,4},{6,7},{7,6},{8,9},{9,8},{10,11... | collective-permute-start | bytes 1327112 | tf_op jit(solution)/shard_map/ppermute | solution.py:1664
  25.7 28.6 %collective-permute-start.3 = (bf16[192,1536]{1,0:T(8,128)(2,1)S(1)}, bf16[192,1536]{1,0:T(8,128)(2,1)}, u32[]{:S(2)}, u32[]{:S(2)}) collective-permute-start(bf16[192,1536]{1,0:T(8,128)(2,1)S(1)} %constant_dynamic-slice_fusion.3), channel_id=1, source_target_pairs={{0,1},{1,0},{2,3},{3,2},{4,5},{5,4},{6,7},{7,6},{8,9},{9,8},{10,11... | collective-permute-start | bytes 1769480 | tf_op jit(solution)/shard_map/ppermute | solution.py:1664
  26.0 13.2 %copy-start.2 = (bf16[192,768]{1,0:T(8,128)(2,1)S(1)}, bf16[192,768]{1,0:T(8,128)(2,1)}, u32[]{:S(2)}) copy-start(bf16[192,768]{1,0:T(8,128)(2,1)} %constant_dynamic-slice_fusion.1) | copy-start | bytes 884740
  37.5 16.9 %collective-permute-start.2 = (bf16[3,192,384]{2,1,0:T(8,128)(2,1)S(1)}, bf16[3,192,384]{2,1,0:T(8,128)(2,1)S(1)}, u32[]{:S(2)}, u32[]{:S(2)}) collective-permute-start(bf16[3,192,384]{2,1,0:T(8,128)(2,1)S(1)} %collective-permute-done.1), channel_id=1, source_target_pairs={{0,4},{2,6},{4,0},{6,2},{8,12},{10,14},{12,8},{14,10},{16,20},{18,... | collective-permute-start | bytes 1327112 | tf_op jit(solution)/shard_map/ppermute | solution.py:1670
  39.2 15.1 %collective-permute-start.4 = (bf16[192,768]{1,0:T(8,128)(2,1)S(1)}, bf16[192,768]{1,0:T(8,128)(2,1)S(1)}, u32[]{:S(2)}, u32[]{:S(2)}) collective-permute-start(bf16[192,768]{1,0:T(8,128)(2,1)S(1)} %copy-done.2), channel_id=1, source_target_pairs={{0,1},{1,0},{2,3},{3,2},{4,5},{5,4},{6,7},{7,6},{8,9},{9,8},{10,11... | collective-permute-start | bytes 884744 | tf_op jit(solution)/shard_map/ppermute | solution.py:1664
  54.3 1.2 copy-start.10
  54.5 8.8 %collective-permute-start.6 = (bf16[3,384,384]{2,1,0:T(8,128)(2,1)S(1)}, bf16[3,384,384]{2,1,0:T(8,128)(2,1)}, u32[]{:S(2)}, u32[]{:S(2)}) collective-permute-start(bf16[3,384,384]{2,1,0:T(8,128)(2,1)S(1)} %pad_maximum_fusion.3), channel_id=1, source_target_pairs={{0,2},{2,0},{4,6},{6,4},{8,10},{10,8},{12,14},{14,12},{16,18},{18,... | collective-permute-start | bytes 2654216 | tf_op jit(solution)/shard_map/ppermute | solution.py:1667
  56.7 32.3 %collective-permute-start.8 = (bf16[768,768]{1,0:T(8,128)(2,1)S(1)}, bf16[768,768]{1,0:T(8,128)(2,1)}, u32[]{:S(2)}, u32[]{:S(2)}) collective-permute-start(bf16[768,768]{1,0:T(8,128)(2,1)S(1)} %constant_dynamic-slice_fusion.2), channel_id=1, source_target_pairs={{0,1},{1,0},{2,3},{3,2},{4,5},{5,4},{6,7},{7,6},{8,9},{9,8},{10,11... | collective-permute-start | bytes 3538952 | tf_op jit(solution)/shard_map/ppermute | solution.py:1664
  61.9 11.7 %collective-permute-start.5 = (bf16[192,768]{1,0:T(8,128)(2,1)S(1)}, bf16[192,768]{1,0:T(8,128)(2,1)}, u32[]{:S(2)}, u32[]{:S(2)}) collective-permute-start(bf16[192,768]{1,0:T(8,128)(2,1)S(1)} %collective-permute-done.4), channel_id=1, source_target_pairs={{0,2},{2,0},{4,6},{6,4},{8,10},{10,8},{12,14},{14,12},{16,18},{18,... | collective-permute-start | bytes 884744 | tf_op jit(solution)/shard_map/ppermute | solution.py:1667
  61.9 27.1 %collective-permute-start.7 = (bf16[192,1536]{1,0:T(8,128)(2,1)}, bf16[192,1536]{1,0:T(8,128)(2,1)}, u32[]{:S(2)}, u32[]{:S(2)}) collective-permute-start(bf16[192,1536]{1,0:T(8,128)(2,1)} %collective-permute-done.3.refs_9_), channel_id=1, source_target_pairs={{0,4},{2,6},{4,0},{6,2},{8,12},{10,14},{12,8},{14,10},{16,20},{18,... | collective-permute-start | bytes 1769480 | tf_op jit(solution)/shard_map/ppermute | solution.py:1670
  180.9 32.3 %collective-permute-start.12 = (bf16[12,16,768]{2,1,0:T(8,128)(2,1)}, bf16[12,16,768]{2,1,0:T(8,128)(2,1)S(1)}, u32[]{:S(2)}, u32[]{:S(2)}) collective-permute-start(bf16[12,16,768]{2,1,0:T(8,128)(2,1)} %get-tuple-element.136), channel_id=1, source_target_pairs={{0,24},{2,26},{4,28},{6,30},{8,16},{10,18},{12,20},{14,22},{16,8},... | collective-permute-start | bytes 884744 | tf_op jit(solution)/shard_map/ppermute | solution.py:1732
  183.1 30.2 %collective-permute-start.11 = (bf16[12,16,768]{2,1,0:T(8,128)(2,1)}, bf16[12,16,768]{2,1,0:T(8,128)(2,1)S(1)}, u32[]{:S(2)}, u32[]{:S(2)}) collective-permute-start(bf16[12,16,768]{2,1,0:T(8,128)(2,1)} %get-tuple-element.136), channel_id=1, source_target_pairs={{0,16},{2,18},{4,20},{6,22},{8,24},{10,26},{12,28},{14,30},{16,0},... | collective-permute-start | bytes 884744 | tf_op jit(solution)/shard_map/ppermute | solution.py:1732
  183.1 30.2 %collective-permute-start.10 = (bf16[12,16,768]{2,1,0:T(8,128)(2,1)}, bf16[12,16,768]{2,1,0:T(8,128)(2,1)S(1)}, u32[]{:S(2)}, u32[]{:S(2)}) collective-permute-start(bf16[12,16,768]{2,1,0:T(8,128)(2,1)} %get-tuple-element.136), channel_id=1, source_target_pairs={{0,8},{2,10},{4,12},{6,14},{8,0},{10,2},{12,4},{14,6},{16,24},{18,... | collective-permute-start | bytes 884744 | tf_op jit(solution)/shard_map/ppermute | solution.py:1732
  186.9 63.1 %collective-permute-start.14 = (bf16[256,1152]{1,0:T(8,128)(2,1)}, bf16[256,1152]{1,0:T(8,128)(2,1)}, u32[]{:S(2)}, u32[]{:S(2)}) collective-permute-start(bf16[256,1152]{1,0:T(8,128)(2,1)} %get-tuple-element.141), channel_id=1, source_target_pairs={{0,1},{1,0},{2,3},{3,2},{4,5},{5,4},{6,7},{7,6},{8,9},{9,8},{10,11... | collective-permute-start | bytes 1769480 | tf_op jit(solution)/shard_map/ppermute | solution.py:1664
  211.1 1.4 copy-start.11
  211.1 2.1 copy-start.3
  212.5 2.5 collective-permute-start.9
  213.6 1.5 copy-start
  215.4 34.6 %collective-permute-start.13 = (bf16[9,128,384]{2,1,0:T(8,128)(2,1)S(1)}, bf16[9,128,384]{2,1,0:T(8,128)(2,1)}, u32[]{:S(2)}, u32[]{:S(2)}) collective-permute-start(bf16[9,128,384]{2,1,0:T(8,128)(2,1)S(1)} %add_convert_fusion), channel_id=1, source_target_pairs={{0,1},{1,0},{2,3},{3,2},{4,5},{5,4},{6,7},{7,6},{8,9},{9,8},{10,11... | collective-permute-start | bytes 2654216 | tf_op jit(solution)/shard_map/ppermute | solution.py:1664
  219.9 28.2 %collective-permute-start.15 = (bf16[12,64,768]{2,1,0:T(8,128)(2,1)S(1)}, bf16[12,64,768]{2,1,0:T(8,128)(2,1)S(1)}, u32[]{:S(2)}, u32[]{:S(2)}) collective-permute-start(bf16[12,64,768]{2,1,0:T(8,128)(2,1)S(1)} %pad_maximum_fusion.2), channel_id=1, source_target_pairs={{0,4},{2,6},{4,0},{6,2},{8,12},{10,14},{12,8},{14,10},{16,20},{18,... | collective-permute-start | bytes 3538952 | tf_op jit(solution)/shard_map/ppermute | solution.py:1670
  241.6 63.8 %collective-permute-start.17 = (bf16[512,768]{1,0:T(8,128)(2,1)}, bf16[512,768]{1,0:T(8,128)(2,1)}, u32[]{:S(2)}, u32[]{:S(2)}) collective-permute-start(bf16[512,768]{1,0:T(8,128)(2,1)} %get-tuple-element.156), channel_id=1, source_target_pairs={{0,1},{1,0},{2,3},{3,2},{4,5},{5,4},{6,7},{7,6},{8,9},{9,8},{10,11... | collective-permute-start | bytes 2359304 | tf_op jit(solution)/shard_map/ppermute | solution.py:1664
  249.9 55.4 %collective-permute-start.16 = (bf16[12,128,768]{2,1,0:T(8,128)(2,1)}, bf16[12,128,768]{2,1,0:T(8,128)(2,1)}, u32[]{:S(2)}, u32[]{:S(2)}) collective-permute-start(bf16[12,128,768]{2,1,0:T(8,128)(2,1)} %pad_maximum_fusion.down_mine.up_mine), channel_id=1, source_target_pairs={{0,2},{2,0},{4,6},{6,4},{8,10},{10,8},{12,14},{14,12},{16,18},{18,... | collective-permute-start | bytes 7077896 | tf_op jit(solution)/shard_map/ppermute | solution.py:1667
  313.8 9.0 %copy-start.1 = (bf16[1024,768]{1,0:T(8,128)(2,1)S(1)}, bf16[1024,768]{1,0:T(8,128)(2,1)}, u32[]{:S(2)}) copy-start(bf16[1024,768]{1,0:T(8,128)(2,1)} %get-tuple-element.130) | copy-start | bytes 4718596

commit v9 on v8

--- a/solution.py
+++ b/solution.py
@@ -1000,7 +1000,7 @@
         each((i - 3) // 2, odd, stage_c)
         each(i // 2, even, stage_b)
 
-    def epilogue(r, _):
+    def epilogue(r):
         rows = pl.ds(pl.multiple_of(r * ROW_TILE, ROW_TILE), ROW_TILE)
         out_ref[rows, :] = total_ref[rows, :].astype(bf16)
         unit, scale = normal(mid_ref[rows, :])
@@ -1021,7 +1021,6 @@
         small_ref[0:1, :] += add(d_rows * unit)
         small_ref[1:2, :] += add(d_rows)
         small_ref[2:3, :] += add(dy)
-        return 0
 
     def out_grads():
         for source, target in ((att_ref, gout_ref), (att2_ref, gout2_ref)):
@@ -1039,7 +1038,8 @@
         @pl.when(jnp.logical_and(i >= tiles, i < tiles + 2))
         def _():
             first = (i - tiles) * (blocks // 2)
-            lax.fori_loop(first, first + blocks // 2, epilogue, 0)
+            for r in range(blocks // 2):
+                epilogue(first + r)
 
         @pl.when(i == tiles + 2)
         def _():
@@ -1508,14 +1508,14 @@
 
 def finish(rows, got, tokens, vectors, d_mid):
     count, width = rows.shape
-    spec = pl.BlockSpec((TILE, width), lambda b: (b, 0))
-    half = count // TILE // 2
+    spec = pl.BlockSpec((ROW_TILE, width), lambda b: (b, 0))
+    half = count // ROW_TILE // 2
     return pl.pallas_call(
         finish_kernel,
-        grid=(count // TILE,),
+        grid=(count // ROW_TILE,),
         in_specs=[
             spec,
-            pl.BlockSpec((TILE, width), lambda b: (jnp.maximum(b - half, 0), 0)),
+            pl.BlockSpec((ROW_TILE, width), lambda b: (jnp.maximum(b - half, 0), 0)),
             spec,
             pl.BlockSpec(vectors.shape, lambda b: (0, 0)),
             spec,

time: 329 us -> 326 us (level); the launches traced: 324 us -> 325 us
  starting transfers between devices: 33.6 us -> 28.6 us
  Pallas kernels: 250 us -> 254 us
    ppermute x8, starting transfers between devices: 23.1 us -> 16.6 us  [across(): return lax.ppermute(array, 'mp', [(0, 1), (1, 0)])]
    pallas_call x2, Pallas kernels: 27.1 us -> 31.3 us  [attend_forward(): pl.pallas_call(forward_kernel, in_specs=[pl.BlockSpec(memory_space=pltpu....]
    pallas_call x2, Pallas kernels: 41.9 us -> 45.4 us  [attend_backward(): pl.pallas_call(functools.partial(backward_kernel, giving), in_specs=[pl.B...]
  transfers between devices with their start and end apart: 18 -> 18, of which waited for: 4 -> 3; matrix products, arithmetic and copies ran while one was open for 8% -> 8% of each run, Pallas kernels for 43% -> 46%
where the time goes in v9:
time: 326 us; the launch traced here: 325 us
  Pallas kernels  254 us (78%)
  starting transfers between devices  28.6 us (9%)
  other arithmetic  16.1 us (5%)
  local copies, waits for them, and re-layouts  15 us (5%)
  waiting for transfers between devices  9.48 us (3%)
    pallas_call x1, Pallas kernels, middle(): pl.pallas_call(functools.partial(middle_kernel, exchanges, tiles), in_spe...  90.5 us
    pallas_call x1, Pallas kernels, leave(): pl.pallas_call(functools.partial(leave_kernel, exchange), in_specs=[hbm]...  52.4 us
    pallas_call x2, Pallas kernels, attend_backward(): pl.pallas_call(functools.partial(backward_kernel, giving), in_specs=[pl.B...  45.4 us
    pallas_call x2, Pallas kernels, attend_forward(): pl.pallas_call(forward_kernel, in_specs=[pl.BlockSpec(memory_space=pltpu....  31.3 us
    ppermute x8, starting transfers between devices, across(): return lax.ppermute(array, 'mp', [(0, 1), (1, 0)])  16.6 us
    pallas_call x1, Pallas kernels, enter(): pl.pallas_call(enter_kernel, in_specs=[vmem] * 6, out_specs=[vmem] * 5, o...  11.4 us
    pallas_call x1, Pallas kernels, assemble(): pl.pallas_call(assemble_kernel, grid_spec=pltpu.PrefetchScalarGridSpec(nu...  9 us
    ppermute x3, starting transfers between devices, beside(): return lax.ppermute(array, 'dp', [(i, i ^ 2) for i in range(dp_size)])  7.41 us
  transfers between devices with their start and end apart: 18, of which 3 were waited for; matrix products, arithmetic and copies ran while one was open for 8% of the time, Pallas kernels for 46%

profile of v9, /device:TPU:0, one launch (start us, length us, event | category | flops | bytes accessed | tf_op | source)
XLA Modules:
  0.0 324.9 jit_solution(8072547118185820902)
XLA Ops:
  0.7 1.3 slice_bitcast_fusion
  2.0 0.8 select_bitcast_fusion
  2.8 3.0 collective-permute-start
  6.5 0.2 reduce-window.8
  6.8 0.1 fusion.2
  6.9 0.2 reduce_min.21
  7.1 0.1 copy.31
  7.2 0.1 subtract_convert_fusion
  7.3 0.3 fusion.16
  7.6 0.1 copy.35
  7.7 0.7 pad_add_fusion.1.span_ref
  8.4 0.6 pad_add_fusion.noisy_ref
  9.0 0.6 add_add_fusion.clean_ref
  9.6 0.7 constant_dynamic-slice_fusion.1
  10.3 1.1 dynamic-slice_bitcast_fusion
  11.4 1.4 constant_dynamic-slice_fusion.2
  12.7 0.6 stack.29.vectors_ref.refs_6_
  13.4 1.1 constant_dynamic-slice_fusion.3
  14.5 4.4 %fusion = (f32[1584,128]{1,0:T(8,128)}, f32[1584,128]{1,0:T(8,128)}) fusion(f32[128]{0:T(128)S(1)} %get-tuple-element.207, f32[128]{0:T(128)S(1)} %get-tuple-element.208, f32[1584]{0:T(1024)S(1)} %get-tuple-element.201), kind=kLoop, calls=%fused_computation.11 | loop fusion | flops 405504 | bytes 1629376 | tf_op jit(solution)/shard_map/mul | solution.py:1626
  18.9 5.1 %collective-permute-done.context_ref.refs_9_ = bf16[528,768]{1,0:T(8,128)(2,1)} collective-permute-done((bf16[528,768]{1,0:T(8,128)(2,1)S(1)}, bf16[528,768]{1,0:T(8,128)(2,1)}, u32[]{:S(2)}, u32[]{:S(2)}) %collective-permute-start) | collective-permute-done | bytes 811040 | tf_op jit(solution)/shard_map/ppermute | solution.py:1664
  24.0 1.7 collective-permute-start.1
  25.7 0.3 collective-permute-start.3
  26.0 11.4 %enter.1 = (bf16[1584,768]{1,0:T(8,128)(2,1)}, bf16[768,1584]{1,0:T(8,128)(2,1)}, bf16[1584,384]{1,0:T(8,128)(2,1)}, bf16[1584,384]{1,0:T(8,128)(2,1)}, bf16[1584,384]{1,0:T(8,128)(2,1)}) custom-call(bf16[2,512,768]{2,1,0:T(8,128)(2,1)} %tokens_ref.1, bf16[528,768]{1,0:T(8,128)(2,1)} %collective-permute-done.context_ref.refs_9_, ...), custom_call_target="tpu_custom_call" | custom-call | flops 10000000000 | bytes 16000000 | tf_op jit(solution)/shard_map/enter/pallas_call | solution.py:157
  37.5 1.7 collective-permute-start.2
  39.2 1.5 collective-permute-start.4
  40.7 15.6 %attend_forward.2 = (bf16[1024,384]{1,0:T(8,128)(2,1)}, f32[3,4,2,256]{3,2,1,0:T(2,128)}) custom-call(s32[4,2]{1,0:T(4,128)} %pad_add_fusion.1.span_ref, s32[4,2,256]{2,1,0:T(2,128)} %add_add_fusion.clean_ref, s32[4,2,128]{2,1,0:T(2,128)} %pad_add_fusion.noisy_ref, bf16[1584,384]{1,0:T(8,128)(2,1)} %get-tuple-element.101.q_ref, ...), custom_call_target="tpu_custom_call" | custom-call | flops 1610612736 | bytes 4866048 | tf_op jit(solution)/shard_map/attend_forward/pallas_call | solution.py:290
  56.7 0.4 copy-done.10
  57.1 0.6 reshape.345.refs_7_
  57.7 0.6 pad.5.clone
  58.2 2.6 collective-permute-start.8
  60.9 2.5 collective-permute-start.7
  63.3 1.5 broadcast_select_fusion.3
  64.8 1.4 pad_maximum_fusion.1.w_ref.refs_2_.refs_7_
  66.3 7.4 %project.1 = (bf16[1584,384]{1,0:T(8,128)(2,1)}, bf16[1584,384]{1,0:T(8,128)(2,1)}, bf16[1584,384]{1,0:T(8,128)(2,1)}) custom-call(bf16[1584,768]{1,0:T(8,128)(2,1)} %get-tuple-element.109.rows_ref, bf16[3,768,384]{2,1,0:T(8,128)(2,1)} %pad_maximum_fusion.1.w_ref.refs_2_.refs_7_, f32[1584,128]{1,0:T(8,128)} %get-tuple-element.96.cos_ref, ...), custom_call_target="tpu_custom_call" | custom-call | flops 2802843648 | bytes 7852032 | tf_op jit(solution)/shard_map/project/pallas_call | solution.py:78
  73.6 1.0 broadcast_select_fusion.13
  74.6 0.9 pad_maximum_fusion.5.refs_4_
  75.5 15.6 %attend_forward.3 = (bf16[1024,384]{1,0:T(8,128)(2,1)}, f32[3,4,2,256]{3,2,1,0:T(2,128)}) custom-call(s32[4,2]{1,0:T(4,128)} %pad_add_fusion.1.span_ref, s32[4,2,256]{2,1,0:T(2,128)} %add_add_fusion.clean_ref, s32[4,2,128]{2,1,0:T(2,128)} %pad_add_fusion.noisy_ref, bf16[1584,384]{1,0:T(8,128)(2,1)} %get-tuple-element.120.q_ref, ...), custom_call_target="tpu_custom_call" | custom-call | flops 1610612736 | bytes 4866048 | tf_op jit(solution)/shard_map/attend_forward/pallas_call | solution.py:290
  91.1 90.5 %middle.1 = (bf16[1024,768]{1,0:T(8,128)(2,1)}, f32[1024,768]{1,0:T(8,128)}, bf16[1024,384]{1,0:T(8,128)(2,1)}, bf16[1024,384]{1,0:T(8,128)(2,1)}, bf16[256,1152...) custom-call(bf16[1024,768]{1,0:T(8,128)(2,1)} %bitcast.30, ...), custom_call_target="tpu_custom_call" | custom-call | flops 60000002048 | bytes 40000000 | tf_op jit(solution)/shard_map/middle/pallas_call | solution.py:1089
  181.6 2.5 collective-permute-start.12
  184.1 2.0 collective-permute-start.10
  186.0 0.7 slice.53
  186.8 0.7 slice_reduce_fusion
  187.6 3.5 %collective-permute-start.14 = (bf16[256,1152]{1,0:T(8,128)(2,1)}, bf16[256,1152]{1,0:T(8,128)(2,1)}, u32[]{:S(2)}, u32[]{:S(2)}) collective-permute-start(bf16[256,1152]{1,0:T(8,128)(2,1)} %get-tuple-element.141), channel_id=1, source_target_pairs={{0,1},{1,0},{2,3},{3,2},{4,5},{5,4},{6,7},{7,6},{8,9},{9,8},{10,11... | collective-permute-start | bytes 1769480 | tf_op jit(solution)/shard_map/ppermute | solution.py:1664
  191.1 24.2 %attend_backward.2 = (bf16[3,1584,384]{2,1,0:T(8,128)(2,1)}, bf16[3,768,384]{2,1,0:T(8,128)(2,1)}) custom-call(s32[4,2]{1,0:T(4,128)} %pad_add_fusion.1.span_ref, s32[4,2,256]{2,1,0:T(2,128)} %add_add_fusion.clean_ref, s32[4,2,128]{2,1,0:T(2,128)} %pad_add_fusion.noisy_ref, bf16[1584,384]{1,0:T(8,128)(2,1)} %get-tuple-element.120.q_ref, ...), custom_call_target="tpu_custom_call" | custom-call | flops 35999997952 | bytes 36000000 | tf_op jit(solution)/shard_map/attend_backward/pallas_call | solution.py:503
  215.3 1.3 constant_dynamic-slice_fusion
  216.7 0.7 fusion.4
  217.5 0.3 broadcast_select_fusion.5
  217.9 1.2 collective-permute-done.9
  219.1 0.2 copy-done
  219.2 0.3 add_convert_fusion
  219.5 1.9 collective-permute-start.13
  221.4 3.2 %collective-permute-start.15 = (bf16[12,64,768]{2,1,0:T(8,128)(2,1)S(1)}, bf16[12,64,768]{2,1,0:T(8,128)(2,1)S(1)}, u32[]{:S(2)}, u32[]{:S(2)}) collective-permute-start(bf16[12,64,768]{2,1,0:T(8,128)(2,1)S(1)} %pad_maximum_fusion.2), channel_id=1, source_target_pairs={{0,4},{2,6},{4,0},{6,2},{8,12},{10,14},{12,8},{14,10},{16,20},{18,... | collective-permute-start | bytes 3538952 | tf_op jit(solution)/shard_map/ppermute | solution.py:1670
  224.6 21.3 %attend_backward.3 = (bf16[3,1584,384]{2,1,0:T(8,128)(2,1)}, f32[512,768]{1,0:T(8,128)}, bf16[512,768]{1,0:T(8,128)(2,1)}) custom-call(s32[4,2]{1,0:T(4,128)} %pad_add_fusion.1.span_ref, s32[4,2,256]{2,1,0:T(2,128)} %add_add_fusion.clean_ref, s32[4,2,128]{2,1,0:T(2,128)} %pad_add_fusion.noisy_ref, bf16[1584,384]{1,0:T(8,128)(2,1)} %get-tuple-element.101.q_ref, ...), custom_call_target="tpu_custom_call" | custom-call | flops 35999997952 | bytes 36000000 | tf_op jit(solution)/shard_map/attend_backward/pallas_call | solution.py:503
  245.9 2.0 collective-permute-start.17
  247.9 3.1 collective-permute-done.15
  251.0 0.2 broadcast_select_fusion.1
  251.1 1.6 pad_maximum_fusion.down_mine.up_mine
  252.8 52.4 %leave.1 = (bf16[3,768,384]{2,1,0:T(8,128)(2,1)}, bf16[384,768]{1,0:T(8,128)(2,1)}, f32[1024,768]{1,0:T(8,128)}, f32[16,768]{1,0:T(8,128)}) custom-call(bf16[768,1584]{1,0:T(8,128)(2,1)} %get-tuple-element.131.refs_0_, bf16[256,1152]{1,0:T(8,128)(2,1)} %get-tuple-element.132.refs_1_, bf16[9,128,384]{2,1,0:T(8,128)(2,1)} %collective-permute-done.13.refs_2_, ...), custom_call_target="tpu_custom_call" | custom-call | flops 40000000000 | bytes 40000000 | tf_op jit(solution)/shard_map/leave/pallas_call | solution.py:1454
  305.2 0.7 slice.58
  306.0 0.6 reshape.343
  306.6 1.6 slice_reduce_fusion.2
  308.2 6.6 %finish.1 = f32[1024,768]{1,0:T(8,128)} custom-call(f32[1024,768]{1,0:T(8,128)} %get-tuple-element.154.rows_ref, bf16[512,768]{1,0:T(8,128)(2,1)} %collective-permute-done.17.got_ref, bf16[1024,768]{1,0:T(8,128)(2,1)} %bitcast.32, f32[5,768]{1,0:T(8,128)} %stack.29.vectors_ref.refs_6_, f32[1024,768]{1,0:T(8,128)} %get-tuple-element.159.dmid_ref), custom_call_target="tpu_custom_call" | custom-call | flops 10000000 | bytes 12000000 | tf_op jit(solution)/shard_map/finish/pallas_call | solution.py:1513
  314.7 9.0 %assemble.1 = (f32[1536,768]{1,0:T(8,128)}, f32[768,1536]{1,0:T(8,128)}, f32[2304,384]{1,0:T(8,128)}, f32[384,768]{1,0:T(8,128)}) custom-call(s32[1]{0:T(128)} %bitcast.18.core_ref, bf16[12,128,768]{2,1,0:T(8,128)(2,1)} %pad_maximum_fusion.down_mine.up_mine, bf16[12,128,768]{2,1,0:T(8,128)(2,1)} %pad_maximum_fusion.down_mine.up_mine, ...), custom_call_target="tpu_custom_call" | custom-call | flops 1000000 | bytes 14000000 | tf_op jit(solution)/shard_map/assemble/pallas_call | solution.py:1561
  323.7 1.1 copy.38
  (65 shorter events, 0.8 us)
Async XLA Ops:
  0.6 5.8 %copy-start.12 = (s32[1,4]{1,0:T(1,128)S(1)}, s32[1,4]{1,0:T(1,128)}, u32[]{:S(2)}) copy-start(s32[1,4]{1,0:T(1,128)} %param.15) | copy-start | bytes 52
  0.7 6.0 %copy-start.5 = (f32[768]{0:T(1024)S(1)}, f32[768]{0:T(1024)}, u32[]{:S(2)}) copy-start(f32[768]{0:T(1024)} %param.18) | copy-start | bytes 9220
  0.7 6.0 %copy-start.6 = (f32[768]{0:T(1024)S(1)}, f32[768]{0:T(1024)}, u32[]{:S(2)}) copy-start(f32[768]{0:T(1024)} %param.19) | copy-start | bytes 9220
  0.7 6.0 %copy-start.7 = (f32[768]{0:T(1024)S(1)}, f32[768]{0:T(1024)}, u32[]{:S(2)}) copy-start(f32[768]{0:T(1024)} %param.22) | copy-start | bytes 9220
  0.7 6.1 %copy-start.8 = (f32[768]{0:T(1024)S(1)}, f32[768]{0:T(1024)}, u32[]{:S(2)}) copy-start(f32[768]{0:T(1024)} %param.23) | copy-start | bytes 9220
  0.7 6.1 %copy-start.9 = (f32[768]{0:T(1024)S(1)}, f32[768]{0:T(1024)}, u32[]{:S(2)}) copy-start(f32[768]{0:T(1024)} %param.27) | copy-start | bytes 9220
  0.7 8.9 %copy-start.4 = (bf16[384,768]{1,0:T(8,128)(2,1)S(1)}, bf16[384,768]{1,0:T(8,128)(2,1)}, u32[]{:S(2)}) copy-start(bf16[384,768]{1,0:T(8,128)(2,1)} %refs_3_.1) | copy-start | bytes 1769476
  2.8 21.2 %collective-permute-start = (bf16[528,768]{1,0:T(8,128)(2,1)S(1)}, bf16[528,768]{1,0:T(8,128)(2,1)}, u32[]{:S(2)}, u32[]{:S(2)}) collective-permute-start(bf16[528,768]{1,0:T(8,128)(2,1)S(1)} %pad_maximum_fusion.4), channel_id=1, source_target_pairs={{0,1},{1,0},{2,3},{3,2},{4,5},{5,4},{6,7},{7,6},{8,9},{9,8},{10,11... | collective-permute-start | bytes 2433032 | tf_op jit(solution)/shard_map/ppermute | solution.py:1664
  24.0 13.5 %collective-permute-start.1 = (bf16[3,192,384]{2,1,0:T(8,128)(2,1)S(1)}, bf16[3,192,384]{2,1,0:T(8,128)(2,1)S(1)}, u32[]{:S(2)}, u32[]{:S(2)}) collective-permute-start(bf16[3,192,384]{2,1,0:T(8,128)(2,1)S(1)} %dynamic-slice_bitcast_fusion), channel_id=1, source_target_pairs={{0,1},{1,0},{2,3},{3,2},{4,5},{5,4},{6,7},{7,6},{8,9},{9,8},{10,11... | collective-permute-start | bytes 1327112 | tf_op jit(solution)/shard_map/ppermute | solution.py:1664
  25.7 30.6 %collective-permute-start.3 = (bf16[192,1536]{1,0:T(8,128)(2,1)S(1)}, bf16[192,1536]{1,0:T(8,128)(2,1)}, u32[]{:S(2)}, u32[]{:S(2)}) collective-permute-start(bf16[192,1536]{1,0:T(8,128)(2,1)S(1)} %constant_dynamic-slice_fusion.3), channel_id=1, source_target_pairs={{0,1},{1,0},{2,3},{3,2},{4,5},{5,4},{6,7},{7,6},{8,9},{9,8},{10,11... | collective-permute-start | bytes 1769480 | tf_op jit(solution)/shard_map/ppermute | solution.py:1664
  26.0 13.2 %copy-start.2 = (bf16[192,768]{1,0:T(8,128)(2,1)S(1)}, bf16[192,768]{1,0:T(8,128)(2,1)}, u32[]{:S(2)}) copy-start(bf16[192,768]{1,0:T(8,128)(2,1)} %constant_dynamic-slice_fusion.1) | copy-start | bytes 884740
  37.5 18.9 %collective-permute-start.2 = (bf16[3,192,384]{2,1,0:T(8,128)(2,1)S(1)}, bf16[3,192,384]{2,1,0:T(8,128)(2,1)S(1)}, u32[]{:S(2)}, u32[]{:S(2)}) collective-permute-start(bf16[3,192,384]{2,1,0:T(8,128)(2,1)S(1)} %collective-permute-done.1), channel_id=1, source_target_pairs={{0,4},{2,6},{4,0},{6,2},{8,12},{10,14},{12,8},{14,10},{16,20},{18,... | collective-permute-start | bytes 1327112 | tf_op jit(solution)/shard_map/ppermute | solution.py:1670
  39.2 17.2 %collective-permute-start.4 = (bf16[192,768]{1,0:T(8,128)(2,1)S(1)}, bf16[192,768]{1,0:T(8,128)(2,1)S(1)}, u32[]{:S(2)}, u32[]{:S(2)}) collective-permute-start(bf16[192,768]{1,0:T(8,128)(2,1)S(1)} %copy-done.2), channel_id=1, source_target_pairs={{0,1},{1,0},{2,3},{3,2},{4,5},{5,4},{6,7},{7,6},{8,9},{9,8},{10,11... | collective-permute-start | bytes 884744 | tf_op jit(solution)/shard_map/ppermute | solution.py:1664
  56.4 0.7 copy-start.10
  56.6 6.8 %collective-permute-start.6 = (bf16[3,384,384]{2,1,0:T(8,128)(2,1)S(1)}, bf16[3,384,384]{2,1,0:T(8,128)(2,1)}, u32[]{:S(2)}, u32[]{:S(2)}) collective-permute-start(bf16[3,384,384]{2,1,0:T(8,128)(2,1)S(1)} %pad_maximum_fusion.3), channel_id=1, source_target_pairs={{0,2},{2,0},{4,6},{6,4},{8,10},{10,8},{12,14},{14,12},{16,18},{18,... | collective-permute-start | bytes 2654216 | tf_op jit(solution)/shard_map/ppermute | solution.py:1667
  58.2 32.9 %collective-permute-start.8 = (bf16[768,768]{1,0:T(8,128)(2,1)S(1)}, bf16[768,768]{1,0:T(8,128)(2,1)}, u32[]{:S(2)}, u32[]{:S(2)}) collective-permute-start(bf16[768,768]{1,0:T(8,128)(2,1)S(1)} %constant_dynamic-slice_fusion.2), channel_id=1, source_target_pairs={{0,1},{1,0},{2,3},{3,2},{4,5},{5,4},{6,7},{7,6},{8,9},{9,8},{10,11... | collective-permute-start | bytes 3538952 | tf_op jit(solution)/shard_map/ppermute | solution.py:1664
  60.9 12.7 %collective-permute-start.5 = (bf16[192,768]{1,0:T(8,128)(2,1)S(1)}, bf16[192,768]{1,0:T(8,128)(2,1)}, u32[]{:S(2)}, u32[]{:S(2)}) collective-permute-start(bf16[192,768]{1,0:T(8,128)(2,1)S(1)} %collective-permute-done.4), channel_id=1, source_target_pairs={{0,2},{2,0},{4,6},{6,4},{8,10},{10,8},{12,14},{14,12},{16,18},{18,... | collective-permute-start | bytes 884744 | tf_op jit(solution)/shard_map/ppermute | solution.py:1667
  60.9 30.2 %collective-permute-start.7 = (bf16[192,1536]{1,0:T(8,128)(2,1)}, bf16[192,1536]{1,0:T(8,128)(2,1)}, u32[]{:S(2)}, u32[]{:S(2)}) collective-permute-start(bf16[192,1536]{1,0:T(8,128)(2,1)} %collective-permute-done.3.refs_9_), channel_id=1, source_target_pairs={{0,4},{2,6},{4,0},{6,2},{8,12},{10,14},{12,8},{14,10},{16,20},{18,... | collective-permute-start | bytes 1769480 | tf_op jit(solution)/shard_map/ppermute | solution.py:1670
  181.6 35.8 %collective-permute-start.12 = (bf16[12,16,768]{2,1,0:T(8,128)(2,1)}, bf16[12,16,768]{2,1,0:T(8,128)(2,1)S(1)}, u32[]{:S(2)}, u32[]{:S(2)}) collective-permute-start(bf16[12,16,768]{2,1,0:T(8,128)(2,1)} %get-tuple-element.136), channel_id=1, source_target_pairs={{0,24},{2,26},{4,28},{6,30},{8,16},{10,18},{12,20},{14,22},{16,8},... | collective-permute-start | bytes 884744 | tf_op jit(solution)/shard_map/ppermute | solution.py:1732
  184.1 33.3 %collective-permute-start.11 = (bf16[12,16,768]{2,1,0:T(8,128)(2,1)}, bf16[12,16,768]{2,1,0:T(8,128)(2,1)S(1)}, u32[]{:S(2)}, u32[]{:S(2)}) collective-permute-start(bf16[12,16,768]{2,1,0:T(8,128)(2,1)} %get-tuple-element.136), channel_id=1, source_target_pairs={{0,16},{2,18},{4,20},{6,22},{8,24},{10,26},{12,28},{14,30},{16,0},... | collective-permute-start | bytes 884744 | tf_op jit(solution)/shard_map/ppermute | solution.py:1732
  184.1 33.3 %collective-permute-start.10 = (bf16[12,16,768]{2,1,0:T(8,128)(2,1)}, bf16[12,16,768]{2,1,0:T(8,128)(2,1)S(1)}, u32[]{:S(2)}, u32[]{:S(2)}) collective-permute-start(bf16[12,16,768]{2,1,0:T(8,128)(2,1)} %get-tuple-element.136), channel_id=1, source_target_pairs={{0,8},{2,10},{4,12},{6,14},{8,0},{10,2},{12,4},{14,6},{16,24},{18,... | collective-permute-start | bytes 884744 | tf_op jit(solution)/shard_map/ppermute | solution.py:1732
  187.6 65.2 %collective-permute-start.14 = (bf16[256,1152]{1,0:T(8,128)(2,1)}, bf16[256,1152]{1,0:T(8,128)(2,1)}, u32[]{:S(2)}, u32[]{:S(2)}) collective-permute-start(bf16[256,1152]{1,0:T(8,128)(2,1)} %get-tuple-element.141), channel_id=1, source_target_pairs={{0,1},{1,0},{2,3},{3,2},{4,5},{5,4},{6,7},{7,6},{8,9},{9,8},{10,11... | collective-permute-start | bytes 1769480 | tf_op jit(solution)/shard_map/ppermute | solution.py:1664
  215.3 1.4 copy-start.11
  215.3 2.1 copy-start.3
  216.6 2.5 collective-permute-start.9
  217.8 1.5 copy-start
  219.5 33.3 %collective-permute-start.13 = (bf16[9,128,384]{2,1,0:T(8,128)(2,1)S(1)}, bf16[9,128,384]{2,1,0:T(8,128)(2,1)}, u32[]{:S(2)}, u32[]{:S(2)}) collective-permute-start(bf16[9,128,384]{2,1,0:T(8,128)(2,1)S(1)} %add_convert_fusion), channel_id=1, source_target_pairs={{0,1},{1,0},{2,3},{3,2},{4,5},{5,4},{6,7},{7,6},{8,9},{9,8},{10,11... | collective-permute-start | bytes 2654216 | tf_op jit(solution)/shard_map/ppermute | solution.py:1664
  221.4 29.6 %collective-permute-start.15 = (bf16[12,64,768]{2,1,0:T(8,128)(2,1)S(1)}, bf16[12,64,768]{2,1,0:T(8,128)(2,1)S(1)}, u32[]{:S(2)}, u32[]{:S(2)}) collective-permute-start(bf16[12,64,768]{2,1,0:T(8,128)(2,1)S(1)} %pad_maximum_fusion.2), channel_id=1, source_target_pairs={{0,4},{2,6},{4,0},{6,2},{8,12},{10,14},{12,8},{14,10},{16,20},{18,... | collective-permute-start | bytes 3538952 | tf_op jit(solution)/shard_map/ppermute | solution.py:1670
  245.9 62.3 %collective-permute-start.17 = (bf16[512,768]{1,0:T(8,128)(2,1)}, bf16[512,768]{1,0:T(8,128)(2,1)}, u32[]{:S(2)}, u32[]{:S(2)}) collective-permute-start(bf16[512,768]{1,0:T(8,128)(2,1)} %get-tuple-element.156), channel_id=1, source_target_pairs={{0,1},{1,0},{2,3},{3,2},{4,5},{5,4},{6,7},{7,6},{8,9},{9,8},{10,11... | collective-permute-start | bytes 2359304 | tf_op jit(solution)/shard_map/ppermute | solution.py:1664
  252.8 55.4 %collective-permute-start.16 = (bf16[12,128,768]{2,1,0:T(8,128)(2,1)}, bf16[12,128,768]{2,1,0:T(8,128)(2,1)}, u32[]{:S(2)}, u32[]{:S(2)}) collective-permute-start(bf16[12,128,768]{2,1,0:T(8,128)(2,1)} %pad_maximum_fusion.down_mine.up_mine), channel_id=1, source_target_pairs={{0,2},{2,0},{4,6},{6,4},{8,10},{10,8},{12,14},{14,12},{16,18},{18,... | collective-permute-start | bytes 7077896 | tf_op jit(solution)/shard_map/ppermute | solution.py:1667
  314.7 9.0 %copy-start.1 = (bf16[1024,768]{1,0:T(8,128)(2,1)S(1)}, bf16[1024,768]{1,0:T(8,128)(2,1)}, u32[]{:S(2)}) copy-start(bf16[1024,768]{1,0:T(8,128)(2,1)} %get-tuple-element.130) | copy-start | bytes 4718596

commit v10 on v9

--- a/solution.py
+++ b/solution.py
@@ -333,7 +333,9 @@
         for load in loads:
             load.start()
     else:
-        rows_ref, out_ref, grad_ref, dk_ref, dv_ref, bias_ref = refs
+        rows_hbm, out_ref, grad_ref, dk_ref, dv_ref, bias_ref, rows_ref, load_sem = refs
+        load_rows = pltpu.make_async_copy(rows_hbm, rows_ref, load_sem.at[0])
+        load_rows.start()
     pairs = q_ref.shape[1] // LANES
     lanes = [slice(p * LANES, (p + 1) * LANES) for p in range(pairs)]
     dk_ref[...] = jnp.zeros_like(dk_ref)
@@ -466,6 +468,7 @@
         give_ref[...] = total
         low_ref[...] = total.astype(bf16)
     else:
+        load_rows.wait()
         lax.fori_loop(0, rows_ref.shape[0] // ROW_TILE, weight_rows, 0)
 
 
@@ -499,12 +502,12 @@
         ]
     else:
         second = [shape((3, rest[0].shape[0], cols), bf16)]
-        scratch = []
+        scratch = [pltpu.VMEM(rest[0].shape, bf16), pltpu.SemaphoreType.DMA((1,))]
     return pl.pallas_call(
         functools.partial(backward_kernel, giving),
         in_specs=[pl.BlockSpec(memory_space=pltpu.SMEM)]
         + [vmem] * 10
-        + [hbm if giving else vmem] * len(rest),
+        + [hbm] * len(rest),
         out_specs=[vmem] * (1 + len(second)),
         scratch_shapes=[
             pltpu.VMEM((count, cols), f32),
@@ -1147,9 +1150,9 @@
         d2_hbm,
         w_hbm,
         w2_hbm,
-        tokens_ref,
-        context_ref,
-        given_ref,
+        tokens_hbm,
+        context_hbm,
+        given_hbm,
         small_ref,
         small2_ref,
         gqkv_ref,
@@ -1163,6 +1166,9 @@
         d2_ref,
         w_ref,
         w2_ref,
+        tokens_ref,
+        context_ref,
+        given_ref,
         load_sem,
         rows_ref,
         give_ref,
@@ -1188,6 +1194,9 @@
                 (w_hbm, w_ref),
                 (w2_hbm, w2_ref),
                 (d2_hbm, d2_ref),
+                (tokens_hbm, tokens_ref),
+                (context_hbm, context_ref),
+                (given_hbm, given_ref),
             )
         )
     ]
@@ -1295,7 +1304,7 @@
         return pl.ds(pl.multiple_of(b * TILE, TILE), TILE)
 
     def ready():
-        for load in loads[2:5]:
+        for load in loads[2:]:
             load.wait()
 
     def give_edges():
@@ -1453,7 +1462,7 @@
     shape = jax.ShapeDtypeStruct
     return pl.pallas_call(
         functools.partial(leave_kernel, exchange),
-        in_specs=[hbm] + [vmem] * 3 + [hbm] * 4 + [vmem] * 5,
+        in_specs=[hbm] + [vmem] * 3 + [hbm] * 7 + [vmem] * 2,
         out_specs=[vmem] * 2 + [hbm, vmem],
         out_shape=[
             shape(weights[0].shape, bf16),
@@ -1469,7 +1478,10 @@
             pltpu.VMEM(d_fields[1].shape, bf16),
             pltpu.VMEM(weights[0].shape, bf16),
             pltpu.VMEM(weights[1].shape, bf16),
-            pltpu.SemaphoreType.DMA((5,)),
+            pltpu.VMEM(tokens.shape, bf16),
+            pltpu.VMEM(context.shape, bf16),
+            pltpu.VMEM(given.shape, f32),
+            pltpu.SemaphoreType.DMA((8,)),
             pltpu.VMEM((KEY_ROWS, width), f32),
             pltpu.VMEM((2 * EDGE, width), bf16),
             pltpu.VMEM((2 * EDGE, width), bf16),

time: 326 us -> 322 us (0.988)
  Pallas kernels: 254 us -> 246 us
    ppermute x8, starting transfers between devices: 16.6 us -> 23.7 us  [across(): return lax.ppermute(array, 'mp', [(0, 1), (1, 0)])]
    ppermute x3, starting transfers between devices: 7.41 us -> 2.82 us  [beside(): return lax.ppermute(array, 'dp', [(i, i ^ 2) for i in range(dp_size)])]
  transfers between devices with their start and end apart: 18 -> 18, of which waited for: 3 -> 3; matrix products, arithmetic and copies ran while one was open for 8% -> 9% of each run, Pallas kernels for 46% -> 44%
where the time goes in v10:
time: 322 us; the launch traced here: 319 us
  Pallas kernels  246 us (76%)
  starting transfers between devices  31.1 us (10%)
  other arithmetic  16.1 us (5%)
  local copies, waits for them, and re-layouts  15 us (5%)
  waiting for transfers between devices  8.53 us (3%)
    pallas_call x1, Pallas kernels, middle(): pl.pallas_call(functools.partial(middle_kernel, exchanges, tiles), in_spe...  89.8 us
    pallas_call x1, Pallas kernels, leave(): pl.pallas_call(functools.partial(leave_kernel, exchange), in_specs=[hbm]...  50.1 us
    pallas_call x2, Pallas kernels, attend_backward(): pl.pallas_call(functools.partial(backward_kernel, giving), in_specs=[pl.B...  42.9 us
    pallas_call x2, Pallas kernels, attend_forward(): pl.pallas_call(forward_kernel, in_specs=[pl.BlockSpec(memory_space=pltpu....  29.2 us
    ppermute x8, starting transfers between devices, across(): return lax.ppermute(array, 'mp', [(0, 1), (1, 0)])  23.7 us
    pallas_call x1, Pallas kernels, enter(): pl.pallas_call(enter_kernel, in_specs=[vmem] * 6, out_specs=[vmem] * 5, o...  11.4 us
    pallas_call x1, Pallas kernels, assemble(): pl.pallas_call(assemble_kernel, grid_spec=pltpu.PrefetchScalarGridSpec(nu...  9 us
    pallas_call x1, Pallas kernels, project(): pl.pallas_call(project_kernel, grid=(3,), in_specs=[row_spec, pl.BlockSpe...  7.36 us
  transfers between devices with their start and end apart: 18, of which 3 were waited for; matrix products, arithmetic and copies ran while one was open for 9% of the time, Pallas kernels for 44%

profile of v10, /device:TPU:0, one launch (start us, length us, event | category | flops | bytes accessed | tf_op | source)
XLA Modules:
  0.0 318.9 jit_solution(13296815160234867931)
XLA Ops:
  0.7 1.3 slice_bitcast_fusion
  2.0 0.8 select_bitcast_fusion
  2.8 3.0 collective-permute-start
  6.5 0.2 reduce-window.8
  6.8 0.1 fusion.2
  6.9 0.2 reduce_min.21
  7.1 0.1 copy.31
  7.2 0.1 subtract_convert_fusion
  7.3 0.3 fusion.16
  7.6 0.1 copy.35
  7.7 0.7 pad_add_fusion.1.span_ref
  8.4 0.6 pad_add_fusion.noisy_ref
  9.0 0.6 add_add_fusion.clean_ref
  9.6 0.7 constant_dynamic-slice_fusion.1
  10.3 1.1 dynamic-slice_bitcast_fusion
  11.4 1.4 constant_dynamic-slice_fusion.2
  12.7 0.6 stack.29.vectors_ref.refs_6_
  13.4 1.1 constant_dynamic-slice_fusion.3
  14.5 4.4 %fusion = (f32[1584,128]{1,0:T(8,128)}, f32[1584,128]{1,0:T(8,128)}) fusion(f32[128]{0:T(128)S(1)} %get-tuple-element.207, f32[128]{0:T(128)S(1)} %get-tuple-element.208, f32[1584]{0:T(1024)S(1)} %get-tuple-element.201), kind=kLoop, calls=%fused_computation.11 | loop fusion | flops 405504 | bytes 1629376 | tf_op jit(solution)/shard_map/mul | solution.py:1638
  18.9 5.1 %collective-permute-done.context_ref.refs_9_ = bf16[528,768]{1,0:T(8,128)(2,1)} collective-permute-done((bf16[528,768]{1,0:T(8,128)(2,1)S(1)}, bf16[528,768]{1,0:T(8,128)(2,1)}, u32[]{:S(2)}, u32[]{:S(2)}) %collective-permute-start) | collective-permute-done | bytes 811040 | tf_op jit(solution)/shard_map/ppermute | solution.py:1676
  24.0 1.7 collective-permute-start.1
  25.7 0.3 collective-permute-start.3
  26.0 11.4 %enter.1 = (bf16[1584,768]{1,0:T(8,128)(2,1)}, bf16[768,1584]{1,0:T(8,128)(2,1)}, bf16[1584,384]{1,0:T(8,128)(2,1)}, bf16[1584,384]{1,0:T(8,128)(2,1)}, bf16[1584,384]{1,0:T(8,128)(2,1)}) custom-call(bf16[2,512,768]{2,1,0:T(8,128)(2,1)} %tokens_ref.1, bf16[528,768]{1,0:T(8,128)(2,1)} %collective-permute-done.context_ref.refs_9_, ...), custom_call_target="tpu_custom_call" | custom-call | flops 10000000000 | bytes 16000000 | tf_op jit(solution)/shard_map/enter/pallas_call | solution.py:157
  37.5 1.7 collective-permute-start.2
  39.2 1.5 collective-permute-start.4
  40.7 14.6 %attend_forward.2 = (bf16[1024,384]{1,0:T(8,128)(2,1)}, f32[3,4,2,256]{3,2,1,0:T(2,128)}) custom-call(s32[4,2]{1,0:T(4,128)} %pad_add_fusion.1.span_ref, s32[4,2,256]{2,1,0:T(2,128)} %add_add_fusion.clean_ref, s32[4,2,128]{2,1,0:T(2,128)} %pad_add_fusion.noisy_ref, bf16[1584,384]{1,0:T(8,128)(2,1)} %get-tuple-element.101.q_ref, ...), custom_call_target="tpu_custom_call" | custom-call | flops 1610612736 | bytes 4866048 | tf_op jit(solution)/shard_map/attend_forward/pallas_call | solution.py:290
  55.6 0.4 copy-done.10
  56.0 0.6 reshape.345.refs_7_
  56.6 0.6 pad.5.clone
  57.2 5.8 %collective-permute-start.8 = (bf16[768,768]{1,0:T(8,128)(2,1)S(1)}, bf16[768,768]{1,0:T(8,128)(2,1)}, u32[]{:S(2)}, u32[]{:S(2)}) collective-permute-start(bf16[768,768]{1,0:T(8,128)(2,1)S(1)} %constant_dynamic-slice_fusion.2), channel_id=1, source_target_pairs={{0,1},{1,0},{2,3},{3,2},{4,5},{5,4},{6,7},{7,6},{8,9},{9,8},{10,11... | collective-permute-start | bytes 3538952 | tf_op jit(solution)/shard_map/ppermute | solution.py:1676
  63.0 0.3 collective-permute-start.7
  63.3 1.5 broadcast_select_fusion.3
  64.8 1.4 pad_maximum_fusion.1.w_ref.refs_2_.refs_7_
  66.3 7.4 %project.1 = (bf16[1584,384]{1,0:T(8,128)(2,1)}, bf16[1584,384]{1,0:T(8,128)(2,1)}, bf16[1584,384]{1,0:T(8,128)(2,1)}) custom-call(bf16[1584,768]{1,0:T(8,128)(2,1)} %get-tuple-element.109.rows_ref, bf16[3,768,384]{2,1,0:T(8,128)(2,1)} %pad_maximum_fusion.1.w_ref.refs_2_.refs_7_, f32[1584,128]{1,0:T(8,128)} %get-tuple-element.96.cos_ref, ...), custom_call_target="tpu_custom_call" | custom-call | flops 2802843648 | bytes 7852032 | tf_op jit(solution)/shard_map/project/pallas_call | solution.py:78
  73.6 1.0 broadcast_select_fusion.13
  74.6 0.9 pad_maximum_fusion.5.refs_4_
  75.5 14.6 %attend_forward.3 = (bf16[1024,384]{1,0:T(8,128)(2,1)}, f32[3,4,2,256]{3,2,1,0:T(2,128)}) custom-call(s32[4,2]{1,0:T(4,128)} %pad_add_fusion.1.span_ref, s32[4,2,256]{2,1,0:T(2,128)} %add_add_fusion.clean_ref, s32[4,2,128]{2,1,0:T(2,128)} %pad_add_fusion.noisy_ref, bf16[1584,384]{1,0:T(8,128)(2,1)} %get-tuple-element.120.q_ref, ...), custom_call_target="tpu_custom_call" | custom-call | flops 1610612736 | bytes 4866048 | tf_op jit(solution)/shard_map/attend_forward/pallas_call | solution.py:290
  90.1 89.8 %middle.1 = (bf16[1024,768]{1,0:T(8,128)(2,1)}, f32[1024,768]{1,0:T(8,128)}, bf16[1024,384]{1,0:T(8,128)(2,1)}, bf16[1024,384]{1,0:T(8,128)(2,1)}, bf16[256,1152...) custom-call(bf16[1024,768]{1,0:T(8,128)(2,1)} %bitcast.30, ...), custom_call_target="tpu_custom_call" | custom-call | flops 60000002048 | bytes 40000000 | tf_op jit(solution)/shard_map/middle/pallas_call | solution.py:1092
  179.9 2.5 collective-permute-start.12
  182.5 1.9 collective-permute-start.10
  184.4 0.7 slice.53
  185.1 0.7 slice_reduce_fusion
  185.9 0.7 collective-permute-start.14
  186.6 22.5 %attend_backward.2 = (bf16[3,1584,384]{2,1,0:T(8,128)(2,1)}, bf16[3,768,384]{2,1,0:T(8,128)(2,1)}) custom-call(s32[4,2]{1,0:T(4,128)} %pad_add_fusion.1.span_ref, s32[4,2,256]{2,1,0:T(2,128)} %add_add_fusion.clean_ref, s32[4,2,128]{2,1,0:T(2,128)} %pad_add_fusion.noisy_ref, bf16[1584,384]{1,0:T(8,128)(2,1)} %get-tuple-element.120.q_ref, ...), custom_call_target="tpu_custom_call" | custom-call | flops 35999997952 | bytes 36000000 | tf_op jit(solution)/shard_map/attend_backward/pallas_call | solution.py:506
  209.1 1.3 constant_dynamic-slice_fusion
  210.5 0.7 fusion.4
  211.4 0.3 broadcast_select_fusion.5
  211.7 1.2 collective-permute-done.9
  212.9 0.2 copy-done
  213.1 0.3 add_convert_fusion
  213.4 5.9 %collective-permute-start.13 = (bf16[9,128,384]{2,1,0:T(8,128)(2,1)S(1)}, bf16[9,128,384]{2,1,0:T(8,128)(2,1)}, u32[]{:S(2)}, u32[]{:S(2)}) collective-permute-start(bf16[9,128,384]{2,1,0:T(8,128)(2,1)S(1)} %add_convert_fusion), channel_id=1, source_target_pairs={{0,1},{1,0},{2,3},{3,2},{4,5},{5,4},{6,7},{7,6},{8,9},{9,8},{10,11... | collective-permute-start | bytes 2654216 | tf_op jit(solution)/shard_map/ppermute | solution.py:1676
  219.3 0.8 collective-permute-start.15
  220.1 20.4 %attend_backward.3 = (bf16[3,1584,384]{2,1,0:T(8,128)(2,1)}, f32[512,768]{1,0:T(8,128)}, bf16[512,768]{1,0:T(8,128)(2,1)}) custom-call(s32[4,2]{1,0:T(4,128)} %pad_add_fusion.1.span_ref, s32[4,2,256]{2,1,0:T(2,128)} %add_add_fusion.clean_ref, s32[4,2,128]{2,1,0:T(2,128)} %pad_add_fusion.noisy_ref, bf16[1584,384]{1,0:T(8,128)(2,1)} %get-tuple-element.101.q_ref, ...), custom_call_target="tpu_custom_call" | custom-call | flops 35999997952 | bytes 36000000 | tf_op jit(solution)/shard_map/attend_backward/pallas_call | solution.py:506
  240.5 4.7 %collective-permute-start.17 = (bf16[512,768]{1,0:T(8,128)(2,1)}, bf16[512,768]{1,0:T(8,128)(2,1)}, u32[]{:S(2)}, u32[]{:S(2)}) collective-permute-start(bf16[512,768]{1,0:T(8,128)(2,1)} %get-tuple-element.156), channel_id=1, source_target_pairs={{0,1},{1,0},{2,3},{3,2},{4,5},{5,4},{6,7},{7,6},{8,9},{9,8},{10,11... | collective-permute-start | bytes 2359304 | tf_op jit(solution)/shard_map/ppermute | solution.py:1676
  245.2 2.1 collective-permute-done.15
  247.3 0.2 broadcast_select_fusion.1
  247.5 1.6 pad_maximum_fusion.down_mine.up_mine
  249.2 50.1 %leave.1 = (bf16[3,768,384]{2,1,0:T(8,128)(2,1)}, bf16[384,768]{1,0:T(8,128)(2,1)}, f32[1024,768]{1,0:T(8,128)}, f32[16,768]{1,0:T(8,128)}) custom-call(bf16[768,1584]{1,0:T(8,128)(2,1)} %get-tuple-element.131.refs_0_, bf16[256,1152]{1,0:T(8,128)(2,1)} %get-tuple-element.132.refs_1_, bf16[9,128,384]{2,1,0:T(8,128)(2,1)} %collective-permute-done.13.refs_2_, ...), custom_call_target="tpu_custom_call" | custom-call | flops 40000000000 | bytes 40000000 | tf_op jit(solution)/shard_map/leave/pallas_call | solution.py:1463
  299.2 0.7 slice.58
  300.0 0.6 reshape.343
  300.6 1.6 slice_reduce_fusion.2
  302.2 6.6 %finish.1 = f32[1024,768]{1,0:T(8,128)} custom-call(f32[1024,768]{1,0:T(8,128)} %get-tuple-element.154.rows_ref, bf16[512,768]{1,0:T(8,128)(2,1)} %collective-permute-done.17.got_ref, bf16[1024,768]{1,0:T(8,128)(2,1)} %bitcast.32, f32[5,768]{1,0:T(8,128)} %stack.29.vectors_ref.refs_6_, f32[1024,768]{1,0:T(8,128)} %get-tuple-element.159.dmid_ref), custom_call_target="tpu_custom_call" | custom-call | flops 10000000 | bytes 12000000 | tf_op jit(solution)/shard_map/finish/pallas_call | solution.py:1525
  308.7 9.0 %assemble.1 = (f32[1536,768]{1,0:T(8,128)}, f32[768,1536]{1,0:T(8,128)}, f32[2304,384]{1,0:T(8,128)}, f32[384,768]{1,0:T(8,128)}) custom-call(s32[1]{0:T(128)} %bitcast.18.core_ref, bf16[12,128,768]{2,1,0:T(8,128)(2,1)} %pad_maximum_fusion.down_mine.up_mine, bf16[12,128,768]{2,1,0:T(8,128)(2,1)} %pad_maximum_fusion.down_mine.up_mine, ...), custom_call_target="tpu_custom_call" | custom-call | flops 1000000 | bytes 14000000 | tf_op jit(solution)/shard_map/assemble/pallas_call | solution.py:1573
  317.7 1.1 copy.38
  (65 shorter events, 0.8 us)
Async XLA Ops:
  0.6 5.8 %copy-start.12 = (s32[1,4]{1,0:T(1,128)S(1)}, s32[1,4]{1,0:T(1,128)}, u32[]{:S(2)}) copy-start(s32[1,4]{1,0:T(1,128)} %param.15) | copy-start | bytes 52
  0.7 6.0 %copy-start.5 = (f32[768]{0:T(1024)S(1)}, f32[768]{0:T(1024)}, u32[]{:S(2)}) copy-start(f32[768]{0:T(1024)} %param.18) | copy-start | bytes 9220
  0.7 6.0 %copy-start.6 = (f32[768]{0:T(1024)S(1)}, f32[768]{0:T(1024)}, u32[]{:S(2)}) copy-start(f32[768]{0:T(1024)} %param.19) | copy-start | bytes 9220
  0.7 6.0 %copy-start.7 = (f32[768]{0:T(1024)S(1)}, f32[768]{0:T(1024)}, u32[]{:S(2)}) copy-start(f32[768]{0:T(1024)} %param.22) | copy-start | bytes 9220
  0.7 6.1 %copy-start.8 = (f32[768]{0:T(1024)S(1)}, f32[768]{0:T(1024)}, u32[]{:S(2)}) copy-start(f32[768]{0:T(1024)} %param.23) | copy-start | bytes 9220
  0.7 6.1 %copy-start.9 = (f32[768]{0:T(1024)S(1)}, f32[768]{0:T(1024)}, u32[]{:S(2)}) copy-start(f32[768]{0:T(1024)} %param.27) | copy-start | bytes 9220
  0.7 8.9 %copy-start.4 = (bf16[384,768]{1,0:T(8,128)(2,1)S(1)}, bf16[384,768]{1,0:T(8,128)(2,1)}, u32[]{:S(2)}) copy-start(bf16[384,768]{1,0:T(8,128)(2,1)} %refs_3_.1) | copy-start | bytes 1769476
  2.8 21.2 %collective-permute-start = (bf16[528,768]{1,0:T(8,128)(2,1)S(1)}, bf16[528,768]{1,0:T(8,128)(2,1)}, u32[]{:S(2)}, u32[]{:S(2)}) collective-permute-start(bf16[528,768]{1,0:T(8,128)(2,1)S(1)} %pad_maximum_fusion.4), channel_id=1, source_target_pairs={{0,1},{1,0},{2,3},{3,2},{4,5},{5,4},{6,7},{7,6},{8,9},{9,8},{10,11... | collective-permute-start | bytes 2433032 | tf_op jit(solution)/shard_map/ppermute | solution.py:1676
  24.0 13.5 %collective-permute-start.1 = (bf16[3,192,384]{2,1,0:T(8,128)(2,1)S(1)}, bf16[3,192,384]{2,1,0:T(8,128)(2,1)S(1)}, u32[]{:S(2)}, u32[]{:S(2)}) collective-permute-start(bf16[3,192,384]{2,1,0:T(8,128)(2,1)S(1)} %dynamic-slice_bitcast_fusion), channel_id=1, source_target_pairs={{0,1},{1,0},{2,3},{3,2},{4,5},{5,4},{6,7},{7,6},{8,9},{9,8},{10,11... | collective-permute-start | bytes 1327112 | tf_op jit(solution)/shard_map/ppermute | solution.py:1676
  25.7 29.6 %collective-permute-start.3 = (bf16[192,1536]{1,0:T(8,128)(2,1)S(1)}, bf16[192,1536]{1,0:T(8,128)(2,1)}, u32[]{:S(2)}, u32[]{:S(2)}) collective-permute-start(bf16[192,1536]{1,0:T(8,128)(2,1)S(1)} %constant_dynamic-slice_fusion.3), channel_id=1, source_target_pairs={{0,1},{1,0},{2,3},{3,2},{4,5},{5,4},{6,7},{7,6},{8,9},{9,8},{10,11... | collective-permute-start | bytes 1769480 | tf_op jit(solution)/shard_map/ppermute | solution.py:1676
  26.0 13.2 %copy-start.2 = (bf16[192,768]{1,0:T(8,128)(2,1)S(1)}, bf16[192,768]{1,0:T(8,128)(2,1)}, u32[]{:S(2)}) copy-start(bf16[192,768]{1,0:T(8,128)(2,1)} %constant_dynamic-slice_fusion.1) | copy-start | bytes 884740
  37.5 17.9 %collective-permute-start.2 = (bf16[3,192,384]{2,1,0:T(8,128)(2,1)S(1)}, bf16[3,192,384]{2,1,0:T(8,128)(2,1)S(1)}, u32[]{:S(2)}, u32[]{:S(2)}) collective-permute-start(bf16[3,192,384]{2,1,0:T(8,128)(2,1)S(1)} %collective-permute-done.1), channel_id=1, source_target_pairs={{0,4},{2,6},{4,0},{6,2},{8,12},{10,14},{12,8},{14,10},{16,20},{18,... | collective-permute-start | bytes 1327112 | tf_op jit(solution)/shard_map/ppermute | solution.py:1682
  39.2 16.1 %collective-permute-start.4 = (bf16[192,768]{1,0:T(8,128)(2,1)S(1)}, bf16[192,768]{1,0:T(8,128)(2,1)S(1)}, u32[]{:S(2)}, u32[]{:S(2)}) collective-permute-start(bf16[192,768]{1,0:T(8,128)(2,1)S(1)} %copy-done.2), channel_id=1, source_target_pairs={{0,1},{1,0},{2,3},{3,2},{4,5},{5,4},{6,7},{7,6},{8,9},{9,8},{10,11... | collective-permute-start | bytes 884744 | tf_op jit(solution)/shard_map/ppermute | solution.py:1676
  55.3 0.7 copy-start.10
  55.5 7.8 %collective-permute-start.6 = (bf16[3,384,384]{2,1,0:T(8,128)(2,1)S(1)}, bf16[3,384,384]{2,1,0:T(8,128)(2,1)}, u32[]{:S(2)}, u32[]{:S(2)}) collective-permute-start(bf16[3,384,384]{2,1,0:T(8,128)(2,1)S(1)} %pad_maximum_fusion.3), channel_id=1, source_target_pairs={{0,2},{2,0},{4,6},{6,4},{8,10},{10,8},{12,14},{14,12},{16,18},{18,... | collective-permute-start | bytes 2654216 | tf_op jit(solution)/shard_map/ppermute | solution.py:1679
  57.2 32.9 %collective-permute-start.8 = (bf16[768,768]{1,0:T(8,128)(2,1)S(1)}, bf16[768,768]{1,0:T(8,128)(2,1)}, u32[]{:S(2)}, u32[]{:S(2)}) collective-permute-start(bf16[768,768]{1,0:T(8,128)(2,1)S(1)} %constant_dynamic-slice_fusion.2), channel_id=1, source_target_pairs={{0,1},{1,0},{2,3},{3,2},{4,5},{5,4},{6,7},{7,6},{8,9},{9,8},{10,11... | collective-permute-start | bytes 3538952 | tf_op jit(solution)/shard_map/ppermute | solution.py:1676
  63.0 10.6 %collective-permute-start.5 = (bf16[192,768]{1,0:T(8,128)(2,1)S(1)}, bf16[192,768]{1,0:T(8,128)(2,1)}, u32[]{:S(2)}, u32[]{:S(2)}) collective-permute-start(bf16[192,768]{1,0:T(8,128)(2,1)S(1)} %collective-permute-done.4), channel_id=1, source_target_pairs={{0,2},{2,0},{4,6},{6,4},{8,10},{10,8},{12,14},{14,12},{16,18},{18,... | collective-permute-start | bytes 884744 | tf_op jit(solution)/shard_map/ppermute | solution.py:1679
  63.0 27.1 %collective-permute-start.7 = (bf16[192,1536]{1,0:T(8,128)(2,1)}, bf16[192,1536]{1,0:T(8,128)(2,1)}, u32[]{:S(2)}, u32[]{:S(2)}) collective-permute-start(bf16[192,1536]{1,0:T(8,128)(2,1)} %collective-permute-done.3.refs_9_), channel_id=1, source_target_pairs={{0,4},{2,6},{4,0},{6,2},{8,12},{10,14},{12,8},{14,10},{16,20},{18,... | collective-permute-start | bytes 1769480 | tf_op jit(solution)/shard_map/ppermute | solution.py:1682
  179.9 31.3 %collective-permute-start.12 = (bf16[12,16,768]{2,1,0:T(8,128)(2,1)}, bf16[12,16,768]{2,1,0:T(8,128)(2,1)S(1)}, u32[]{:S(2)}, u32[]{:S(2)}) collective-permute-start(bf16[12,16,768]{2,1,0:T(8,128)(2,1)} %get-tuple-element.136), channel_id=1, source_target_pairs={{0,24},{2,26},{4,28},{6,30},{8,16},{10,18},{12,20},{14,22},{16,8},... | collective-permute-start | bytes 884744 | tf_op jit(solution)/shard_map/ppermute | solution.py:1744
  182.5 28.8 %collective-permute-start.11 = (bf16[12,16,768]{2,1,0:T(8,128)(2,1)}, bf16[12,16,768]{2,1,0:T(8,128)(2,1)S(1)}, u32[]{:S(2)}, u32[]{:S(2)}) collective-permute-start(bf16[12,16,768]{2,1,0:T(8,128)(2,1)} %get-tuple-element.136), channel_id=1, source_target_pairs={{0,16},{2,18},{4,20},{6,22},{8,24},{10,26},{12,28},{14,30},{16,0},... | collective-permute-start | bytes 884744 | tf_op jit(solution)/shard_map/ppermute | solution.py:1744
  182.5 28.8 %collective-permute-start.10 = (bf16[12,16,768]{2,1,0:T(8,128)(2,1)}, bf16[12,16,768]{2,1,0:T(8,128)(2,1)S(1)}, u32[]{:S(2)}, u32[]{:S(2)}) collective-permute-start(bf16[12,16,768]{2,1,0:T(8,128)(2,1)} %get-tuple-element.136), channel_id=1, source_target_pairs={{0,8},{2,10},{4,12},{6,14},{8,0},{10,2},{12,4},{14,6},{16,24},{18,... | collective-permute-start | bytes 884744 | tf_op jit(solution)/shard_map/ppermute | solution.py:1744
  185.9 63.3 %collective-permute-start.14 = (bf16[256,1152]{1,0:T(8,128)(2,1)}, bf16[256,1152]{1,0:T(8,128)(2,1)}, u32[]{:S(2)}, u32[]{:S(2)}) collective-permute-start(bf16[256,1152]{1,0:T(8,128)(2,1)} %get-tuple-element.141), channel_id=1, source_target_pairs={{0,1},{1,0},{2,3},{3,2},{4,5},{5,4},{6,7},{7,6},{8,9},{9,8},{10,11... | collective-permute-start | bytes 1769480 | tf_op jit(solution)/shard_map/ppermute | solution.py:1676
  209.1 1.4 copy-start.11
  209.1 2.1 copy-start.3
  210.4 2.5 collective-permute-start.9
  211.6 1.5 copy-start
  213.4 35.8 %collective-permute-start.13 = (bf16[9,128,384]{2,1,0:T(8,128)(2,1)S(1)}, bf16[9,128,384]{2,1,0:T(8,128)(2,1)}, u32[]{:S(2)}, u32[]{:S(2)}) collective-permute-start(bf16[9,128,384]{2,1,0:T(8,128)(2,1)S(1)} %add_convert_fusion), channel_id=1, source_target_pairs={{0,1},{1,0},{2,3},{3,2},{4,5},{5,4},{6,7},{7,6},{8,9},{9,8},{10,11... | collective-permute-start | bytes 2654216 | tf_op jit(solution)/shard_map/ppermute | solution.py:1676
  219.3 28.1 %collective-permute-start.15 = (bf16[12,64,768]{2,1,0:T(8,128)(2,1)S(1)}, bf16[12,64,768]{2,1,0:T(8,128)(2,1)S(1)}, u32[]{:S(2)}, u32[]{:S(2)}) collective-permute-start(bf16[12,64,768]{2,1,0:T(8,128)(2,1)S(1)} %pad_maximum_fusion.2), channel_id=1, source_target_pairs={{0,4},{2,6},{4,0},{6,2},{8,12},{10,14},{12,8},{14,10},{16,20},{18,... | collective-permute-start | bytes 3538952 | tf_op jit(solution)/shard_map/ppermute | solution.py:1682
  240.5 61.7 %collective-permute-start.17 = (bf16[512,768]{1,0:T(8,128)(2,1)}, bf16[512,768]{1,0:T(8,128)(2,1)}, u32[]{:S(2)}, u32[]{:S(2)}) collective-permute-start(bf16[512,768]{1,0:T(8,128)(2,1)} %get-tuple-element.156), channel_id=1, source_target_pairs={{0,1},{1,0},{2,3},{3,2},{4,5},{5,4},{6,7},{7,6},{8,9},{9,8},{10,11... | collective-permute-start | bytes 2359304 | tf_op jit(solution)/shard_map/ppermute | solution.py:1676
  249.2 53.0 %collective-permute-start.16 = (bf16[12,128,768]{2,1,0:T(8,128)(2,1)}, bf16[12,128,768]{2,1,0:T(8,128)(2,1)}, u32[]{:S(2)}, u32[]{:S(2)}) collective-permute-start(bf16[12,128,768]{2,1,0:T(8,128)(2,1)} %pad_maximum_fusion.down_mine.up_mine), channel_id=1, source_target_pairs={{0,2},{2,0},{4,6},{6,4},{8,10},{10,8},{12,14},{14,12},{16,18},{18,... | collective-permute-start | bytes 7077896 | tf_op jit(solution)/shard_map/ppermute | solution.py:1679
  308.7 9.0 %copy-start.1 = (bf16[1024,768]{1,0:T(8,128)(2,1)S(1)}, bf16[1024,768]{1,0:T(8,128)(2,1)}, u32[]{:S(2)}) copy-start(bf16[1024,768]{1,0:T(8,128)(2,1)} %get-tuple-element.130) | copy-start | bytes 4718596
